TPU v7x, 32 devices: a whole 2x2x4 slice. The times are simulated.
32 devices in a mesh: batch: 4 (over z), seq: 2 (over core), ch: 4 (over y, x).
Axes of the slice: x: 2, y: 2, z: 4, core: 2. Of those that a mesh axis runs over, the one named last changes fastest.
Arguments:
- inputs: bfloat16 [16, 1280, 2048], P('batch', 'ch', 'seq'), may hold values from -6 to 6
- segment_ids: int32 [16, 2048], P('batch', 'seq'), may hold values from 0 to 7, never falling along the last dimension, each value on 1 to 512 neighbouring positions
- norm0_gain: float32 [1280], P('ch'), may hold values from 0.1 to 1.9
- norm0_shift: float32 [1280], P('ch'), may hold values from -3 to 3
- w_inner: bfloat16 [1280, 640], P('ch'), may hold values from -0.15625 to 0.15625
- b_inner: float32 [640], P('ch'), may hold values from -3 to 3
- norm1_gain: float32 [640], P('ch'), may hold values from 0.1 to 1.9
- norm1_shift: float32 [640], P('ch'), may hold values from -3 to 3
- w_conv: bfloat16 [5, 640, 640], P(None, 'ch'), may hold values from -0.109375 to 0.109375
- b_conv: float32 [640], P('ch'), may hold values from -3 to 3
- norm2_gain: float32 [640], P('ch'), may hold values from 0.1 to 1.9
- norm2_shift: float32 [640], P('ch'), may hold values from -3 to 3
- w_outer: bfloat16 [640, 1280], P('ch'), may hold values from -0.25 to 0.25
- b_outer: float32 [1280], P('ch'), may hold values from -3 to 3
- cotangent: bfloat16 [16, 1280, 2048], P('batch', 'ch', 'seq'), may hold values from -6 to 6
Outputs:
- output: bfloat16 [16, 1280, 2048], P('batch', 'ch', 'seq')
- input_grad: bfloat16 [16, 1280, 2048], P('batch', 'ch', 'seq')
- grad_norm0_gain: float32 [1280], P('ch')
- grad_norm0_shift: float32 [1280], P('ch')
- grad_w_inner: float32 [1280, 640], P('ch')
- grad_b_inner: float32 [640], P('ch')
- grad_norm1_gain: float32 [640], P('ch')
- grad_norm1_shift: float32 [640], P('ch')
- grad_w_conv: float32 [5, 640, 640], P(None, 'ch')
- grad_b_conv: float32 [640], P('ch')
- grad_norm2_gain: float32 [640], P('ch')
- grad_norm2_shift: float32 [640], P('ch')
- grad_w_outer: float32 [640, 1280], P('ch')
- grad_b_outer: float32 [1280], P('ch')
Inputs may be any that keep to these rules, and one draw needn't show every extreme that they name: `segment_ids`: along a row the ids never fall; each protein is one run of 1 to 512 residues, one run of each row has exactly 512, and every row holds all 8 ids.
All inputs are finite; a program needn't handle non-finite values.
Results may differ from a plain program's by a relative error of at most 0.0065.
Values may be sent and summed in bfloat16 or wider, within the bound.
A program may use at most 192 MiB of HBM per device.

v0:
```python
import functools
import math

import jax
import jax.numpy as jnp
from jax import lax
from jax.experimental import pallas as pl
from jax.experimental.pallas import tpu as pltpu
from jax.sharding import PartitionSpec as P

KERNEL_TAPS = 5
DILATION_SPACING = 32


EPSILON = 1e-05


MESH_AXES = ("batch", "seq", "ch")
MESH_ID = pl.DeviceIdType.MESH


def _group_index(group, sizes, coords):
    me = 0
    for a in group:
        me = me * sizes[a] + coords[a]
    return me


def _exchange_kernel(sizes, group, gather, count_arrays, *refs):
    x_refs = refs[:count_arrays]
    o_refs = refs[count_arrays : 2 * count_arrays]
    send_sem, recv_sem = refs[2 * count_arrays :]
    coords = {a: lax.axis_index(a) for a in MESH_AXES}
    me = _group_index(group, sizes, coords)
    count = math.prod(sizes[a] for a in group)

    def device(index):
        where = dict(coords)
        rest = index
        for a in reversed(group):
            where[a] = lax.rem(rest, sizes[a])
            rest = rest // sizes[a]
        return tuple(where[a] for a in MESH_AXES)

    barrier = pltpu.get_barrier_semaphore()
    for j in range(1, count):
        pl.semaphore_signal(barrier, 1, device_id=device(lax.rem(me + j, count)), device_id_type=MESH_ID)
    pl.semaphore_wait(barrier, count - 1)
    copies = []
    for j in range(1, count):
        peer = lax.rem(me + j, count)
        for i in range(count_arrays):
            copy = pltpu.make_async_remote_copy(
                src_ref=x_refs[i] if gather else x_refs[i].at[peer],
                dst_ref=o_refs[i].at[me],
                send_sem=send_sem.at[i, j - 1],
                recv_sem=recv_sem.at[i, j - 1],
                device_id=device(peer),
                device_id_type=MESH_ID,
            )
            copy.start()
            copies.append(copy)
    for copy in copies:
        copy.wait()


def exchange(xs, group, collective_id, gather=False):
    sizes = {a: lax.axis_size(a) for a in MESH_AXES}
    count = math.prod(sizes[a] for a in group)
    if count == 1:
        return [x[None] if gather else x for x in xs]
    shapes = [jax.ShapeDtypeStruct((count,) + x.shape if gather else x.shape, x.dtype) for x in xs]
    moved = sum(x.size * x.dtype.itemsize * (count if gather else 1) for x in xs)
    outs = pl.pallas_call(
        functools.partial(_exchange_kernel, sizes, group, gather, len(xs)),
        out_shape=shapes,
        in_specs=[pl.BlockSpec(memory_space=pl.ANY)] * len(xs),
        out_specs=[pl.BlockSpec(memory_space=pl.ANY)] * len(xs),
        scratch_shapes=[
            pltpu.SemaphoreType.DMA((len(xs), count - 1)),
            pltpu.SemaphoreType.DMA((len(xs), count - 1)),
        ],
        compiler_params=pltpu.CompilerParams(collective_id=collective_id, has_side_effects=True),
        cost_estimate=pl.CostEstimate(flops=0, transcendentals=0, bytes_accessed=2 * moved),
    )(*xs)
    me = _group_index(group, sizes, {a: lax.axis_index(a) for a in group})
    placed = []
    for x, out in zip(xs, outs):
        own = x if gather else lax.dynamic_index_in_dim(x, me, 0, keepdims=False)
        placed.append(lax.dynamic_update_index_in_dim(out, own, me, 0))
    return placed


def gelu_exact(values):
    return jax.nn.gelu(values, approximate=False)


def gelu_back(point, grad):
    return jax.vjp(gelu_exact, point)[1](grad)[0]


def normalize(values, gain, shift):
    center = jnp.mean(values, axis=1, keepdims=True)
    offset = values - center
    spread = jnp.mean(offset * offset, axis=1, keepdims=True)
    scale = lax.rsqrt(spread + EPSILON)
    unit = offset * scale
    return (unit * gain[:, None] + shift[:, None], unit, scale)


def normalize_back(grad, unit, scale, gain):
    scaled = grad * gain[:, None]
    first = jnp.mean(scaled, axis=1, keepdims=True)
    second = jnp.mean(scaled * unit, axis=1, keepdims=True)
    return scale * (scaled - first - unit * second)


def neighbour_pairs(seqs, nch, q_count):
    pairs = []
    for s in range(seqs):
        for c in range(nch):
            q = c % q_count
            if q < q_count - 1:
                pairs.append((s * nch + c, s * nch + c + 1))
            elif s < seqs - 1:
                pairs.append((s * nch + c, (s + 1) * nch + c - (q_count - 1)))
    return pairs


def extended(x, width, pairs):
    down = [(j, i) for i, j in pairs]
    length = x.shape[-1]
    before = lax.ppermute(x[..., length - width :], ("seq", "ch"), pairs)
    after = lax.ppermute(x[..., :width], ("seq", "ch"), down)
    return jnp.concatenate([before, x, after], axis=-1)


def shifted_taps(wide, wide_ids, own_ids, offsets, border):
    length = own_ids.shape[-1]
    pieces = []
    for offset in offsets:
        lower = border + offset
        shifted = wide[:, :, lower : lower + length]
        matching = wide_ids[:, lower : lower + length] == own_ids
        pieces.append(jnp.where(matching[:, None, :], shifted, jnp.zeros_like(shifted)))
    return jnp.concatenate(pieces, axis=1)


def to_positions(x, nch, q_count):
    rows, width, length = x.shape
    if q_count > 1:
        x = x.reshape(rows, width, q_count, length // q_count).transpose(0, 2, 1, 3)
        x = x.reshape(rows * q_count, width, length // q_count)
    x = lax.all_to_all(x, "ch", 0, 0, tiled=True)
    return _join(x, nch)


def _join(x, nch):
    total, width, length = x.shape
    p = total // nch
    return x.reshape(nch, p, width, length).transpose(1, 0, 2, 3).reshape(p, nch * width, length)


def to_channels(x, nch, q_count, rows):
    p, width, length = x.shape
    x = x.reshape(p, nch, width // nch, length).transpose(1, 0, 2, 3).reshape(nch * p, width // nch, length)
    x = lax.all_to_all(x, "ch", 0, 0, tiled=True)
    if q_count > 1:
        _, width, part = x.shape
        x = x.reshape(rows, q_count, width, part).transpose(0, 2, 1, 3).reshape(rows, width, q_count * part)
    return x


def local(
    inputs,
    segment_ids,
    norm0_gain,
    norm0_shift,
    w_inner,
    b_inner,
    norm1_gain,
    norm1_shift,
    w_conv,
    b_conv,
    norm2_gain,
    norm2_shift,
    w_outer,
    b_outer,
    cotangent,
):
    nch = lax.axis_size("ch")
    seqs = lax.axis_size("seq")
    batches = lax.axis_size("batch")
    rows, dloc, length = inputs.shape
    hloc = w_conv.shape[1]
    hid = hloc * nch
    dim = dloc * nch
    if rows % nch == 0:
        q_count = 1
    else:
        q_count = nch // rows
    part = length // q_count
    border = 2 * DILATION_SPACING
    offsets = [(k - KERNEL_TAPS // 2) * DILATION_SPACING for k in range(KERNEL_TAPS)]
    back_offsets = [-o for o in offsets]
    pairs = neighbour_pairs(seqs, nch, q_count)
    me = lax.axis_index("ch")

    smalls = [norm0_gain, norm0_shift, b_inner, norm1_gain, norm1_shift, b_conv, norm2_gain, norm2_shift, b_outer]
    sidx = lax.axis_index("seq")
    halves = [
        lax.dynamic_slice_in_dim(w_inner, sidx * (dloc // seqs), dloc // seqs, 0),
        lax.dynamic_slice_in_dim(w_conv, sidx * (hloc // seqs), hloc // seqs, 1),
        lax.dynamic_slice_in_dim(w_outer, sidx * (hloc // seqs), hloc // seqs, 0),
    ]
    small_all, w_in, w_cv, w_out = exchange([jnp.concatenate(smalls)] + halves, ("ch",), 0, gather=True)
    cut = 0
    full = []
    for v in smalls:
        n = v.shape[0]
        full.append(small_all[:, cut : cut + n].reshape(n * nch))
        cut += n
    g0, s0, b_in, g1, s1, b_cv, g2, s2, b_out = full
    w_in = lax.all_gather(w_in, "seq", axis=1, tiled=True).reshape(dim, hid)
    w_cv = lax.all_gather(w_cv, "seq", axis=2, tiled=True).transpose(1, 0, 2, 3).reshape(KERNEL_TAPS, hid, hid)
    w_out = lax.all_gather(w_out, "seq", axis=1, tiled=True).reshape(hid, dim)

    x = to_positions(inputs, nch, q_count)
    cot = to_positions(cotangent, nch, q_count)
    prow = x.shape[0]
    if q_count == 1:
        ids = lax.dynamic_slice_in_dim(segment_ids, me * prow, prow, axis=0)
    else:
        ids = lax.dynamic_slice_in_dim(segment_ids, me // q_count, 1, axis=0)
        ids = lax.dynamic_slice_in_dim(ids, (me % q_count) * part, part, axis=1)
    own_ids = ids + 1
    wide_ids = extended(own_ids, border, pairs)

    residual = x.astype(jnp.float32)
    normed0, unit0, scale0 = normalize(residual, g0, s0)
    hidden0 = gelu_exact(normed0).astype(jnp.bfloat16)
    inner = jnp.einsum("dh,rdl->rhl", w_in, hidden0, preferred_element_type=jnp.float32) + b_in[:, None]
    normed1, unit1, scale1 = normalize(inner, g1, s1)
    hidden1 = gelu_exact(normed1).astype(jnp.bfloat16)
    wide_hidden = extended(hidden1, border, pairs)
    taps = shifted_taps(wide_hidden, wide_ids, own_ids, offsets, border)
    kernel_flat = w_cv.reshape(KERNEL_TAPS * hid, hid)
    mixed = jnp.einsum("co,rcl->rol", kernel_flat, taps, preferred_element_type=jnp.float32) + b_cv[:, None]
    normed2, unit2, scale2 = normalize(mixed, g2, s2)
    hidden2 = gelu_exact(normed2).astype(jnp.bfloat16)
    branch = jnp.einsum("hd,rhl->rdl", w_out, hidden2, preferred_element_type=jnp.float32)
    output = (residual + branch + b_out[:, None]).astype(jnp.bfloat16)

    grad_b_outer = jnp.sum(cot.astype(jnp.float32), axis=(0, 2))
    grad_w_outer = jnp.einsum("rhl,rdl->hd", hidden2, cot, preferred_element_type=jnp.float32)
    grad_hidden2 = jnp.einsum("hd,rdl->rhl", w_out, cot, preferred_element_type=jnp.float32)
    grad_normed2 = gelu_back(normed2, grad_hidden2)
    grad_norm2_gain = jnp.sum(grad_normed2 * unit2, axis=(0, 2))
    grad_norm2_shift = jnp.sum(grad_normed2, axis=(0, 2))
    grad_mixed = normalize_back(grad_normed2, unit2, scale2, g2).astype(jnp.bfloat16)
    grad_b_conv = jnp.sum(grad_mixed.astype(jnp.float32), axis=(0, 2))
    grad_w_conv = jnp.einsum(
        "rkcil,rol->ckio",
        taps.reshape(prow, KERNEL_TAPS, nch, hloc, part),
        grad_mixed,
        preferred_element_type=jnp.float32,
    )
    wide_grad = extended(grad_mixed, border, pairs)
    back_taps = shifted_taps(wide_grad, wide_ids, own_ids, back_offsets, border)
    kernel_back = jnp.transpose(w_cv, (0, 2, 1)).reshape(KERNEL_TAPS * hid, hid)
    grad_hidden1 = jnp.einsum("oc,rol->rcl", kernel_back, back_taps, preferred_element_type=jnp.float32)
    grad_normed1 = gelu_back(normed1, grad_hidden1)
    grad_norm1_gain = jnp.sum(grad_normed1 * unit1, axis=(0, 2))
    grad_norm1_shift = jnp.sum(grad_normed1, axis=(0, 2))
    grad_inner = normalize_back(grad_normed1, unit1, scale1, g1).astype(jnp.bfloat16)
    grad_b_inner = jnp.sum(grad_inner.astype(jnp.float32), axis=(0, 2))
    grad_w_inner = jnp.einsum("rdl,rhl->dh", hidden0, grad_inner, preferred_element_type=jnp.float32)
    grad_hidden0 = jnp.einsum("dh,rhl->rdl", w_in, grad_inner, preferred_element_type=jnp.float32)
    grad_normed0 = gelu_back(normed0, grad_hidden0)
    grad_norm0_gain = jnp.sum(grad_normed0 * unit0, axis=(0, 2))
    grad_norm0_shift = jnp.sum(grad_normed0, axis=(0, 2))
    input_grad = (cot.astype(jnp.float32) + normalize_back(grad_normed0, unit0, scale0, g0)).astype(jnp.bfloat16)

    output = to_channels(output, nch, q_count, rows)
    input_grad = to_channels(input_grad, nch, q_count, rows)

    vectors = [
        grad_norm0_gain,
        grad_norm0_shift,
        grad_b_inner,
        grad_norm1_gain,
        grad_norm1_shift,
        grad_b_conv,
        grad_norm2_gain,
        grad_norm2_shift,
        grad_b_outer,
    ]
    flat = jnp.concatenate([v.reshape(nch, -1) for v in vectors], axis=1)
    vec_len = flat.shape[1]
    vec_rows = -(-vec_len // dim)
    vec_rows = -(-(hloc + vec_rows) // 32) * 32 - hloc
    flat = jnp.pad(flat, ((0, 0), (0, vec_rows * dim - vec_len))).reshape(nch, vec_rows, dim)
    outer_plus = jnp.concatenate([grad_w_outer.reshape(nch, hloc, dim), flat], axis=1)
    outer_plus = outer_plus.reshape(nch, (hloc + vec_rows) * dim // 128, 128)

    def reduce_seq_batch(g, split_dim, after=None):
        if after is not None:
            g, _ = lax.optimization_barrier((g, after))
        g = lax.psum_scatter(g, "seq", scatter_dimension=split_dim, tiled=True)
        return lax.psum_scatter(g, "batch", scatter_dimension=split_dim, tiled=True)

    part_outer = reduce_seq_batch(outer_plus, 1)
    part_conv = reduce_seq_batch(grad_w_conv, 3, part_outer)
    part_inner = reduce_seq_batch(grad_w_inner.reshape(nch, dloc, hid), 1, part_conv)
    parts = [part_outer, part_conv, part_inner]
    parts = [jnp.sum(p, axis=0) for p in exchange(parts, ("ch",), 1)]
    parts = exchange(parts, ("batch",), 2, gather=True)
    parts = [p.reshape((seqs * batches,) + p.shape[2:]) for p in exchange(parts, ("seq",), 3, gather=True)]
    red_outer = parts[0].reshape(hloc + vec_rows, dim)
    red_w_outer = red_outer[:hloc]
    mine = red_outer[hloc:].reshape(-1)[:vec_len]
    red_w_conv = jnp.moveaxis(parts[1], 0, 2).reshape(KERNEL_TAPS, hloc, hid)
    red_w_inner = parts[2].reshape(dloc, hid)
    reds = []
    cut = 0
    for v in vectors:
        n = v.shape[0] // nch
        reds.append(mine[cut : cut + n])
        cut += n
    return (
        output,
        input_grad,
        reds[0],
        reds[1],
        red_w_inner,
        reds[2],
        reds[3],
        reds[4],
        red_w_conv,
        reds[5],
        reds[6],
        reds[7],
        red_w_outer,
        reds[8],
    )


def solution(mesh):
    return jax.shard_map(
        local,
        mesh=mesh,
        in_specs=(
            P("batch", "ch", "seq"),
            P("batch", "seq"),
            P("ch"),
            P("ch"),
            P("ch", None),
            P("ch"),
            P("ch"),
            P("ch"),
            P(None, "ch", None),
            P("ch"),
            P("ch"),
            P("ch"),
            P("ch", None),
            P("ch"),
            P("batch", "ch", "seq"),
        ),
        out_specs=(
            P("batch", "ch", "seq"),
            P("batch", "ch", "seq"),
            P("ch"),
            P("ch"),
            P("ch", None),
            P("ch"),
            P("ch"),
            P("ch"),
            P(None, "ch", None),
            P("ch"),
            P("ch"),
            P("ch"),
            P("ch", None),
            P("ch"),
        ),
        check_vma=False,
    )
```

profile of v0, /device:TPU:9, one launch (start us, length us, event | category | flops | bytes accessed | tf_op | source)
XLA Modules:
  0.0 667.9 jit_solution(15541232263195957469)
XLA Ops:
  14.0 43.9 %shard_map.254 = (f32[4,1920]{1,0:T(4,128)}, bf16[4,160,640]{2,1,0:T(8,128)(2,1)}, bf16[4,5,80,640]{3,2,1,0:T(8,128)(2,1)}, bf16[4,80,1280]{2,1,0:T(8,128)(2,1)}) custom-call(f32[1920]{0:T(1024)} %concatenate.43.refs_0_, bf16[160,640]{1,0:T(8,128)(2,1)} %constant_dynamic-slice_fusion.2.refs_1_, bf16[5,80,640]{2,1,0:T(8,128)(2,1)} %constant_dynamic-slice_fusion.1.refs_2_, ...), custom_call_target="tpu_custom_call" | custom-call | bytes 7434240 | tf_op jit(solution)/shard_map/pallas_call | solution.py:74
  59.7 3.8 all-to-all-start
  64.3 2.4 collective-permute-start.2
  70.5 23.0 %all-to-all-done = bf16[4,320,1024]{2,1,0:T(8,128)(2,1)S(1)} async-done(((bf16[4,320,1024]{2,1,0:T(8,128)(2,1)}), bf16[4,320,1024]{2,1,0:T(8,128)(2,1)S(1)}, u32[]{:S(2)}, u32[]{:S(2)}) %all-to-all-start) | async-done | bytes 2621472 | tf_op jit(solution)/shard_map/all_to_all | solution.py:154
  93.5 4.6 all-to-all-start.2
  99.4 3.0 convert_element_type.149
  102.4 16.8 %fusion.88 = (f32[1024]{0:T(1024)S(1)}, f32[1024,640]{1,0:T(8,128)S(1)}) fusion(f32[640]{0:T(1024)S(1)} %add.205, bf16[1280,640]{1,0:T(8,128)(2,1)} %bitcast.297, f32[1280]{0:T(1024)S(1)} %add.202, f32[1280]{0:T(1024)S(1)} %mul.438, f32[1024]{0:T(1024)S(1)} %add_rsqrt_fusion.2, f32[1,1280,1,1,1,1,1024]{6,1,5,4,3,2,0:T(8,128)} %bitcast.281, ...), kind=kOutput, calls=%fused_computation.162 | convolution fusion | flops 1769470976 | bytes 9527808 | tf_op jit(solution)/shard_map/dh,rdl->rhl/dot_general | solution.py:242
  119.8 7.3 %multiply_convert_fusion.1 = bf16[1,640,1024]{1,2,0:T(8,128)(2,1)S(1)} fusion(f32[640]{0:T(1024)S(1)} %add.209, f32[640]{0:T(1024)S(1)} %mul.448, f32[1024]{0:T(1024)S(1)} %add_rsqrt_fusion.1, f32[1024]{0:T(1024)S(1)} %broadcast_multiply_fusion.5, f32[640]{0:T(1024)S(1)} %add.205, f32[1024,640]{1,0:T(8,128)S(1)} %get-tuple-element.92), kind=kLoop, calls=%fused_computation.144 | loop fusion | flops 45875200 | bytes 3948032 | tf_op jit(solution)/shard_map/convert_element_type | solution.py:244
  129.5 2.2 convert_reduce_fusion.3
  131.6 5.9 copy.56
  137.6 14.3 %collective-permute-start.3 = (bf16[1,640,64]{1,2,0:T(8,128)(2,1)S(1)}, bf16[1,640,64]{1,2,0:T(8,128)(2,1)S(1)}, u32[]{:S(2)}, u32[]{:S(2)}) collective-permute-start(bf16[1,640,64]{1,2,0:T(8,128)(2,1)S(1)} %get-tuple-element.69), channel_id=1, source_target_pairs={{4,0},{5,1},{6,2},{7,3},{12,8},{13,9},{14,10},{15,11},{20,16},{21,... | collective-permute-start | bytes 245768 | tf_op jit(solution)/shard_map/ppermute | solution.py:134
  151.8 2.8 fusion.106
  156.1 8.0 %constant_dynamic-update-slice_fusion = bf16[1,3200,1024]{1,2,0:T(8,128)(2,1)} fusion(bf16[1,3200,1024]{1,2,0:T(8,128)(2,1)} %fusion.114, f32[640]{0:T(1024)S(1)} %add.209, f32[640]{0:T(1024)S(1)} %mul.448, f32[1024]{0:T(1024)S(1)} %add_rsqrt_fusion.1, f32[1024]{0:T(1024)S(1)} %broadcast_multiply_fusion.5, f32[640]{0:T(1024)S(1)} %add.205, ...), kind=kLoop, calls=%fused_computation.219 | loop fusion | flops 45875200 | bytes 3948032
  167.0 2.6 copy.55
  169.6 9.2 %fusion.90 = (f32[1024]{0:T(1024)S(1)}, f32[1024,640]{1,0:T(8,128)S(1)}) fusion(f32[640]{0:T(1024)S(1)} %add.212, bf16[3200,640]{1,0:T(8,128)(2,1)S(1)} %bitcast.283, bf16[1,3200,1024]{1,2,0:T(8,128)(2,1)} %fusion.112), kind=kOutput, calls=%fused_computation.164 | convolution fusion | flops 4195613696 | bytes 13277696 | tf_op jit(solution)/shard_map/co,rcl->rol/dot_general | solution.py:248
  179.5 11.9 %fusion.65 = (f32[640]{0:T(1024)S(1)}, f32[1024]{0:T(1024)S(1)}, f32[1024]{0:T(1024)S(1)}, f32[640]{0:T(1024)S(1)}, f32[1,640,1024]{1,2,0:T(8,128)S(1)}) fusion(f32[1024]{0:T(1024)S(1)} %add_rsqrt_fusion, f32[1024]{0:T(1024)S(1)} %broadcast_multiply_fusion.4, f32[640]{0:T(1024)S(1)} %add.212, f32[1024,640]{1,0:T(8,128)S(1)} %get-tuple-element.94, ...), kind=kOutput, calls=%fused_computation.113 | convolution fusion | flops 1732113152 | bytes 9531904 | tf_op jit(solution)/shard_map/hd,rdl->rhl/dot_general | solution.py:256
  191.3 8.5 %convert_reduce_fusion.1 = (f32[640]{0:T(1024)S(1)}, bf16[1,640,1024]{1,2,0:T(8,128)(2,1)S(1)}, bf16[1,640,1024]{1,2,0:T(8,128)(2,1)S(1)}) fusion(f32[1024]{0:T(1024)S(1)} %get-tuple-element.98, f32[1024]{0:T(1024)S(1)} %add_rsqrt_fusion, f32[1024]{0:T(1024)S(1)} %broadcast_multiply_fusion.4, f32[640]{0:T(1024)S(1)} %add.212, f32[1024,640]{1,0:T(8,128)} %copy-done.7, ...), kind=kLoop, calls=%fused_computation.128 | loop fusion | flops 51117440 | bytes 7890944 | tf_op jit(solution)/shard_map/reduce_sum | solution.py:261
  202.7 5.7 fusion.191
  208.4 7.8 %copy.61 = bf16[5,640,640]{2,1,0:T(8,128)(2,1)} copy(bf16[5,640,640]{1,2,0:T(8,128)(2,1)} %bitcast.284) | data formatting | bytes 8192000 | tf_op jit(solution)/shard_map/transpose | solution.py:270
  221.9 11.3 %fusion.71 = (f32[640]{0:T(1024)S(1)}, f32[1024]{0:T(1024)S(1)}, f32[1024]{0:T(1024)S(1)}, f32[640]{0:T(1024)S(1)}, f32[1,640,1024]{1,2,0:T(8,128)S(1)}) fusion(f32[1024]{0:T(1024)S(1)} %add_rsqrt_fusion.1, f32[1024]{0:T(1024)S(1)} %broadcast_multiply_fusion.5, f32[640]{0:T(1024)S(1)} %add.205, f32[1024,640]{1,0:T(8,128)S(1)} %copy-done.3, ...), kind=kOutput, calls=%fused_computation.124 | convolution fusion | flops 4248695808 | bytes 15921664 | tf_op jit(solution)/shard_map/oc,rol->rcl/dot_general | solution.py:271
  234.7 17.2 %multiply_reduce_fusion = (f32[1280]{0:T(1024)S(1)}, f32[1024]{0:T(1024)S(1)}, f32[1024]{0:T(1024)S(1)}, f32[1280]{0:T(1024)S(1)}, f32[1,1280,1024]{1,2,0:T(8,128)}) fusion(f32[1,1280,1024]{1,2,0:T(8,128)S(1)} %bitcast.280, f32[1024]{0:T(1024)S(1)} %broadcast_multiply_fusion.8, f32[1024]{0:T(1024)S(1)} %add_rsqrt_fusion.2, f32[1280]{0:T(1024)S(1)} %mul.438, ...), kind=kOutput, calls=%fused_computation.41 | convolution fusion | flops 1785196032 | bytes 13471744 | tf_op jit(solution)/shard_map/dh,rhl->rdl/dot_general | solution.py:278
  252.6 4.1 pad_maximum_fusion
  256.7 4.7 reshape.1423
  261.4 14.7 %reduce-scatter.11.cloned.1.call-done = f32[4,960,128]{2,1,0:T(8,128)} async-done(((f32[4,1920,128]{2,1,0:T(8,128)}), f32[4,960,128]{2,1,0:T(8,128)}) %reduce-scatter.11.cloned.1.call-update) | async-done | bytes 1966096 | tf_op jit(solution)/shard_map/reduce_scatter | solution.py:309
  276.2 9.6 %copy.65 = bf16[1,3200,1024]{2,1,0:T(8,128)(2,1)} copy(bf16[1,3200,1024]{1,2,0:T(8,128)(2,1)} %fusion.112) | data formatting | bytes 13107200 | tf_op jit(solution)/shard_map/concatenate | solution.py:146
  285.8 9.8 %fusion.43 = f32[4,5,160,640]{3,2,1,0:T(8,128)} fusion(bf16[5,4,160,1024]{3,2,1,0:T(8,128)(2,1)} %bitcast.287, bf16[1,640,1024]{1,2,0:T(8,128)(2,1)S(1)} %get-tuple-element.63), kind=kOutput, calls=%fused_computation.85 | convolution fusion | flops 4194304000 | bytes 16056320 | tf_op jit(solution)/shard_map/rkcil,rol->ckio/dot_general | solution.py:262
  295.6 23.9 %reduce-scatter.13.cloned.1.call-done.refs_0_ = f32[4,240,128]{2,1,0:T(8,128)} async-done(((f32[4,960,128]{2,1,0:T(8,128)}), f32[4,240,128]{2,1,0:T(8,128)}) %reduce-scatter.13.cloned.1.call-update) | async-done | bytes 491536 | tf_op jit(solution)/shard_map/reduce_scatter | solution.py:310
  319.4 18.7 %copy.76 = f32[4,5,160,640]{2,1,0,3:T(8,128)} copy(f32[4,5,160,640]{3,2,1,0:T(8,128)} %fusion.43) | data formatting | bytes 16384000
  338.1 16.8 %reshape.1435 = f32[640,3200]{1,0:T(8,128)} reshape(f32[640,4,5,160]{3,2,1,0:T(8,128)} %bitcast.278) | data formatting | bytes 16384000
  355.0 17.5 %reduce-scatter.19.cloned.1.call-done = f32[320,3200]{1,0:T(8,128)} async-done(((f32[640,3200]{1,0:T(8,128)}), f32[320,3200]{1,0:T(8,128)}) %reduce-scatter.19.cloned.1.call-update) | async-done | bytes 4096016
  372.7 17.0 %fusion.84 = f32[4,320,640]{2,1,0:T(8,128)} fusion(bf16[4,320,1024]{2,1,0:T(8,128)(2,1)S(1)} %copy-done.1, f32[4,320]{1,0:T(4,128)S(1)} %copy-done.29, f32[4,320]{1,0:T(4,128)S(1)} %copy-done.27, f32[1024]{0:T(1024)S(1)} %add_rsqrt_fusion.2, f32[1024]{0:T(1024)S(1)} %broadcast_multiply_fusion.8, bf16[1,640,1024]{1,2,0:T(8,128)(2,1)} %copy-done.16), kind=kOutput, calls=%fused_computation.158 | convolution fusion | flops 1769472000 | bytes 7227392 | tf_op jit(solution)/shard_map/rdl,rhl->dh/dot_general | solution.py:277
  389.6 61.0 %reduce-scatter.21.cloned.1.call-done = f32[80,3200]{1,0:T(8,128)} async-done(((f32[320,3200]{1,0:T(8,128)}), f32[80,3200]{1,0:T(8,128)}) %reduce-scatter.21.cloned.1.call-update) | async-done | bytes 1024016
  450.6 2.3 reshape.1438
  456.3 6.9 %fusion.17 = bf16[1,1280,1024]{1,2,0:T(8,128)(2,1)} fusion(f32[1,1280,1024]{1,2,0:T(8,128)} %copy.56, bf16[640,1280]{1,0:T(8,128)(2,1)} %bitcast.296, f32[1280]{0:T(1024)S(1)} %add.220, bf16[1,640,1024]{1,2,0:T(8,128)(2,1)S(1)} %copy-done.12), kind=kOutput, calls=%fused_computation.21 | convolution fusion | flops 1681653760 | bytes 10818560 | tf_op jit(solution)/shard_map/hd,rhl->rdl/dot_general | solution.py:251
  463.2 4.5 copy.57
  467.7 4.6 all-to-all-start.1
  472.3 5.2 copy.62
  477.6 6.5 add_convert_fusion
  484.0 2.6 copy.63
  486.6 16.0 %all-to-all-done.1 = bf16[4,320,1024]{2,1,0:T(8,128)(2,1)} async-done(((bf16[4,320,1024]{2,1,0:T(8,128)(2,1)}), bf16[4,320,1024]{2,1,0:T(8,128)(2,1)}, u32[]{:S(2)}, u32[]{:S(2)}) %all-to-all-start.1) | async-done | bytes 2621472 | tf_op jit(solution)/shard_map/all_to_all | solution.py:167
  502.6 3.7 all-to-all-start.3
  506.3 29.9 %all-to-all-done.3 = bf16[4,320,1024]{2,1,0:T(8,128)(2,1)S(1)} async-done(((bf16[4,320,1024]{2,1,0:T(8,128)(2,1)}), bf16[4,320,1024]{2,1,0:T(8,128)(2,1)S(1)}, u32[]{:S(2)}, u32[]{:S(2)}) %all-to-all-start.3) | async-done | bytes 2621472 | tf_op jit(solution)/shard_map/all_to_all | solution.py:167
  536.2 29.9 %shard_map.255 = (f32[4,240,128]{2,1,0:T(8,128)}, f32[4,5,160,80]{3,2,1,0:T(8,128)}, f32[4,40,640]{2,1,0:T(8,128)}) custom-call(f32[4,240,128]{2,1,0:T(8,128)} %reduce-scatter.13.cloned.1.call-done.refs_0_, f32[4,5,160,80]{3,2,1,0:T(8,128)} %copy.79.refs_1_, f32[4,40,640]{2,1,0:T(8,128)} %reduce-scatter.17.cloned.1.call-done.refs_2_), custom_call_target="tpu_custom_call" | custom-call | bytes 3850240 | tf_op jit(solution)/shard_map/pallas_call | solution.py:74
  571.2 2.3 reduce_sum.238.refs_1_
  575.2 56.7 %shard_map.256 = (f32[4,240,128]{2,1,0:T(8,128)}, f32[4,5,160,80]{3,2,1,0:T(8,128)}, f32[4,40,640]{2,1,0:T(8,128)}) custom-call(f32[240,128]{1,0:T(8,128)} %reduce_sum.237.refs_0_, f32[5,160,80]{2,1,0:T(8,128)} %reduce_sum.238.refs_1_, f32[40,640]{1,0:T(8,128)} %reduce_sum.239.refs_2_), custom_call_target="tpu_custom_call" | custom-call | bytes 3850240 | tf_op jit(solution)/shard_map/pallas_call | solution.py:74
  635.9 6.2 shard_map.257
  648.9 3.8 copy.69
  654.7 3.6 copy.111
  (183 shorter events, 58.3 us)
Async XLA Ops:
  7.2 51.5 %copy-start.18 = (bf16[5,160,640]{2,1,0:T(8,128)(2,1)S(1)}, bf16[5,160,640]{2,1,0:T(8,128)(2,1)}, u32[]{:S(2)}) copy-start(bf16[5,160,640]{2,1,0:T(8,128)(2,1)} %param.23) | copy-start | bytes 3072004
  7.2 50.7 %copy-start.20 = (bf16[320,640]{1,0:T(8,128)(2,1)S(1)}, bf16[320,640]{1,0:T(8,128)(2,1)}, u32[]{:S(2)}) copy-start(bf16[320,640]{1,0:T(8,128)(2,1)} %param.19) | copy-start | bytes 1228804
  7.2 95.2 %all-gather.4.cloned.1.call-start = ((), (), s32[]{:S(2)}) async-start(), calls=%async_computation.10 | async-start | bytes 2457600 | tf_op jit(solution)/shard_map/all_gather | solution.py:224
  58.7 108.3 %all-gather.6.cloned.1.call-start = ((), (), s32[]{:S(2)}) async-start(), calls=%async_computation.11 | async-start | bytes 6144000 | tf_op jit(solution)/shard_map/all_gather | solution.py:225
  59.6 8.5 %copy-start.21 = (bf16[160,1280]{1,0:T(8,128)(2,1)S(1)}, bf16[160,1280]{1,0:T(8,128)(2,1)}, u32[]{:S(2)}) copy-start(bf16[160,1280]{1,0:T(8,128)(2,1)} %param.27) | copy-start | bytes 1228804
  59.6 9.2 %copy-start.23 = (f32[1920]{0:T(1024)S(1)}, f32[1920]{0:T(1024)}, u32[]{:S(2)}) copy-start(f32[1920]{0:T(1024)} %concatenate.43.refs_0_) | copy-start | bytes 23044
  59.6 9.2 %copy-start.24 = (f32[4,1920]{1,0:T(4,128)S(1)}, f32[4,1920]{1,0:T(4,128)}, u32[]{:S(2)}) copy-start(f32[4,1920]{1,0:T(4,128)} %get-tuple-element.29) | copy-start | bytes 92164
  59.7 33.8 %all-to-all-start = ((bf16[4,320,1024]{2,1,0:T(8,128)(2,1)}), bf16[4,320,1024]{2,1,0:T(8,128)(2,1)S(1)}, u32[]{:S(2)}, u32[]{:S(2)}) async-start(bf16[4,320,1024]{2,1,0:T(8,128)(2,1)} %param.15), calls=%async_computation | async-start | bytes 5242880 | tf_op jit(solution)/shard_map/all_to_all | solution.py:154
  63.5 116.0 %all-gather.8.cloned.1.call-start = ((), (), s32[]{:S(2)}) async-start(), calls=%async_computation.12 | async-start | bytes 2457600 | tf_op jit(solution)/shard_map/all_gather | solution.py:226
  64.3 6.0 collective-permute-start.2
  66.8 3.6 collective-permute-start
  70.0 23.5 %copy-start.26 = (f32[4,320]{1,0:T(4,128)}, f32[4,320]{1,0:T(4,128)S(1)}, u32[]{:S(2)}) copy-start(f32[4,320]{1,0:T(4,128)S(1)} %get-tuple-element.86) | copy-start | bytes 15364
  70.0 23.5 %copy-start.28 = (f32[4,320]{1,0:T(4,128)}, f32[4,320]{1,0:T(4,128)S(1)}, u32[]{:S(2)}) copy-start(f32[4,320]{1,0:T(4,128)S(1)} %get-tuple-element.88) | copy-start | bytes 15364
  93.5 5.9 copy-start
  93.5 35.9 %all-to-all-start.2 = ((bf16[4,320,1024]{2,1,0:T(8,128)(2,1)}), bf16[4,320,1024]{2,1,0:T(8,128)(2,1)}, u32[]{:S(2)}, u32[]{:S(2)}) async-start(bf16[4,320,1024]{2,1,0:T(8,128)(2,1)} %param.29), calls=%async_computation.2 | async-start | bytes 5242880 | tf_op jit(solution)/shard_map/all_to_all | solution.py:154
  98.1 178.0 %reduce-scatter.11.cloned.1.call-start = ((), (), s32[]{:S(2)}) async-start(), calls=%async_computation.13 | async-start | bytes 5898240 | tf_op jit(solution)/shard_map/reduce_scatter | solution.py:309
  119.2 36.9 %copy-start.2 = (f32[1024,640]{1,0:T(8,128)}, f32[1024,640]{1,0:T(8,128)S(1)}, u32[]{:S(2)}) copy-start(f32[1024,640]{1,0:T(8,128)S(1)} %get-tuple-element.92) | copy-start | bytes 7864324
  128.2 23.7 %collective-permute-start.1 = (bf16[1,640,64]{1,2,0:T(8,128)(2,1)S(1)}, bf16[1,640,64]{1,2,0:T(8,128)(2,1)S(1)}, u32[]{:S(2)}, u32[]{:S(2)}) collective-permute-start(bf16[1,640,64]{1,2,0:T(8,128)(2,1)S(1)} %get-tuple-element.70), channel_id=1, source_target_pairs={{0,4},{1,5},{2,6},{3,7},{8,12},{9,13},{10,14},{11,15},{16,20},{17,... | collective-permute-start | bytes 245768 | tf_op jit(solution)/shard_map/ppermute | solution.py:133
  137.6 17.1 %copy-start.5 = (bf16[1,640,1024]{1,2,0:T(8,128)(2,1)S(1)}, bf16[1,640,1024]{1,2,0:T(8,128)(2,1)}, u32[]{:S(2)}) copy-start(bf16[1,640,1024]{1,2,0:T(8,128)(2,1)} %copy-done.4) | copy-start | bytes 3932164
  137.6 26.5 %collective-permute-start.3 = (bf16[1,640,64]{1,2,0:T(8,128)(2,1)S(1)}, bf16[1,640,64]{1,2,0:T(8,128)(2,1)S(1)}, u32[]{:S(2)}, u32[]{:S(2)}) collective-permute-start(bf16[1,640,64]{1,2,0:T(8,128)(2,1)S(1)} %get-tuple-element.69), channel_id=1, source_target_pairs={{4,0},{5,1},{6,2},{7,3},{12,8},{13,9},{14,10},{15,11},{20,16},{21,... | collective-permute-start | bytes 245768 | tf_op jit(solution)/shard_map/ppermute | solution.py:134
  169.6 9.2 %copy-start.6 = (bf16[5,4,160,640]{3,2,1,0:T(8,128)(2,1)}, bf16[5,4,160,640]{3,2,1,0:T(8,128)(2,1)S(1)}, u32[]{:S(2)}) copy-start(bf16[5,4,160,640]{3,2,1,0:T(8,128)(2,1)S(1)} %copy.55) | copy-start | bytes 12288004
  178.9 12.5 %copy-start.7 = (f32[1024,640]{1,0:T(8,128)}, f32[1024,640]{1,0:T(8,128)S(1)}, u32[]{:S(2)}) copy-start(f32[1024,640]{1,0:T(8,128)S(1)} %get-tuple-element.94) | copy-start | bytes 7864324
  199.9 8.5 %copy-start.11 = (bf16[1,640,1024]{1,2,0:T(8,128)(2,1)}, bf16[1,640,1024]{1,2,0:T(8,128)(2,1)S(1)}, u32[]{:S(2)}) copy-start(bf16[1,640,1024]{1,2,0:T(8,128)(2,1)S(1)} %get-tuple-element.66) | copy-start | bytes 3932164
  199.9 18.3 %collective-permute-start.4 = (bf16[1,640,64]{1,2,0:T(8,128)(2,1)S(1)}, bf16[1,640,64]{1,2,0:T(8,128)(2,1)S(1)}, u32[]{:S(2)}, u32[]{:S(2)}) collective-permute-start(bf16[1,640,64]{1,2,0:T(8,128)(2,1)S(1)} %get-tuple-element.68), channel_id=1, source_target_pairs={{4,0},{5,1},{6,2},{7,3},{12,8},{13,9},{14,10},{15,11},{20,16},{21,... | collective-permute-start | bytes 245768 | tf_op jit(solution)/shard_map/ppermute | solution.py:134
  216.2 3.2 collective-permute-start.5
  218.9 2.2 copy-start.13
  219.1 2.8 copy-start.3
  219.4 15.2 %slice-start = ((s8[5242880]{0:T(1024)(128)(4,1)}), s8[4194304]{0:T(1024)(128)(4,1)S(1)}, s32[]{:S(2)}) async-start(s8[5242880]{0:T(1024)(128)(4,1)} %bitcast.279), calls=%async_computation.19 | async-start | bytes 8388608
  221.9 12.7 %slice-start.1 = ((s8[5242880]{0:T(1024)(128)(4,1)}), s8[1048576]{0:T(1024)(128)(4,1)S(1)}, s32[]{:S(2)}) async-start(s8[5242880]{0:T(1024)(128)(4,1)} %bitcast.279), calls=%async_computation.20 | async-start | bytes 2097152
  234.6 17.2 %copy-start.16 = (bf16[1,640,1024]{1,2,0:T(8,128)(2,1)}, bf16[1,640,1024]{1,2,0:T(8,128)(2,1)S(1)}, u32[]{:S(2)}) copy-start(bf16[1,640,1024]{1,2,0:T(8,128)(2,1)S(1)} %get-tuple-element.65) | copy-start | bytes 3932164
  261.4 58.1 %reduce-scatter.13.cloned.1.call-start = ((), (), s32[]{:S(2)}) async-start(), calls=%async_computation.14 | async-start | bytes 2457600 | tf_op jit(solution)/shard_map/reduce_scatter | solution.py:310
  276.1 96.4 %reduce-scatter.19.cloned.1.call-start = ((), (), s32[]{:S(2)}) async-start(), calls=%async_computation.17 | async-start | bytes 12288000
  354.9 17.7 %copy-start.1 = (bf16[4,320,1024]{2,1,0:T(8,128)(2,1)S(1)}, bf16[4,320,1024]{2,1,0:T(8,128)(2,1)}, u32[]{:S(2)}) copy-start(bf16[4,320,1024]{2,1,0:T(8,128)(2,1)} %copy-done) | copy-start | bytes 7864324
  355.0 17.7 %copy-start.27 = (f32[4,320]{1,0:T(4,128)S(1)}, f32[4,320]{1,0:T(4,128)}, u32[]{:S(2)}) copy-start(f32[4,320]{1,0:T(4,128)} %copy-done.26) | copy-start | bytes 15364
  355.0 17.7 %copy-start.29 = (f32[4,320]{1,0:T(4,128)S(1)}, f32[4,320]{1,0:T(4,128)}, u32[]{:S(2)}) copy-start(f32[4,320]{1,0:T(4,128)} %copy-done.28) | copy-start | bytes 15364
  355.0 95.7 %reduce-scatter.21.cloned.1.call-start = ((), (), s32[]{:S(2)}) async-start(), calls=%async_computation.18 | async-start | bytes 5120000
  372.6 104.9 %reduce-scatter.15.cloned.1.call-start = ((), (), s32[]{:S(2)}) async-start(), calls=%async_computation.15 | async-start | bytes 4915200 | tf_op jit(solution)/shard_map/reduce_scatter | solution.py:309
  467.7 34.9 %all-to-all-start.1 = ((bf16[4,320,1024]{2,1,0:T(8,128)(2,1)}), bf16[4,320,1024]{2,1,0:T(8,128)(2,1)}, u32[]{:S(2)}, u32[]{:S(2)}) async-start(bf16[4,320,1024]{2,1,0:T(8,128)(2,1)} %bitcast.18), calls=%async_computation.1 | async-start | bytes 5242880 | tf_op jit(solution)/shard_map/all_to_all | solution.py:167
  472.3 63.9 %reduce-scatter.17.cloned.1.call-start = ((), (), s32[]{:S(2)}) async-start(), calls=%async_computation.16 | async-start | bytes 2048000 | tf_op jit(solution)/shard_map/reduce_scatter | solution.py:310
  502.6 33.6 %all-to-all-start.3 = ((bf16[4,320,1024]{2,1,0:T(8,128)(2,1)}), bf16[4,320,1024]{2,1,0:T(8,128)(2,1)S(1)}, u32[]{:S(2)}, u32[]{:S(2)}) async-start(bf16[4,320,1024]{2,1,0:T(8,128)(2,1)} %bitcast.285), calls=%async_computation.3 | async-start | bytes 5242880 | tf_op jit(solution)/shard_map/all_to_all | solution.py:167
  536.2 37.4 %copy-start.8 = (bf16[4,320,1024]{2,1,0:T(8,128)(2,1)}, bf16[4,320,1024]{2,1,0:T(8,128)(2,1)S(1)}, u32[]{:S(2)}) copy-start(bf16[4,320,1024]{2,1,0:T(8,128)(2,1)S(1)} %all-to-all-done.3) | copy-start | bytes 7864324
  566.1 7.5 %copy-start.22 = (f32[4,40,640]{2,1,0:T(8,128)S(1)}, f32[4,40,640]{2,1,0:T(8,128)}, u32[]{:S(2)}) copy-start(f32[4,40,640]{2,1,0:T(8,128)} %get-tuple-element.37) | copy-start | bytes 1228804
  569.4 62.4 %copy-start.17 = (f32[240,128]{1,0:T(8,128)S(1)}, f32[240,128]{1,0:T(8,128)}, u32[]{:S(2)}) copy-start(f32[240,128]{1,0:T(8,128)} %reduce_sum.237.refs_0_) | copy-start | bytes 368644
  632.5 9.6 %copy-start.14 = (f32[4,240,128]{2,1,0:T(8,128)S(1)}, f32[4,240,128]{2,1,0:T(8,128)}, u32[]{:S(2)}) copy-start(f32[4,240,128]{2,1,0:T(8,128)} %bitcast_dynamic-update-slice_fusion.7.refs_0_) | copy-start | bytes 1474564
  642.2 4.7 copy-start.15
  643.0 4.6 copy-start.10
  654.7 3.6 copy-start.9
  658.3 1.7 copy-start.19
  (4 other events, 4.5 us)
Sparse Core Ops, SparseCore 0:
  58.8 11.5 all-gather.3
  72.0 14.6 all-gather.5
  88.2 11.0 all-gather.7
  261.5 14.5 reduce-scatter.10
  278.4 41.0 reduce-scatter.12
  355.1 17.4 reduce-scatter.18
  374.9 75.7 reduce-scatter.20
  455.1 12.2 reduce-scatter.14
  477.7 35.0 reduce-scatter.16
where the time goes:
time: 680 us; the launch traced here: 668 us
  waiting for transfers between devices  186 us (27%)
  Pallas kernels  137 us (20%)
  local copies, waits for them, and re-layouts  127 us (19%)
  matrix products  106 us (16%)
  other arithmetic  57.3 us (8%)
  starting transfers between devices  39.3 us (6%)
  between operations  15 us (2%)
    pallas_call x4, Pallas kernels, exchange(): pl.pallas_call(functools.partial(_exchange_kernel, sizes, group, gather,...  137 us
    unnamed x11, waiting for transfers between devices  78.7 us
    unnamed x75, local copies, waits for them, and re-layouts  50.5 us
    all_to_all x2, waiting for transfers between devices, to_channels(): x = lax.all_to_all(x, 'ch', 0, 0, tiled=True)  45.9 us
    reduce_scatter x2, waiting for transfers between devices, reduce_seq_batch(): return lax.psum_scatter(g, 'batch', scatter_dimension=split_dim, tiled=True)  23.9 us
    all_to_all x2, waiting for transfers between devices, to_positions(): x = lax.all_to_all(x, 'ch', 0, 0, tiled=True)  23 us
    ppermute x3, starting transfers between devices, extended(): after = lax.ppermute(x[..., :width], ('seq', 'ch'), down)  18 us
    dot_general x1, matrix products, local(): jnp.einsum('dh,rhl->rdl', w_in, grad_inner, preferred_element_type=jnp.fl...  17.2 us
  transfers between devices with their start and end apart: 19, of which 8 were waited for; matrix products, arithmetic and copies ran while one was open for 22% of the time, Pallas kernels for 0%

commit v1 on v0

--- a/solution.py
+++ b/solution.py
@@ -253,6 +253,13 @@
 
     grad_b_outer = jnp.sum(cot.astype(jnp.float32), axis=(0, 2))
     grad_w_outer = jnp.einsum("rhl,rdl->hd", hidden2, cot, preferred_element_type=jnp.float32)
+    def reduce_seq_batch(g, split_dim, after=None):
+        if after is not None:
+            g, _ = lax.optimization_barrier((g, after))
+        g = lax.psum_scatter(g, "seq", scatter_dimension=split_dim, tiled=True)
+        return lax.psum_scatter(g, "batch", scatter_dimension=split_dim, tiled=True)
+
+    part_outer = reduce_seq_batch(grad_w_outer.reshape(nch, hloc * dim // 128, 128), 1)
     grad_hidden2 = jnp.einsum("hd,rdl->rhl", w_out, cot, preferred_element_type=jnp.float32)
     grad_normed2 = gelu_back(normed2, grad_hidden2)
     grad_norm2_gain = jnp.sum(grad_normed2 * unit2, axis=(0, 2))
@@ -273,6 +280,7 @@
     grad_norm1_gain = jnp.sum(grad_normed1 * unit1, axis=(0, 2))
     grad_norm1_shift = jnp.sum(grad_normed1, axis=(0, 2))
     grad_inner = normalize_back(grad_normed1, unit1, scale1, g1).astype(jnp.bfloat16)
+    grad_inner, _ = lax.optimization_barrier((grad_inner, part_outer))
     grad_b_inner = jnp.sum(grad_inner.astype(jnp.float32), axis=(0, 2))
     grad_w_inner = jnp.einsum("rdl,rhl->dh", hidden0, grad_inner, preferred_element_type=jnp.float32)
     grad_hidden0 = jnp.einsum("dh,rhl->rdl", w_in, grad_inner, preferred_element_type=jnp.float32)
@@ -297,30 +305,23 @@
     ]
     flat = jnp.concatenate([v.reshape(nch, -1) for v in vectors], axis=1)
     vec_len = flat.shape[1]
-    vec_rows = -(-vec_len // dim)
-    vec_rows = -(-(hloc + vec_rows) // 32) * 32 - hloc
-    flat = jnp.pad(flat, ((0, 0), (0, vec_rows * dim - vec_len))).reshape(nch, vec_rows, dim)
-    outer_plus = jnp.concatenate([grad_w_outer.reshape(nch, hloc, dim), flat], axis=1)
-    outer_plus = outer_plus.reshape(nch, (hloc + vec_rows) * dim // 128, 128)
-
-    def reduce_seq_batch(g, split_dim, after=None):
-        if after is not None:
-            g, _ = lax.optimization_barrier((g, after))
-        g = lax.psum_scatter(g, "seq", scatter_dimension=split_dim, tiled=True)
-        return lax.psum_scatter(g, "batch", scatter_dimension=split_dim, tiled=True)
-
-    part_outer = reduce_seq_batch(outer_plus, 1)
+    vec_rows = -(-vec_len // hid)
+    vec_rows = -(-(dloc + vec_rows) // 64) * 64 - dloc
+    flat = jnp.pad(flat, ((0, 0), (0, vec_rows * hid - vec_len))).reshape(nch, vec_rows, hid)
+    inner_plus = jnp.concatenate([grad_w_inner.reshape(nch, dloc, hid), flat], axis=1)
+    inner_plus = inner_plus.reshape(nch, (dloc + vec_rows) * hid // 128, 128)
+
     part_conv = reduce_seq_batch(grad_w_conv, 3, part_outer)
-    part_inner = reduce_seq_batch(grad_w_inner.reshape(nch, dloc, hid), 1, part_conv)
+    part_inner = reduce_seq_batch(inner_plus, 1, part_conv)
     parts = [part_outer, part_conv, part_inner]
     parts = [jnp.sum(p, axis=0) for p in exchange(parts, ("ch",), 1)]
     parts = exchange(parts, ("batch",), 2, gather=True)
     parts = [p.reshape((seqs * batches,) + p.shape[2:]) for p in exchange(parts, ("seq",), 3, gather=True)]
-    red_outer = parts[0].reshape(hloc + vec_rows, dim)
-    red_w_outer = red_outer[:hloc]
-    mine = red_outer[hloc:].reshape(-1)[:vec_len]
+    red_w_outer = parts[0].reshape(hloc, dim)
     red_w_conv = jnp.moveaxis(parts[1], 0, 2).reshape(KERNEL_TAPS, hloc, hid)
-    red_w_inner = parts[2].reshape(dloc, hid)
+    red_inner = parts[2].reshape(dloc + vec_rows, hid)
+    red_w_inner = red_inner[:dloc]
+    mine = red_inner[dloc:].reshape(-1)[:vec_len]
     reds = []
     cut = 0
     for v in vectors:

time: 680 us -> 622 us (0.915)
  waiting for transfers between devices: 186 us -> 124 us
  matrix products: 106 us -> 118 us
  local copies, waits for them, and re-layouts: 127 us -> 136 us
  starting transfers between devices: 39.3 us -> 30.8 us
  other arithmetic: 57.3 us -> 49.7 us
    unnamed x11, waiting for transfers between devices: 78.7 us -> 29 us
    reduce_scatter x2, waiting for transfers between devices: 14.7 us -> 1.51 us  [reduce_seq_batch(): g = lax.psum_scatter(g, 'seq', scatter_dimension=split_dim, tiled=True)]
    all_gather x1, waiting for transfers between devices: 0.02 us -> 12.5 us  [local(): w_out = lax.all_gather(w_out, 'seq', axis=1, tiled=True).reshape(hid, dim)]
    reduce_scatter x2, waiting for transfers between devices: 23.9 us -> 14.2 us  [reduce_seq_batch(): return lax.psum_scatter(g, 'batch', scatter_dimension=split_dim, tiled=True)]
    ppermute x3, starting transfers between devices: 18 us -> 9.71 us  [extended(): after = lax.ppermute(x[..., :width], ('seq', 'ch'), down)]
    unnamed x75 -> x82, local copies, waits for them, and re-layouts: 50.5 us -> 52.7 us
    unnamed x8 -> x7, other arithmetic: 14.8 us -> 13.5 us
  transfers between devices with their start and end apart: 19 -> 19, of which waited for: 8 -> 8; matrix products, arithmetic and copies ran while one was open for 22% -> 33% of each run, Pallas kernels for 0% -> 0%
where the time goes in v1:
time: 622 us; the launch traced here: 610 us
  Pallas kernels  137 us (22%)
  local copies, waits for them, and re-layouts  136 us (22%)
  waiting for transfers between devices  124 us (20%)
  matrix products  118 us (19%)
  other arithmetic  49.7 us (8%)
  starting transfers between devices  30.8 us (5%)
  between operations  14.8 us (2%)
    pallas_call x4, Pallas kernels, exchange(): pl.pallas_call(functools.partial(_exchange_kernel, sizes, group, gather,...  137 us
    unnamed x82, local copies, waits for them, and re-layouts  52.7 us
    all_to_all x2, waiting for transfers between devices, to_channels(): x = lax.all_to_all(x, 'ch', 0, 0, tiled=True)  45.1 us
    unnamed x11, waiting for transfers between devices  29 us
    all_to_all x2, waiting for transfers between devices, to_positions(): x = lax.all_to_all(x, 'ch', 0, 0, tiled=True)  21.4 us
    dot_general x1, matrix products, local(): jnp.einsum('dh,rhl->rdl', w_in, grad_inner, preferred_element_type=jnp.fl...  19.7 us
    dot_general x1, matrix products, local(): jnp.einsum('dh,rdl->rhl', w_in, hidden0, preferred_element_type=jnp.float32)  16.8 us
    dot_general x1, matrix products, local(): jnp.einsum('rdl,rhl->dh', hidden0, grad_inner, preferred_element_type=jnp...  15.5 us
  transfers between devices with their start and end apart: 19, of which 8 were waited for; matrix products, arithmetic and copies ran while one was open for 33% of the time, Pallas kernels for 0%

profile of v1, /device:TPU:9, one launch (start us, length us, event | category | flops | bytes accessed | tf_op | source)
XLA Modules:
  0.0 610.1 jit_solution(18391510600090243937)
XLA Ops:
  13.9 43.9 %shard_map.254 = (f32[4,1920]{1,0:T(4,128)}, bf16[4,160,640]{2,1,0:T(8,128)(2,1)}, bf16[4,5,80,640]{3,2,1,0:T(8,128)(2,1)}, bf16[4,80,1280]{2,1,0:T(8,128)(2,1)}) custom-call(f32[1920]{0:T(1024)} %concatenate.43.refs_0_, bf16[160,640]{1,0:T(8,128)(2,1)} %constant_dynamic-slice_fusion.2.refs_1_, bf16[5,80,640]{2,1,0:T(8,128)(2,1)} %constant_dynamic-slice_fusion.1.refs_2_, ...), custom_call_target="tpu_custom_call" | custom-call | bytes 7434240 | tf_op jit(solution)/shard_map/pallas_call | solution.py:74
  58.6 3.7 all-to-all-start
  64.4 3.0 collective-permute-start.2
  70.9 21.4 %all-to-all-done = bf16[4,320,1024]{2,1,0:T(8,128)(2,1)S(1)} async-done(((bf16[4,320,1024]{2,1,0:T(8,128)(2,1)}), bf16[4,320,1024]{2,1,0:T(8,128)(2,1)S(1)}, u32[]{:S(2)}, u32[]{:S(2)}) %all-to-all-start) | async-done | bytes 2621472 | tf_op jit(solution)/shard_map/all_to_all | solution.py:154
  92.3 4.6 all-to-all-start.2
  98.2 2.9 convert_element_type.149
  101.1 16.8 %fusion.88 = (f32[1024]{0:T(1024)S(1)}, f32[1024,640]{1,0:T(8,128)S(1)}) fusion(f32[640]{0:T(1024)S(1)} %add.205, bf16[1280,640]{1,0:T(8,128)(2,1)} %bitcast.293, f32[1280]{0:T(1024)S(1)} %add.202, f32[1280]{0:T(1024)S(1)} %mul.438, f32[1024]{0:T(1024)S(1)} %add_rsqrt_fusion.2, f32[1,1280,1,1,1,1,1024]{6,1,5,4,3,2,0:T(8,128)} %bitcast.281, ...), kind=kOutput, calls=%fused_computation.162 | convolution fusion | flops 1769470976 | bytes 9527808 | tf_op jit(solution)/shard_map/dh,rdl->rhl/dot_general | solution.py:242
  118.6 7.3 %multiply_convert_fusion.1 = bf16[1,640,1024]{1,2,0:T(8,128)(2,1)S(1)} fusion(f32[640]{0:T(1024)S(1)} %add.209, f32[640]{0:T(1024)S(1)} %mul.448, f32[1024]{0:T(1024)S(1)} %add_rsqrt_fusion.1, f32[1024]{0:T(1024)S(1)} %broadcast_multiply_fusion.5, f32[640]{0:T(1024)S(1)} %add.205, f32[1024,640]{1,0:T(8,128)S(1)} %get-tuple-element.91), kind=kLoop, calls=%fused_computation.144 | loop fusion | flops 45875200 | bytes 3948032 | tf_op jit(solution)/shard_map/convert_element_type | solution.py:244
  127.3 3.3 collective-permute-start.3
  133.6 8.0 %constant_dynamic-update-slice_fusion = bf16[1,3200,1024]{1,2,0:T(8,128)(2,1)} fusion(bf16[1,3200,1024]{1,2,0:T(8,128)(2,1)} %fusion.115, f32[640]{0:T(1024)S(1)} %add.209, f32[640]{0:T(1024)S(1)} %mul.448, f32[1024]{0:T(1024)S(1)} %add_rsqrt_fusion.1, f32[1024]{0:T(1024)S(1)} %broadcast_multiply_fusion.5, f32[640]{0:T(1024)S(1)} %add.205, ...), kind=kLoop, calls=%fused_computation.219 | loop fusion | flops 45875200 | bytes 3948032
  144.5 2.6 copy.53
  147.1 9.6 %fusion.90 = (f32[1024]{0:T(1024)S(1)}, f32[1024,640]{1,0:T(8,128)S(1)}) fusion(f32[640]{0:T(1024)S(1)} %add.212, bf16[3200,640]{1,0:T(8,128)(2,1)S(1)} %bitcast.283, bf16[1,3200,1024]{1,2,0:T(8,128)(2,1)} %fusion.113), kind=kOutput, calls=%fused_computation.164 | convolution fusion | flops 4195613696 | bytes 13277696 | tf_op jit(solution)/shard_map/co,rcl->rol/dot_general | solution.py:248
  157.4 11.8 %fusion.182 = f32[640,1280]{1,0:T(8,128)} fusion(bf16[1280,1024]{1,0:T(8,128)(2,1)} %bitcast.20, f32[640]{0:T(1024)S(1)} %add.216, f32[640]{0:T(1024)S(1)} %mul.458, f32[1024]{0:T(1024)S(1)} %add_rsqrt_fusion, f32[1024]{0:T(1024)S(1)} %broadcast_multiply_fusion.4, f32[640]{0:T(1024)S(1)} %add.212, f32[1024,640]{1,0:T(8,128)S(1)} %get-tuple-element.93), kind=kOutput, calls=%fused_computation.310 | convolution fusion | flops 1723596800 | bytes 8535552 | tf_op jit(solution)/shard_map/rhl,rdl->hd/dot_general | solution.py:255
  169.1 4.5 reshape.1412
  175.4 9.7 %copy.62 = bf16[1,3200,1024]{2,1,0:T(8,128)(2,1)} copy(bf16[1,3200,1024]{1,2,0:T(8,128)(2,1)} %fusion.113) | data formatting | bytes 13107200 | tf_op jit(solution)/shard_map/concatenate | solution.py:146
  186.7 12.5 %all-gather.8.cloned.1.call-done = bf16[4,160,1280]{2,1,0:T(8,128)(2,1)} async-done(((bf16[4,80,1280]{2,1,0:T(8,128)(2,1)}), bf16[4,160,1280]{2,1,0:T(8,128)(2,1)}) %all-gather.8.cloned.1.call-update) | async-done | bytes 1638416 | tf_op jit(solution)/shard_map/all_gather | solution.py:226
  199.2 11.7 %fusion.65 = (f32[640]{0:T(1024)S(1)}, f32[1024]{0:T(1024)S(1)}, f32[1024]{0:T(1024)S(1)}, f32[640]{0:T(1024)S(1)}, f32[1,640,1024]{1,2,0:T(8,128)S(1)}) fusion(f32[1024]{0:T(1024)S(1)} %add_rsqrt_fusion, f32[1024]{0:T(1024)S(1)} %broadcast_multiply_fusion.4, f32[640]{0:T(1024)S(1)} %add.212, f32[1024,640]{1,0:T(8,128)S(1)} %get-tuple-element.93, ...), kind=kOutput, calls=%fused_computation.113 | convolution fusion | flops 1732113152 | bytes 9531904 | tf_op jit(solution)/shard_map/hd,rdl->rhl/dot_general | solution.py:263
  211.0 2.6 convert_reduce_fusion.1
  214.6 7.5 %fusion.43 = f32[4,5,160,640]{3,2,1,0:T(8,128)} fusion(bf16[5,4,160,1024]{3,2,1,0:T(8,128)(2,1)S(1)} %bitcast.287, bf16[1,640,1024]{1,2,0:T(8,128)(2,1)S(1)} %get-tuple-element.65), kind=kOutput, calls=%fused_computation.85 | convolution fusion | flops 4194304000 | bytes 16056320 | tf_op jit(solution)/shard_map/rkcil,rol->ckio/dot_general | solution.py:269
  222.1 14.2 %reduce-scatter.13.cloned.1.call-done.refs_0_ = f32[4,200,128]{2,1,0:T(8,128)} async-done(((f32[4,800,128]{2,1,0:T(8,128)}), f32[4,200,128]{2,1,0:T(8,128)}) %reduce-scatter.13.cloned.1.call-update) | async-done | bytes 409616 | tf_op jit(solution)/shard_map/reduce_scatter | solution.py:260
  236.4 18.7 %copy.73 = f32[4,5,160,640]{2,1,0,3:T(8,128)} copy(f32[4,5,160,640]{3,2,1,0:T(8,128)} %fusion.43) | data formatting | bytes 16384000
  255.1 16.8 %reshape.1433 = f32[640,3200]{1,0:T(8,128)} reshape(f32[640,4,5,160]{3,2,1,0:T(8,128)} %bitcast.280) | data formatting | bytes 16384000
  271.9 3.4 collective-permute-start.4
  277.5 6.0 copy.54
  283.5 8.3 %copy.59 = bf16[5,640,640]{2,1,0:T(8,128)(2,1)} copy(bf16[5,640,640]{1,2,0:T(8,128)(2,1)} %bitcast.284) | data formatting | bytes 8192000 | tf_op jit(solution)/shard_map/transpose | solution.py:277
  297.3 13.3 %fusion.71 = (f32[640]{0:T(1024)S(1)}, f32[1024]{0:T(1024)S(1)}, f32[1024]{0:T(1024)S(1)}, f32[640]{0:T(1024)S(1)}, f32[1,640,1024]{1,2,0:T(8,128)}) fusion(f32[1024]{0:T(1024)S(1)} %add_rsqrt_fusion.1, f32[1024]{0:T(1024)S(1)} %broadcast_multiply_fusion.5, f32[640]{0:T(1024)S(1)} %add.205, f32[1024,640]{1,0:T(8,128)S(1)} %copy-done.3, f32[640]{0:T(1024)S(1)} %mul.448, ...), kind=kOutput, calls=%fused_computation.124 | convolution fusion | flops 4248695808 | bytes 15921664 | tf_op jit(solution)/shard_map/oc,rol->rcl/dot_general | solution.py:278
  312.3 2.4 fusion.70
  316.1 19.7 %multiply_reduce_fusion = (f32[1280]{0:T(1024)S(1)}, f32[1024]{0:T(1024)S(1)}, f32[1024]{0:T(1024)S(1)}, f32[1280]{0:T(1024)S(1)}, f32[1,1280,1024]{1,2,0:T(8,128)}) fusion(f32[1,1280,1024]{1,2,0:T(8,128)} %copy.54, f32[1024]{0:T(1024)S(1)} %broadcast_multiply_fusion.8, f32[1024]{0:T(1024)S(1)} %add_rsqrt_fusion.2, f32[1280]{0:T(1024)S(1)} %mul.438, ...), kind=kOutput, calls=%fused_computation.27 | convolution fusion | flops 1785196032 | bytes 13471744 | tf_op jit(solution)/shard_map/dh,rhl->rdl/dot_general | solution.py:286
  336.3 15.5 %fusion.84 = f32[4,320,640]{2,1,0:T(8,128)S(1)} fusion(bf16[4,320,1024]{2,1,0:T(8,128)(2,1)S(1)} %copy-done.1, f32[4,320]{1,0:T(4,128)S(1)} %copy-done.32, f32[4,320]{1,0:T(4,128)S(1)} %copy-done.30, f32[1024]{0:T(1024)S(1)} %add_rsqrt_fusion.2, f32[1024]{0:T(1024)S(1)} %broadcast_multiply_fusion.8, bf16[1,640,1024]{1,2,0:T(8,128)(2,1)} %copy-done.12), kind=kOutput, calls=%fused_computation.158 | convolution fusion | flops 1769472000 | bytes 7227392 | tf_op jit(solution)/shard_map/rdl,rhl->dh/dot_general | solution.py:285
  351.8 2.2 pad_maximum_fusion
  354.1 4.7 reshape.1425
  358.8 28.1 %reduce-scatter.21.cloned.1.call-done = f32[80,3200]{1,0:T(8,128)} async-done(((f32[320,3200]{1,0:T(8,128)}), f32[80,3200]{1,0:T(8,128)}) %reduce-scatter.21.cloned.1.call-update) | async-done | bytes 1024016
  386.9 2.3 reshape.1436
  393.0 11.7 %fusion.17 = bf16[1,1280,1024]{1,2,0:T(8,128)(2,1)} fusion(f32[1,1280,1024]{1,2,0:T(8,128)} %copy.54, bf16[640,1280]{1,0:T(8,128)(2,1)} %bitcast.296, f32[1280]{0:T(1024)S(1)} %add.220, f32[640]{0:T(1024)S(1)} %copy-done.36, f32[640]{0:T(1024)S(1)} %copy-done.34, f32[1024]{0:T(1024)S(1)} %copy-done.27, f32[1024]{0:T(1024)S(1)} %copy-done.25, ...), kind=kOutput, calls=%fused_computation.21 | convolution fusion | flops 1727528960 | bytes 12145152 | tf_op jit(solution)/shard_map/hd,rhl->rdl/dot_general | solution.py:251
  404.7 4.4 copy.55
  409.1 4.6 all-to-all-start.1
  414.4 4.9 copy.60
  419.3 6.6 %add_convert_fusion = bf16[1,1280,1024]{1,2,0:T(8,128)(2,1)S(1)} fusion(f32[1,1280,1024]{1,2,0:T(8,128)} %copy.60, f32[1,1280,1024]{1,2,0:T(8,128)} %get-tuple-element.96, f32[1,1280,1024]{1,2,0:T(8,128)} %copy.54, f32[1024]{0:T(1024)S(1)} %broadcast_multiply_fusion.6, f32[1024]{0:T(1024)S(1)} %broadcast_multiply_fusion.7, f32[1280]{0:T(1024)S(1)} %mul.438, ...), kind=kLoop, calls=%fused_computation.42 | loop fusion | flops 11796480 | bytes 18371584 | tf_op jit(solution)/shard_map/convert_element_type | solution.py:290
  425.9 2.6 copy.61
  428.5 15.2 %all-to-all-done.1 = bf16[4,320,1024]{2,1,0:T(8,128)(2,1)} async-done(((bf16[4,320,1024]{2,1,0:T(8,128)(2,1)}), bf16[4,320,1024]{2,1,0:T(8,128)(2,1)}, u32[]{:S(2)}, u32[]{:S(2)}) %all-to-all-start.1) | async-done | bytes 2621472 | tf_op jit(solution)/shard_map/all_to_all | solution.py:167
  443.7 3.9 all-to-all-start.3
  447.6 29.9 %all-to-all-done.3 = bf16[4,320,1024]{2,1,0:T(8,128)(2,1)S(1)} async-done(((bf16[4,320,1024]{2,1,0:T(8,128)(2,1)}), bf16[4,320,1024]{2,1,0:T(8,128)(2,1)S(1)}, u32[]{:S(2)}, u32[]{:S(2)}) %all-to-all-start.3) | async-done | bytes 2621472 | tf_op jit(solution)/shard_map/all_to_all | solution.py:167
  477.5 29.3 %shard_map.255 = (f32[4,200,128]{2,1,0:T(8,128)}, f32[4,5,160,80]{3,2,1,0:T(8,128)}, f32[4,240,128]{2,1,0:T(8,128)}) custom-call(f32[4,200,128]{2,1,0:T(8,128)} %reduce-scatter.13.cloned.1.call-done.refs_0_, f32[4,5,160,80]{3,2,1,0:T(8,128)} %copy.76.refs_1_, f32[4,240,128]{2,1,0:T(8,128)} %reduce-scatter.17.cloned.1.call-done.refs_2_), custom_call_target="tpu_custom_call" | custom-call | bytes 3850240 | tf_op jit(solution)/shard_map/pallas_call | solution.py:74
  512.0 2.3 reduce_sum.238.refs_1_
  515.9 57.7 %shard_map.256 = (f32[4,200,128]{2,1,0:T(8,128)}, f32[4,5,160,80]{3,2,1,0:T(8,128)}, f32[4,240,128]{2,1,0:T(8,128)}) custom-call(f32[200,128]{1,0:T(8,128)} %reduce_sum.237.refs_0_, f32[5,160,80]{2,1,0:T(8,128)} %reduce_sum.238.refs_1_, f32[240,128]{1,0:T(8,128)} %reduce_sum.239.refs_2_), custom_call_target="tpu_custom_call" | custom-call | bytes 3850240 | tf_op jit(solution)/shard_map/pallas_call | solution.py:74
  577.7 6.0 shard_map.257
  590.3 3.8 copy.66
  598.2 3.6 copy.107
  (191 shorter events, 65.8 us)
Async XLA Ops:
  7.2 50.7 %copy-start.17 = (bf16[320,640]{1,0:T(8,128)(2,1)S(1)}, bf16[320,640]{1,0:T(8,128)(2,1)}, u32[]{:S(2)}) copy-start(bf16[320,640]{1,0:T(8,128)(2,1)} %param.19) | copy-start | bytes 1228804
  7.2 93.9 %all-gather.4.cloned.1.call-start = ((), (), s32[]{:S(2)}) async-start(), calls=%async_computation.10 | async-start | bytes 2457600 | tf_op jit(solution)/shard_map/all_gather | solution.py:224
  58.6 33.7 %all-to-all-start = ((bf16[4,320,1024]{2,1,0:T(8,128)(2,1)}), bf16[4,320,1024]{2,1,0:T(8,128)(2,1)S(1)}, u32[]{:S(2)}, u32[]{:S(2)}) async-start(bf16[4,320,1024]{2,1,0:T(8,128)(2,1)} %param.15), calls=%async_computation | async-start | bytes 5242880 | tf_op jit(solution)/shard_map/all_to_all | solution.py:154
  62.2 7.1 %copy-start.20 = (f32[1920]{0:T(1024)S(1)}, f32[1920]{0:T(1024)}, u32[]{:S(2)}) copy-start(f32[1920]{0:T(1024)} %concatenate.43.refs_0_) | copy-start | bytes 23044
  62.3 7.1 %copy-start.21 = (f32[4,1920]{1,0:T(4,128)S(1)}, f32[4,1920]{1,0:T(4,128)}, u32[]{:S(2)}) copy-start(f32[4,1920]{1,0:T(4,128)} %get-tuple-element.30) | copy-start | bytes 92164
  62.3 82.2 %all-gather.6.cloned.1.call-start = ((), (), s32[]{:S(2)}) async-start(), calls=%async_computation.11 | async-start | bytes 6144000 | tf_op jit(solution)/shard_map/all_gather | solution.py:225
  63.1 64.1 %collective-permute-start = (s32[1,64]{1,0:T(1,128)S(1)}, s32[1,64]{1,0:T(1,128)S(1)}, u32[]{:S(2)}, u32[]{:S(2)}) collective-permute-start(s32[1,64]{1,0:T(1,128)S(1)} %get-tuple-element.88), channel_id=1, source_target_pairs={{0,4},{1,5},{2,6},{3,7},{8,12},{9,13},{10,14},{11,15},{16,20},{17,... | collective-permute-start | bytes 776 | tf_op jit(solution)/shard_map/ppermute | solution.py:133
  64.4 62.8 %collective-permute-start.2 = (s32[1,64]{1,0:T(1,128)S(1)}, s32[1,64]{1,0:T(1,128)S(1)}, u32[]{:S(2)}, u32[]{:S(2)}) collective-permute-start(s32[1,64]{1,0:T(1,128)S(1)} %get-tuple-element.89), channel_id=1, source_target_pairs={{4,0},{5,1},{6,2},{7,3},{12,8},{13,9},{14,10},{15,11},{20,16},{21,... | collective-permute-start | bytes 776 | tf_op jit(solution)/shard_map/ppermute | solution.py:134
  69.7 141.2 %copy-start.22 = (f32[640]{0:T(1024)}, f32[640]{0:T(1024)S(1)}, u32[]{:S(2)}) copy-start(f32[640]{0:T(1024)S(1)} %add.212) | copy-start | bytes 7684
  69.8 141.1 %copy-start.33 = (f32[640]{0:T(1024)}, f32[640]{0:T(1024)S(1)}, u32[]{:S(2)}) copy-start(f32[640]{0:T(1024)S(1)} %mul.458) | copy-start | bytes 7684
  70.0 129.2 %copy-start.35 = (f32[640]{0:T(1024)}, f32[640]{0:T(1024)S(1)}, u32[]{:S(2)}) copy-start(f32[640]{0:T(1024)S(1)} %add.216) | copy-start | bytes 7684
  70.8 21.5 %copy-start.29 = (f32[4,320]{1,0:T(4,128)}, f32[4,320]{1,0:T(4,128)S(1)}, u32[]{:S(2)}) copy-start(f32[4,320]{1,0:T(4,128)S(1)} %get-tuple-element.76) | copy-start | bytes 15364
  70.8 21.5 %copy-start.31 = (f32[4,320]{1,0:T(4,128)}, f32[4,320]{1,0:T(4,128)S(1)}, u32[]{:S(2)}) copy-start(f32[4,320]{1,0:T(4,128)S(1)} %get-tuple-element.78) | copy-start | bytes 15364
  92.3 5.9 copy-start
  92.3 65.1 %all-to-all-start.2 = ((bf16[4,320,1024]{2,1,0:T(8,128)(2,1)}), bf16[4,320,1024]{2,1,0:T(8,128)(2,1)}, u32[]{:S(2)}, u32[]{:S(2)}) async-start(bf16[4,320,1024]{2,1,0:T(8,128)(2,1)} %param.29), calls=%async_computation.2 | async-start | bytes 5242880 | tf_op jit(solution)/shard_map/all_to_all | solution.py:154
  96.9 89.7 %reduce-scatter.11.cloned.1.call-start = ((), (), s32[]{:S(2)}) async-start(), calls=%async_computation.13 | async-start | bytes 4915200 | tf_op jit(solution)/shard_map/reduce_scatter | solution.py:259
  118.0 15.6 %copy-start.2 = (f32[1024,640]{1,0:T(8,128)}, f32[1024,640]{1,0:T(8,128)S(1)}, u32[]{:S(2)}) copy-start(f32[1024,640]{1,0:T(8,128)S(1)} %get-tuple-element.91) | copy-start | bytes 7864324
  125.9 4.7 collective-permute-start.1
  127.3 14.3 %collective-permute-start.3 = (bf16[1,640,64]{1,2,0:T(8,128)(2,1)S(1)}, bf16[1,640,64]{1,2,0:T(8,128)(2,1)S(1)}, u32[]{:S(2)}, u32[]{:S(2)}) collective-permute-start(bf16[1,640,64]{1,2,0:T(8,128)(2,1)S(1)} %get-tuple-element.68), channel_id=1, source_target_pairs={{4,0},{5,1},{6,2},{7,3},{12,8},{13,9},{14,10},{15,11},{20,16},{21,... | collective-permute-start | bytes 245768 | tf_op jit(solution)/shard_map/ppermute | solution.py:134
  147.1 9.6 %copy-start.5 = (bf16[5,4,160,640]{3,2,1,0:T(8,128)(2,1)}, bf16[5,4,160,640]{3,2,1,0:T(8,128)(2,1)S(1)}, u32[]{:S(2)}) copy-start(bf16[5,4,160,640]{3,2,1,0:T(8,128)(2,1)S(1)} %copy.53) | copy-start | bytes 12288004
  156.8 42.4 %copy-start.6 = (f32[1024,640]{1,0:T(8,128)}, f32[1024,640]{1,0:T(8,128)S(1)}, u32[]{:S(2)}) copy-start(f32[1024,640]{1,0:T(8,128)S(1)} %get-tuple-element.93) | copy-start | bytes 7864324
  156.8 54.1 %copy-start.24 = (f32[1024]{0:T(1024)}, f32[1024]{0:T(1024)S(1)}, u32[]{:S(2)}) copy-start(f32[1024]{0:T(1024)S(1)} %broadcast_multiply_fusion.4) | copy-start | bytes 12292
  157.4 53.6 %copy-start.26 = (f32[1024]{0:T(1024)}, f32[1024]{0:T(1024)S(1)}, u32[]{:S(2)}) copy-start(f32[1024]{0:T(1024)S(1)} %add_rsqrt_fusion) | copy-start | bytes 12292
  173.6 25.5 %all-gather.8.cloned.1.call-start = ((), (), s32[]{:S(2)}) async-start(), calls=%async_computation.12 | async-start | bytes 2457600 | tf_op jit(solution)/shard_map/all_gather | solution.py:226
  175.3 61.0 %reduce-scatter.13.cloned.1.call-start = ((), (), s32[]{:S(2)}) async-start(), calls=%async_computation.14 | async-start | bytes 2048000 | tf_op jit(solution)/shard_map/reduce_scatter | solution.py:260
  186.6 124.2 %reduce-scatter.19.cloned.1.call-start = ((), (), s32[]{:S(2)}) async-start(), calls=%async_computation.17 | async-start | bytes 12288000
  211.0 3.7 copy-start.10
  271.9 115.1 %reduce-scatter.21.cloned.1.call-start = ((), (), s32[]{:S(2)}) async-start(), calls=%async_computation.18 | async-start | bytes 5120000
  271.9 21.6 %collective-permute-start.4 = (bf16[1,640,64]{1,2,0:T(8,128)(2,1)S(1)}, bf16[1,640,64]{1,2,0:T(8,128)(2,1)S(1)}, u32[]{:S(2)}, u32[]{:S(2)}) collective-permute-start(bf16[1,640,64]{1,2,0:T(8,128)(2,1)S(1)} %get-tuple-element.67), channel_id=1, source_target_pairs={{4,0},{5,1},{6,2},{7,3},{12,8},{13,9},{14,10},{15,11},{20,16},{21,... | collective-permute-start | bytes 245768 | tf_op jit(solution)/shard_map/ppermute | solution.py:134
  292.0 3.2 collective-permute-start.5
  294.2 2.2 copy-start.13
  294.5 2.8 copy-start.3
  310.8 102.9 %reduce-scatter.15.cloned.1.call-start = ((), (), s32[]{:S(2)}) async-start(), calls=%async_computation.15 | async-start | bytes 5898240 | tf_op jit(solution)/shard_map/reduce_scatter | solution.py:259
  316.1 20.2 %copy-start.1 = (bf16[4,320,1024]{2,1,0:T(8,128)(2,1)S(1)}, bf16[4,320,1024]{2,1,0:T(8,128)(2,1)}, u32[]{:S(2)}) copy-start(bf16[4,320,1024]{2,1,0:T(8,128)(2,1)} %copy-done) | copy-start | bytes 7864324
  316.1 20.2 %copy-start.30 = (f32[4,320]{1,0:T(4,128)S(1)}, f32[4,320]{1,0:T(4,128)}, u32[]{:S(2)}) copy-start(f32[4,320]{1,0:T(4,128)} %copy-done.29) | copy-start | bytes 15364
  316.1 20.2 %copy-start.32 = (f32[4,320]{1,0:T(4,128)S(1)}, f32[4,320]{1,0:T(4,128)}, u32[]{:S(2)}) copy-start(f32[4,320]{1,0:T(4,128)} %copy-done.31) | copy-start | bytes 15364
  391.2 1.8 copy-start.23
  391.2 1.8 copy-start.25
  409.1 34.6 %all-to-all-start.1 = ((bf16[4,320,1024]{2,1,0:T(8,128)(2,1)}), bf16[4,320,1024]{2,1,0:T(8,128)(2,1)}, u32[]{:S(2)}, u32[]{:S(2)}) async-start(bf16[4,320,1024]{2,1,0:T(8,128)(2,1)} %bitcast.18), calls=%async_computation.1 | async-start | bytes 5242880 | tf_op jit(solution)/shard_map/all_to_all | solution.py:167
  413.6 63.9 %reduce-scatter.17.cloned.1.call-start = ((), (), s32[]{:S(2)}) async-start(), calls=%async_computation.16 | async-start | bytes 2457600 | tf_op jit(solution)/shard_map/reduce_scatter | solution.py:260
  443.7 33.8 %all-to-all-start.3 = ((bf16[4,320,1024]{2,1,0:T(8,128)(2,1)}), bf16[4,320,1024]{2,1,0:T(8,128)(2,1)S(1)}, u32[]{:S(2)}, u32[]{:S(2)}) async-start(bf16[4,320,1024]{2,1,0:T(8,128)(2,1)} %bitcast.285), calls=%async_computation.5 | async-start | bytes 5242880 | tf_op jit(solution)/shard_map/all_to_all | solution.py:167
  477.5 36.8 %copy-start.8 = (bf16[4,320,1024]{2,1,0:T(8,128)(2,1)}, bf16[4,320,1024]{2,1,0:T(8,128)(2,1)S(1)}, u32[]{:S(2)}) copy-start(bf16[4,320,1024]{2,1,0:T(8,128)(2,1)S(1)} %all-to-all-done.3) | copy-start | bytes 7864324
  506.9 7.5 %copy-start.19 = (f32[4,200,128]{2,1,0:T(8,128)S(1)}, f32[4,200,128]{2,1,0:T(8,128)}, u32[]{:S(2)}) copy-start(f32[4,200,128]{2,1,0:T(8,128)} %get-tuple-element.37) | copy-start | bytes 1228804
  510.2 65.0 %copy-start.16 = (f32[240,128]{1,0:T(8,128)S(1)}, f32[240,128]{1,0:T(8,128)}, u32[]{:S(2)}) copy-start(f32[240,128]{1,0:T(8,128)} %reduce_sum.239.refs_2_) | copy-start | bytes 368644
  575.8 7.8 %copy-start.14 = (f32[4,240,128]{2,1,0:T(8,128)S(1)}, f32[4,240,128]{2,1,0:T(8,128)}, u32[]{:S(2)}) copy-start(f32[4,240,128]{2,1,0:T(8,128)} %bitcast_dynamic-update-slice_fusion.7.refs_2_) | copy-start | bytes 1474564
  583.7 4.5 copy-start.15
  583.7 5.3 copy-start.11
  598.2 3.6 copy-start.9
  (8 other events, 11.5 us)
Sparse Core Ops, SparseCore 0:
  58.7 11.5 all-gather.3
  71.9 14.6 all-gather.5
  173.8 12.7 reduce-scatter.10
  188.1 11.0 all-gather.7
  201.4 34.8 reduce-scatter.12
  272.0 18.2 reduce-scatter.18
  310.9 75.9 reduce-scatter.20
  391.4 13.0 reduce-scatter.14
  416.9 41.5 reduce-scatter.16

commit v2 on v1

--- a/solution.py
+++ b/solution.py
@@ -26,7 +26,8 @@
     return me
 
 
-def _exchange_kernel(sizes, group, gather, count_arrays, *refs):
+def _exchange_kernel(sizes, group, gather, axes, *refs):
+    count_arrays = len(axes)
     x_refs = refs[:count_arrays]
     o_refs = refs[count_arrays : 2 * count_arrays]
     send_sem, recv_sem = refs[2 * count_arrays :]
@@ -50,9 +51,10 @@
     for j in range(1, count):
         peer = lax.rem(me + j, count)
         for i in range(count_arrays):
+            lead = (slice(None),) * axes[i]
             copy = pltpu.make_async_remote_copy(
-                src_ref=x_refs[i] if gather else x_refs[i].at[peer],
-                dst_ref=o_refs[i].at[me],
+                src_ref=x_refs[i] if gather else x_refs[i].at[lead + (peer,)],
+                dst_ref=o_refs[i].at[lead + (me,)],
                 send_sem=send_sem.at[i, j - 1],
                 recv_sem=recv_sem.at[i, j - 1],
                 device_id=device(peer),
@@ -64,15 +66,16 @@
         copy.wait()
 
 
-def exchange(xs, group, collective_id, gather=False):
+def exchange(xs, group, collective_id, gather=False, axes=None):
     sizes = {a: lax.axis_size(a) for a in MESH_AXES}
     count = math.prod(sizes[a] for a in group)
+    axes = tuple(axes or (0,) * len(xs))
     if count == 1:
         return [x[None] if gather else x for x in xs]
     shapes = [jax.ShapeDtypeStruct((count,) + x.shape if gather else x.shape, x.dtype) for x in xs]
     moved = sum(x.size * x.dtype.itemsize * (count if gather else 1) for x in xs)
     outs = pl.pallas_call(
-        functools.partial(_exchange_kernel, sizes, group, gather, len(xs)),
+        functools.partial(_exchange_kernel, sizes, group, gather, axes),
         out_shape=shapes,
         in_specs=[pl.BlockSpec(memory_space=pl.ANY)] * len(xs),
         out_specs=[pl.BlockSpec(memory_space=pl.ANY)] * len(xs),
@@ -85,9 +88,9 @@
     )(*xs)
     me = _group_index(group, sizes, {a: lax.axis_index(a) for a in group})
     placed = []
-    for x, out in zip(xs, outs):
-        own = x if gather else lax.dynamic_index_in_dim(x, me, 0, keepdims=False)
-        placed.append(lax.dynamic_update_index_in_dim(out, own, me, 0))
+    for x, out, axis in zip(xs, outs, axes):
+        own = x if gather else lax.dynamic_index_in_dim(x, me, axis, keepdims=False)
+        placed.append(lax.dynamic_update_index_in_dim(out, own, me, axis))
     return placed
 
 
@@ -267,9 +270,9 @@
     grad_mixed = normalize_back(grad_normed2, unit2, scale2, g2).astype(jnp.bfloat16)
     grad_b_conv = jnp.sum(grad_mixed.astype(jnp.float32), axis=(0, 2))
     grad_w_conv = jnp.einsum(
-        "rkcil,rol->ckio",
+        "rol,rkcil->okci",
+        grad_mixed,
         taps.reshape(prow, KERNEL_TAPS, nch, hloc, part),
-        grad_mixed,
         preferred_element_type=jnp.float32,
     )
     wide_grad = extended(grad_mixed, border, pairs)
@@ -311,14 +314,17 @@
     inner_plus = jnp.concatenate([grad_w_inner.reshape(nch, dloc, hid), flat], axis=1)
     inner_plus = inner_plus.reshape(nch, (dloc + vec_rows) * hid // 128, 128)
 
-    part_conv = reduce_seq_batch(grad_w_conv, 3, part_outer)
+    conv_tail = grad_w_conv.shape[1:]
+    part_conv = reduce_seq_batch(grad_w_conv.reshape(hid, math.prod(conv_tail) // 128, 128), 0, part_outer)
+    part_conv = part_conv.reshape((part_conv.shape[0],) + conv_tail)
     part_inner = reduce_seq_batch(inner_plus, 1, part_conv)
     parts = [part_outer, part_conv, part_inner]
-    parts = [jnp.sum(p, axis=0) for p in exchange(parts, ("ch",), 1)]
+    parts = exchange(parts, ("ch",), 1, axes=(0, 2, 0))
+    parts = [jnp.sum(p, axis=a) for p, a in zip(parts, (0, 2, 0))]
     parts = exchange(parts, ("batch",), 2, gather=True)
     parts = [p.reshape((seqs * batches,) + p.shape[2:]) for p in exchange(parts, ("seq",), 3, gather=True)]
     red_w_outer = parts[0].reshape(hloc, dim)
-    red_w_conv = jnp.moveaxis(parts[1], 0, 2).reshape(KERNEL_TAPS, hloc, hid)
+    red_w_conv = parts[1].reshape(hid, KERNEL_TAPS, hloc).transpose(1, 2, 0)
     red_inner = parts[2].reshape(dloc + vec_rows, hid)
     red_w_inner = red_inner[:dloc]
     mine = red_inner[dloc:].reshape(-1)[:vec_len]

time: 622 us -> 624 us (level)
  Pallas kernels: 137 us -> 159 us
  local copies, waits for them, and re-layouts: 136 us -> 114 us
    unnamed x82 -> x52, local copies, waits for them, and re-layouts: 52.7 us -> 12.6 us
    reduce_scatter x2 -> x3, waiting for transfers between devices: 14.2 us -> 42.5 us  [reduce_seq_batch(): return lax.psum_scatter(g, 'batch', scatter_dimension=split_dim, tiled=True)]
    unnamed x11 -> x9, waiting for transfers between devices: 29 us -> 0.79 us
    pallas_call x4, Pallas kernels: 137 us -> 159 us  [exchange(): pl.pallas_call(functools.partial(_exchange_kernel, sizes, group, gather,...]
    dynamic_update_slice x13, local copies, waits for them, and re-layouts: 14.7 us -> 25.4 us  [exchange(): placed.append(lax.dynamic_update_index_in_dim(out, own, me, axis))]
where the time goes in v2:
time: 624 us; the launch traced here: 612 us
  Pallas kernels  159 us (25%)
  waiting for transfers between devices  125 us (20%)
  matrix products  118 us (19%)
  local copies, waits for them, and re-layouts  114 us (18%)
  other arithmetic  51.6 us (8%)
  starting transfers between devices  30.6 us (5%)
  between operations  14.7 us (2%)
    pallas_call x4, Pallas kernels, exchange(): pl.pallas_call(functools.partial(_exchange_kernel, sizes, group, gather,...  159 us
    all_to_all x2, waiting for transfers between devices, to_channels(): x = lax.all_to_all(x, 'ch', 0, 0, tiled=True)  45.1 us
    reduce_scatter x3, waiting for transfers between devices, reduce_seq_batch(): return lax.psum_scatter(g, 'batch', scatter_dimension=split_dim, tiled=True)  42.5 us
    dynamic_update_slice x13, local copies, waits for them, and re-layouts, exchange(): placed.append(lax.dynamic_update_index_in_dim(out, own, me, axis))  25.4 us
    all_to_all x2, waiting for transfers between devices, to_positions(): x = lax.all_to_all(x, 'ch', 0, 0, tiled=True)  21.4 us
    dot_general x1, matrix products, local(): jnp.einsum('dh,rhl->rdl', w_in, grad_inner, preferred_element_type=jnp.fl...  19.8 us
    dot_general x1, matrix products, local(): jnp.einsum('dh,rdl->rhl', w_in, hidden0, preferred_element_type=jnp.float32)  16.8 us
    dot_general x1, matrix products, local(): jnp.einsum('rdl,rhl->dh', hidden0, grad_inner, preferred_element_type=jnp...  15.6 us
  transfers between devices with their start and end apart: 19, of which 8 were waited for; matrix products, arithmetic and copies ran while one was open for 33% of the time, Pallas kernels for 0%

profile of v2, /device:TPU:9, one launch (start us, length us, event | category | flops | bytes accessed | tf_op | source)
XLA Modules:
  0.0 612.3 jit_solution(16401651201395561613)
XLA Ops:
  13.9 43.9 %shard_map.254 = (f32[4,1920]{1,0:T(4,128)}, bf16[4,160,640]{2,1,0:T(8,128)(2,1)}, bf16[4,5,80,640]{3,2,1,0:T(8,128)(2,1)}, bf16[4,80,1280]{2,1,0:T(8,128)(2,1)}) custom-call(f32[1920]{0:T(1024)} %concatenate.43.refs_0_, bf16[160,640]{1,0:T(8,128)(2,1)} %constant_dynamic-slice_fusion.3.refs_1_, bf16[5,80,640]{2,1,0:T(8,128)(2,1)} %constant_dynamic-slice_fusion.2.refs_2_, ...), custom_call_target="tpu_custom_call" | custom-call | bytes 7434240 | tf_op jit(solution)/shard_map/pallas_call | solution.py:77
  58.6 3.7 all-to-all-start
  64.4 3.0 collective-permute-start.2
  70.9 21.4 %all-to-all-done = bf16[4,320,1024]{2,1,0:T(8,128)(2,1)S(1)} async-done(((bf16[4,320,1024]{2,1,0:T(8,128)(2,1)}), bf16[4,320,1024]{2,1,0:T(8,128)(2,1)S(1)}, u32[]{:S(2)}, u32[]{:S(2)}) %all-to-all-start) | async-done | bytes 2621472 | tf_op jit(solution)/shard_map/all_to_all | solution.py:157
  92.3 4.6 all-to-all-start.2
  98.1 2.9 convert_element_type.149
  101.1 16.8 %fusion.83 = (f32[1024]{0:T(1024)S(1)}, f32[1024,640]{1,0:T(8,128)S(1)}) fusion(f32[640]{0:T(1024)S(1)} %add.206, bf16[1280,640]{1,0:T(8,128)(2,1)} %bitcast.281, f32[1280]{0:T(1024)S(1)} %add.203, f32[1280]{0:T(1024)S(1)} %mul.438, f32[1024]{0:T(1024)S(1)} %add_rsqrt_fusion.2, f32[1,1280,1,1,1,1,1024]{6,1,5,4,3,2,0:T(8,128)} %bitcast.269, ...), kind=kOutput, calls=%fused_computation.160 | convolution fusion | flops 1769470976 | bytes 9527808 | tf_op jit(solution)/shard_map/dh,rdl->rhl/dot_general | solution.py:245
  118.5 7.3 %multiply_convert_fusion.1 = bf16[1,640,1024]{1,2,0:T(8,128)(2,1)S(1)} fusion(f32[640]{0:T(1024)S(1)} %add.210, f32[640]{0:T(1024)S(1)} %mul.448, f32[1024]{0:T(1024)S(1)} %add_rsqrt_fusion.1, f32[1024]{0:T(1024)S(1)} %broadcast_multiply_fusion.5, f32[640]{0:T(1024)S(1)} %add.206, f32[1024,640]{1,0:T(8,128)S(1)} %get-tuple-element.91), kind=kLoop, calls=%fused_computation.142 | loop fusion | flops 45875200 | bytes 3948032 | tf_op jit(solution)/shard_map/convert_element_type | solution.py:247
  127.3 3.3 collective-permute-start.3
  133.5 8.0 %constant_dynamic-update-slice_fusion = bf16[1,3200,1024]{1,2,0:T(8,128)(2,1)} fusion(bf16[1,3200,1024]{1,2,0:T(8,128)(2,1)} %fusion.110, f32[640]{0:T(1024)S(1)} %add.210, f32[640]{0:T(1024)S(1)} %mul.448, f32[1024]{0:T(1024)S(1)} %add_rsqrt_fusion.1, f32[1024]{0:T(1024)S(1)} %broadcast_multiply_fusion.5, f32[640]{0:T(1024)S(1)} %add.206, ...), kind=kLoop, calls=%fused_computation.216 | loop fusion | flops 45875200 | bytes 3948032
  144.4 2.6 copy.39
  147.1 9.6 %fusion.85 = (f32[1024]{0:T(1024)S(1)}, f32[1024,640]{1,0:T(8,128)S(1)}) fusion(f32[640]{0:T(1024)S(1)} %add.213, bf16[3200,640]{1,0:T(8,128)(2,1)S(1)} %bitcast.271, bf16[1,3200,1024]{1,2,0:T(8,128)(2,1)} %fusion.108), kind=kOutput, calls=%fused_computation.162 | convolution fusion | flops 4195613696 | bytes 13277696 | tf_op jit(solution)/shard_map/co,rcl->rol/dot_general | solution.py:251
  157.3 11.8 %fusion.178 = f32[640,1280]{1,0:T(8,128)} fusion(bf16[1280,1024]{1,0:T(8,128)(2,1)} %bitcast.20, f32[640]{0:T(1024)S(1)} %add.217, f32[640]{0:T(1024)S(1)} %mul.458, f32[1024]{0:T(1024)S(1)} %add_rsqrt_fusion, f32[1024]{0:T(1024)S(1)} %broadcast_multiply_fusion.4, f32[640]{0:T(1024)S(1)} %add.213, f32[1024,640]{1,0:T(8,128)S(1)} %get-tuple-element.93), kind=kOutput, calls=%fused_computation.308 | convolution fusion | flops 1723596800 | bytes 8535552 | tf_op jit(solution)/shard_map/rhl,rdl->hd/dot_general | solution.py:258
  169.1 4.5 reshape.1410
  175.3 9.7 %copy.48 = bf16[1,3200,1024]{2,1,0:T(8,128)(2,1)} copy(bf16[1,3200,1024]{1,2,0:T(8,128)(2,1)} %fusion.108) | data formatting | bytes 13107200 | tf_op jit(solution)/shard_map/concatenate | solution.py:149
  186.6 12.5 %all-gather.8.cloned.1.call-done = bf16[4,160,1280]{2,1,0:T(8,128)(2,1)} async-done(((bf16[4,80,1280]{2,1,0:T(8,128)(2,1)}), bf16[4,160,1280]{2,1,0:T(8,128)(2,1)}) %all-gather.8.cloned.1.call-update) | async-done | bytes 1638416 | tf_op jit(solution)/shard_map/all_gather | solution.py:229
  199.1 11.7 %fusion.60 = (f32[640]{0:T(1024)S(1)}, f32[1024]{0:T(1024)S(1)}, f32[1024]{0:T(1024)S(1)}, f32[640]{0:T(1024)S(1)}, f32[1,640,1024]{1,2,0:T(8,128)S(1)}) fusion(f32[1024]{0:T(1024)S(1)} %add_rsqrt_fusion, f32[1024]{0:T(1024)S(1)} %broadcast_multiply_fusion.4, f32[640]{0:T(1024)S(1)} %add.213, f32[1024,640]{1,0:T(8,128)S(1)} %get-tuple-element.93, ...), kind=kOutput, calls=%fused_computation.111 | convolution fusion | flops 1732113152 | bytes 9531904 | tf_op jit(solution)/shard_map/hd,rdl->rhl/dot_general | solution.py:266
  210.8 2.6 convert_reduce_fusion.1
  214.5 7.1 %fusion.112 = f32[640,25,128]{2,0,1:T(8,128)} fusion(bf16[25,128,1024]{2,1,0:T(8,128)(2,1)S(1)} %bitcast.274, bf16[1,640,1024]{1,2,0:T(8,128)(2,1)S(1)} %get-tuple-element.65), kind=kOutput, calls=%fused_computation.201 | convolution fusion | flops 4194304000 | bytes 16056320 | tf_op jit(solution)/shard_map/rol,rkcil->okci/dot_general | solution.py:272
  221.6 14.7 %reduce-scatter.9.cloned.1.call-done.refs_0_ = f32[4,200,128]{2,1,0:T(8,128)} async-done(((f32[4,800,128]{2,1,0:T(8,128)}), f32[4,200,128]{2,1,0:T(8,128)}) %reduce-scatter.9.cloned.1.call-update) | async-done | bytes 409616 | tf_op jit(solution)/shard_map/reduce_scatter | solution.py:263
  236.4 3.4 collective-permute-start.4
  242.0 6.3 %copy.40 = f32[1,1280,1024]{1,2,0:T(8,128)} copy(f32[1,1280,1024]{2,1,0:T(8,128)} %bitcast.270) | data formatting | bytes 10485760 | tf_op jit(solution)/shard_map/convert_element_type | solution.py:242
  248.3 8.4 %copy.45 = bf16[5,640,640]{2,1,0:T(8,128)(2,1)} copy(bf16[5,640,640]{1,2,0:T(8,128)(2,1)} %bitcast.272) | data formatting | bytes 8192000 | tf_op jit(solution)/shard_map/transpose | solution.py:280
  262.0 13.6 %fusion.66 = (f32[640]{0:T(1024)S(1)}, f32[1024]{0:T(1024)S(1)}, f32[1024]{0:T(1024)S(1)}, f32[640]{0:T(1024)S(1)}, f32[1,640,1024]{1,2,0:T(8,128)}) fusion(f32[1024]{0:T(1024)S(1)} %add_rsqrt_fusion.1, f32[1024]{0:T(1024)S(1)} %broadcast_multiply_fusion.5, f32[640]{0:T(1024)S(1)} %add.206, f32[1024,640]{1,0:T(8,128)S(1)} %copy-done.3, f32[640]{0:T(1024)S(1)} %mul.448, ...), kind=kOutput, calls=%fused_computation.122 | convolution fusion | flops 4248695808 | bytes 15921664 | tf_op jit(solution)/shard_map/oc,rol->rcl/dot_general | solution.py:281
  277.3 2.4 fusion.65
  281.1 19.8 %multiply_reduce_fusion = (f32[1280]{0:T(1024)S(1)}, f32[1024]{0:T(1024)S(1)}, f32[1024]{0:T(1024)S(1)}, f32[1280]{0:T(1024)S(1)}, f32[1,1280,1024]{1,2,0:T(8,128)}) fusion(f32[1,1280,1024]{1,2,0:T(8,128)} %copy.40, f32[1024]{0:T(1024)S(1)} %broadcast_multiply_fusion.8, f32[1024]{0:T(1024)S(1)} %add_rsqrt_fusion.2, f32[1280]{0:T(1024)S(1)} %mul.438, ...), kind=kOutput, calls=%fused_computation.25 | convolution fusion | flops 1785196032 | bytes 13471744 | tf_op jit(solution)/shard_map/dh,rhl->rdl/dot_general | solution.py:289
  301.3 15.6 %fusion.79 = f32[4,320,640]{2,1,0:T(8,128)S(1)} fusion(bf16[4,320,1024]{2,1,0:T(8,128)(2,1)S(1)} %copy-done.1, f32[4,320]{1,0:T(4,128)S(1)} %copy-done.23, f32[4,320]{1,0:T(4,128)S(1)} %copy-done.21, f32[1024]{0:T(1024)S(1)} %add_rsqrt_fusion.2, f32[1024]{0:T(1024)S(1)} %broadcast_multiply_fusion.8, bf16[1,640,1024]{1,2,0:T(8,128)(2,1)} %copy-done.9), kind=kOutput, calls=%fused_computation.156 | convolution fusion | flops 1769472000 | bytes 7227392 | tf_op jit(solution)/shard_map/rdl,rhl->dh/dot_general | solution.py:288
  319.1 4.7 reshape.1423
  323.8 27.8 %reduce-scatter.13.cloned.1.call-done = f32[80,25,128]{2,0,1:T(8,128)} async-done(((f32[320,25,128]{2,0,1:T(8,128)}), f32[80,25,128]{2,0,1:T(8,128)}) %reduce-scatter.13.cloned.1.call-update) | async-done | bytes 1024016 | tf_op jit(solution)/shard_map/reduce_scatter | solution.py:263
  353.2 2.4 reshape.1413.refs_1_
  357.4 11.7 %fusion.15 = bf16[1,1280,1024]{1,2,0:T(8,128)(2,1)} fusion(f32[1,1280,1024]{1,2,0:T(8,128)} %copy.40, bf16[640,1280]{1,0:T(8,128)(2,1)} %bitcast.284, f32[1280]{0:T(1024)S(1)} %add.221, f32[640]{0:T(1024)S(1)} %add.217, f32[640]{0:T(1024)S(1)} %mul.458, f32[1024]{0:T(1024)S(1)} %add_rsqrt_fusion, f32[1024]{0:T(1024)S(1)} %broadcast_multiply_fusion.4, ...), kind=kOutput, calls=%fused_computation.19 | convolution fusion | flops 1727528960 | bytes 12145152 | tf_op jit(solution)/shard_map/hd,rhl->rdl/dot_general | solution.py:254
  369.1 4.4 copy.41
  373.4 4.5 all-to-all-start.1
  378.7 4.9 copy.46
  383.6 6.6 %add_convert_fusion = bf16[1,1280,1024]{1,2,0:T(8,128)(2,1)S(1)} fusion(f32[1,1280,1024]{1,2,0:T(8,128)} %copy.46, f32[1,1280,1024]{1,2,0:T(8,128)} %get-tuple-element.96, f32[1,1280,1024]{1,2,0:T(8,128)} %copy.40, f32[1024]{0:T(1024)S(1)} %broadcast_multiply_fusion.6, f32[1024]{0:T(1024)S(1)} %broadcast_multiply_fusion.7, f32[1280]{0:T(1024)S(1)} %mul.438, ...), kind=kLoop, calls=%fused_computation.40 | loop fusion | flops 11796480 | bytes 18371584 | tf_op jit(solution)/shard_map/convert_element_type | solution.py:293
  390.2 2.6 copy.47
  392.9 15.2 %all-to-all-done.1 = bf16[4,320,1024]{2,1,0:T(8,128)(2,1)} async-done(((bf16[4,320,1024]{2,1,0:T(8,128)(2,1)}), bf16[4,320,1024]{2,1,0:T(8,128)(2,1)}, u32[]{:S(2)}, u32[]{:S(2)}) %all-to-all-start.1) | async-done | bytes 2621472 | tf_op jit(solution)/shard_map/all_to_all | solution.py:170
  408.1 3.9 all-to-all-start.3
  411.9 29.9 %all-to-all-done.3 = bf16[4,320,1024]{2,1,0:T(8,128)(2,1)S(1)} async-done(((bf16[4,320,1024]{2,1,0:T(8,128)(2,1)}), bf16[4,320,1024]{2,1,0:T(8,128)(2,1)S(1)}, u32[]{:S(2)}, u32[]{:S(2)}) %all-to-all-start.3) | async-done | bytes 2621472 | tf_op jit(solution)/shard_map/all_to_all | solution.py:170
  443.7 29.4 %shard_map.255 = (f32[4,200,128]{2,1,0:T(8,128)}, f32[80,5,4,160]{3,2,1,0:T(4,128)}, f32[4,240,128]{2,1,0:T(8,128)}) custom-call(f32[4,200,128]{2,1,0:T(8,128)} %reduce-scatter.9.cloned.1.call-done.refs_0_, f32[80,5,4,160]{3,2,1,0:T(4,128)} %reshape.1413.refs_1_, f32[4,240,128]{2,1,0:T(8,128)} %reduce-scatter.17.cloned.1.call-done.refs_2_), custom_call_target="tpu_custom_call" | custom-call | bytes 3850240 | tf_op jit(solution)/shard_map/pallas_call | solution.py:77
  476.3 9.5 %dynamic_update_slice.55 = f32[80,5,4,160]{3,2,1,0:T(4,128)} dynamic-update-slice(f32[80,5,4,160]{3,2,1,0:T(4,128)} %get-tuple-element.38, f32[80,5,1,160]{3,2,1,0:T(1,128)S(1)} %constant_dynamic-slice_fusion, s32[]{:T(128)} %constant.51.clone.1, s32[]{:T(128)} %constant.51.clone.1, s32[]{:T(128)S(6)} %select_n.71, s32[]{:T(128)} %constant.51.clone.1) | dynamic-update-slice | bytes 512004 | tf_op jit(solution)/shard_map/jit(dynamic_update_index_in_dim)/dynamic_update_slice | solution.py:93
  485.8 3.3 reduce_sum.238.refs_1_
  492.3 78.8 %shard_map.256 = (f32[4,200,128]{2,1,0:T(8,128)}, f32[4,80,5,160]{3,2,1,0:T(8,128)}, f32[4,240,128]{2,1,0:T(8,128)}) custom-call(f32[200,128]{1,0:T(8,128)} %reduce_sum.237.refs_0_, f32[80,5,160]{2,1,0:T(8,128)} %reduce_sum.238.refs_1_, f32[240,128]{1,0:T(8,128)} %reduce_sum.239.refs_2_), custom_call_target="tpu_custom_call" | custom-call | bytes 3850240 | tf_op jit(solution)/shard_map/pallas_call | solution.py:77
  575.3 7.4 %shard_map.257 = (f32[2,4,200,128]{3,2,1,0:T(8,128)}, f32[2,4,80,5,160]{4,3,2,1,0:T(8,128)}, f32[2,4,240,128]{3,2,1,0:T(8,128)}) custom-call(f32[4,200,128]{2,1,0:T(8,128)} %bitcast_dynamic-update-slice_fusion.8.refs_0_, f32[4,80,5,160]{3,2,1,0:T(8,128)} %bitcast_dynamic-update-slice_fusion.1.refs_1_, f32[4,240,128]{2,1,0:T(8,128)} %bitcast_dynamic-update-slice_fusion.7.refs_2_), custom_call_target="tpu_custom_call" | custom-call | bytes 7700480 | tf_op jit(solution)/shard_map/pallas_call | solution.py:77
  583.6 2.3 reshape_reshape.13
  590.9 3.4 bitcast_dynamic-update-slice_fusion
  594.4 5.2 copy.52
  600.6 3.5 copy.84
  (163 shorter events, 65.2 us)
Async XLA Ops:
  7.2 50.7 %copy-start.15 = (bf16[320,640]{1,0:T(8,128)(2,1)S(1)}, bf16[320,640]{1,0:T(8,128)(2,1)}, u32[]{:S(2)}) copy-start(bf16[320,640]{1,0:T(8,128)(2,1)} %param.19) | copy-start | bytes 1228804
  7.2 93.9 %all-gather.4.cloned.1.call-start = ((), (), s32[]{:S(2)}) async-start(), calls=%async_computation.10 | async-start | bytes 2457600 | tf_op jit(solution)/shard_map/all_gather | solution.py:227
  58.6 33.7 %all-to-all-start = ((bf16[4,320,1024]{2,1,0:T(8,128)(2,1)}), bf16[4,320,1024]{2,1,0:T(8,128)(2,1)S(1)}, u32[]{:S(2)}, u32[]{:S(2)}) async-start(bf16[4,320,1024]{2,1,0:T(8,128)(2,1)} %param.15), calls=%async_computation | async-start | bytes 5242880 | tf_op jit(solution)/shard_map/all_to_all | solution.py:157
  62.3 7.1 %copy-start.17 = (f32[1920]{0:T(1024)S(1)}, f32[1920]{0:T(1024)}, u32[]{:S(2)}) copy-start(f32[1920]{0:T(1024)} %concatenate.43.refs_0_) | copy-start | bytes 23044
  62.3 7.1 %copy-start.18 = (f32[4,1920]{1,0:T(4,128)S(1)}, f32[4,1920]{1,0:T(4,128)}, u32[]{:S(2)}) copy-start(f32[4,1920]{1,0:T(4,128)} %get-tuple-element.30) | copy-start | bytes 92164
  62.3 82.1 %all-gather.6.cloned.1.call-start = ((), (), s32[]{:S(2)}) async-start(), calls=%async_computation.11 | async-start | bytes 6144000 | tf_op jit(solution)/shard_map/all_gather | solution.py:228
  63.1 64.0 %collective-permute-start = (s32[1,64]{1,0:T(1,128)S(1)}, s32[1,64]{1,0:T(1,128)S(1)}, u32[]{:S(2)}, u32[]{:S(2)}) collective-permute-start(s32[1,64]{1,0:T(1,128)S(1)} %get-tuple-element.88), channel_id=1, source_target_pairs={{0,4},{1,5},{2,6},{3,7},{8,12},{9,13},{10,14},{11,15},{16,20},{17,... | collective-permute-start | bytes 776 | tf_op jit(solution)/shard_map/ppermute | solution.py:136
  64.4 62.7 %collective-permute-start.2 = (s32[1,64]{1,0:T(1,128)S(1)}, s32[1,64]{1,0:T(1,128)S(1)}, u32[]{:S(2)}, u32[]{:S(2)}) collective-permute-start(s32[1,64]{1,0:T(1,128)S(1)} %get-tuple-element.89), channel_id=1, source_target_pairs={{4,0},{5,1},{6,2},{7,3},{12,8},{13,9},{14,10},{15,11},{20,16},{21,... | collective-permute-start | bytes 776 | tf_op jit(solution)/shard_map/ppermute | solution.py:137
  70.8 21.5 %copy-start.20 = (f32[4,320]{1,0:T(4,128)}, f32[4,320]{1,0:T(4,128)S(1)}, u32[]{:S(2)}) copy-start(f32[4,320]{1,0:T(4,128)S(1)} %get-tuple-element.76) | copy-start | bytes 15364
  70.8 21.5 %copy-start.22 = (f32[4,320]{1,0:T(4,128)}, f32[4,320]{1,0:T(4,128)S(1)}, u32[]{:S(2)}) copy-start(f32[4,320]{1,0:T(4,128)S(1)} %get-tuple-element.78) | copy-start | bytes 15364
  92.3 5.8 copy-start
  92.3 65.0 %all-to-all-start.2 = ((bf16[4,320,1024]{2,1,0:T(8,128)(2,1)}), bf16[4,320,1024]{2,1,0:T(8,128)(2,1)}, u32[]{:S(2)}, u32[]{:S(2)}) async-start(bf16[4,320,1024]{2,1,0:T(8,128)(2,1)} %param.29), calls=%async_computation.2 | async-start | bytes 5242880 | tf_op jit(solution)/shard_map/all_to_all | solution.py:157
  96.9 89.7 %reduce-scatter.7.cloned.1.call-start = ((), (), s32[]{:S(2)}) async-start(), calls=%async_computation.13 | async-start | bytes 4915200 | tf_op jit(solution)/shard_map/reduce_scatter | solution.py:262
  117.9 15.6 %copy-start.2 = (f32[1024,640]{1,0:T(8,128)}, f32[1024,640]{1,0:T(8,128)S(1)}, u32[]{:S(2)}) copy-start(f32[1024,640]{1,0:T(8,128)S(1)} %get-tuple-element.91) | copy-start | bytes 7864324
  125.8 4.7 collective-permute-start.1
  127.3 14.3 %collective-permute-start.3 = (bf16[1,640,64]{1,2,0:T(8,128)(2,1)S(1)}, bf16[1,640,64]{1,2,0:T(8,128)(2,1)S(1)}, u32[]{:S(2)}, u32[]{:S(2)}) collective-permute-start(bf16[1,640,64]{1,2,0:T(8,128)(2,1)S(1)} %get-tuple-element.68), channel_id=1, source_target_pairs={{4,0},{5,1},{6,2},{7,3},{12,8},{13,9},{14,10},{15,11},{20,16},{21,... | collective-permute-start | bytes 245768 | tf_op jit(solution)/shard_map/ppermute | solution.py:137
  147.1 9.6 %copy-start.5 = (bf16[5,4,160,640]{3,2,1,0:T(8,128)(2,1)}, bf16[5,4,160,640]{3,2,1,0:T(8,128)(2,1)S(1)}, u32[]{:S(2)}) copy-start(bf16[5,4,160,640]{3,2,1,0:T(8,128)(2,1)S(1)} %copy.39) | copy-start | bytes 12288004
  156.7 42.4 %copy-start.6 = (f32[1024,640]{1,0:T(8,128)}, f32[1024,640]{1,0:T(8,128)S(1)}, u32[]{:S(2)}) copy-start(f32[1024,640]{1,0:T(8,128)S(1)} %get-tuple-element.93) | copy-start | bytes 7864324
  173.5 1.0 copy-start.16
  173.6 25.5 %all-gather.8.cloned.1.call-start = ((), (), s32[]{:S(2)}) async-start(), calls=%async_computation.12 | async-start | bytes 2457600 | tf_op jit(solution)/shard_map/all_gather | solution.py:229
  175.3 61.0 %reduce-scatter.9.cloned.1.call-start = ((), (), s32[]{:S(2)}) async-start(), calls=%async_computation.14 | async-start | bytes 2048000 | tf_op jit(solution)/shard_map/reduce_scatter | solution.py:263
  186.6 89.2 %reduce-scatter.11.cloned.1.call-start = ((), (), s32[]{:S(2)}) async-start(), calls=%async_computation.15 | async-start | bytes 12288000 | tf_op jit(solution)/shard_map/reduce_scatter | solution.py:262
  210.8 3.7 copy-start.8
  236.3 115.3 %reduce-scatter.13.cloned.1.call-start = ((), (), s32[]{:S(2)}) async-start(), calls=%async_computation.16 | async-start | bytes 5120000 | tf_op jit(solution)/shard_map/reduce_scatter | solution.py:263
  236.4 21.8 %collective-permute-start.4 = (bf16[1,640,64]{1,2,0:T(8,128)(2,1)S(1)}, bf16[1,640,64]{1,2,0:T(8,128)(2,1)S(1)}, u32[]{:S(2)}, u32[]{:S(2)}) collective-permute-start(bf16[1,640,64]{1,2,0:T(8,128)(2,1)S(1)} %get-tuple-element.67), channel_id=1, source_target_pairs={{4,0},{5,1},{6,2},{7,3},{12,8},{13,9},{14,10},{15,11},{20,16},{21,... | collective-permute-start | bytes 245768 | tf_op jit(solution)/shard_map/ppermute | solution.py:137
  256.9 3.2 collective-permute-start.5
  258.9 2.2 copy-start.10
  259.1 2.8 copy-start.3
  275.5 1.7 copy-start.4
  275.8 102.3 %reduce-scatter.15.cloned.1.call-start = ((), (), s32[]{:S(2)}) async-start(), calls=%async_computation.17 | async-start | bytes 5898240 | tf_op jit(solution)/shard_map/reduce_scatter | solution.py:262
  279.7 1.1 copy-start.9
  281.1 20.3 %copy-start.1 = (bf16[4,320,1024]{2,1,0:T(8,128)(2,1)S(1)}, bf16[4,320,1024]{2,1,0:T(8,128)(2,1)}, u32[]{:S(2)}) copy-start(bf16[4,320,1024]{2,1,0:T(8,128)(2,1)} %copy-done) | copy-start | bytes 7864324
  281.1 20.3 %copy-start.21 = (f32[4,320]{1,0:T(4,128)S(1)}, f32[4,320]{1,0:T(4,128)}, u32[]{:S(2)}) copy-start(f32[4,320]{1,0:T(4,128)} %copy-done.20) | copy-start | bytes 15364
  281.1 20.3 %copy-start.23 = (f32[4,320]{1,0:T(4,128)S(1)}, f32[4,320]{1,0:T(4,128)}, u32[]{:S(2)}) copy-start(f32[4,320]{1,0:T(4,128)} %copy-done.22) | copy-start | bytes 15364
  355.6 0.7 copy-start.19
  355.6 1.8 copy-start.7
  373.4 34.6 %all-to-all-start.1 = ((bf16[4,320,1024]{2,1,0:T(8,128)(2,1)}), bf16[4,320,1024]{2,1,0:T(8,128)(2,1)}, u32[]{:S(2)}, u32[]{:S(2)}) async-start(bf16[4,320,1024]{2,1,0:T(8,128)(2,1)} %bitcast.18), calls=%async_computation.1 | async-start | bytes 5242880 | tf_op jit(solution)/shard_map/all_to_all | solution.py:170
  378.0 65.6 %reduce-scatter.17.cloned.1.call-start = ((), (), s32[]{:S(2)}) async-start(), calls=%async_computation.18 | async-start | bytes 2457600 | tf_op jit(solution)/shard_map/reduce_scatter | solution.py:263
  408.1 33.8 %all-to-all-start.3 = ((bf16[4,320,1024]{2,1,0:T(8,128)(2,1)}), bf16[4,320,1024]{2,1,0:T(8,128)(2,1)S(1)}, u32[]{:S(2)}, u32[]{:S(2)}) async-start(bf16[4,320,1024]{2,1,0:T(8,128)(2,1)} %bitcast.273), calls=%async_computation.5 | async-start | bytes 5242880 | tf_op jit(solution)/shard_map/all_to_all | solution.py:170
  476.3 96.3 %copy-start.13 = (f32[240,128]{1,0:T(8,128)S(1)}, f32[240,128]{1,0:T(8,128)}, u32[]{:S(2)}) copy-start(f32[240,128]{1,0:T(8,128)} %reduce_sum.239.refs_2_) | copy-start | bytes 368644
  573.3 9.4 %copy-start.11 = (f32[4,240,128]{2,1,0:T(8,128)S(1)}, f32[4,240,128]{2,1,0:T(8,128)}, u32[]{:S(2)}) copy-start(f32[4,240,128]{2,1,0:T(8,128)} %bitcast_dynamic-update-slice_fusion.7.refs_2_) | copy-start | bytes 1474564
  582.7 7.4 %copy-start.12 = (f32[4,200,128]{2,1,0:T(8,128)S(1)}, f32[4,200,128]{2,1,0:T(8,128)}, u32[]{:S(2)}) copy-start(f32[4,200,128]{2,1,0:T(8,128)} %bitcast_dynamic-update-slice_fusion.8.refs_0_) | copy-start | bytes 1228804
  594.4 5.2 copy-start.14
Sparse Core Ops, SparseCore 0:
  58.7 11.5 all-gather.3
  71.9 14.6 all-gather.5
  173.7 12.7 reduce-scatter.6
  188.0 11.0 all-gather.7
  201.4 34.8 reduce-scatter.8
  238.5 18.2 reduce-scatter.10
  275.9 75.7 reduce-scatter.12
  355.8 13.0 reduce-scatter.14
  381.3 41.5 reduce-scatter.16

commit v3 on v2

--- a/solution.py
+++ b/solution.py
@@ -253,6 +253,7 @@
     hidden2 = gelu_exact(normed2).astype(jnp.bfloat16)
     branch = jnp.einsum("hd,rhl->rdl", w_out, hidden2, preferred_element_type=jnp.float32)
     output = (residual + branch + b_out[:, None]).astype(jnp.bfloat16)
+    output = to_channels(output, nch, q_count, rows)
 
     grad_b_outer = jnp.sum(cot.astype(jnp.float32), axis=(0, 2))
     grad_w_outer = jnp.einsum("rhl,rdl->hd", hidden2, cot, preferred_element_type=jnp.float32)
@@ -283,7 +284,7 @@
     grad_norm1_gain = jnp.sum(grad_normed1 * unit1, axis=(0, 2))
     grad_norm1_shift = jnp.sum(grad_normed1, axis=(0, 2))
     grad_inner = normalize_back(grad_normed1, unit1, scale1, g1).astype(jnp.bfloat16)
-    grad_inner, _ = lax.optimization_barrier((grad_inner, part_outer))
+    grad_inner, _, output = lax.optimization_barrier((grad_inner, part_outer, output))
     grad_b_inner = jnp.sum(grad_inner.astype(jnp.float32), axis=(0, 2))
     grad_w_inner = jnp.einsum("rdl,rhl->dh", hidden0, grad_inner, preferred_element_type=jnp.float32)
     grad_hidden0 = jnp.einsum("dh,rhl->rdl", w_in, grad_inner, preferred_element_type=jnp.float32)
@@ -292,7 +293,6 @@
     grad_norm0_shift = jnp.sum(grad_normed0, axis=(0, 2))
     input_grad = (cot.astype(jnp.float32) + normalize_back(grad_normed0, unit0, scale0, g0)).astype(jnp.bfloat16)
 
-    output = to_channels(output, nch, q_count, rows)
     input_grad = to_channels(input_grad, nch, q_count, rows)
 
     vectors = [
@@ -315,17 +315,25 @@
     inner_plus = inner_plus.reshape(nch, (dloc + vec_rows) * hid // 128, 128)
 
     conv_tail = grad_w_conv.shape[1:]
+    def finish(part, axis, cid):
+        part = exchange([part], ("ch",), cid, axes=(axis,))[0]
+        part = jnp.sum(part, axis=axis)
+        shape = part.shape
+        if part.size % 128 == 0:
+            part = part.reshape(part.size // 128, 128)
+        part = exchange([part], ("batch",), cid + 1, gather=True)[0]
+        part = exchange([part], ("seq",), cid + 2, gather=True)[0]
+        return part.reshape((seqs * batches,) + shape)
+
+    conv_tail = grad_w_conv.shape[1:]
     part_conv = reduce_seq_batch(grad_w_conv.reshape(hid, math.prod(conv_tail) // 128, 128), 0, part_outer)
     part_conv = part_conv.reshape((part_conv.shape[0],) + conv_tail)
+    part_outer, _ = lax.optimization_barrier((part_outer, grad_w_conv))
+    red_w_outer = finish(part_outer, 0, 1).reshape(hloc, dim)
     part_inner = reduce_seq_batch(inner_plus, 1, part_conv)
-    parts = [part_outer, part_conv, part_inner]
-    parts = exchange(parts, ("ch",), 1, axes=(0, 2, 0))
-    parts = [jnp.sum(p, axis=a) for p, a in zip(parts, (0, 2, 0))]
-    parts = exchange(parts, ("batch",), 2, gather=True)
-    parts = [p.reshape((seqs * batches,) + p.shape[2:]) for p in exchange(parts, ("seq",), 3, gather=True)]
-    red_w_outer = parts[0].reshape(hloc, dim)
-    red_w_conv = parts[1].reshape(hid, KERNEL_TAPS, hloc).transpose(1, 2, 0)
-    red_inner = parts[2].reshape(dloc + vec_rows, hid)
+    part_conv, _ = lax.optimization_barrier((part_conv, inner_plus))
+    red_w_conv = finish(part_conv, 2, 4).reshape(hid, KERNEL_TAPS, hloc).transpose(1, 2, 0)
+    red_inner = finish(part_inner, 0, 7).reshape(dloc + vec_rows, hid)
     red_w_inner = red_inner[:dloc]
     mine = red_inner[dloc:].reshape(-1)[:vec_len]
     reds = []

time: 624 us -> 632 us (1.013)
  waiting for transfers between devices: 125 us -> 105 us
  local copies, waits for them, and re-layouts: 114 us -> 129 us
  Pallas kernels: 159 us -> 169 us
    all_to_all x2, waiting for transfers between devices: 45.1 us -> 7.47 us  [to_channels(): x = lax.all_to_all(x, 'ch', 0, 0, tiled=True)]
    optimization_barrier x0 -> x1, local copies, waits for them, and re-layouts: none -> 11.2 us  [reduce_seq_batch(): g, _ = lax.optimization_barrier((g, after))]
    reduce_scatter x3, waiting for transfers between devices: 42.5 us -> 52.8 us  [reduce_seq_batch(): return lax.psum_scatter(g, 'batch', scatter_dimension=split_dim, tiled=True)]
    pallas_call x4 -> x10, Pallas kernels: 159 us -> 169 us  [exchange(): pl.pallas_call(functools.partial(_exchange_kernel, sizes, group, gather,...]
    reduce_scatter x3, waiting for transfers between devices: 1.54 us -> 9.77 us  [reduce_seq_batch(): g = lax.psum_scatter(g, 'seq', scatter_dimension=split_dim, tiled=True)]
    unnamed x52 -> x55, local copies, waits for them, and re-layouts: 12.6 us -> 16.6 us
  transfers between devices with their start and end apart: 19 -> 19, of which waited for: 8 -> 7; matrix products, arithmetic and copies ran while one was open for 33% -> 38% of each run, Pallas kernels for 0% -> 16%
where the time goes in v3:
time: 632 us; the launch traced here: 620 us
  Pallas kernels  169 us (27%)
  local copies, waits for them, and re-layouts  129 us (20%)
  matrix products  118 us (19%)
  waiting for transfers between devices  105 us (17%)
  other arithmetic  53.1 us (8%)
  starting transfers between devices  30.7 us (5%)
  between operations  15 us (2%)
    pallas_call x10, Pallas kernels, exchange(): pl.pallas_call(functools.partial(_exchange_kernel, sizes, group, gather,...  169 us
    reduce_scatter x3, waiting for transfers between devices, reduce_seq_batch(): return lax.psum_scatter(g, 'batch', scatter_dimension=split_dim, tiled=True)  52.8 us
    dynamic_update_slice x13, local copies, waits for them, and re-layouts, exchange(): placed.append(lax.dynamic_update_index_in_dim(out, own, me, axis))  25.8 us
    all_to_all x2, waiting for transfers between devices, to_positions(): x = lax.all_to_all(x, 'ch', 0, 0, tiled=True)  22 us
    dot_general x1, matrix products, local(): jnp.einsum('dh,rhl->rdl', w_in, grad_inner, preferred_element_type=jnp.fl...  19.3 us
    dot_general x1, matrix products, local(): jnp.einsum('dh,rdl->rhl', w_in, hidden0, preferred_element_type=jnp.float32)  16.9 us
    unnamed x55, local copies, waits for them, and re-layouts  16.6 us
    dot_general x1, matrix products, local(): jnp.einsum('rdl,rhl->dh', hidden0, grad_inner, preferred_element_type=jnp...  15.6 us
  transfers between devices with their start and end apart: 19, of which 7 were waited for; matrix products, arithmetic and copies ran while one was open for 38% of the time, Pallas kernels for 16%

profile of v3, /device:TPU:9, one launch (start us, length us, event | category | flops | bytes accessed | tf_op | source)
XLA Modules:
  0.0 619.6 jit_solution(9428517192387108220)
XLA Ops:
  13.9 43.9 %shard_map.254 = (f32[4,1920]{1,0:T(4,128)}, bf16[4,160,640]{2,1,0:T(8,128)(2,1)}, bf16[4,5,80,640]{3,2,1,0:T(8,128)(2,1)}, bf16[4,80,1280]{2,1,0:T(8,128)(2,1)}) custom-call(f32[1920]{0:T(1024)} %concatenate.42.refs_0_, bf16[160,640]{1,0:T(8,128)(2,1)} %constant_dynamic-slice_fusion.4.refs_1_, bf16[5,80,640]{2,1,0:T(8,128)(2,1)} %constant_dynamic-slice_fusion.3.refs_2_, ...), custom_call_target="tpu_custom_call" | custom-call | bytes 7434240 | tf_op jit(solution)/shard_map/pallas_call | solution.py:77
  58.6 3.7 all-to-all-start
  70.3 22.0 %all-to-all-done = bf16[4,320,1024]{2,1,0:T(8,128)(2,1)S(1)} async-done(((bf16[4,320,1024]{2,1,0:T(8,128)(2,1)}), bf16[4,320,1024]{2,1,0:T(8,128)(2,1)S(1)}, u32[]{:S(2)}, u32[]{:S(2)}) %all-to-all-start) | async-done | bytes 2621472 | tf_op jit(solution)/shard_map/all_to_all | solution.py:157
  92.3 4.6 all-to-all-start.1
  98.2 3.0 convert_element_type.149
  101.2 16.9 %fusion.83 = (f32[1024]{0:T(1024)S(1)}, f32[1024,640]{1,0:T(8,128)S(1)}) fusion(f32[640]{0:T(1024)S(1)} %add.204, bf16[1280,640]{1,0:T(8,128)(2,1)} %bitcast.280, f32[1280]{0:T(1024)S(1)} %add.201, f32[1280]{0:T(1024)S(1)} %mul.438, f32[1024]{0:T(1024)S(1)} %add_rsqrt_fusion.2, f32[1,1280,1,1,1,1,1024]{6,1,5,4,3,2,0:T(8,128)} %bitcast.268, ...), kind=kOutput, calls=%fused_computation.159 | convolution fusion | flops 1769470976 | bytes 9527808 | tf_op jit(solution)/shard_map/dh,rdl->rhl/dot_general | solution.py:245
  118.7 7.3 %multiply_convert_fusion.1 = bf16[1,640,1024]{1,2,0:T(8,128)(2,1)S(1)} fusion(f32[640]{0:T(1024)S(1)} %add.208, f32[640]{0:T(1024)S(1)} %mul.449, f32[1024]{0:T(1024)S(1)} %add_rsqrt_fusion.1, f32[1024]{0:T(1024)S(1)} %broadcast_multiply_fusion.5, f32[640]{0:T(1024)S(1)} %add.204, f32[1024,640]{1,0:T(8,128)S(1)} %get-tuple-element.93), kind=kLoop, calls=%fused_computation.141 | loop fusion | flops 45875200 | bytes 3948032 | tf_op jit(solution)/shard_map/convert_element_type | solution.py:247
  127.4 3.3 collective-permute-start.3
  133.7 8.0 %constant_dynamic-update-slice_fusion = bf16[1,3200,1024]{1,2,0:T(8,128)(2,1)} fusion(bf16[1,3200,1024]{1,2,0:T(8,128)(2,1)} %fusion.110, f32[640]{0:T(1024)S(1)} %add.208, f32[640]{0:T(1024)S(1)} %mul.449, f32[1024]{0:T(1024)S(1)} %add_rsqrt_fusion.1, f32[1024]{0:T(1024)S(1)} %broadcast_multiply_fusion.5, f32[640]{0:T(1024)S(1)} %add.204, ...), kind=kLoop, calls=%fused_computation.215 | loop fusion | flops 45875200 | bytes 3948032
  144.6 2.6 copy.39
  147.2 9.6 %fusion.85 = (f32[1024]{0:T(1024)S(1)}, f32[1024,640]{1,0:T(8,128)S(1)}) fusion(f32[640]{0:T(1024)S(1)} %add.213, bf16[3200,640]{1,0:T(8,128)(2,1)S(1)} %bitcast.270, bf16[1,3200,1024]{1,2,0:T(8,128)(2,1)} %fusion.108), kind=kOutput, calls=%fused_computation.161 | convolution fusion | flops 4195613696 | bytes 13277696 | tf_op jit(solution)/shard_map/co,rcl->rol/dot_general | solution.py:251
  157.4 11.8 %fusion.179 = f32[640,1280]{1,0:T(8,128)} fusion(bf16[1280,1024]{1,0:T(8,128)(2,1)} %bitcast.14, f32[640]{0:T(1024)S(1)} %add.217, f32[640]{0:T(1024)S(1)} %mul.460, f32[1024]{0:T(1024)S(1)} %add_rsqrt_fusion, f32[1024]{0:T(1024)S(1)} %broadcast_multiply_fusion.4, f32[640]{0:T(1024)S(1)} %add.213, f32[1024,640]{1,0:T(8,128)S(1)} %get-tuple-element.95), kind=kOutput, calls=%fused_computation.308 | convolution fusion | flops 1723596800 | bytes 8535552 | tf_op jit(solution)/shard_map/rhl,rdl->hd/dot_general | solution.py:259
  169.2 4.4 reshape.1416
  175.4 9.7 %copy.49 = bf16[1,3200,1024]{2,1,0:T(8,128)(2,1)} copy(bf16[1,3200,1024]{1,2,0:T(8,128)(2,1)} %fusion.108) | data formatting | bytes 13107200 | tf_op jit(solution)/shard_map/concatenate | solution.py:149
  186.7 12.5 %all-gather.8.cloned.1.call-done = bf16[4,160,1280]{2,1,0:T(8,128)(2,1)} async-done(((bf16[4,80,1280]{2,1,0:T(8,128)(2,1)}), bf16[4,160,1280]{2,1,0:T(8,128)(2,1)}) %all-gather.8.cloned.1.call-update) | async-done | bytes 1638416 | tf_op jit(solution)/shard_map/all_gather | solution.py:229
  199.2 11.7 %fusion.60 = (f32[640]{0:T(1024)S(1)}, f32[1024]{0:T(1024)S(1)}, f32[1024]{0:T(1024)S(1)}, f32[640]{0:T(1024)S(1)}, f32[1,640,1024]{1,2,0:T(8,128)S(1)}) fusion(f32[1024]{0:T(1024)S(1)} %add_rsqrt_fusion, f32[1024]{0:T(1024)S(1)} %broadcast_multiply_fusion.4, f32[640]{0:T(1024)S(1)} %add.213, f32[1024,640]{1,0:T(8,128)S(1)} %get-tuple-element.95, ...), kind=kOutput, calls=%fused_computation.110 | convolution fusion | flops 1732113152 | bytes 9531904 | tf_op jit(solution)/shard_map/hd,rdl->rhl/dot_general | solution.py:267
  214.7 7.6 %fusion.111 = f32[640,5,4,160]{0,3,2,1:T(8,128)} fusion(bf16[5,4,160,1024]{3,2,1,0:T(8,128)(2,1)S(1)} %bitcast.275, bf16[1,640,1024]{1,2,0:T(8,128)(2,1)S(1)} %get-tuple-element.67), kind=kOutput, calls=%fused_computation.199 | convolution fusion | flops 4194304000 | bytes 16056320 | tf_op jit(solution)/shard_map/rol,rkcil->okci/dot_general | solution.py:273
  222.2 14.2 %reduce-scatter.9.cloned.1.call-done.refs_0_ = f32[4,200,128]{2,1,0:T(8,128)} async-done(((f32[4,800,128]{2,1,0:T(8,128)}), f32[4,200,128]{2,1,0:T(8,128)}) %reduce-scatter.9.cloned.1.call-update) | async-done | bytes 409616 | tf_op jit(solution)/shard_map/reduce_scatter | solution.py:264
  236.4 11.2 %copy.51 = f32[640,25,128]{2,1,0:T(8,128)} copy(f32[640,25,128]{0,2,1:T(8,128)} %bitcast.274) | data formatting | bytes 16384000 | tf_op jit(solution)/shard_map/optimization_barrier | solution.py:262
  247.7 5.9 copy.43
  255.8 8.2 %copy.42 = bf16[5,640,640]{2,1,0:T(8,128)(2,1)} copy(bf16[5,640,640]{1,2,0:T(8,128)(2,1)} %bitcast.271) | data formatting | bytes 8192000 | tf_op jit(solution)/shard_map/transpose | solution.py:281
  264.0 4.1 collective-permute-start.4
  269.4 12.7 %fusion.15 = bf16[1,1280,1024]{1,2,0:T(8,128)(2,1)} fusion(f32[1,1280,1024]{1,2,0:T(8,128)} %copy.43, bf16[640,1280]{1,0:T(8,128)(2,1)} %bitcast.283, f32[1280]{0:T(1024)S(1)} %add.221, f32[640]{0:T(1024)S(1)} %add.217, f32[640]{0:T(1024)S(1)} %mul.460, f32[1024]{0:T(1024)S(1)} %add_rsqrt_fusion, f32[1024]{0:T(1024)S(1)} %broadcast_multiply_fusion.4, ...), kind=kOutput, calls=%fused_computation.19 | convolution fusion | flops 1727528960 | bytes 12145152 | tf_op jit(solution)/shard_map/hd,rhl->rdl/dot_general | solution.py:254
  282.0 4.4 copy.44
  286.4 4.5 all-to-all-start.2
  295.0 13.3 %fusion.66 = (f32[640]{0:T(1024)S(1)}, f32[1024]{0:T(1024)S(1)}, f32[1024]{0:T(1024)S(1)}, f32[640]{0:T(1024)S(1)}, f32[1,640,1024]{1,2,0:T(8,128)}) fusion(f32[1024]{0:T(1024)S(1)} %add_rsqrt_fusion.1, f32[1024]{0:T(1024)S(1)} %broadcast_multiply_fusion.5, f32[640]{0:T(1024)S(1)} %add.204, f32[1024,640]{1,0:T(8,128)S(1)} %copy-done.3, f32[640]{0:T(1024)S(1)} %mul.449, ...), kind=kOutput, calls=%fused_computation.121 | convolution fusion | flops 4248695808 | bytes 15921664 | tf_op jit(solution)/shard_map/oc,rol->rcl/dot_general | solution.py:282
  310.3 3.2 fusion.65
  313.5 7.5 %all-to-all-done.2 = bf16[4,320,1024]{2,1,0:T(8,128)(2,1)} async-done(((bf16[4,320,1024]{2,1,0:T(8,128)(2,1)}), bf16[4,320,1024]{2,1,0:T(8,128)(2,1)}, u32[]{:S(2)}, u32[]{:S(2)}) %all-to-all-start.2) | async-done | bytes 2621472 | tf_op jit(solution)/shard_map/all_to_all | solution.py:170
  321.0 19.3 %multiply_reduce_fusion = (f32[1280]{0:T(1024)S(1)}, f32[1024]{0:T(1024)S(1)}, f32[1024]{0:T(1024)S(1)}, f32[1280]{0:T(1024)S(1)}, f32[1,1280,1024]{1,2,0:T(8,128)}) fusion(f32[1,1280,1024]{1,2,0:T(8,128)} %copy.43, f32[1024]{0:T(1024)S(1)} %copy-done.14, f32[1024]{0:T(1024)S(1)} %copy-done.22, f32[1280]{0:T(1024)S(1)} %copy-done.16, ...), kind=kOutput, calls=%fused_computation.25 | convolution fusion | flops 1785196032 | bytes 13471744 | tf_op jit(solution)/shard_map/dh,rhl->rdl/dot_general | solution.py:290
  342.6 15.6 %fusion.79 = f32[4,320,640]{2,1,0:T(8,128)S(1)} fusion(bf16[4,320,1024]{2,1,0:T(8,128)(2,1)S(1)} %copy-done.1, f32[4,320]{1,0:T(4,128)S(1)} %copy-done.18, f32[4,320]{1,0:T(4,128)S(1)} %copy-done.20, f32[1024]{0:T(1024)S(1)} %copy-done.22, f32[1024]{0:T(1024)S(1)} %copy-done.14, bf16[1,640,1024]{1,2,0:T(8,128)(2,1)} %fusion.65), kind=kOutput, calls=%fused_computation.155 | convolution fusion | flops 1769472000 | bytes 7227392 | tf_op jit(solution)/shard_map/rdl,rhl->dh/dot_general | solution.py:289
  360.3 4.8 reshape.1427
  365.1 38.6 %reduce-scatter.13.cloned.1.call-done = f32[80,25,128]{2,1,0:T(8,128)} async-done(((f32[320,25,128]{2,1,0:T(8,128)}), f32[80,25,128]{2,1,0:T(8,128)}) %reduce-scatter.13.cloned.1.call-update) | async-done | bytes 1024016 | tf_op jit(solution)/shard_map/reduce_scatter | solution.py:264
  403.6 3.3 reshape.1431.refs_0_
  407.0 4.9 copy.46
  411.9 8.2 %reduce-scatter.15.cloned.1.call-done = f32[4,960,128]{2,1,0:T(8,128)} async-done(((f32[4,1920,128]{2,1,0:T(8,128)}), f32[4,960,128]{2,1,0:T(8,128)}) %reduce-scatter.15.cloned.1.call-update) | async-done | bytes 1966096 | tf_op jit(solution)/shard_map/reduce_scatter | solution.py:263
  420.2 6.4 %add_convert_fusion = bf16[1,1280,1024]{1,2,0:T(8,128)(2,1)S(1)} fusion(f32[1,1280,1024]{1,2,0:T(8,128)} %copy.46, f32[1,1280,1024]{1,2,0:T(8,128)} %get-tuple-element.98, f32[1,1280,1024]{1,2,0:T(8,128)} %copy.43, f32[1024]{0:T(1024)S(1)} %broadcast_multiply_fusion.6, f32[1024]{0:T(1024)S(1)} %broadcast_multiply_fusion.7, f32[1280]{0:T(1024)S(1)} %copy-done.16, ...), kind=kLoop, calls=%fused_computation.40 | loop fusion | flops 11796480 | bytes 18371584 | tf_op jit(solution)/shard_map/convert_element_type | solution.py:294
  429.3 3.9 all-to-all-start.3
  433.2 35.0 %shard_map.261 = f32[4,200,128]{2,1,0:T(8,128)} custom-call(f32[4,200,128]{2,1,0:T(8,128)} %reduce-scatter.9.cloned.1.call-done.refs_0_), custom_call_target="tpu_custom_call" | custom-call | bytes 819200 | tf_op jit(solution)/shard_map/pallas_call | solution.py:77
  471.4 12.4 %shard_map.262 = f32[4,200,128]{2,1,0:T(8,128)} custom-call(f32[200,128]{1,0:T(8,128)} %reduce_sum.239.refs_0_), custom_call_target="tpu_custom_call" | custom-call | bytes 819200 | tf_op jit(solution)/shard_map/pallas_call | solution.py:77
  491.7 21.5 %shard_map.258 = f32[80,5,4,160]{3,2,1,0:T(4,128)} custom-call(f32[80,5,4,160]{3,2,1,0:T(4,128)} %reshape.1431.refs_0_), custom_call_target="tpu_custom_call" | custom-call | bytes 2048000 | tf_op jit(solution)/shard_map/pallas_call | solution.py:77
  515.0 9.5 %dynamic_update_slice.57 = f32[80,5,4,160]{3,2,1,0:T(4,128)} dynamic-update-slice(f32[80,5,4,160]{3,2,1,0:T(4,128)} %shard_map.258, f32[80,5,1,160]{3,2,1,0:T(1,128)S(1)} %constant_dynamic-slice_fusion, s32[]{:T(128)} %constant.56.clone.1, s32[]{:T(128)} %constant.56.clone.1, s32[]{:T(128)S(6)} %select_n.73, s32[]{:T(128)} %constant.56.clone.1) | dynamic-update-slice | bytes 512004 | tf_op jit(solution)/shard_map/jit(dynamic_update_index_in_dim)/dynamic_update_slice | solution.py:93
  528.1 25.9 %shard_map.259 = f32[4,500,128]{2,1,0:T(8,128)} custom-call(f32[500,128]{1,0:T(8,128)} %reshape.1432.refs_0_), custom_call_target="tpu_custom_call" | custom-call | bytes 2048000 | tf_op jit(solution)/shard_map/pallas_call | solution.py:77
  554.8 3.1 shard_map.260
  560.2 4.8 reshape_reshape.14
  564.9 5.1 copy.52
  570.1 7.7 %shard_map.255 = f32[4,240,128]{2,1,0:T(8,128)} custom-call(f32[4,240,128]{2,1,0:T(8,128)} %reduce-scatter.17.cloned.1.call-done.refs_0_), custom_call_target="tpu_custom_call" | custom-call | bytes 983040 | tf_op jit(solution)/shard_map/pallas_call | solution.py:77
  581.1 14.3 %shard_map.256 = f32[4,240,128]{2,1,0:T(8,128)} custom-call(f32[240,128]{1,0:T(8,128)} %reduce_sum.237.refs_0_), custom_call_target="tpu_custom_call" | custom-call | bytes 983040 | tf_op jit(solution)/shard_map/pallas_call | solution.py:77
  607.7 3.5 copy.84
  (174 shorter events, 85.3 us)
Async XLA Ops:
  7.2 50.7 %copy-start.9 = (bf16[320,640]{1,0:T(8,128)(2,1)S(1)}, bf16[320,640]{1,0:T(8,128)(2,1)}, u32[]{:S(2)}) copy-start(bf16[320,640]{1,0:T(8,128)(2,1)} %param.19) | copy-start | bytes 1228804
  7.2 94.0 %all-gather.4.cloned.1.call-start = ((), (), s32[]{:S(2)}) async-start(), calls=%async_computation.10 | async-start | bytes 2457600 | tf_op jit(solution)/shard_map/all_gather | solution.py:227
  58.6 33.7 %all-to-all-start = ((bf16[4,320,1024]{2,1,0:T(8,128)(2,1)}), bf16[4,320,1024]{2,1,0:T(8,128)(2,1)S(1)}, u32[]{:S(2)}, u32[]{:S(2)}) async-start(bf16[4,320,1024]{2,1,0:T(8,128)(2,1)} %param.15), calls=%async_computation | async-start | bytes 5242880 | tf_op jit(solution)/shard_map/all_to_all | solution.py:157
  62.3 6.6 %copy-start.11 = (f32[1920]{0:T(1024)S(1)}, f32[1920]{0:T(1024)}, u32[]{:S(2)}) copy-start(f32[1920]{0:T(1024)} %concatenate.42.refs_0_) | copy-start | bytes 23044
  62.3 6.6 %copy-start.12 = (f32[4,1920]{1,0:T(4,128)S(1)}, f32[4,1920]{1,0:T(4,128)}, u32[]{:S(2)}) copy-start(f32[4,1920]{1,0:T(4,128)} %get-tuple-element.24) | copy-start | bytes 92164
  62.3 82.3 %all-gather.6.cloned.1.call-start = ((), (), s32[]{:S(2)}) async-start(), calls=%async_computation.11 | async-start | bytes 6144000 | tf_op jit(solution)/shard_map/all_gather | solution.py:228
  63.1 64.1 %collective-permute-start = (s32[1,64]{1,0:T(1,128)S(1)}, s32[1,64]{1,0:T(1,128)S(1)}, u32[]{:S(2)}, u32[]{:S(2)}) collective-permute-start(s32[1,64]{1,0:T(1,128)S(1)} %get-tuple-element.91), channel_id=1, source_target_pairs={{4,0},{5,1},{6,2},{7,3},{12,8},{13,9},{14,10},{15,11},{20,16},{21,... | collective-permute-start | bytes 776 | tf_op jit(solution)/shard_map/ppermute | solution.py:137
  65.6 61.7 %collective-permute-start.1 = (s32[1,64]{1,0:T(1,128)S(1)}, s32[1,64]{1,0:T(1,128)S(1)}, u32[]{:S(2)}, u32[]{:S(2)}) collective-permute-start(s32[1,64]{1,0:T(1,128)S(1)} %get-tuple-element.90), channel_id=1, source_target_pairs={{0,4},{1,5},{2,6},{3,7},{8,12},{9,13},{10,14},{11,15},{16,20},{17,... | collective-permute-start | bytes 776 | tf_op jit(solution)/shard_map/ppermute | solution.py:136
  69.2 0.6 copy-start.17
  69.2 23.1 %copy-start.19 = (f32[4,320]{1,0:T(4,128)}, f32[4,320]{1,0:T(4,128)S(1)}, u32[]{:S(2)}) copy-start(f32[4,320]{1,0:T(4,128)S(1)} %get-tuple-element.74) | copy-start | bytes 15364
  69.8 31.3 %copy-start.23 = (f32[1280]{0:T(1024)}, f32[1280]{0:T(1024)S(1)}, u32[]{:S(2)}) copy-start(f32[1280]{0:T(1024)S(1)} %add.201) | copy-start | bytes 15364
  69.9 31.3 %copy-start.15 = (f32[1280]{0:T(1024)}, f32[1280]{0:T(1024)S(1)}, u32[]{:S(2)}) copy-start(f32[1280]{0:T(1024)S(1)} %mul.438) | copy-start | bytes 15364
  92.3 5.9 copy-start
  92.3 65.1 %all-to-all-start.1 = ((bf16[4,320,1024]{2,1,0:T(8,128)(2,1)}), bf16[4,320,1024]{2,1,0:T(8,128)(2,1)}, u32[]{:S(2)}, u32[]{:S(2)}) async-start(bf16[4,320,1024]{2,1,0:T(8,128)(2,1)} %param.29), calls=%async_computation.1 | async-start | bytes 5242880 | tf_op jit(solution)/shard_map/all_to_all | solution.py:157
  96.9 89.8 %reduce-scatter.7.cloned.1.call-start = ((), (), s32[]{:S(2)}) async-start(), calls=%async_computation.13 | async-start | bytes 4915200 | tf_op jit(solution)/shard_map/reduce_scatter | solution.py:263
  97.4 3.8 copy-start.13
  98.2 3.0 copy-start.21
  118.1 15.6 %copy-start.2 = (f32[1024,640]{1,0:T(8,128)}, f32[1024,640]{1,0:T(8,128)S(1)}, u32[]{:S(2)}) copy-start(f32[1024,640]{1,0:T(8,128)S(1)} %get-tuple-element.93) | copy-start | bytes 7864324
  126.0 4.7 collective-permute-start.2
  127.4 14.3 %collective-permute-start.3 = (bf16[1,640,64]{1,2,0:T(8,128)(2,1)S(1)}, bf16[1,640,64]{1,2,0:T(8,128)(2,1)S(1)}, u32[]{:S(2)}, u32[]{:S(2)}) collective-permute-start(bf16[1,640,64]{1,2,0:T(8,128)(2,1)S(1)} %get-tuple-element.70), channel_id=1, source_target_pairs={{4,0},{5,1},{6,2},{7,3},{12,8},{13,9},{14,10},{15,11},{20,16},{21,... | collective-permute-start | bytes 245768 | tf_op jit(solution)/shard_map/ppermute | solution.py:137
  147.2 9.6 %copy-start.5 = (bf16[5,4,160,640]{3,2,1,0:T(8,128)(2,1)}, bf16[5,4,160,640]{3,2,1,0:T(8,128)(2,1)S(1)}, u32[]{:S(2)}) copy-start(bf16[5,4,160,640]{3,2,1,0:T(8,128)(2,1)S(1)} %copy.39) | copy-start | bytes 12288004
  156.9 42.4 %copy-start.6 = (f32[1024,640]{1,0:T(8,128)}, f32[1024,640]{1,0:T(8,128)S(1)}, u32[]{:S(2)}) copy-start(f32[1024,640]{1,0:T(8,128)S(1)} %get-tuple-element.95) | copy-start | bytes 7864324
  173.7 1.0 copy-start.10
  173.7 25.5 %all-gather.8.cloned.1.call-start = ((), (), s32[]{:S(2)}) async-start(), calls=%async_computation.12 | async-start | bytes 2457600 | tf_op jit(solution)/shard_map/all_gather | solution.py:229
  175.4 61.0 %reduce-scatter.9.cloned.1.call-start = ((), (), s32[]{:S(2)}) async-start(), calls=%async_computation.14 | async-start | bytes 2048000 | tf_op jit(solution)/shard_map/reduce_scatter | solution.py:264
  186.7 121.8 %reduce-scatter.11.cloned.1.call-start = ((), (), s32[]{:S(2)}) async-start(), calls=%async_computation.15 | async-start | bytes 15728640 | tf_op jit(solution)/shard_map/reduce_scatter | solution.py:263
  211.0 3.7 copy-start.7
  264.0 27.2 %collective-permute-start.4 = (bf16[1,640,64]{1,2,0:T(8,128)(2,1)S(1)}, bf16[1,640,64]{1,2,0:T(8,128)(2,1)S(1)}, u32[]{:S(2)}, u32[]{:S(2)}) collective-permute-start(bf16[1,640,64]{1,2,0:T(8,128)(2,1)S(1)} %get-tuple-element.69), channel_id=1, source_target_pairs={{4,0},{5,1},{6,2},{7,3},{12,8},{13,9},{14,10},{15,11},{20,16},{21,... | collective-permute-start | bytes 245768 | tf_op jit(solution)/shard_map/ppermute | solution.py:137
  268.1 24.2 %collective-permute-start.5 = (bf16[1,640,64]{1,2,0:T(8,128)(2,1)S(1)}, bf16[1,640,64]{1,2,0:T(8,128)(2,1)S(1)}, u32[]{:S(2)}, u32[]{:S(2)}) collective-permute-start(bf16[1,640,64]{1,2,0:T(8,128)(2,1)S(1)} %get-tuple-element.68), channel_id=1, source_target_pairs={{0,4},{1,5},{2,6},{3,7},{8,12},{9,13},{10,14},{11,15},{16,20},{17,... | collective-permute-start | bytes 245768 | tf_op jit(solution)/shard_map/ppermute | solution.py:136
  286.4 34.6 %all-to-all-start.2 = ((bf16[4,320,1024]{2,1,0:T(8,128)(2,1)}), bf16[4,320,1024]{2,1,0:T(8,128)(2,1)}, u32[]{:S(2)}, u32[]{:S(2)}) async-start(bf16[4,320,1024]{2,1,0:T(8,128)(2,1)} %bitcast.272), calls=%async_computation.4 | async-start | bytes 5242880 | tf_op jit(solution)/shard_map/all_to_all | solution.py:170
  291.0 112.7 %reduce-scatter.13.cloned.1.call-start = ((), (), s32[]{:S(2)}) async-start(), calls=%async_computation.16 | async-start | bytes 6553600 | tf_op jit(solution)/shard_map/reduce_scatter | solution.py:264
  292.0 2.2 copy-start.8
  292.2 2.8 copy-start.3
  308.5 1.7 copy-start.4
  308.5 111.6 %reduce-scatter.15.cloned.1.call-start = ((), (), s32[]{:S(2)}) async-start(), calls=%async_computation.17 | async-start | bytes 5898240 | tf_op jit(solution)/shard_map/reduce_scatter | solution.py:263
  310.2 10.7 %copy-start.14 = (f32[1024]{0:T(1024)S(1)}, f32[1024]{0:T(1024)}, u32[]{:S(2)}) copy-start(f32[1024]{0:T(1024)} %copy-done.13) | copy-start | bytes 12292
  310.3 10.7 %copy-start.16 = (f32[1280]{0:T(1024)S(1)}, f32[1280]{0:T(1024)}, u32[]{:S(2)}) copy-start(f32[1280]{0:T(1024)} %copy-done.15) | copy-start | bytes 15364
  310.3 10.7 %copy-start.22 = (f32[1024]{0:T(1024)S(1)}, f32[1024]{0:T(1024)}, u32[]{:S(2)}) copy-start(f32[1024]{0:T(1024)} %copy-done.21) | copy-start | bytes 12292
  310.3 10.7 %copy-start.24 = (f32[1280]{0:T(1024)S(1)}, f32[1280]{0:T(1024)}, u32[]{:S(2)}) copy-start(f32[1280]{0:T(1024)} %copy-done.23) | copy-start | bytes 15364
  340.3 2.2 copy-start.1
  340.3 2.2 copy-start.18
  340.3 2.2 copy-start.20
  407.0 163.1 %reduce-scatter.17.cloned.1.call-start = ((), (), s32[]{:S(2)}) async-start(), calls=%async_computation.18 | async-start | bytes 2457600 | tf_op jit(solution)/shard_map/reduce_scatter | solution.py:264
  429.3 62.4 %all-to-all-start.3 = ((bf16[4,320,1024]{2,1,0:T(8,128)(2,1)}), bf16[4,320,1024]{2,1,0:T(8,128)(2,1)S(1)}, u32[]{:S(2)}, u32[]{:S(2)}) async-start(bf16[4,320,1024]{2,1,0:T(8,128)(2,1)} %bitcast.273), calls=%async_computation.5 | async-start | bytes 5242880 | tf_op jit(solution)/shard_map/all_to_all | solution.py:170
Sparse Core Ops, SparseCore 0:
  58.7 11.5 all-gather.3
  71.8 14.6 all-gather.5
  173.8 12.7 reduce-scatter.6
  188.1 11.0 all-gather.7
  201.5 34.8 reduce-scatter.8
  247.7 20.6 reduce-scatter.10
  308.7 94.9 reduce-scatter.12
  407.1 13.0 reduce-scatter.14
  422.6 41.1 reduce-scatter.16

commit v4 on v2

--- a/solution.py
+++ b/solution.py
@@ -262,7 +262,7 @@
         g = lax.psum_scatter(g, "seq", scatter_dimension=split_dim, tiled=True)
         return lax.psum_scatter(g, "batch", scatter_dimension=split_dim, tiled=True)
 
-    part_outer = reduce_seq_batch(grad_w_outer.reshape(nch, hloc * dim // 128, 128), 1)
+    part_outer = reduce_seq_batch(grad_w_outer.reshape(nch, hloc, dim), 2)
     grad_hidden2 = jnp.einsum("hd,rdl->rhl", w_out, cot, preferred_element_type=jnp.float32)
     grad_normed2 = gelu_back(normed2, grad_hidden2)
     grad_norm2_gain = jnp.sum(grad_normed2 * unit2, axis=(0, 2))
@@ -277,8 +277,12 @@
     )
     wide_grad = extended(grad_mixed, border, pairs)
     back_taps = shifted_taps(wide_grad, wide_ids, own_ids, back_offsets, border)
-    kernel_back = jnp.transpose(w_cv, (0, 2, 1)).reshape(KERNEL_TAPS * hid, hid)
-    grad_hidden1 = jnp.einsum("oc,rol->rcl", kernel_back, back_taps, preferred_element_type=jnp.float32)
+    grad_hidden1 = jnp.einsum(
+        "kco,rkol->rcl",
+        w_cv,
+        back_taps.reshape(prow, KERNEL_TAPS, hid, part),
+        preferred_element_type=jnp.float32,
+    )
     grad_normed1 = gelu_back(normed1, grad_hidden1)
     grad_norm1_gain = jnp.sum(grad_normed1 * unit1, axis=(0, 2))
     grad_norm1_shift = jnp.sum(grad_normed1, axis=(0, 2))
@@ -321,9 +325,10 @@
     parts = [part_outer, part_conv, part_inner]
     parts = exchange(parts, ("ch",), 1, axes=(0, 2, 0))
     parts = [jnp.sum(p, axis=a) for p, a in zip(parts, (0, 2, 0))]
+    outer_shape = parts[0].shape
     parts = exchange(parts, ("batch",), 2, gather=True)
     parts = [p.reshape((seqs * batches,) + p.shape[2:]) for p in exchange(parts, ("seq",), 3, gather=True)]
-    red_w_outer = parts[0].reshape(hloc, dim)
+    red_w_outer = jnp.moveaxis(parts[0].reshape((seqs * batches,) + outer_shape), 0, 1).reshape(hloc, dim)
     red_w_conv = parts[1].reshape(hid, KERNEL_TAPS, hloc).transpose(1, 2, 0)
     red_inner = parts[2].reshape(dloc + vec_rows, hid)
     red_w_inner = red_inner[:dloc]

time: 624 us -> 661 us (1.059)
  other arithmetic: 51.6 us -> 62.4 us
  Pallas kernels: 159 us -> 167 us
  local copies, waits for them, and re-layouts: 114 us -> 122 us
    unnamed x9 -> x10, waiting for transfers between devices: 0.79 us -> 17.2 us
    reduce_scatter x3 -> x2, waiting for transfers between devices: 42.5 us -> 29.4 us  [reduce_seq_batch(): return lax.psum_scatter(g, 'batch', scatter_dimension=split_dim, tiled=True)]
    all_gather x1, waiting for transfers between devices: 12.5 us -> 0.02 us  [local(): w_out = lax.all_gather(w_out, 'seq', axis=1, tiled=True).reshape(hid, dim)]
    dot_general x1, matrix products: 16.8 us -> 29 us  [local(): jnp.einsum('dh,rdl->rhl', w_in, hidden0, preferred_element_type=jnp.float32)]
    reduce_scatter x3, waiting for transfers between devices: 1.54 us -> 13 us  [reduce_seq_batch(): g = lax.psum_scatter(g, 'seq', scatter_dimension=split_dim, tiled=True)]
    concatenate x1 -> x2, local copies, waits for them, and re-layouts: 9.71 us -> 19.4 us  [shifted_taps(): return jnp.concatenate(pieces, axis=1)]
    pallas_call x4, Pallas kernels: 159 us -> 167 us  [exchange(): pl.pallas_call(functools.partial(_exchange_kernel, sizes, group, gather,...]
  transfers between devices with their start and end apart: 19 -> 19, of which waited for: 8 -> 6; matrix products, arithmetic and copies ran while one was open for 33% -> 32% of each run, Pallas kernels for 0% -> 0%
where the time goes in v4:
time: 661 us; the launch traced here: 649 us
  Pallas kernels  167 us (25%)
  waiting for transfers between devices  127 us (19%)
  matrix products  124 us (19%)
  local copies, waits for them, and re-layouts  122 us (18%)
  other arithmetic  62.4 us (9%)
  starting transfers between devices  30.7 us (5%)
  between operations  14.7 us (2%)
    pallas_call x4, Pallas kernels, exchange(): pl.pallas_call(functools.partial(_exchange_kernel, sizes, group, gather,...  167 us
    all_to_all x2, waiting for transfers between devices, to_channels(): x = lax.all_to_all(x, 'ch', 0, 0, tiled=True)  45.2 us
    reduce_scatter x2, waiting for transfers between devices, reduce_seq_batch(): return lax.psum_scatter(g, 'batch', scatter_dimension=split_dim, tiled=True)  29.4 us
    dot_general x1, matrix products, local(): jnp.einsum('dh,rdl->rhl', w_in, hidden0, preferred_element_type=jnp.float32)  29 us
    dynamic_update_slice x13, local copies, waits for them, and re-layouts, exchange(): placed.append(lax.dynamic_update_index_in_dim(out, own, me, axis))  24.7 us
    all_to_all x2, waiting for transfers between devices, to_positions(): x = lax.all_to_all(x, 'ch', 0, 0, tiled=True)  22.6 us
    dot_general x1, matrix products, local(): jnp.einsum('dh,rhl->rdl', w_in, grad_inner, preferred_element_type=jnp.fl...  19.5 us
    concatenate x2, local copies, waits for them, and re-layouts, shifted_taps(): return jnp.concatenate(pieces, axis=1)  19.4 us
  transfers between devices with their start and end apart: 19, of which 6 were waited for; matrix products, arithmetic and copies ran while one was open for 32% of the time, Pallas kernels for 0%

profile of v4, /device:TPU:9, one launch (start us, length us, event | category | flops | bytes accessed | tf_op | source)
XLA Modules:
  0.0 649.0 jit_solution(946218170482010047)
XLA Ops:
  14.0 43.9 %shard_map.254 = (f32[4,1920]{1,0:T(4,128)}, bf16[4,160,640]{2,1,0:T(8,128)(2,1)}, bf16[4,5,80,640]{3,2,1,0:T(8,128)(2,1)}, bf16[4,80,1280]{2,1,0:T(8,128)(2,1)}) custom-call(f32[1920]{0:T(1024)} %concatenate.43.refs_0_, bf16[160,640]{1,0:T(8,128)(2,1)} %constant_dynamic-slice_fusion.3.refs_1_, bf16[5,80,640]{2,1,0:T(8,128)(2,1)} %constant_dynamic-slice_fusion.2.refs_2_, ...), custom_call_target="tpu_custom_call" | custom-call | bytes 7434240 | tf_op jit(solution)/shard_map/pallas_call | solution.py:77
  59.7 3.8 all-to-all-start
  65.6 3.0 collective-permute-start.2
  71.0 22.6 %all-to-all-done = bf16[4,320,1024]{2,1,0:T(8,128)(2,1)S(1)} async-done(((bf16[4,320,1024]{2,1,0:T(8,128)(2,1)}), bf16[4,320,1024]{2,1,0:T(8,128)(2,1)S(1)}, u32[]{:S(2)}, u32[]{:S(2)}) %all-to-all-start) | async-done | bytes 2621472 | tf_op jit(solution)/shard_map/all_to_all | solution.py:157
  93.5 4.6 all-to-all-start.2
  99.4 2.9 convert_element_type.149
  102.4 29.0 %fusion.81 = (f32[1024]{0:T(1024)S(1)}, f32[1024,640]{1,0:T(8,128)S(1)}) fusion(f32[640]{0:T(1024)S(1)} %add.206, bf16[1280,640]{1,0:T(8,128)(2,1)} %bitcast.280, f32[1280]{0:T(1024)S(1)} %add.203, f32[1280]{0:T(1024)S(1)} %mul.438, f32[1024]{0:T(1024)S(1)} %add_rsqrt_fusion.2, f32[1,1280,1,1,1,1,1024]{6,1,5,4,3,2,0:T(8,128)} %bitcast.262, ...), kind=kOutput, calls=%fused_computation.158 | convolution fusion | flops 1769470976 | bytes 9527808 | tf_op jit(solution)/shard_map/dh,rdl->rhl/dot_general | solution.py:245
  132.0 7.3 %multiply_convert_fusion.1 = bf16[1,640,1024]{1,2,0:T(8,128)(2,1)S(1)} fusion(f32[640]{0:T(1024)S(1)} %add.210, f32[640]{0:T(1024)S(1)} %mul.448, f32[1024]{0:T(1024)S(1)} %add_rsqrt_fusion.1, f32[1024]{0:T(1024)S(1)} %broadcast_multiply_fusion.5, f32[640]{0:T(1024)S(1)} %add.206, f32[1024,640]{1,0:T(8,128)S(1)} %get-tuple-element.92), kind=kLoop, calls=%fused_computation.140 | loop fusion | flops 45875200 | bytes 3948032 | tf_op jit(solution)/shard_map/convert_element_type | solution.py:247
  140.7 3.2 collective-permute-start.3
  146.9 8.0 %constant_dynamic-update-slice_fusion = bf16[1,3200,1024]{1,2,0:T(8,128)(2,1)} fusion(bf16[1,3200,1024]{1,2,0:T(8,128)(2,1)} %fusion.105, f32[640]{0:T(1024)S(1)} %add.210, f32[640]{0:T(1024)S(1)} %mul.448, f32[1024]{0:T(1024)S(1)} %add_rsqrt_fusion.1, f32[1024]{0:T(1024)S(1)} %broadcast_multiply_fusion.5, f32[640]{0:T(1024)S(1)} %add.206, ...), kind=kLoop, calls=%fused_computation.214 | loop fusion | flops 45875200 | bytes 3948032
  157.7 2.6 copy.59
  160.4 9.2 %fusion.83 = (f32[1024]{0:T(1024)S(1)}, f32[1024,640]{1,0:T(8,128)S(1)}) fusion(f32[640]{0:T(1024)S(1)} %add.213, bf16[3200,640]{1,0:T(8,128)(2,1)S(1)} %bitcast.270, bf16[1,3200,1024]{1,2,0:T(8,128)(2,1)} %fusion.103), kind=kOutput, calls=%fused_computation.160 | convolution fusion | flops 4195613696 | bytes 13277696 | tf_op jit(solution)/shard_map/co,rcl->rol/dot_general | solution.py:251
  170.2 11.9 %fusion.58 = (f32[640]{0:T(1024)S(1)}, f32[1024]{0:T(1024)S(1)}, f32[1024]{0:T(1024)S(1)}, f32[640]{0:T(1024)S(1)}, f32[1,640,1024]{1,2,0:T(8,128)S(1)}) fusion(f32[1024]{0:T(1024)S(1)} %add_rsqrt_fusion, f32[1024]{0:T(1024)S(1)} %broadcast_multiply_fusion.4, f32[640]{0:T(1024)S(1)} %add.213, f32[1024,640]{1,0:T(8,128)S(1)} %get-tuple-element.94, ...), kind=kOutput, calls=%fused_computation.109 | convolution fusion | flops 1732113152 | bytes 9531904 | tf_op jit(solution)/shard_map/hd,rdl->rhl/dot_general | solution.py:266
  182.1 8.9 %convert_reduce_fusion.1 = (f32[640]{0:T(1024)S(1)}, bf16[1,640,1024]{1,2,0:T(8,128)(2,1)S(1)}, bf16[1,640,1024]{1,2,0:T(8,128)(2,1)S(1)}) fusion(f32[1024]{0:T(1024)S(1)} %get-tuple-element.98, f32[1024]{0:T(1024)S(1)} %add_rsqrt_fusion, f32[1024]{0:T(1024)S(1)} %broadcast_multiply_fusion.4, f32[640]{0:T(1024)S(1)} %add.213, f32[1024,640]{1,0:T(8,128)} %copy-done.4, ...), kind=kLoop, calls=%fused_computation.124 | loop fusion | flops 51117440 | bytes 7890944 | tf_op jit(solution)/shard_map/reduce_sum | solution.py:271
  192.5 5.8 fusion.182
  198.4 12.9 %reduce-scatter.9.cloned.1.call-done = f32[4,160,640]{2,1,0:T(8,128)} async-done(((f32[4,160,1280]{2,1,0:T(8,128)}), f32[4,160,640]{2,1,0:T(8,128)}) %reduce-scatter.9.cloned.1.call-update) | async-done | bytes 1638416 | tf_op jit(solution)/shard_map/reduce_scatter | solution.py:262
  211.3 3.8 copy.82
  215.1 3.9 reshape.1436
  219.0 9.6 %copy.70 = bf16[1,3200,1024]{2,1,0:T(8,128)(2,1)} copy(bf16[1,3200,1024]{1,2,0:T(8,128)(2,1)} %fusion.103) | data formatting | bytes 13107200 | tf_op jit(solution)/shard_map/concatenate | solution.py:149
  228.6 9.0 %fusion.107 = f32[640,25,128]{2,0,1:T(8,128)} fusion(bf16[25,128,1024]{2,1,0:T(8,128)(2,1)} %bitcast.267, bf16[1,640,1024]{1,2,0:T(8,128)(2,1)S(1)} %get-tuple-element.65), kind=kOutput, calls=%fused_computation.198 | convolution fusion | flops 4194304000 | bytes 16056320 | tf_op jit(solution)/shard_map/rol,rkcil->okci/dot_general | solution.py:272
  237.7 16.4 %reduce-scatter.19.cloned.1.call-done = f32[160,640]{1,0:T(8,128)} async-done(((f32[640,640]{1,0:T(8,128)}), f32[160,640]{1,0:T(8,128)}) %reduce-scatter.19.cloned.1.call-update) | async-done | bytes 409616
  256.8 3.4 collective-permute-start.4
  262.3 6.1 copy.60
  276.9 9.8 %copy.64 = bf16[1,3200,1024]{2,1,0:T(8,128)(2,1)} copy(bf16[1,3200,1024]{1,2,0:T(8,128)(2,1)} %fusion.99) | data formatting | bytes 13107200 | tf_op jit(solution)/shard_map/concatenate | solution.py:149
  286.8 17.0 %fusion.64 = (f32[640]{0:T(1024)S(1)}, f32[1024]{0:T(1024)S(1)}, f32[1024]{0:T(1024)S(1)}, f32[640]{0:T(1024)S(1)}, f32[1,640,1024]{1,2,0:T(8,128)}) fusion(f32[1024]{0:T(1024)S(1)} %add_rsqrt_fusion.1, f32[1024]{0:T(1024)S(1)} %broadcast_multiply_fusion.5, f32[640]{0:T(1024)S(1)} %add.206, f32[1024,640]{1,0:T(8,128)S(1)} %copy-done.3, f32[640]{0:T(1024)S(1)} %mul.448, ...), kind=kOutput, calls=%fused_computation.120 | convolution fusion | flops 4248695808 | bytes 15921664 | tf_op jit(solution)/shard_map/kco,rkol->rcl/dot_general | solution.py:280
  307.9 19.5 %multiply_reduce_fusion = (f32[1280]{0:T(1024)S(1)}, f32[1024]{0:T(1024)S(1)}, f32[1024]{0:T(1024)S(1)}, f32[1280]{0:T(1024)S(1)}, f32[1,1280,1024]{1,2,0:T(8,128)}) fusion(f32[1,1280,1024]{1,2,0:T(8,128)} %copy.60, f32[1024]{0:T(1024)S(1)} %broadcast_multiply_fusion.8, f32[1024]{0:T(1024)S(1)} %add_rsqrt_fusion.2, f32[1280]{0:T(1024)S(1)} %mul.438, ...), kind=kOutput, calls=%fused_computation.23 | convolution fusion | flops 1785196032 | bytes 13471744 | tf_op jit(solution)/shard_map/dh,rhl->rdl/dot_general | solution.py:293
  327.9 15.8 %fusion.77 = f32[4,320,640]{2,1,0:T(8,128)S(1)} fusion(bf16[4,320,1024]{2,1,0:T(8,128)(2,1)S(1)} %copy-done.1, f32[4,320]{1,0:T(4,128)S(1)} %copy-done.21, f32[4,320]{1,0:T(4,128)S(1)} %copy-done.19, f32[1024]{0:T(1024)S(1)} %add_rsqrt_fusion.2, f32[1024]{0:T(1024)S(1)} %broadcast_multiply_fusion.8, bf16[1,640,1024]{1,2,0:T(8,128)(2,1)} %copy-done.7), kind=kOutput, calls=%fused_computation.154 | convolution fusion | flops 1769472000 | bytes 7227392 | tf_op jit(solution)/shard_map/rdl,rhl->dh/dot_general | solution.py:292
  345.8 4.8 reshape.1426
  350.6 29.3 %reduce-scatter.13.cloned.1.call-done = f32[80,25,128]{2,0,1:T(8,128)} async-done(((f32[320,25,128]{2,0,1:T(8,128)}), f32[80,25,128]{2,0,1:T(8,128)}) %reduce-scatter.13.cloned.1.call-update) | async-done | bytes 1024016 | tf_op jit(solution)/shard_map/reduce_scatter | solution.py:263
  385.2 6.9 %fusion.13 = bf16[1,1280,1024]{1,2,0:T(8,128)(2,1)} fusion(f32[1,1280,1024]{1,2,0:T(8,128)} %copy.60, bf16[640,1280]{1,0:T(8,128)(2,1)} %bitcast.279, f32[1280]{0:T(1024)S(1)} %add.221, bf16[1,640,1024]{1,2,0:T(8,128)(2,1)S(1)} %copy-done.6), kind=kOutput, calls=%fused_computation.17 | convolution fusion | flops 1681653760 | bytes 10818560 | tf_op jit(solution)/shard_map/hd,rhl->rdl/dot_general | solution.py:254
  392.2 4.6 copy.61
  396.8 4.6 all-to-all-start.1
  402.1 4.9 copy.68
  407.0 6.8 %add_convert_fusion = bf16[1,1280,1024]{1,2,0:T(8,128)(2,1)S(1)} fusion(f32[1,1280,1024]{1,2,0:T(8,128)} %copy.68, f32[1,1280,1024]{1,2,0:T(8,128)} %get-tuple-element.97, f32[1,1280,1024]{1,2,0:T(8,128)} %copy.60, f32[1024]{0:T(1024)S(1)} %broadcast_multiply_fusion.6, f32[1024]{0:T(1024)S(1)} %broadcast_multiply_fusion.7, f32[1280]{0:T(1024)S(1)} %mul.438, ...), kind=kLoop, calls=%fused_computation.38 | loop fusion | flops 11796480 | bytes 18371584 | tf_op jit(solution)/shard_map/convert_element_type | solution.py:297
  413.8 2.6 copy.69
  416.4 15.3 %all-to-all-done.1 = bf16[4,320,1024]{2,1,0:T(8,128)(2,1)} async-done(((bf16[4,320,1024]{2,1,0:T(8,128)(2,1)}), bf16[4,320,1024]{2,1,0:T(8,128)(2,1)}, u32[]{:S(2)}, u32[]{:S(2)}) %all-to-all-start.1) | async-done | bytes 2621472 | tf_op jit(solution)/shard_map/all_to_all | solution.py:170
  431.7 3.8 all-to-all-start.3
  435.5 29.9 %all-to-all-done.3 = bf16[4,320,1024]{2,1,0:T(8,128)(2,1)S(1)} async-done(((bf16[4,320,1024]{2,1,0:T(8,128)(2,1)}), bf16[4,320,1024]{2,1,0:T(8,128)(2,1)S(1)}, u32[]{:S(2)}, u32[]{:S(2)}) %all-to-all-start.3) | async-done | bytes 2621472 | tf_op jit(solution)/shard_map/all_to_all | solution.py:170
  467.2 32.4 %shard_map.255 = (f32[4,160,160]{2,1,0:T(8,128)}, f32[80,5,4,160]{3,2,1,0:T(4,128)}, f32[4,240,128]{2,1,0:T(8,128)}) custom-call(f32[4,160,160]{2,1,0:T(8,128)} %copy.83.refs_0_, f32[80,5,4,160]{3,2,1,0:T(4,128)} %reshape.1416.refs_1_, f32[4,240,128]{2,1,0:T(8,128)} %reduce-scatter.17.cloned.1.call-done.refs_2_), custom_call_target="tpu_custom_call" | custom-call | bytes 3850240 | tf_op jit(solution)/shard_map/pallas_call | solution.py:77
  506.4 9.5 %dynamic_update_slice.55 = f32[80,5,4,160]{3,2,1,0:T(4,128)} dynamic-update-slice(f32[80,5,4,160]{3,2,1,0:T(4,128)} %get-tuple-element.38, f32[80,5,1,160]{3,2,1,0:T(1,128)S(1)} %constant_dynamic-slice_fusion, s32[]{:T(128)} %constant.51.clone.1, s32[]{:T(128)} %constant.51.clone.1, s32[]{:T(128)S(6)} %select_n.71, s32[]{:T(128)} %constant.51.clone.1) | dynamic-update-slice | bytes 512004 | tf_op jit(solution)/shard_map/jit(dynamic_update_index_in_dim)/dynamic_update_slice | solution.py:93
  515.9 3.3 reduce_sum.238.refs_1_
  519.1 83.0 %shard_map.256 = (f32[4,160,160]{2,1,0:T(8,128)}, f32[4,80,5,160]{3,2,1,0:T(8,128)}, f32[4,240,128]{2,1,0:T(8,128)}) custom-call(f32[160,160]{1,0:T(8,128)} %reduce_sum.237.refs_0_, f32[80,5,160]{2,1,0:T(8,128)} %reduce_sum.238.refs_1_, f32[240,128]{1,0:T(8,128)} %reduce_sum.239.refs_2_), custom_call_target="tpu_custom_call" | custom-call | bytes 3850240 | tf_op jit(solution)/shard_map/pallas_call | solution.py:77
  605.5 8.0 %shard_map.257 = (f32[2,4,160,160]{3,2,1,0:T(8,128)}, f32[2,4,80,5,160]{4,3,2,1,0:T(8,128)}, f32[2,4,240,128]{3,2,1,0:T(8,128)}) custom-call(f32[4,160,160]{2,1,0:T(8,128)} %bitcast_dynamic-update-slice_fusion.7.refs_0_, f32[4,80,5,160]{3,2,1,0:T(8,128)} %bitcast_dynamic-update-slice_fusion.2.refs_1_, f32[4,240,128]{2,1,0:T(8,128)} %bitcast_dynamic-update-slice_fusion.8.refs_2_), custom_call_target="tpu_custom_call" | custom-call | bytes 7700480 | tf_op jit(solution)/shard_map/pallas_call | solution.py:77
  622.8 3.4 bitcast_dynamic-update-slice_fusion
  626.3 5.1 copy.74
  631.4 3.1 copy.75
  634.5 2.8 reshape.1428
  637.3 3.5 copy.110
  (164 shorter events, 72.7 us)
Async XLA Ops:
  7.2 51.6 %copy-start.12 = (bf16[5,160,640]{2,1,0:T(8,128)(2,1)S(1)}, bf16[5,160,640]{2,1,0:T(8,128)(2,1)}, u32[]{:S(2)}) copy-start(bf16[5,160,640]{2,1,0:T(8,128)(2,1)} %param.23) | copy-start | bytes 3072004
  7.2 50.7 %copy-start.13 = (bf16[320,640]{1,0:T(8,128)(2,1)S(1)}, bf16[320,640]{1,0:T(8,128)(2,1)}, u32[]{:S(2)}) copy-start(bf16[320,640]{1,0:T(8,128)(2,1)} %param.19) | copy-start | bytes 1228804
  7.2 95.2 %all-gather.4.cloned.1.call-start = ((), (), s32[]{:S(2)}) async-start(), calls=%async_computation.10 | async-start | bytes 2457600 | tf_op jit(solution)/shard_map/all_gather | solution.py:227
  58.7 99.0 %all-gather.6.cloned.1.call-start = ((), (), s32[]{:S(2)}) async-start(), calls=%async_computation.11 | async-start | bytes 6144000 | tf_op jit(solution)/shard_map/all_gather | solution.py:228
  59.6 9.0 %copy-start.14 = (bf16[160,1280]{1,0:T(8,128)(2,1)S(1)}, bf16[160,1280]{1,0:T(8,128)(2,1)}, u32[]{:S(2)}) copy-start(bf16[160,1280]{1,0:T(8,128)(2,1)} %param.27) | copy-start | bytes 1228804
  59.6 9.8 %copy-start.15 = (f32[1920]{0:T(1024)S(1)}, f32[1920]{0:T(1024)}, u32[]{:S(2)}) copy-start(f32[1920]{0:T(1024)} %concatenate.43.refs_0_) | copy-start | bytes 23044
  59.7 9.8 %copy-start.16 = (f32[4,1920]{1,0:T(4,128)S(1)}, f32[4,1920]{1,0:T(4,128)}, u32[]{:S(2)}) copy-start(f32[4,1920]{1,0:T(4,128)} %get-tuple-element.30) | copy-start | bytes 92164
  59.7 33.8 %all-to-all-start = ((bf16[4,320,1024]{2,1,0:T(8,128)(2,1)}), bf16[4,320,1024]{2,1,0:T(8,128)(2,1)S(1)}, u32[]{:S(2)}, u32[]{:S(2)}) async-start(bf16[4,320,1024]{2,1,0:T(8,128)(2,1)} %param.15), calls=%async_computation | async-start | bytes 5242880 | tf_op jit(solution)/shard_map/all_to_all | solution.py:157
  63.5 106.7 %all-gather.8.cloned.1.call-start = ((), (), s32[]{:S(2)}) async-start(), calls=%async_computation.12 | async-start | bytes 2457600 | tf_op jit(solution)/shard_map/all_gather | solution.py:229
  64.3 76.3 %collective-permute-start = (s32[1,64]{1,0:T(1,128)S(1)}, s32[1,64]{1,0:T(1,128)S(1)}, u32[]{:S(2)}, u32[]{:S(2)}) collective-permute-start(s32[1,64]{1,0:T(1,128)S(1)} %get-tuple-element.89), channel_id=1, source_target_pairs={{0,4},{1,5},{2,6},{3,7},{8,12},{9,13},{10,14},{11,15},{16,20},{17,... | collective-permute-start | bytes 776 | tf_op jit(solution)/shard_map/ppermute | solution.py:136
  65.6 75.0 %collective-permute-start.2 = (s32[1,64]{1,0:T(1,128)S(1)}, s32[1,64]{1,0:T(1,128)S(1)}, u32[]{:S(2)}, u32[]{:S(2)}) collective-permute-start(s32[1,64]{1,0:T(1,128)S(1)} %get-tuple-element.90), channel_id=1, source_target_pairs={{4,0},{5,1},{6,2},{7,3},{12,8},{13,9},{14,10},{15,11},{20,16},{21,... | collective-permute-start | bytes 776 | tf_op jit(solution)/shard_map/ppermute | solution.py:137
  70.8 22.7 %copy-start.18 = (f32[4,320]{1,0:T(4,128)}, f32[4,320]{1,0:T(4,128)S(1)}, u32[]{:S(2)}) copy-start(f32[4,320]{1,0:T(4,128)S(1)} %get-tuple-element.77) | copy-start | bytes 15364
  70.8 22.7 %copy-start.20 = (f32[4,320]{1,0:T(4,128)}, f32[4,320]{1,0:T(4,128)S(1)}, u32[]{:S(2)}) copy-start(f32[4,320]{1,0:T(4,128)S(1)} %get-tuple-element.79) | copy-start | bytes 15364
  93.5 5.9 copy-start
  93.5 76.7 %all-to-all-start.2 = ((bf16[4,320,1024]{2,1,0:T(8,128)(2,1)}), bf16[4,320,1024]{2,1,0:T(8,128)(2,1)}, u32[]{:S(2)}, u32[]{:S(2)}) async-start(bf16[4,320,1024]{2,1,0:T(8,128)(2,1)} %param.29), calls=%async_computation.2 | async-start | bytes 5242880 | tf_op jit(solution)/shard_map/all_to_all | solution.py:157
  98.2 113.2 %reduce-scatter.9.cloned.1.call-start = ((), (), s32[]{:S(2)}) async-start(), calls=%async_computation.13 | async-start | bytes 4915200 | tf_op jit(solution)/shard_map/reduce_scatter | solution.py:262
  131.4 15.5 %copy-start.2 = (f32[1024,640]{1,0:T(8,128)}, f32[1024,640]{1,0:T(8,128)S(1)}, u32[]{:S(2)}) copy-start(f32[1024,640]{1,0:T(8,128)S(1)} %get-tuple-element.92) | copy-start | bytes 7864324
  139.3 4.7 collective-permute-start.1
  140.7 14.1 %collective-permute-start.3 = (bf16[1,640,64]{1,2,0:T(8,128)(2,1)S(1)}, bf16[1,640,64]{1,2,0:T(8,128)(2,1)S(1)}, u32[]{:S(2)}, u32[]{:S(2)}) collective-permute-start(bf16[1,640,64]{1,2,0:T(8,128)(2,1)S(1)} %get-tuple-element.69), channel_id=1, source_target_pairs={{4,0},{5,1},{6,2},{7,3},{12,8},{13,9},{14,10},{15,11},{20,16},{21,... | collective-permute-start | bytes 245768 | tf_op jit(solution)/shard_map/ppermute | solution.py:137
  160.4 9.2 %copy-start.8 = (bf16[5,4,160,640]{3,2,1,0:T(8,128)(2,1)}, bf16[5,4,160,640]{3,2,1,0:T(8,128)(2,1)S(1)}, u32[]{:S(2)}) copy-start(bf16[5,4,160,640]{3,2,1,0:T(8,128)(2,1)S(1)} %copy.59) | copy-start | bytes 12288004
  169.6 12.5 %copy-start.4 = (f32[1024,640]{1,0:T(8,128)}, f32[1024,640]{1,0:T(8,128)S(1)}, u32[]{:S(2)}) copy-start(f32[1024,640]{1,0:T(8,128)S(1)} %get-tuple-element.94) | copy-start | bytes 7864324
  191.0 7.3 %copy-start.5 = (bf16[1,640,1024]{1,2,0:T(8,128)(2,1)}, bf16[1,640,1024]{1,2,0:T(8,128)(2,1)S(1)}, u32[]{:S(2)}) copy-start(bf16[1,640,1024]{1,2,0:T(8,128)(2,1)S(1)} %get-tuple-element.66) | copy-start | bytes 3932164
  198.3 55.7 %reduce-scatter.19.cloned.1.call-start = ((), (), s32[]{:S(2)}) async-start(), calls=%async_computation.18 | async-start | bytes 2048000
  219.0 85.0 %reduce-scatter.11.cloned.1.call-start = ((), (), s32[]{:S(2)}) async-start(), calls=%async_computation.14 | async-start | bytes 12288000 | tf_op jit(solution)/shard_map/reduce_scatter | solution.py:262
  256.7 123.3 %reduce-scatter.13.cloned.1.call-start = ((), (), s32[]{:S(2)}) async-start(), calls=%async_computation.15 | async-start | bytes 5120000 | tf_op jit(solution)/shard_map/reduce_scatter | solution.py:263
  256.8 13.2 %collective-permute-start.4 = (bf16[1,640,64]{1,2,0:T(8,128)(2,1)S(1)}, bf16[1,640,64]{1,2,0:T(8,128)(2,1)S(1)}, u32[]{:S(2)}, u32[]{:S(2)}) collective-permute-start(bf16[1,640,64]{1,2,0:T(8,128)(2,1)S(1)} %get-tuple-element.68), channel_id=1, source_target_pairs={{4,0},{5,1},{6,2},{7,3},{12,8},{13,9},{14,10},{15,11},{20,16},{21,... | collective-permute-start | bytes 245768 | tf_op jit(solution)/shard_map/ppermute | solution.py:137
  268.6 5.4 collective-permute-start.5
  276.9 9.8 %copy-start.3 = (f32[1024,640]{1,0:T(8,128)S(1)}, f32[1024,640]{1,0:T(8,128)}, u32[]{:S(2)}) copy-start(f32[1024,640]{1,0:T(8,128)} %copy-done.2) | copy-start | bytes 7864324
  304.0 97.4 %reduce-scatter.15.cloned.1.call-start = ((), (), s32[]{:S(2)}) async-start(), calls=%async_computation.16 | async-start | bytes 5898240 | tf_op jit(solution)/shard_map/reduce_scatter | solution.py:262
  306.5 1.1 copy-start.7
  307.9 20.0 %copy-start.1 = (bf16[4,320,1024]{2,1,0:T(8,128)(2,1)S(1)}, bf16[4,320,1024]{2,1,0:T(8,128)(2,1)}, u32[]{:S(2)}) copy-start(bf16[4,320,1024]{2,1,0:T(8,128)(2,1)} %copy-done) | copy-start | bytes 7864324
  307.9 20.0 %copy-start.19 = (f32[4,320]{1,0:T(4,128)S(1)}, f32[4,320]{1,0:T(4,128)}, u32[]{:S(2)}) copy-start(f32[4,320]{1,0:T(4,128)} %copy-done.18) | copy-start | bytes 15364
  307.9 20.0 %copy-start.21 = (f32[4,320]{1,0:T(4,128)S(1)}, f32[4,320]{1,0:T(4,128)}, u32[]{:S(2)}) copy-start(f32[4,320]{1,0:T(4,128)} %copy-done.20) | copy-start | bytes 15364
  383.9 0.7 copy-start.17
  383.9 1.3 copy-start.6
  396.8 34.9 %all-to-all-start.1 = ((bf16[4,320,1024]{2,1,0:T(8,128)(2,1)}), bf16[4,320,1024]{2,1,0:T(8,128)(2,1)}, u32[]{:S(2)}, u32[]{:S(2)}) async-start(bf16[4,320,1024]{2,1,0:T(8,128)(2,1)} %bitcast.18), calls=%async_computation.1 | async-start | bytes 5242880 | tf_op jit(solution)/shard_map/all_to_all | solution.py:170
  401.4 65.9 %reduce-scatter.17.cloned.1.call-start = ((), (), s32[]{:S(2)}) async-start(), calls=%async_computation.17 | async-start | bytes 2457600 | tf_op jit(solution)/shard_map/reduce_scatter | solution.py:263
  431.7 33.7 %all-to-all-start.3 = ((bf16[4,320,1024]{2,1,0:T(8,128)(2,1)}), bf16[4,320,1024]{2,1,0:T(8,128)(2,1)S(1)}, u32[]{:S(2)}, u32[]{:S(2)}) async-start(bf16[4,320,1024]{2,1,0:T(8,128)(2,1)} %bitcast.264), calls=%async_computation.4 | async-start | bytes 5242880 | tf_op jit(solution)/shard_map/all_to_all | solution.py:170
  504.5 98.3 %copy-start.11 = (f32[240,128]{1,0:T(8,128)S(1)}, f32[240,128]{1,0:T(8,128)}, u32[]{:S(2)}) copy-start(f32[240,128]{1,0:T(8,128)} %reduce_sum.239.refs_2_) | copy-start | bytes 368644
  506.4 95.8 %copy-start.10 = (f32[160,160]{1,0:T(8,128)S(1)}, f32[160,160]{1,0:T(8,128)}, u32[]{:S(2)}) copy-start(f32[160,160]{1,0:T(8,128)} %reduce_sum.237.refs_0_) | copy-start | bytes 307204
  613.5 8.4 %copy-start.9 = (f32[4,160,160]{2,1,0:T(8,128)S(1)}, f32[4,160,160]{2,1,0:T(8,128)}, u32[]{:S(2)}) copy-start(f32[4,160,160]{2,1,0:T(8,128)} %bitcast_dynamic-update-slice_fusion.7.refs_0_) | copy-start | bytes 1228804
Sparse Core Ops, SparseCore 0:
  58.8 11.5 all-gather.3
  71.9 14.6 all-gather.5
  88.2 11.0 all-gather.7
  198.4 12.8 reduce-scatter.8
  219.1 34.8 reduce-scatter.18
  256.8 18.3 reduce-scatter.10
  304.1 75.7 reduce-scatter.12
  384.1 13.0 reduce-scatter.14
  404.6 41.1 reduce-scatter.16

commit v5 on v2

--- a/solution.py
+++ b/solution.py
@@ -321,8 +321,8 @@
     parts = [part_outer, part_conv, part_inner]
     parts = exchange(parts, ("ch",), 1, axes=(0, 2, 0))
     parts = [jnp.sum(p, axis=a) for p, a in zip(parts, (0, 2, 0))]
-    parts = exchange(parts, ("batch",), 2, gather=True)
-    parts = [p.reshape((seqs * batches,) + p.shape[2:]) for p in exchange(parts, ("seq",), 3, gather=True)]
+    parts = [lax.all_gather(p, "batch", axis=0) for p in parts]
+    parts = [lax.all_gather(p, "seq", axis=0, tiled=True).reshape((seqs * batches,) + p.shape[1:]) for p in parts]
     red_w_outer = parts[0].reshape(hloc, dim)
     red_w_conv = parts[1].reshape(hid, KERNEL_TAPS, hloc).transpose(1, 2, 0)
     red_inner = parts[2].reshape(dloc + vec_rows, hid)

time: 624 us -> 617 us (0.989)
  the two profiles are of different devices: /device:TPU:9 before, /device:TPU:0 now
where the time goes in v5:
time: 617 us; the launch traced here: 605 us
  matrix products  118 us (19%)
  waiting for transfers between devices  111 us (18%)
  local copies, waits for them, and re-layouts  105 us (17%)
  Pallas kernels  101 us (16%)
  blocking collectives  81.5 us (13%)
  other arithmetic  47.3 us (8%)
  starting transfers between devices  26.5 us (4%)
  between operations  15 us (2%)
    pallas_call x2, Pallas kernels, exchange(): pl.pallas_call(functools.partial(_exchange_kernel, sizes, group, gather,...  101 us
    all_gather x3, blocking collectives, local(): parts = [lax.all_gather(p, 'batch', axis=0) for p in parts]  76.4 us
    reduce_scatter x3, waiting for transfers between devices, reduce_seq_batch(): return lax.psum_scatter(g, 'batch', scatter_dimension=split_dim, tiled=True)  43.8 us
    all_to_all x2, waiting for transfers between devices, to_positions(): x = lax.all_to_all(x, 'ch', 0, 0, tiled=True)  23.3 us
    dot_general x1, matrix products, local(): jnp.einsum('dh,rhl->rdl', w_in, grad_inner, preferred_element_type=jnp.fl...  20 us
    all_to_all x2, waiting for transfers between devices, to_channels(): x = lax.all_to_all(x, 'ch', 0, 0, tiled=True)  17.3 us
    dot_general x1, matrix products, local(): jnp.einsum('dh,rdl->rhl', w_in, hidden0, preferred_element_type=jnp.float32)  16.8 us
    dot_general x1, matrix products, local(): jnp.einsum('rdl,rhl->dh', hidden0, grad_inner, preferred_element_type=jnp...  15.5 us
  transfers between devices with their start and end apart: 20, of which 7 were waited for; matrix products, arithmetic and copies ran while one was open for 37% of the time, Pallas kernels for 9%

profile of v5, /device:TPU:0, one launch (start us, length us, event | category | flops | bytes accessed | tf_op | source)
XLA Modules:
  0.0 605.3 jit_solution(4629394410128526255)
XLA Ops:
  13.9 45.3 %shard_map.254 = (f32[4,1920]{1,0:T(4,128)}, bf16[4,160,640]{2,1,0:T(8,128)(2,1)}, bf16[4,5,80,640]{3,2,1,0:T(8,128)(2,1)}, bf16[4,80,1280]{2,1,0:T(8,128)(2,1)}) custom-call(f32[1920]{0:T(1024)} %concatenate.43.refs_0_, bf16[160,640]{1,0:T(8,128)(2,1)} %constant_dynamic-slice_fusion.3.refs_1_, bf16[5,80,640]{2,1,0:T(8,128)(2,1)} %constant_dynamic-slice_fusion.2.refs_2_, ...), custom_call_target="tpu_custom_call" | custom-call | bytes 7434240 | tf_op jit(solution)/shard_map/pallas_call | solution.py:77
  59.9 3.7 all-to-all-start
  71.1 23.3 %all-to-all-done = bf16[4,320,1024]{2,1,0:T(8,128)(2,1)S(1)} async-done(((bf16[4,320,1024]{2,1,0:T(8,128)(2,1)}), bf16[4,320,1024]{2,1,0:T(8,128)(2,1)S(1)}, u32[]{:S(2)}, u32[]{:S(2)}) %all-to-all-start) | async-done | bytes 2621472 | tf_op jit(solution)/shard_map/all_to_all | solution.py:157
  94.4 4.6 all-to-all-start.2
  100.3 2.9 convert_element_type.149
  103.2 16.8 %fusion.83 = (f32[1024]{0:T(1024)S(1)}, f32[1024,640]{1,0:T(8,128)S(1)}) fusion(f32[640]{0:T(1024)S(1)} %add.192, bf16[1280,640]{1,0:T(8,128)(2,1)} %bitcast.273, f32[1280]{0:T(1024)S(1)} %add.189, f32[1280]{0:T(1024)S(1)} %mul.438, f32[1024]{0:T(1024)S(1)} %add_rsqrt_fusion.2, f32[1,1280,1,1,1,1,1024]{6,1,5,4,3,2,0:T(8,128)} %bitcast.259, ...), kind=kOutput, calls=%fused_computation.159 | convolution fusion | flops 1769470976 | bytes 9527808 | tf_op jit(solution)/shard_map/dh,rdl->rhl/dot_general | solution.py:245
  120.6 7.3 %multiply_convert_fusion.1 = bf16[1,640,1024]{1,2,0:T(8,128)(2,1)S(1)} fusion(f32[640]{0:T(1024)S(1)} %add.196, f32[640]{0:T(1024)S(1)} %mul.448, f32[1024]{0:T(1024)S(1)} %add_rsqrt_fusion.1, f32[1024]{0:T(1024)S(1)} %broadcast_multiply_fusion.5, f32[640]{0:T(1024)S(1)} %add.192, f32[1024,640]{1,0:T(8,128)S(1)} %get-tuple-element.79), kind=kLoop, calls=%fused_computation.141 | loop fusion | flops 45875200 | bytes 3948032 | tf_op jit(solution)/shard_map/convert_element_type | solution.py:247
  133.7 8.0 %constant_dynamic-update-slice_fusion = bf16[1,3200,1024]{1,2,0:T(8,128)(2,1)} fusion(bf16[1,3200,1024]{1,2,0:T(8,128)(2,1)} %fusion.110, f32[640]{0:T(1024)S(1)} %add.196, f32[640]{0:T(1024)S(1)} %mul.448, f32[1024]{0:T(1024)S(1)} %add_rsqrt_fusion.1, f32[1024]{0:T(1024)S(1)} %broadcast_multiply_fusion.5, f32[640]{0:T(1024)S(1)} %add.192, ...), kind=kLoop, calls=%fused_computation.210 | loop fusion | flops 45875200 | bytes 3948032
  144.6 2.6 copy.65
  147.3 9.6 %fusion.85 = (f32[1024]{0:T(1024)S(1)}, f32[1024,640]{1,0:T(8,128)S(1)}) fusion(f32[640]{0:T(1024)S(1)} %add.199, bf16[3200,640]{1,0:T(8,128)(2,1)S(1)} %bitcast.261, bf16[1,3200,1024]{1,2,0:T(8,128)(2,1)} %fusion.108), kind=kOutput, calls=%fused_computation.161 | convolution fusion | flops 4195613696 | bytes 13277696 | tf_op jit(solution)/shard_map/co,rcl->rol/dot_general | solution.py:251
  157.4 11.8 %fusion.177 = f32[640,1280]{1,0:T(8,128)} fusion(bf16[1280,1024]{1,0:T(8,128)(2,1)} %bitcast.20, f32[640]{0:T(1024)S(1)} %add.203, f32[640]{0:T(1024)S(1)} %mul.458, f32[1024]{0:T(1024)S(1)} %add_rsqrt_fusion, f32[1024]{0:T(1024)S(1)} %broadcast_multiply_fusion.4, f32[640]{0:T(1024)S(1)} %add.199, f32[1024,640]{1,0:T(8,128)S(1)} %get-tuple-element.81), kind=kOutput, calls=%fused_computation.301 | convolution fusion | flops 1723596800 | bytes 8535552 | tf_op jit(solution)/shard_map/rhl,rdl->hd/dot_general | solution.py:258
  169.2 4.5 reshape.1419
  175.5 9.7 %copy.74 = bf16[1,3200,1024]{2,1,0:T(8,128)(2,1)} copy(bf16[1,3200,1024]{1,2,0:T(8,128)(2,1)} %fusion.108) | data formatting | bytes 13107200 | tf_op jit(solution)/shard_map/concatenate | solution.py:149
  187.4 12.5 %all-gather.12.cloned.1.call-done = bf16[4,160,1280]{2,1,0:T(8,128)(2,1)} async-done(((bf16[4,80,1280]{2,1,0:T(8,128)(2,1)}), bf16[4,160,1280]{2,1,0:T(8,128)(2,1)}) %all-gather.12.cloned.1.call-update) | async-done | bytes 1638416 | tf_op jit(solution)/shard_map/all_gather | solution.py:229
  199.9 11.7 %fusion.60 = (f32[640]{0:T(1024)S(1)}, f32[1024]{0:T(1024)S(1)}, f32[1024]{0:T(1024)S(1)}, f32[640]{0:T(1024)S(1)}, f32[1,640,1024]{1,2,0:T(8,128)S(1)}) fusion(f32[1024]{0:T(1024)S(1)} %add_rsqrt_fusion, f32[1024]{0:T(1024)S(1)} %broadcast_multiply_fusion.4, f32[640]{0:T(1024)S(1)} %add.199, f32[1024,640]{1,0:T(8,128)S(1)} %get-tuple-element.81, ...), kind=kOutput, calls=%fused_computation.110 | convolution fusion | flops 1732113152 | bytes 9531904 | tf_op jit(solution)/shard_map/hd,rdl->rhl/dot_general | solution.py:266
  211.7 2.6 convert_reduce_fusion.1
  215.3 7.1 %fusion.112 = f32[640,25,128]{2,0,1:T(8,128)} fusion(bf16[25,128,1024]{2,1,0:T(8,128)(2,1)S(1)} %bitcast.265, bf16[1,640,1024]{1,2,0:T(8,128)(2,1)S(1)} %get-tuple-element.53), kind=kOutput, calls=%fused_computation.200 | convolution fusion | flops 4194304000 | bytes 16056320 | tf_op jit(solution)/shard_map/rol,rkcil->okci/dot_general | solution.py:272
  222.4 17.3 %reduce-scatter.9.cloned.1.call-done.refs_0_ = f32[4,200,128]{2,1,0:T(8,128)} async-done(((f32[4,800,128]{2,1,0:T(8,128)}), f32[4,200,128]{2,1,0:T(8,128)}) %reduce-scatter.9.cloned.1.call-update) | async-done | bytes 409616 | tf_op jit(solution)/shard_map/reduce_scatter | solution.py:263
  243.3 6.4 %copy.66 = f32[1,1280,1024]{1,2,0:T(8,128)} copy(f32[1,1280,1024]{2,1,0:T(8,128)} %bitcast.260) | data formatting | bytes 10485760 | tf_op jit(solution)/shard_map/convert_element_type | solution.py:242
  249.6 8.3 %copy.71 = bf16[5,640,640]{2,1,0:T(8,128)(2,1)} copy(bf16[5,640,640]{1,2,0:T(8,128)(2,1)} %bitcast.262) | data formatting | bytes 8192000 | tf_op jit(solution)/shard_map/transpose | solution.py:280
  258.2 2.7 collective-permute-start.5
  264.6 13.6 %fusion.66 = (f32[640]{0:T(1024)S(1)}, f32[1024]{0:T(1024)S(1)}, f32[1024]{0:T(1024)S(1)}, f32[640]{0:T(1024)S(1)}, f32[1,640,1024]{1,2,0:T(8,128)}) fusion(f32[1024]{0:T(1024)S(1)} %add_rsqrt_fusion.1, f32[1024]{0:T(1024)S(1)} %broadcast_multiply_fusion.5, f32[640]{0:T(1024)S(1)} %add.192, f32[1024,640]{1,0:T(8,128)S(1)} %copy-done.3, f32[640]{0:T(1024)S(1)} %mul.448, ...), kind=kOutput, calls=%fused_computation.121 | convolution fusion | flops 4248695808 | bytes 15921664 | tf_op jit(solution)/shard_map/oc,rol->rcl/dot_general | solution.py:281
  279.9 2.4 fusion.65
  283.7 20.0 %multiply_reduce_fusion = (f32[1280]{0:T(1024)S(1)}, f32[1024]{0:T(1024)S(1)}, f32[1024]{0:T(1024)S(1)}, f32[1280]{0:T(1024)S(1)}, f32[1,1280,1024]{1,2,0:T(8,128)}) fusion(f32[1,1280,1024]{1,2,0:T(8,128)} %copy.66, f32[1024]{0:T(1024)S(1)} %broadcast_multiply_fusion.8, f32[1024]{0:T(1024)S(1)} %add_rsqrt_fusion.2, f32[1280]{0:T(1024)S(1)} %mul.438, ...), kind=kOutput, calls=%fused_computation.25 | convolution fusion | flops 1785196032 | bytes 13471744 | tf_op jit(solution)/shard_map/dh,rhl->rdl/dot_general | solution.py:289
  304.2 15.5 %fusion.79 = f32[4,320,640]{2,1,0:T(8,128)S(1)} fusion(bf16[4,320,1024]{2,1,0:T(8,128)(2,1)S(1)} %copy-done.1, f32[4,320]{1,0:T(4,128)S(1)} %copy-done.23, f32[4,320]{1,0:T(4,128)S(1)} %copy-done.21, f32[1024]{0:T(1024)S(1)} %add_rsqrt_fusion.2, f32[1024]{0:T(1024)S(1)} %broadcast_multiply_fusion.8, bf16[1,640,1024]{1,2,0:T(8,128)(2,1)} %copy-done.11), kind=kOutput, calls=%fused_computation.155 | convolution fusion | flops 1769472000 | bytes 7227392 | tf_op jit(solution)/shard_map/rdl,rhl->dh/dot_general | solution.py:288
  322.0 4.7 reshape.1432
  326.7 26.6 %reduce-scatter.13.cloned.1.call-done = f32[80,25,128]{2,0,1:T(8,128)} async-done(((f32[320,25,128]{2,0,1:T(8,128)}), f32[80,25,128]{2,0,1:T(8,128)}) %reduce-scatter.13.cloned.1.call-update) | async-done | bytes 1024016 | tf_op jit(solution)/shard_map/reduce_scatter | solution.py:263
  354.8 2.4 reshape.1422.refs_1_
  357.9 11.7 %reduce-scatter.15.cloned.1.call-done = f32[4,960,128]{2,1,0:T(8,128)} async-done(((f32[4,1920,128]{2,1,0:T(8,128)}), f32[4,960,128]{2,1,0:T(8,128)}) %reduce-scatter.15.cloned.1.call-update) | async-done | bytes 1966096 | tf_op jit(solution)/shard_map/reduce_scatter | solution.py:262
  369.7 11.7 %fusion.15 = bf16[1,1280,1024]{1,2,0:T(8,128)(2,1)} fusion(f32[1,1280,1024]{1,2,0:T(8,128)} %copy.66, bf16[640,1280]{1,0:T(8,128)(2,1)} %bitcast.276, f32[1280]{0:T(1024)S(1)} %add.207, f32[640]{0:T(1024)S(1)} %add.203, f32[640]{0:T(1024)S(1)} %mul.458, f32[1024]{0:T(1024)S(1)} %add_rsqrt_fusion, f32[1024]{0:T(1024)S(1)} %broadcast_multiply_fusion.4, ...), kind=kOutput, calls=%fused_computation.19 | convolution fusion | flops 1727528960 | bytes 12145152 | tf_op jit(solution)/shard_map/hd,rhl->rdl/dot_general | solution.py:254
  381.4 4.4 copy.67
  385.8 4.6 all-to-all-start.1
  390.3 4.9 copy.72
  395.3 6.5 %add_convert_fusion = bf16[1,1280,1024]{1,2,0:T(8,128)(2,1)S(1)} fusion(f32[1,1280,1024]{1,2,0:T(8,128)} %copy.72, f32[1,1280,1024]{1,2,0:T(8,128)} %get-tuple-element.84, f32[1,1280,1024]{1,2,0:T(8,128)} %copy.66, f32[1024]{0:T(1024)S(1)} %broadcast_multiply_fusion.6, f32[1024]{0:T(1024)S(1)} %broadcast_multiply_fusion.7, f32[1280]{0:T(1024)S(1)} %mul.438, ...), kind=kLoop, calls=%fused_computation.40 | loop fusion | flops 11796480 | bytes 18371584 | tf_op jit(solution)/shard_map/convert_element_type | solution.py:293
  401.8 2.6 copy.73
  404.4 17.3 %all-to-all-done.1 = bf16[4,320,1024]{2,1,0:T(8,128)(2,1)} async-done(((bf16[4,320,1024]{2,1,0:T(8,128)(2,1)}), bf16[4,320,1024]{2,1,0:T(8,128)(2,1)}, u32[]{:S(2)}, u32[]{:S(2)}) %all-to-all-start.1) | async-done | bytes 2621472 | tf_op jit(solution)/shard_map/all_to_all | solution.py:170
  421.7 3.7 all-to-all-start.3
  427.2 56.1 %shard_map.255 = (f32[4,200,128]{2,1,0:T(8,128)}, f32[80,5,4,160]{3,2,1,0:T(4,128)}, f32[4,240,128]{2,1,0:T(8,128)}) custom-call(f32[4,200,128]{2,1,0:T(8,128)} %reduce-scatter.9.cloned.1.call-done.refs_0_, f32[80,5,4,160]{3,2,1,0:T(4,128)} %reshape.1422.refs_1_, f32[4,240,128]{2,1,0:T(8,128)} %reduce-scatter.17.cloned.1.call-done.refs_2_), custom_call_target="tpu_custom_call" | custom-call | bytes 3850240 | tf_op jit(solution)/shard_map/pallas_call | solution.py:77
  483.3 9.5 %dynamic_update_slice.33 = f32[80,5,4,160]{3,2,1,0:T(4,128)} dynamic-update-slice(f32[80,5,4,160]{3,2,1,0:T(4,128)} %get-tuple-element.32, f32[80,5,1,160]{3,2,1,0:T(1,128)S(1)} %constant_dynamic-slice_fusion, s32[]{:T(128)} %constant.45.clone.1, s32[]{:T(128)} %constant.45.clone.1, s32[]{:T(128)S(6)} %select_n.57, s32[]{:T(128)} %constant.45.clone.1) | dynamic-update-slice | bytes 512004 | tf_op jit(solution)/shard_map/jit(dynamic_update_index_in_dim)/dynamic_update_slice | solution.py:93
  492.8 2.4 reduce_sum.238
  495.3 46.0 %all-gather.1 = f32[320,5,160]{2,1,0:T(8,128)S(1)} all-gather(f32[80,5,160]{2,1,0:T(8,128)S(1)} %reduce_sum.238), channel_id=3, replica_groups=mesh['batch'=4,'seq'=2,'ch'=4] {'batch'}, dimensions={0}, use_global_device_ids=true | all-gather | bytes 1280000 | tf_op jit(solution)/shard_map/all_gather | solution.py:324
  544.1 15.1 %all-gather = f32[960,128]{1,0:T(8,128)S(1)} all-gather(f32[240,128]{1,0:T(8,128)S(1)} %reduce_sum.237), channel_id=2, replica_groups=mesh['batch'=4,'seq'=2,'ch'=4] {'batch'}, dimensions={0}, use_global_device_ids=true | all-gather | bytes 614400 | tf_op jit(solution)/shard_map/all_gather | solution.py:324
  559.3 2.8 all_gather.41
  562.0 2.3 reshape.1433
  567.4 15.2 %all-gather.2 = f32[800,128]{1,0:T(8,128)S(1)} all-gather(f32[200,128]{1,0:T(8,128)S(1)} %reduce_sum.239), channel_id=4, replica_groups=mesh['batch'=4,'seq'=2,'ch'=4] {'batch'}, dimensions={0}, use_global_device_ids=true | all-gather | bytes 512000 | tf_op jit(solution)/shard_map/all_gather | solution.py:324
  582.6 2.4 all_gather.47
  587.4 3.8 copy.79
  593.1 3.6 copy.105
  (166 shorter events, 60.0 us)
Async XLA Ops:
  7.2 52.0 %copy-start.14 = (bf16[320,640]{1,0:T(8,128)(2,1)S(1)}, bf16[320,640]{1,0:T(8,128)(2,1)}, u32[]{:S(2)}) copy-start(bf16[320,640]{1,0:T(8,128)(2,1)} %param.19) | copy-start | bytes 1228804
  7.2 96.0 %all-gather.8.cloned.1.call-start = ((), (), s32[]{:S(2)}) async-start(), calls=%async_computation.10 | async-start | bytes 2457600 | tf_op jit(solution)/shard_map/all_gather | solution.py:227
  59.9 34.5 %all-to-all-start = ((bf16[4,320,1024]{2,1,0:T(8,128)(2,1)}), bf16[4,320,1024]{2,1,0:T(8,128)(2,1)S(1)}, u32[]{:S(2)}, u32[]{:S(2)}) async-start(bf16[4,320,1024]{2,1,0:T(8,128)(2,1)} %param.15), calls=%async_computation | async-start | bytes 5242880 | tf_op jit(solution)/shard_map/all_to_all | solution.py:157
  63.6 6.0 copy-start.17
  63.6 6.0 copy-start.18
  63.6 81.0 %all-gather.10.cloned.1.call-start = ((), (), s32[]{:S(2)}) async-start(), calls=%async_computation.11 | async-start | bytes 6144000 | tf_op jit(solution)/shard_map/all_gather | solution.py:228
  64.5 64.8 %collective-permute-start = (s32[1,64]{1,0:T(1,128)S(1)}, s32[1,64]{1,0:T(1,128)S(1)}, u32[]{:S(2)}, u32[]{:S(2)}) collective-permute-start(s32[1,64]{1,0:T(1,128)S(1)} %get-tuple-element.76), channel_id=1, source_target_pairs={{0,4},{1,5},{2,6},{3,7},{8,12},{9,13},{10,14},{11,15},{16,20},{17,... | collective-permute-start | bytes 776 | tf_op jit(solution)/shard_map/ppermute | solution.py:136
  66.3 63.0 %collective-permute-start.2 = (s32[1,64]{1,0:T(1,128)S(1)}, s32[1,64]{1,0:T(1,128)S(1)}, u32[]{:S(2)}, u32[]{:S(2)}) collective-permute-start(s32[1,64]{1,0:T(1,128)S(1)} %get-tuple-element.77), channel_id=1, source_target_pairs={{4,0},{5,1},{6,2},{7,3},{12,8},{13,9},{14,10},{15,11},{20,16},{21,... | collective-permute-start | bytes 776 | tf_op jit(solution)/shard_map/ppermute | solution.py:137
  71.0 23.5 %copy-start.20 = (f32[4,320]{1,0:T(4,128)}, f32[4,320]{1,0:T(4,128)S(1)}, u32[]{:S(2)}) copy-start(f32[4,320]{1,0:T(4,128)S(1)} %get-tuple-element.64) | copy-start | bytes 15364
  71.0 23.5 %copy-start.22 = (f32[4,320]{1,0:T(4,128)}, f32[4,320]{1,0:T(4,128)S(1)}, u32[]{:S(2)}) copy-start(f32[4,320]{1,0:T(4,128)S(1)} %get-tuple-element.66) | copy-start | bytes 15364
  94.4 5.8 copy-start
  94.4 63.0 %all-to-all-start.2 = ((bf16[4,320,1024]{2,1,0:T(8,128)(2,1)}), bf16[4,320,1024]{2,1,0:T(8,128)(2,1)}, u32[]{:S(2)}, u32[]{:S(2)}) async-start(bf16[4,320,1024]{2,1,0:T(8,128)(2,1)} %param.29), calls=%async_computation.2 | async-start | bytes 5242880 | tf_op jit(solution)/shard_map/all_to_all | solution.py:157
  99.0 88.4 %reduce-scatter.7.cloned.1.call-start = ((), (), s32[]{:S(2)}) async-start(), calls=%async_computation.13 | async-start | bytes 4915200 | tf_op jit(solution)/shard_map/reduce_scatter | solution.py:262
  120.0 13.6 %copy-start.2 = (f32[1024,640]{1,0:T(8,128)}, f32[1024,640]{1,0:T(8,128)S(1)}, u32[]{:S(2)}) copy-start(f32[1024,640]{1,0:T(8,128)S(1)} %get-tuple-element.79) | copy-start | bytes 7864324
  128.0 2.8 collective-permute-start.1
  129.4 12.3 %collective-permute-start.3 = (bf16[1,640,64]{1,2,0:T(8,128)(2,1)S(1)}, bf16[1,640,64]{1,2,0:T(8,128)(2,1)S(1)}, u32[]{:S(2)}, u32[]{:S(2)}) collective-permute-start(bf16[1,640,64]{1,2,0:T(8,128)(2,1)S(1)} %get-tuple-element.56), channel_id=1, source_target_pairs={{4,0},{5,1},{6,2},{7,3},{12,8},{13,9},{14,10},{15,11},{20,16},{21,... | collective-permute-start | bytes 245768 | tf_op jit(solution)/shard_map/ppermute | solution.py:137
  147.2 9.6 %copy-start.5 = (bf16[5,4,160,640]{3,2,1,0:T(8,128)(2,1)}, bf16[5,4,160,640]{3,2,1,0:T(8,128)(2,1)S(1)}, u32[]{:S(2)}) copy-start(bf16[5,4,160,640]{3,2,1,0:T(8,128)(2,1)S(1)} %copy.65) | copy-start | bytes 12288004
  156.9 43.1 %copy-start.6 = (f32[1024,640]{1,0:T(8,128)}, f32[1024,640]{1,0:T(8,128)S(1)}, u32[]{:S(2)}) copy-start(f32[1024,640]{1,0:T(8,128)S(1)} %get-tuple-element.81) | copy-start | bytes 7864324
  173.7 1.0 copy-start.15
  173.7 26.2 %all-gather.12.cloned.1.call-start = ((), (), s32[]{:S(2)}) async-start(), calls=%async_computation.12 | async-start | bytes 2457600 | tf_op jit(solution)/shard_map/all_gather | solution.py:229
  175.4 64.3 %reduce-scatter.9.cloned.1.call-start = ((), (), s32[]{:S(2)}) async-start(), calls=%async_computation.14 | async-start | bytes 2048000 | tf_op jit(solution)/shard_map/reduce_scatter | solution.py:263
  187.4 91.0 %reduce-scatter.11.cloned.1.call-start = ((), (), s32[]{:S(2)}) async-start(), calls=%async_computation.15 | async-start | bytes 12288000 | tf_op jit(solution)/shard_map/reduce_scatter | solution.py:262
  211.7 3.6 copy-start.10
  239.7 113.5 %reduce-scatter.13.cloned.1.call-start = ((), (), s32[]{:S(2)}) async-start(), calls=%async_computation.16 | async-start | bytes 5120000 | tf_op jit(solution)/shard_map/reduce_scatter | solution.py:263
  239.8 21.1 %collective-permute-start.4 = (bf16[1,640,64]{1,2,0:T(8,128)(2,1)S(1)}, bf16[1,640,64]{1,2,0:T(8,128)(2,1)S(1)}, u32[]{:S(2)}, u32[]{:S(2)}) collective-permute-start(bf16[1,640,64]{1,2,0:T(8,128)(2,1)S(1)} %get-tuple-element.55), channel_id=1, source_target_pairs={{4,0},{5,1},{6,2},{7,3},{12,8},{13,9},{14,10},{15,11},{20,16},{21,... | collective-permute-start | bytes 245768 | tf_op jit(solution)/shard_map/ppermute | solution.py:137
  258.2 3.6 collective-permute-start.5
  261.6 2.2 copy-start.12
  261.8 2.8 copy-start.3
  278.2 1.7 copy-start.4
  278.4 91.2 %reduce-scatter.15.cloned.1.call-start = ((), (), s32[]{:S(2)}) async-start(), calls=%async_computation.17 | async-start | bytes 5898240 | tf_op jit(solution)/shard_map/reduce_scatter | solution.py:262
  282.3 1.1 copy-start.11
  283.7 20.5 %copy-start.1 = (bf16[4,320,1024]{2,1,0:T(8,128)(2,1)S(1)}, bf16[4,320,1024]{2,1,0:T(8,128)(2,1)}, u32[]{:S(2)}) copy-start(bf16[4,320,1024]{2,1,0:T(8,128)(2,1)} %copy-done) | copy-start | bytes 7864324
  283.7 20.5 %copy-start.21 = (f32[4,320]{1,0:T(4,128)S(1)}, f32[4,320]{1,0:T(4,128)}, u32[]{:S(2)}) copy-start(f32[4,320]{1,0:T(4,128)} %copy-done.20) | copy-start | bytes 15364
  283.7 20.5 %copy-start.23 = (f32[4,320]{1,0:T(4,128)S(1)}, f32[4,320]{1,0:T(4,128)}, u32[]{:S(2)}) copy-start(f32[4,320]{1,0:T(4,128)} %copy-done.22) | copy-start | bytes 15364
  357.2 0.7 copy-start.19
  357.2 12.5 %copy-start.7 = (f32[1024,640]{1,0:T(8,128)S(1)}, f32[1024,640]{1,0:T(8,128)}, u32[]{:S(2)}) copy-start(f32[1024,640]{1,0:T(8,128)} %copy-done.6) | copy-start | bytes 7864324
  357.2 70.0 %reduce-scatter.17.cloned.1.call-start = ((), (), s32[]{:S(2)}) async-start(), calls=%async_computation.18 | async-start | bytes 2457600 | tf_op jit(solution)/shard_map/reduce_scatter | solution.py:263
  385.8 35.9 %all-to-all-start.1 = ((bf16[4,320,1024]{2,1,0:T(8,128)(2,1)}), bf16[4,320,1024]{2,1,0:T(8,128)(2,1)}, u32[]{:S(2)}, u32[]{:S(2)}) async-start(bf16[4,320,1024]{2,1,0:T(8,128)(2,1)} %bitcast.18), calls=%async_computation.1 | async-start | bytes 5242880 | tf_op jit(solution)/shard_map/all_to_all | solution.py:170
  421.7 121.3 %all-to-all-start.3 = ((bf16[4,320,1024]{2,1,0:T(8,128)(2,1)}), bf16[4,320,1024]{2,1,0:T(8,128)(2,1)S(1)}, u32[]{:S(2)}, u32[]{:S(2)}) async-start(bf16[4,320,1024]{2,1,0:T(8,128)(2,1)} %bitcast.263), calls=%async_computation.5 | async-start | bytes 5242880 | tf_op jit(solution)/shard_map/all_to_all | solution.py:170
  425.3 162.0 %all-gather.14.cloned.1.call-start = ((), (), s32[]{:S(2)}) async-start(), calls=%async_computation.19 | async-start | bytes 4915200 | tf_op jit(solution)/shard_map/all_gather | solution.py:325
  541.3 1.7 copy-start.13
  543.0 23.5 %copy-start.8 = (bf16[4,320,1024]{2,1,0:T(8,128)(2,1)}, bf16[4,320,1024]{2,1,0:T(8,128)(2,1)S(1)}, u32[]{:S(2)}) copy-start(bf16[4,320,1024]{2,1,0:T(8,128)(2,1)S(1)} %all-to-all-done.3) | copy-start | bytes 7864324
  559.3 7.2 %copy-start.16 = (f32[4,200,128]{2,1,0:T(8,128)S(1)}, f32[4,200,128]{2,1,0:T(8,128)}, u32[]{:S(2)}) copy-start(f32[4,200,128]{2,1,0:T(8,128)} %get-tuple-element.33) | copy-start | bytes 1228804
  564.4 21.7 %slice-start = ((f32[384,640]{1,0:T(8,128)}), f32[3,640]{1,0:T(4,128)S(1)}, s32[]{:S(2)}) async-start(f32[384,640]{1,0:T(8,128)} %reshape.1433), calls=%async_computation.20 | async-start | bytes 20480 | tf_op jit(solution)/shard_map/slice | solution.py:330
  593.1 3.6 copy-start.9
Sparse Core Ops, SparseCore 0:
  60.0 11.0 all-gather.7
  72.6 14.7 all-gather.9
  173.9 13.4 reduce-scatter.6
  188.8 11.0 all-gather.11
  202.2 37.4 reduce-scatter.8
  241.9 15.6 reduce-scatter.10
  278.5 74.6 reduce-scatter.12
  357.3 12.2 reduce-scatter.14
  372.1 42.6 reduce-scatter.16
  543.1 12.1 all-gather.13

commit v6 on v5

--- a/solution.py
+++ b/solution.py
@@ -26,7 +26,7 @@
     return me
 
 
-def _exchange_kernel(sizes, group, gather, axes, *refs):
+def _exchange_kernel(sizes, group, gather, reduce, axes, *refs):
     count_arrays = len(axes)
     x_refs = refs[:count_arrays]
     o_refs = refs[count_arrays : 2 * count_arrays]
@@ -52,9 +52,15 @@
         peer = lax.rem(me + j, count)
         for i in range(count_arrays):
             lead = (slice(None),) * axes[i]
+            if gather:
+                src, dst = x_refs[i], o_refs[i].at[me]
+            else:
+                slot = (j - 1) if reduce else me
+                src = x_refs[i].at[lead + (pl.ds(peer, 1),)]
+                dst = o_refs[i].at[lead + (pl.ds(slot, 1),)]
             copy = pltpu.make_async_remote_copy(
-                src_ref=x_refs[i] if gather else x_refs[i].at[lead + (peer,)],
-                dst_ref=o_refs[i].at[lead + (me,)],
+                src_ref=src,
+                dst_ref=dst,
                 send_sem=send_sem.at[i, j - 1],
                 recv_sem=recv_sem.at[i, j - 1],
                 device_id=device(peer),
@@ -66,16 +72,20 @@
         copy.wait()
 
 
-def exchange(xs, group, collective_id, gather=False, axes=None):
+def exchange(xs, group, collective_id, gather=False, axes=None, reduce=False):
     sizes = {a: lax.axis_size(a) for a in MESH_AXES}
     count = math.prod(sizes[a] for a in group)
     axes = tuple(axes or (0,) * len(xs))
     if count == 1:
         return [x[None] if gather else x for x in xs]
     shapes = [jax.ShapeDtypeStruct((count,) + x.shape if gather else x.shape, x.dtype) for x in xs]
+    if reduce:
+        shapes = [
+            jax.ShapeDtypeStruct(x.shape[:a] + (count - 1,) + x.shape[a + 1 :], x.dtype) for x, a in zip(xs, axes)
+        ]
     moved = sum(x.size * x.dtype.itemsize * (count if gather else 1) for x in xs)
     outs = pl.pallas_call(
-        functools.partial(_exchange_kernel, sizes, group, gather, axes),
+        functools.partial(_exchange_kernel, sizes, group, gather, reduce, axes),
         out_shape=shapes,
         in_specs=[pl.BlockSpec(memory_space=pl.ANY)] * len(xs),
         out_specs=[pl.BlockSpec(memory_space=pl.ANY)] * len(xs),
@@ -88,6 +98,11 @@
     )(*xs)
     me = _group_index(group, sizes, {a: lax.axis_index(a) for a in group})
     placed = []
+    if reduce:
+        for x, out, axis in zip(xs, outs, axes):
+            own = lax.dynamic_index_in_dim(x, me, axis, keepdims=False)
+            placed.append(own + jnp.sum(out, axis=axis))
+        return placed
     for x, out, axis in zip(xs, outs, axes):
         own = x if gather else lax.dynamic_index_in_dim(x, me, axis, keepdims=False)
         placed.append(lax.dynamic_update_index_in_dim(out, own, me, axis))
@@ -319,10 +334,14 @@
     part_conv = part_conv.reshape((part_conv.shape[0],) + conv_tail)
     part_inner = reduce_seq_batch(inner_plus, 1, part_conv)
     parts = [part_outer, part_conv, part_inner]
-    parts = exchange(parts, ("ch",), 1, axes=(0, 2, 0))
-    parts = [jnp.sum(p, axis=a) for p, a in zip(parts, (0, 2, 0))]
+    parts = exchange(parts, ("ch",), 1, axes=(0, 2, 0), reduce=True)
+    piece_shapes = [p.shape for p in parts]
+    parts = [p.reshape(p.size // 128, 128) if p.size % 128 == 0 else p for p in parts]
     parts = [lax.all_gather(p, "batch", axis=0) for p in parts]
-    parts = [lax.all_gather(p, "seq", axis=0, tiled=True).reshape((seqs * batches,) + p.shape[1:]) for p in parts]
+    parts = [
+        lax.all_gather(p, "seq", axis=0, tiled=True).reshape((seqs * batches,) + shape)
+        for p, shape in zip(parts, piece_shapes)
+    ]
     red_w_outer = parts[0].reshape(hloc, dim)
     red_w_conv = parts[1].reshape(hid, KERNEL_TAPS, hloc).transpose(1, 2, 0)
     red_inner = parts[2].reshape(dloc + vec_rows, hid)

time: 617 us -> 590 us (0.956)
  blocking collectives: 81.5 us -> 59.3 us
  local copies, waits for them, and re-layouts: 105 us -> 97.5 us
    all_gather x3, blocking collectives: 76.4 us -> 54.2 us  [local(): parts = [lax.all_gather(p, 'batch', axis=0) for p in parts]]
    dynamic_update_slice x7 -> x4, local copies, waits for them, and re-layouts: 14.9 us -> 3.46 us  [exchange(): placed.append(lax.dynamic_update_index_in_dim(out, own, me, axis))]
    unnamed x52 -> x49, local copies, waits for them, and re-layouts: 12.6 us -> 17.5 us
where the time goes in v6:
time: 590 us; the launch traced here: 578 us
  matrix products  118 us (20%)
  waiting for transfers between devices  111 us (19%)
  Pallas kernels  100 us (17%)
  local copies, waits for them, and re-layouts  97.5 us (17%)
  blocking collectives  59.3 us (10%)
  other arithmetic  50.2 us (9%)
  starting transfers between devices  26.7 us (5%)
  between operations  15 us (3%)
    pallas_call x2, Pallas kernels, exchange(): pl.pallas_call(functools.partial(_exchange_kernel, sizes, group, gather,...  100 us
    all_gather x3, blocking collectives, local(): parts = [lax.all_gather(p, 'batch', axis=0) for p in parts]  54.2 us
    reduce_scatter x3, waiting for transfers between devices, reduce_seq_batch(): return lax.psum_scatter(g, 'batch', scatter_dimension=split_dim, tiled=True)  43.8 us
    all_to_all x2, waiting for transfers between devices, to_positions(): x = lax.all_to_all(x, 'ch', 0, 0, tiled=True)  23.3 us
    dot_general x1, matrix products, local(): jnp.einsum('dh,rhl->rdl', w_in, grad_inner, preferred_element_type=jnp.fl...  20 us
    unnamed x49, local copies, waits for them, and re-layouts  17.5 us
    all_to_all x2, waiting for transfers between devices, to_channels(): x = lax.all_to_all(x, 'ch', 0, 0, tiled=True)  17.3 us
    dot_general x1, matrix products, local(): jnp.einsum('dh,rdl->rhl', w_in, hidden0, preferred_element_type=jnp.float32)  16.8 us
  transfers between devices with their start and end apart: 20, of which 7 were waited for; matrix products, arithmetic and copies ran while one was open for 37% of the time, Pallas kernels for 9%

profile of v6, /device:TPU:0, one launch (start us, length us, event | category | flops | bytes accessed | tf_op | source)
XLA Modules:
  0.0 577.8 jit_solution(13895425521982536167)
XLA Ops:
  13.9 45.3 %shard_map.254 = (f32[4,1920]{1,0:T(4,128)}, bf16[4,160,640]{2,1,0:T(8,128)(2,1)}, bf16[4,5,80,640]{3,2,1,0:T(8,128)(2,1)}, bf16[4,80,1280]{2,1,0:T(8,128)(2,1)}) custom-call(f32[1920]{0:T(1024)} %concatenate.43.refs_0_, bf16[160,640]{1,0:T(8,128)(2,1)} %constant_dynamic-slice_fusion.2.refs_1_, bf16[5,80,640]{2,1,0:T(8,128)(2,1)} %constant_dynamic-slice_fusion.1.refs_2_, ...), custom_call_target="tpu_custom_call" | custom-call | bytes 7434240 | tf_op jit(solution)/shard_map/pallas_call | solution.py:87
  59.9 3.7 all-to-all-start
  71.1 23.3 %all-to-all-done = bf16[4,320,1024]{2,1,0:T(8,128)(2,1)S(1)} async-done(((bf16[4,320,1024]{2,1,0:T(8,128)(2,1)}), bf16[4,320,1024]{2,1,0:T(8,128)(2,1)S(1)}, u32[]{:S(2)}, u32[]{:S(2)}) %all-to-all-start) | async-done | bytes 2621472 | tf_op jit(solution)/shard_map/all_to_all | solution.py:172
  94.4 4.6 all-to-all-start.2
  100.3 2.9 convert_element_type.149
  103.2 16.8 %fusion.83 = (f32[1024]{0:T(1024)S(1)}, f32[1024,640]{1,0:T(8,128)S(1)}) fusion(f32[640]{0:T(1024)S(1)} %add.204, bf16[1280,640]{1,0:T(8,128)(2,1)} %bitcast.267, f32[1280]{0:T(1024)S(1)} %add.201, f32[1280]{0:T(1024)S(1)} %mul.438, f32[1024]{0:T(1024)S(1)} %add_rsqrt_fusion.2, f32[1,1280,1,1,1,1,1024]{6,1,5,4,3,2,0:T(8,128)} %bitcast.257, ...), kind=kOutput, calls=%fused_computation.159 | convolution fusion | flops 1769470976 | bytes 9527808 | tf_op jit(solution)/shard_map/dh,rdl->rhl/dot_general | solution.py:260
  120.6 7.3 %multiply_convert_fusion.1 = bf16[1,640,1024]{1,2,0:T(8,128)(2,1)S(1)} fusion(f32[640]{0:T(1024)S(1)} %add.208, f32[640]{0:T(1024)S(1)} %mul.448, f32[1024]{0:T(1024)S(1)} %add_rsqrt_fusion.1, f32[1024]{0:T(1024)S(1)} %broadcast_multiply_fusion.5, f32[640]{0:T(1024)S(1)} %add.204, f32[1024,640]{1,0:T(8,128)S(1)} %get-tuple-element.107), kind=kLoop, calls=%fused_computation.141 | loop fusion | flops 45875200 | bytes 3948032 | tf_op jit(solution)/shard_map/convert_element_type | solution.py:262
  133.7 8.0 %constant_dynamic-update-slice_fusion = bf16[1,3200,1024]{1,2,0:T(8,128)(2,1)} fusion(bf16[1,3200,1024]{1,2,0:T(8,128)(2,1)} %fusion.110, f32[640]{0:T(1024)S(1)} %add.208, f32[640]{0:T(1024)S(1)} %mul.448, f32[1024]{0:T(1024)S(1)} %add_rsqrt_fusion.1, f32[1024]{0:T(1024)S(1)} %broadcast_multiply_fusion.5, f32[640]{0:T(1024)S(1)} %add.204, ...), kind=kLoop, calls=%fused_computation.211 | loop fusion | flops 45875200 | bytes 3948032
  144.6 2.6 copy.52
  147.3 9.6 %fusion.85 = (f32[1024]{0:T(1024)S(1)}, f32[1024,640]{1,0:T(8,128)S(1)}) fusion(f32[640]{0:T(1024)S(1)} %add.211, bf16[3200,640]{1,0:T(8,128)(2,1)S(1)} %bitcast.259, bf16[1,3200,1024]{1,2,0:T(8,128)(2,1)} %fusion.108), kind=kOutput, calls=%fused_computation.161 | convolution fusion | flops 4195613696 | bytes 13277696 | tf_op jit(solution)/shard_map/co,rcl->rol/dot_general | solution.py:266
  157.4 11.8 %fusion.177 = f32[640,1280]{1,0:T(8,128)} fusion(bf16[1280,1024]{1,0:T(8,128)(2,1)} %bitcast.20, f32[640]{0:T(1024)S(1)} %add.215, f32[640]{0:T(1024)S(1)} %mul.458, f32[1024]{0:T(1024)S(1)} %add_rsqrt_fusion, f32[1024]{0:T(1024)S(1)} %broadcast_multiply_fusion.4, f32[640]{0:T(1024)S(1)} %add.211, f32[1024,640]{1,0:T(8,128)S(1)} %get-tuple-element.109), kind=kOutput, calls=%fused_computation.301 | convolution fusion | flops 1723596800 | bytes 8535552 | tf_op jit(solution)/shard_map/rhl,rdl->hd/dot_general | solution.py:273
  169.2 4.5 reshape.1435
  175.5 9.7 %copy.62 = bf16[1,3200,1024]{2,1,0:T(8,128)(2,1)} copy(bf16[1,3200,1024]{1,2,0:T(8,128)(2,1)} %fusion.108) | data formatting | bytes 13107200 | tf_op jit(solution)/shard_map/concatenate | solution.py:164
  187.4 12.5 %all-gather.9.cloned.1.call-done = bf16[4,160,1280]{2,1,0:T(8,128)(2,1)} async-done(((bf16[4,80,1280]{2,1,0:T(8,128)(2,1)}), bf16[4,160,1280]{2,1,0:T(8,128)(2,1)}) %all-gather.9.cloned.1.call-update) | async-done | bytes 1638416 | tf_op jit(solution)/shard_map/all_gather | solution.py:244
  199.9 11.7 %fusion.60 = (f32[640]{0:T(1024)S(1)}, f32[1024]{0:T(1024)S(1)}, f32[1024]{0:T(1024)S(1)}, f32[640]{0:T(1024)S(1)}, f32[1,640,1024]{1,2,0:T(8,128)S(1)}) fusion(f32[1024]{0:T(1024)S(1)} %add_rsqrt_fusion, f32[1024]{0:T(1024)S(1)} %broadcast_multiply_fusion.4, f32[640]{0:T(1024)S(1)} %add.211, f32[1024,640]{1,0:T(8,128)S(1)} %get-tuple-element.109, ...), kind=kOutput, calls=%fused_computation.110 | convolution fusion | flops 1732113152 | bytes 9531904 | tf_op jit(solution)/shard_map/hd,rdl->rhl/dot_general | solution.py:281
  211.7 2.6 convert_reduce_fusion.1
  215.3 7.1 %fusion.111 = f32[640,25,128]{2,0,1:T(8,128)} fusion(bf16[25,128,1024]{2,1,0:T(8,128)(2,1)S(1)} %bitcast.262, bf16[1,640,1024]{1,2,0:T(8,128)(2,1)S(1)} %get-tuple-element.81), kind=kOutput, calls=%fused_computation.199 | convolution fusion | flops 4194304000 | bytes 16056320 | tf_op jit(solution)/shard_map/rol,rkcil->okci/dot_general | solution.py:287
  222.4 17.3 %reduce-scatter.9.cloned.1.call-done.refs_0_ = f32[4,200,128]{2,1,0:T(8,128)} async-done(((f32[4,800,128]{2,1,0:T(8,128)}), f32[4,200,128]{2,1,0:T(8,128)}) %reduce-scatter.9.cloned.1.call-update) | async-done | bytes 409616 | tf_op jit(solution)/shard_map/reduce_scatter | solution.py:278
  243.3 6.4 %copy.53 = f32[1,1280,1024]{1,2,0:T(8,128)} copy(f32[1,1280,1024]{2,1,0:T(8,128)} %bitcast.258) | data formatting | bytes 10485760 | tf_op jit(solution)/shard_map/convert_element_type | solution.py:257
  249.6 8.3 %copy.58 = bf16[5,640,640]{2,1,0:T(8,128)(2,1)} copy(bf16[5,640,640]{1,2,0:T(8,128)(2,1)} %bitcast.260) | data formatting | bytes 8192000 | tf_op jit(solution)/shard_map/transpose | solution.py:295
  258.2 2.7 collective-permute-start.5
  264.6 13.6 %fusion.66 = (f32[640]{0:T(1024)S(1)}, f32[1024]{0:T(1024)S(1)}, f32[1024]{0:T(1024)S(1)}, f32[640]{0:T(1024)S(1)}, f32[1,640,1024]{1,2,0:T(8,128)}) fusion(f32[1024]{0:T(1024)S(1)} %add_rsqrt_fusion.1, f32[1024]{0:T(1024)S(1)} %broadcast_multiply_fusion.5, f32[640]{0:T(1024)S(1)} %add.204, f32[1024,640]{1,0:T(8,128)S(1)} %copy-done.3, f32[640]{0:T(1024)S(1)} %mul.448, ...), kind=kOutput, calls=%fused_computation.121 | convolution fusion | flops 4248695808 | bytes 15921664 | tf_op jit(solution)/shard_map/oc,rol->rcl/dot_general | solution.py:296
  279.9 2.4 fusion.65
  283.7 20.0 %multiply_reduce_fusion = (f32[1280]{0:T(1024)S(1)}, f32[1024]{0:T(1024)S(1)}, f32[1024]{0:T(1024)S(1)}, f32[1280]{0:T(1024)S(1)}, f32[1,1280,1024]{1,2,0:T(8,128)}) fusion(f32[1,1280,1024]{1,2,0:T(8,128)} %copy.53, f32[1024]{0:T(1024)S(1)} %broadcast_multiply_fusion.8, f32[1024]{0:T(1024)S(1)} %add_rsqrt_fusion.2, f32[1280]{0:T(1024)S(1)} %mul.438, ...), kind=kOutput, calls=%fused_computation.25 | convolution fusion | flops 1785196032 | bytes 13471744 | tf_op jit(solution)/shard_map/dh,rhl->rdl/dot_general | solution.py:304
  304.2 15.5 %fusion.79 = f32[4,320,640]{2,1,0:T(8,128)S(1)} fusion(bf16[4,320,1024]{2,1,0:T(8,128)(2,1)S(1)} %copy-done.1, f32[4,320]{1,0:T(4,128)S(1)} %copy-done.21, f32[4,320]{1,0:T(4,128)S(1)} %copy-done.19, f32[1024]{0:T(1024)S(1)} %add_rsqrt_fusion.2, f32[1024]{0:T(1024)S(1)} %broadcast_multiply_fusion.8, bf16[1,640,1024]{1,2,0:T(8,128)(2,1)} %copy-done.9), kind=kOutput, calls=%fused_computation.155 | convolution fusion | flops 1769472000 | bytes 7227392 | tf_op jit(solution)/shard_map/rdl,rhl->dh/dot_general | solution.py:303
  322.0 4.7 reshape.1446
  326.7 26.6 %reduce-scatter.13.cloned.1.call-done = f32[80,25,128]{2,0,1:T(8,128)} async-done(((f32[320,25,128]{2,0,1:T(8,128)}), f32[80,25,128]{2,0,1:T(8,128)}) %reduce-scatter.13.cloned.1.call-update) | async-done | bytes 1024016 | tf_op jit(solution)/shard_map/reduce_scatter | solution.py:278
  354.8 2.4 reshape.1448.refs_1_
  357.9 11.7 %reduce-scatter.15.cloned.1.call-done = f32[4,960,128]{2,1,0:T(8,128)} async-done(((f32[4,1920,128]{2,1,0:T(8,128)}), f32[4,960,128]{2,1,0:T(8,128)}) %reduce-scatter.15.cloned.1.call-update) | async-done | bytes 1966096 | tf_op jit(solution)/shard_map/reduce_scatter | solution.py:277
  369.7 11.7 %fusion.15 = bf16[1,1280,1024]{1,2,0:T(8,128)(2,1)} fusion(f32[1,1280,1024]{1,2,0:T(8,128)} %copy.53, bf16[640,1280]{1,0:T(8,128)(2,1)} %bitcast.270, f32[1280]{0:T(1024)S(1)} %add.219, f32[640]{0:T(1024)S(1)} %add.215, f32[640]{0:T(1024)S(1)} %mul.458, f32[1024]{0:T(1024)S(1)} %add_rsqrt_fusion, f32[1024]{0:T(1024)S(1)} %broadcast_multiply_fusion.4, ...), kind=kOutput, calls=%fused_computation.19 | convolution fusion | flops 1727528960 | bytes 12145152 | tf_op jit(solution)/shard_map/hd,rhl->rdl/dot_general | solution.py:269
  381.4 4.4 copy.54
  385.8 4.6 all-to-all-start.1
  390.3 4.9 copy.59
  395.3 6.5 %add_convert_fusion = bf16[1,1280,1024]{1,2,0:T(8,128)(2,1)S(1)} fusion(f32[1,1280,1024]{1,2,0:T(8,128)} %copy.59, f32[1,1280,1024]{1,2,0:T(8,128)} %get-tuple-element.112, f32[1,1280,1024]{1,2,0:T(8,128)} %copy.53, f32[1024]{0:T(1024)S(1)} %broadcast_multiply_fusion.6, f32[1024]{0:T(1024)S(1)} %broadcast_multiply_fusion.7, f32[1280]{0:T(1024)S(1)} %mul.438, ...), kind=kLoop, calls=%fused_computation.40 | loop fusion | flops 11796480 | bytes 18371584 | tf_op jit(solution)/shard_map/convert_element_type | solution.py:308
  401.8 2.6 copy.60
  404.4 17.3 %all-to-all-done.1 = bf16[4,320,1024]{2,1,0:T(8,128)(2,1)} async-done(((bf16[4,320,1024]{2,1,0:T(8,128)(2,1)}), bf16[4,320,1024]{2,1,0:T(8,128)(2,1)}, u32[]{:S(2)}, u32[]{:S(2)}) %all-to-all-start.1) | async-done | bytes 2621472 | tf_op jit(solution)/shard_map/all_to_all | solution.py:185
  421.7 3.7 all-to-all-start.3
  425.6 2.6 dynamic-slice_reduce_fusion
  428.5 54.8 %shard_map.255 = (f32[3,200,128]{2,1,0:T(8,128)}, f32[80,5,3,160]{3,2,1,0:T(4,128)}, f32[3,240,128]{2,1,0:T(8,128)}) custom-call(f32[4,200,128]{2,1,0:T(8,128)} %reduce-scatter.9.cloned.1.call-done.refs_0_, f32[80,5,4,160]{3,2,1,0:T(4,128)} %reshape.1448.refs_1_, f32[4,240,128]{2,1,0:T(8,128)} %reduce-scatter.17.cloned.1.call-done.refs_2_), custom_call_target="tpu_custom_call" | custom-call | bytes 3850240 | tf_op jit(solution)/shard_map/pallas_call | solution.py:87
  483.3 2.4 reduce_sum.245
  487.8 23.0 %all_gather.34 = f32[4,500,128]{2,1,0:T(8,128)} all-gather(f32[1,500,128]{2,1,0:T(8,128)S(1)} %add.228), channel_id=1, replica_groups=mesh['batch'=4,'seq'=2,'ch'=4] {'batch'}, dimensions={0}, use_global_device_ids=true | all-gather | bytes 1280000 | tf_op jit(solution)/shard_map/all_gather | solution.py:340
  511.8 15.7 %all_gather.32 = f32[4,240,128]{2,1,0:T(8,128)S(1)} all-gather(f32[1,240,128]{2,1,0:T(8,128)S(1)} %bitcast_add_fusion.3), channel_id=1, replica_groups=mesh['batch'=4,'seq'=2,'ch'=4] {'batch'}, dimensions={0}, use_global_device_ids=true | all-gather | bytes 614400 | tf_op jit(solution)/shard_map/all_gather | solution.py:340
  527.5 2.8 all_gather.33
  535.7 15.5 %all_gather.36 = f32[4,200,128]{2,1,0:T(8,128)S(1)} all-gather(f32[1,200,128]{2,1,0:T(8,128)S(1)} %bitcast_add_fusion.4), channel_id=1, replica_groups=mesh['batch'=4,'seq'=2,'ch'=4] {'batch'}, dimensions={0}, use_global_device_ids=true | all-gather | bytes 512000 | tf_op jit(solution)/shard_map/all_gather | solution.py:340
  551.1 2.4 all_gather.37
  555.9 4.8 reshape_reshape.7
  560.7 5.1 copy.65
  565.8 3.5 copy.88
  (163 shorter events, 59.2 us)
Async XLA Ops:
  7.2 52.0 %copy-start.11 = (bf16[320,640]{1,0:T(8,128)(2,1)S(1)}, bf16[320,640]{1,0:T(8,128)(2,1)}, u32[]{:S(2)}) copy-start(bf16[320,640]{1,0:T(8,128)(2,1)} %param.19) | copy-start | bytes 1228804
  7.2 96.0 %all-gather.5.cloned.1.call-start = ((), (), s32[]{:S(2)}) async-start(), calls=%async_computation.10 | async-start | bytes 2457600 | tf_op jit(solution)/shard_map/all_gather | solution.py:242
  59.9 34.5 %all-to-all-start = ((bf16[4,320,1024]{2,1,0:T(8,128)(2,1)}), bf16[4,320,1024]{2,1,0:T(8,128)(2,1)S(1)}, u32[]{:S(2)}, u32[]{:S(2)}) async-start(bf16[4,320,1024]{2,1,0:T(8,128)(2,1)} %param.15), calls=%async_computation | async-start | bytes 5242880 | tf_op jit(solution)/shard_map/all_to_all | solution.py:172
  63.6 6.0 %copy-start.15 = (f32[1920]{0:T(1024)S(1)}, f32[1920]{0:T(1024)}, u32[]{:S(2)}) copy-start(f32[1920]{0:T(1024)} %concatenate.43.refs_0_) | copy-start | bytes 23044
  63.6 6.0 %copy-start.16 = (f32[4,1920]{1,0:T(4,128)S(1)}, f32[4,1920]{1,0:T(4,128)}, u32[]{:S(2)}) copy-start(f32[4,1920]{1,0:T(4,128)} %get-tuple-element.24) | copy-start | bytes 92164
  63.6 81.0 %all-gather.7.cloned.1.call-start = ((), (), s32[]{:S(2)}) async-start(), calls=%async_computation.11 | async-start | bytes 6144000 | tf_op jit(solution)/shard_map/all_gather | solution.py:243
  64.5 64.8 %collective-permute-start = (s32[1,64]{1,0:T(1,128)S(1)}, s32[1,64]{1,0:T(1,128)S(1)}, u32[]{:S(2)}, u32[]{:S(2)}) collective-permute-start(s32[1,64]{1,0:T(1,128)S(1)} %get-tuple-element.104), channel_id=1, source_target_pairs={{0,4},{1,5},{2,6},{3,7},{8,12},{9,13},{10,14},{11,15},{16,20},{17,... | collective-permute-start | bytes 776 | tf_op jit(solution)/shard_map/ppermute | solution.py:151
  66.3 63.0 %collective-permute-start.2 = (s32[1,64]{1,0:T(1,128)S(1)}, s32[1,64]{1,0:T(1,128)S(1)}, u32[]{:S(2)}, u32[]{:S(2)}) collective-permute-start(s32[1,64]{1,0:T(1,128)S(1)} %get-tuple-element.105), channel_id=1, source_target_pairs={{4,0},{5,1},{6,2},{7,3},{12,8},{13,9},{14,10},{15,11},{20,16},{21,... | collective-permute-start | bytes 776 | tf_op jit(solution)/shard_map/ppermute | solution.py:152
  71.0 23.5 %copy-start.18 = (f32[4,320]{1,0:T(4,128)}, f32[4,320]{1,0:T(4,128)S(1)}, u32[]{:S(2)}) copy-start(f32[4,320]{1,0:T(4,128)S(1)} %get-tuple-element.92) | copy-start | bytes 15364
  71.0 23.5 %copy-start.20 = (f32[4,320]{1,0:T(4,128)}, f32[4,320]{1,0:T(4,128)S(1)}, u32[]{:S(2)}) copy-start(f32[4,320]{1,0:T(4,128)S(1)} %get-tuple-element.94) | copy-start | bytes 15364
  94.4 5.8 %copy-start = (bf16[4,320,1024]{2,1,0:T(8,128)(2,1)}, bf16[4,320,1024]{2,1,0:T(8,128)(2,1)S(1)}, u32[]{:S(2)}) copy-start(bf16[4,320,1024]{2,1,0:T(8,128)(2,1)S(1)} %all-to-all-done) | copy-start | bytes 7864324
  94.4 63.0 %all-to-all-start.2 = ((bf16[4,320,1024]{2,1,0:T(8,128)(2,1)}), bf16[4,320,1024]{2,1,0:T(8,128)(2,1)}, u32[]{:S(2)}, u32[]{:S(2)}) async-start(bf16[4,320,1024]{2,1,0:T(8,128)(2,1)} %param.29), calls=%async_computation.2 | async-start | bytes 5242880 | tf_op jit(solution)/shard_map/all_to_all | solution.py:172
  99.0 88.4 %reduce-scatter.7.cloned.1.call-start = ((), (), s32[]{:S(2)}) async-start(), calls=%async_computation.13 | async-start | bytes 4915200 | tf_op jit(solution)/shard_map/reduce_scatter | solution.py:277
  120.0 13.6 %copy-start.2 = (f32[1024,640]{1,0:T(8,128)}, f32[1024,640]{1,0:T(8,128)S(1)}, u32[]{:S(2)}) copy-start(f32[1024,640]{1,0:T(8,128)S(1)} %get-tuple-element.107) | copy-start | bytes 7864324
  128.0 2.8 collective-permute-start.1
  129.4 12.3 %collective-permute-start.3 = (bf16[1,640,64]{1,2,0:T(8,128)(2,1)S(1)}, bf16[1,640,64]{1,2,0:T(8,128)(2,1)S(1)}, u32[]{:S(2)}, u32[]{:S(2)}) collective-permute-start(bf16[1,640,64]{1,2,0:T(8,128)(2,1)S(1)} %get-tuple-element.84), channel_id=1, source_target_pairs={{4,0},{5,1},{6,2},{7,3},{12,8},{13,9},{14,10},{15,11},{20,16},{21,... | collective-permute-start | bytes 245768 | tf_op jit(solution)/shard_map/ppermute | solution.py:152
  147.2 9.6 %copy-start.5 = (bf16[5,4,160,640]{3,2,1,0:T(8,128)(2,1)}, bf16[5,4,160,640]{3,2,1,0:T(8,128)(2,1)S(1)}, u32[]{:S(2)}) copy-start(bf16[5,4,160,640]{3,2,1,0:T(8,128)(2,1)S(1)} %copy.52) | copy-start | bytes 12288004
  156.9 43.1 %copy-start.6 = (f32[1024,640]{1,0:T(8,128)}, f32[1024,640]{1,0:T(8,128)S(1)}, u32[]{:S(2)}) copy-start(f32[1024,640]{1,0:T(8,128)S(1)} %get-tuple-element.109) | copy-start | bytes 7864324
  173.7 1.0 copy-start.12
  173.7 26.2 %all-gather.9.cloned.1.call-start = ((), (), s32[]{:S(2)}) async-start(), calls=%async_computation.12 | async-start | bytes 2457600 | tf_op jit(solution)/shard_map/all_gather | solution.py:244
  175.4 64.3 %reduce-scatter.9.cloned.1.call-start = ((), (), s32[]{:S(2)}) async-start(), calls=%async_computation.14 | async-start | bytes 2048000 | tf_op jit(solution)/shard_map/reduce_scatter | solution.py:278
  187.4 91.0 %reduce-scatter.11.cloned.1.call-start = ((), (), s32[]{:S(2)}) async-start(), calls=%async_computation.15 | async-start | bytes 12288000 | tf_op jit(solution)/shard_map/reduce_scatter | solution.py:277
  211.7 3.6 copy-start.8
  239.7 113.5 %reduce-scatter.13.cloned.1.call-start = ((), (), s32[]{:S(2)}) async-start(), calls=%async_computation.16 | async-start | bytes 5120000 | tf_op jit(solution)/shard_map/reduce_scatter | solution.py:278
  239.8 21.1 %collective-permute-start.4 = (bf16[1,640,64]{1,2,0:T(8,128)(2,1)S(1)}, bf16[1,640,64]{1,2,0:T(8,128)(2,1)S(1)}, u32[]{:S(2)}, u32[]{:S(2)}) collective-permute-start(bf16[1,640,64]{1,2,0:T(8,128)(2,1)S(1)} %get-tuple-element.83), channel_id=1, source_target_pairs={{4,0},{5,1},{6,2},{7,3},{12,8},{13,9},{14,10},{15,11},{20,16},{21,... | collective-permute-start | bytes 245768 | tf_op jit(solution)/shard_map/ppermute | solution.py:152
  258.2 3.6 collective-permute-start.5
  261.6 2.2 copy-start.10
  261.8 2.8 copy-start.3
  278.2 1.7 copy-start.4
  278.4 91.2 %reduce-scatter.15.cloned.1.call-start = ((), (), s32[]{:S(2)}) async-start(), calls=%async_computation.17 | async-start | bytes 5898240 | tf_op jit(solution)/shard_map/reduce_scatter | solution.py:277
  282.3 1.1 copy-start.9
  283.7 20.5 %copy-start.1 = (bf16[4,320,1024]{2,1,0:T(8,128)(2,1)S(1)}, bf16[4,320,1024]{2,1,0:T(8,128)(2,1)}, u32[]{:S(2)}) copy-start(bf16[4,320,1024]{2,1,0:T(8,128)(2,1)} %copy-done) | copy-start | bytes 7864324
  283.7 20.5 %copy-start.19 = (f32[4,320]{1,0:T(4,128)S(1)}, f32[4,320]{1,0:T(4,128)}, u32[]{:S(2)}) copy-start(f32[4,320]{1,0:T(4,128)} %copy-done.18) | copy-start | bytes 15364
  283.7 20.5 %copy-start.21 = (f32[4,320]{1,0:T(4,128)S(1)}, f32[4,320]{1,0:T(4,128)}, u32[]{:S(2)}) copy-start(f32[4,320]{1,0:T(4,128)} %copy-done.20) | copy-start | bytes 15364
  357.2 0.7 copy-start.17
  357.2 12.5 %copy-start.7 = (f32[1024,640]{1,0:T(8,128)S(1)}, f32[1024,640]{1,0:T(8,128)}, u32[]{:S(2)}) copy-start(f32[1024,640]{1,0:T(8,128)} %copy-done.6) | copy-start | bytes 7864324
  357.2 71.3 %reduce-scatter.17.cloned.1.call-start = ((), (), s32[]{:S(2)}) async-start(), calls=%async_computation.18 | async-start | bytes 2457600 | tf_op jit(solution)/shard_map/reduce_scatter | solution.py:278
  385.8 35.9 %all-to-all-start.1 = ((bf16[4,320,1024]{2,1,0:T(8,128)(2,1)}), bf16[4,320,1024]{2,1,0:T(8,128)(2,1)}, u32[]{:S(2)}, u32[]{:S(2)}) async-start(bf16[4,320,1024]{2,1,0:T(8,128)(2,1)} %bitcast.18), calls=%async_computation.1 | async-start | bytes 5242880 | tf_op jit(solution)/shard_map/all_to_all | solution.py:185
  421.7 89.2 %all-to-all-start.3 = ((bf16[4,320,1024]{2,1,0:T(8,128)(2,1)}), bf16[4,320,1024]{2,1,0:T(8,128)(2,1)S(1)}, u32[]{:S(2)}, u32[]{:S(2)}) async-start(bf16[4,320,1024]{2,1,0:T(8,128)(2,1)} %bitcast.261), calls=%async_computation.5 | async-start | bytes 5242880 | tf_op jit(solution)/shard_map/all_to_all | solution.py:185
  425.3 130.5 %all-gather.11.cloned.1.call-start = ((), (), s32[]{:S(2)}) async-start(), calls=%async_computation.19 | async-start | bytes 3096576 | tf_op jit(solution)/shard_map/all_gather | solution.py:342
  486.8 24.1 %copy-start.13 = (f32[3,240,128]{2,1,0:T(8,128)S(1)}, f32[3,240,128]{2,1,0:T(8,128)}, u32[]{:S(2)}) copy-start(f32[3,240,128]{2,1,0:T(8,128)} %get-tuple-element.31) | copy-start | bytes 1105924
  527.5 7.2 %copy-start.14 = (f32[3,200,128]{2,1,0:T(8,128)S(1)}, f32[3,200,128]{2,1,0:T(8,128)}, u32[]{:S(2)}) copy-start(f32[3,200,128]{2,1,0:T(8,128)} %get-tuple-element.33) | copy-start | bytes 921604
  532.6 21.9 %slice-start = ((f32[384,640]{1,0:T(8,128)}), f32[3,640]{1,0:T(4,128)S(1)}, s32[]{:S(2)}) async-start(f32[384,640]{1,0:T(8,128)} %reshape.1449), calls=%async_computation.20 | async-start | bytes 20480 | tf_op jit(solution)/shard_map/slice | solution.py:349
Sparse Core Ops, SparseCore 0:
  60.0 11.0 all-gather.4
  72.6 14.7 all-gather.6
  173.9 13.4 reduce-scatter.6
  188.8 11.0 all-gather.8
  202.2 37.4 reduce-scatter.8
  241.9 15.6 reduce-scatter.10
  278.5 74.6 reduce-scatter.12
  357.3 12.2 reduce-scatter.14
  372.1 42.6 reduce-scatter.16
  511.0 8.2 all-gather.10

commit v7 on v6

--- a/solution.py
+++ b/solution.py
@@ -231,7 +231,8 @@
         lax.dynamic_slice_in_dim(w_conv, sidx * (hloc // seqs), hloc // seqs, 1),
         lax.dynamic_slice_in_dim(w_outer, sidx * (hloc // seqs), hloc // seqs, 0),
     ]
-    small_all, w_in, w_cv, w_out = exchange([jnp.concatenate(smalls)] + halves, ("ch",), 0, gather=True)
+    small_all, w_in, w_out = exchange([jnp.concatenate(smalls), halves[0], halves[2]], ("ch",), 0, gather=True)
+    w_cv = lax.all_gather(halves[1], "ch", axis=0)
     cut = 0
     full = []
     for v in smalls:

time: 590 us -> 590 us (level)
  Pallas kernels: 100 us -> 78.2 us
  waiting for transfers between devices: 111 us -> 128 us
    pallas_call x2, Pallas kernels: 100 us -> 78.2 us  [exchange(): pl.pallas_call(functools.partial(_exchange_kernel, sizes, group, gather,...]
    all_gather x0 -> x1, waiting for transfers between devices: none -> 12.2 us  [local(): w_cv = lax.all_gather(halves[1], 'ch', axis=0)]
    all_to_all x2, waiting for transfers between devices: 23.3 us -> 30 us  [to_positions(): x = lax.all_to_all(x, 'ch', 0, 0, tiled=True)]
    unnamed x49 -> x53, local copies, waits for them, and re-layouts: 17.5 us -> 17.7 us
  transfers between devices with their start and end apart: 20 -> 21, of which waited for: 7 -> 8; matrix products, arithmetic and copies ran while one was open for 37% -> 38% of each run, Pallas kernels for 9% -> 10%
where the time goes in v7:
time: 590 us; the launch traced here: 578 us
  waiting for transfers between devices  128 us (22%)
  matrix products  117 us (20%)
  local copies, waits for them, and re-layouts  95.5 us (16%)
  Pallas kernels  78.2 us (13%)
  blocking collectives  59.2 us (10%)
  other arithmetic  55.8 us (9%)
  starting transfers between devices  28.4 us (5%)
  between operations  14.9 us (3%)
    pallas_call x2, Pallas kernels, exchange(): pl.pallas_call(functools.partial(_exchange_kernel, sizes, group, gather,...  78.2 us
    all_gather x3, blocking collectives, local(): parts = [lax.all_gather(p, 'batch', axis=0) for p in parts]  54.1 us
    reduce_scatter x3, waiting for transfers between devices, reduce_seq_batch(): return lax.psum_scatter(g, 'batch', scatter_dimension=split_dim, tiled=True)  44.3 us
    all_to_all x2, waiting for transfers between devices, to_positions(): x = lax.all_to_all(x, 'ch', 0, 0, tiled=True)  30 us
    dot_general x1, matrix products, local(): jnp.einsum('dh,rhl->rdl', w_in, grad_inner, preferred_element_type=jnp.fl...  19.5 us
    unnamed x53, local copies, waits for them, and re-layouts  17.7 us
    all_to_all x2, waiting for transfers between devices, to_channels(): x = lax.all_to_all(x, 'ch', 0, 0, tiled=True)  17.2 us
    dot_general x1, matrix products, local(): jnp.einsum('dh,rdl->rhl', w_in, hidden0, preferred_element_type=jnp.float32)  16.8 us
  transfers between devices with their start and end apart: 21, of which 8 were waited for; matrix products, arithmetic and copies ran while one was open for 38% of the time, Pallas kernels for 10%

profile of v7, /device:TPU:0, one launch (start us, length us, event | category | flops | bytes accessed | tf_op | source)
XLA Modules:
  0.0 577.8 jit_solution(12967448530082663875)
XLA Ops:
  12.1 23.3 %shard_map.254 = (f32[4,1920]{1,0:T(4,128)}, bf16[4,160,640]{2,1,0:T(8,128)(2,1)}, bf16[4,80,1280]{2,1,0:T(8,128)(2,1)}) custom-call(f32[1920]{0:T(1024)} %concatenate.43.refs_0_, bf16[160,640]{1,0:T(8,128)(2,1)} %constant_dynamic-slice_fusion.2.refs_1_, bf16[80,1280]{1,0:T(8,128)(2,1)} %constant_dynamic-slice_fusion.1.refs_2_), custom_call_target="tpu_custom_call" | custom-call | bytes 3338240 | tf_op jit(solution)/shard_map/pallas_call | solution.py:87
  37.0 4.7 all-to-all-start
  48.1 30.0 %all-to-all-done = bf16[4,320,1024]{2,1,0:T(8,128)(2,1)} async-done(((bf16[4,320,1024]{2,1,0:T(8,128)(2,1)}), bf16[4,320,1024]{2,1,0:T(8,128)(2,1)}, u32[]{:S(2)}, u32[]{:S(2)}) %all-to-all-start) | async-done | bytes 2621472 | tf_op jit(solution)/shard_map/all_to_all | solution.py:172
  78.1 4.6 all-to-all-start.2
  82.8 2.5 convert_reduce_fusion
  85.3 2.5 multiply_reduce_fusion.2
  87.8 4.7 convert_element_type.149
  92.4 16.8 %fusion.83 = (f32[1024]{0:T(1024)S(1)}, f32[1024,640]{1,0:T(8,128)S(1)}) fusion(f32[640]{0:T(1024)S(1)} %add.202, bf16[1280,640]{1,0:T(8,128)(2,1)} %bitcast.267, f32[1280]{0:T(1024)S(1)} %add.199, f32[1280]{0:T(1024)S(1)} %mul.438, f32[1024]{0:T(1024)S(1)} %add_rsqrt_fusion.2, f32[1,1280,1,1,1,1,1024]{6,1,5,4,3,2,0:T(8,128)} %bitcast.256, ...), kind=kOutput, calls=%fused_computation.159 | convolution fusion | flops 1769470976 | bytes 9527808 | tf_op jit(solution)/shard_map/dh,rdl->rhl/dot_general | solution.py:261
  109.8 12.2 %all-gather.15.cloned.1.call-done = bf16[20,80,640]{2,1,0:T(8,128)(2,1)} async-done(((bf16[5,80,640]{2,1,0:T(8,128)(2,1)}), bf16[20,80,640]{2,1,0:T(8,128)(2,1)}) %all-gather.15.cloned.1.call-update) | async-done | bytes 2048016 | tf_op jit(solution)/shard_map/all_gather | solution.py:235
  122.0 7.3 %multiply_convert_fusion.1 = bf16[1,640,1024]{1,2,0:T(8,128)(2,1)S(1)} fusion(f32[640]{0:T(1024)S(1)} %add.206, f32[640]{0:T(1024)S(1)} %mul.448, f32[1024]{0:T(1024)S(1)} %add_rsqrt_fusion.1, f32[1024]{0:T(1024)S(1)} %broadcast_multiply_fusion.5, f32[640]{0:T(1024)S(1)} %add.202, f32[1024,640]{1,0:T(8,128)S(1)} %get-tuple-element.119), kind=kLoop, calls=%fused_computation.141 | loop fusion | flops 45875200 | bytes 3948032 | tf_op jit(solution)/shard_map/convert_element_type | solution.py:263
  135.7 8.0 %constant_dynamic-update-slice_fusion = bf16[1,3200,1024]{1,2,0:T(8,128)(2,1)} fusion(bf16[1,3200,1024]{1,2,0:T(8,128)(2,1)} %fusion.110, f32[640]{0:T(1024)S(1)} %add.206, f32[640]{0:T(1024)S(1)} %mul.448, f32[1024]{0:T(1024)S(1)} %add_rsqrt_fusion.1, f32[1024]{0:T(1024)S(1)} %broadcast_multiply_fusion.5, f32[640]{0:T(1024)S(1)} %add.202, ...), kind=kLoop, calls=%fused_computation.210 | loop fusion | flops 45875200 | bytes 3948032
  146.6 2.6 copy.64
  149.3 9.6 %fusion.85 = (f32[1024]{0:T(1024)S(1)}, f32[1024,640]{1,0:T(8,128)S(1)}) fusion(f32[640]{0:T(1024)S(1)} %add.209, bf16[3200,640]{1,0:T(8,128)(2,1)S(1)} %bitcast.258, bf16[1,3200,1024]{1,2,0:T(8,128)(2,1)} %fusion.108), kind=kOutput, calls=%fused_computation.161 | convolution fusion | flops 4195613696 | bytes 13277696 | tf_op jit(solution)/shard_map/co,rcl->rol/dot_general | solution.py:267
  159.5 11.8 %fusion.177 = f32[640,1280]{1,0:T(8,128)} fusion(bf16[1280,1024]{1,0:T(8,128)(2,1)} %bitcast.20, f32[640]{0:T(1024)S(1)} %add.213, f32[640]{0:T(1024)S(1)} %mul.458, f32[1024]{0:T(1024)S(1)} %add_rsqrt_fusion, f32[1024]{0:T(1024)S(1)} %broadcast_multiply_fusion.4, f32[640]{0:T(1024)S(1)} %add.209, f32[1024,640]{1,0:T(8,128)S(1)} %get-tuple-element.121), kind=kOutput, calls=%fused_computation.300 | convolution fusion | flops 1723596800 | bytes 8535552 | tf_op jit(solution)/shard_map/rhl,rdl->hd/dot_general | solution.py:274
  171.3 4.5 reshape.1435
  177.5 9.5 %copy.74 = bf16[1,3200,1024]{2,1,0:T(8,128)(2,1)} copy(bf16[1,3200,1024]{1,2,0:T(8,128)(2,1)} %fusion.108) | data formatting | bytes 13107200 | tf_op jit(solution)/shard_map/concatenate | solution.py:164
  187.2 12.5 %all-gather.11.cloned.1.call-done = bf16[4,160,1280]{2,1,0:T(8,128)(2,1)} async-done(((bf16[4,80,1280]{2,1,0:T(8,128)(2,1)}), bf16[4,160,1280]{2,1,0:T(8,128)(2,1)}) %all-gather.11.cloned.1.call-update) | async-done | bytes 1638416 | tf_op jit(solution)/shard_map/all_gather | solution.py:245
  199.7 11.7 %fusion.60 = (f32[640]{0:T(1024)S(1)}, f32[1024]{0:T(1024)S(1)}, f32[1024]{0:T(1024)S(1)}, f32[640]{0:T(1024)S(1)}, f32[1,640,1024]{1,2,0:T(8,128)S(1)}) fusion(f32[1024]{0:T(1024)S(1)} %add_rsqrt_fusion, f32[1024]{0:T(1024)S(1)} %broadcast_multiply_fusion.4, f32[640]{0:T(1024)S(1)} %add.209, f32[1024,640]{1,0:T(8,128)S(1)} %get-tuple-element.121, ...), kind=kOutput, calls=%fused_computation.110 | convolution fusion | flops 1732113152 | bytes 9531904 | tf_op jit(solution)/shard_map/hd,rdl->rhl/dot_general | solution.py:282
  211.4 2.6 convert_reduce_fusion.1
  215.1 7.1 %fusion.111 = f32[640,25,128]{2,0,1:T(8,128)} fusion(bf16[25,128,1024]{2,1,0:T(8,128)(2,1)S(1)} %bitcast.261, bf16[1,640,1024]{1,2,0:T(8,128)(2,1)S(1)} %get-tuple-element.93), kind=kOutput, calls=%fused_computation.199 | convolution fusion | flops 4194304000 | bytes 16056320 | tf_op jit(solution)/shard_map/rol,rkcil->okci/dot_general | solution.py:288
  222.2 17.3 %reduce-scatter.9.cloned.1.call-done.refs_0_ = f32[4,200,128]{2,1,0:T(8,128)} async-done(((f32[4,800,128]{2,1,0:T(8,128)}), f32[4,200,128]{2,1,0:T(8,128)}) %reduce-scatter.9.cloned.1.call-update) | async-done | bytes 409616 | tf_op jit(solution)/shard_map/reduce_scatter | solution.py:279
  243.0 6.4 %copy.65 = f32[1,1280,1024]{1,2,0:T(8,128)} copy(f32[1,1280,1024]{2,1,0:T(8,128)} %bitcast.257) | data formatting | bytes 10485760 | tf_op jit(solution)/shard_map/convert_element_type | solution.py:258
  249.4 8.3 %copy.70 = bf16[5,640,640]{2,1,0:T(8,128)(2,1)} copy(bf16[5,640,640]{1,2,0:T(8,128)(2,1)} %bitcast.259) | data formatting | bytes 8192000 | tf_op jit(solution)/shard_map/transpose | solution.py:296
  257.9 2.8 collective-permute-start.5
  264.5 13.6 %fusion.66 = (f32[640]{0:T(1024)S(1)}, f32[1024]{0:T(1024)S(1)}, f32[1024]{0:T(1024)S(1)}, f32[640]{0:T(1024)S(1)}, f32[1,640,1024]{1,2,0:T(8,128)}) fusion(f32[1024]{0:T(1024)S(1)} %add_rsqrt_fusion.1, f32[1024]{0:T(1024)S(1)} %broadcast_multiply_fusion.5, f32[640]{0:T(1024)S(1)} %add.202, f32[1024,640]{1,0:T(8,128)S(1)} %copy-done.3, f32[640]{0:T(1024)S(1)} %mul.448, ...), kind=kOutput, calls=%fused_computation.121 | convolution fusion | flops 4248695808 | bytes 15921664 | tf_op jit(solution)/shard_map/oc,rol->rcl/dot_general | solution.py:297
  283.6 19.5 %multiply_reduce_fusion = (f32[1280]{0:T(1024)S(1)}, f32[1024]{0:T(1024)S(1)}, f32[1024]{0:T(1024)S(1)}, f32[1280]{0:T(1024)S(1)}, f32[1,1280,1024]{1,2,0:T(8,128)}) fusion(f32[1,1280,1024]{1,2,0:T(8,128)} %copy.65, f32[1024]{0:T(1024)S(1)} %broadcast_multiply_fusion.8, f32[1024]{0:T(1024)S(1)} %add_rsqrt_fusion.2, f32[1280]{0:T(1024)S(1)} %mul.438, ...), kind=kOutput, calls=%fused_computation.25 | convolution fusion | flops 1785196032 | bytes 13471744 | tf_op jit(solution)/shard_map/dh,rhl->rdl/dot_general | solution.py:305
  303.6 15.3 %fusion.79 = f32[4,320,640]{2,1,0:T(8,128)S(1)} fusion(bf16[4,320,1024]{2,1,0:T(8,128)(2,1)} %all-to-all-done, f32[4,320]{1,0:T(4,128)S(1)} %copy-done.23, f32[4,320]{1,0:T(4,128)S(1)} %copy-done.21, f32[1024]{0:T(1024)S(1)} %add_rsqrt_fusion.2, f32[1024]{0:T(1024)S(1)} %broadcast_multiply_fusion.8, bf16[1,640,1024]{1,2,0:T(8,128)(2,1)S(1)} %copy-done.12), kind=kOutput, calls=%fused_computation.155 | convolution fusion | flops 1769472000 | bytes 7227392 | tf_op jit(solution)/shard_map/rdl,rhl->dh/dot_general | solution.py:304
  321.1 4.7 reshape.1446
  325.8 27.0 %reduce-scatter.13.cloned.1.call-done = f32[80,25,128]{2,0,1:T(8,128)} async-done(((f32[320,25,128]{2,0,1:T(8,128)}), f32[80,25,128]{2,0,1:T(8,128)}) %reduce-scatter.13.cloned.1.call-update) | async-done | bytes 1024016 | tf_op jit(solution)/shard_map/reduce_scatter | solution.py:279
  357.6 11.8 %reduce-scatter.15.cloned.1.call-done = f32[4,960,128]{2,1,0:T(8,128)} async-done(((f32[4,1920,128]{2,1,0:T(8,128)}), f32[4,960,128]{2,1,0:T(8,128)}) %reduce-scatter.15.cloned.1.call-update) | async-done | bytes 1966096 | tf_op jit(solution)/shard_map/reduce_scatter | solution.py:278
  369.4 12.0 %fusion.15 = bf16[1,1280,1024]{1,2,0:T(8,128)(2,1)} fusion(f32[1,1280,1024]{1,2,0:T(8,128)} %copy.65, bf16[640,1280]{1,0:T(8,128)(2,1)} %bitcast.270, f32[1280]{0:T(1024)S(1)} %add.217, f32[640]{0:T(1024)S(1)} %add.213, f32[640]{0:T(1024)S(1)} %mul.458, f32[1024]{0:T(1024)S(1)} %add_rsqrt_fusion, f32[1024]{0:T(1024)S(1)} %broadcast_multiply_fusion.4, ...), kind=kOutput, calls=%fused_computation.19 | convolution fusion | flops 1727528960 | bytes 12145152 | tf_op jit(solution)/shard_map/hd,rhl->rdl/dot_general | solution.py:270
  381.4 4.4 copy.66
  385.7 4.6 all-to-all-start.1
  390.3 4.9 copy.71
  395.2 6.5 %add_convert_fusion = bf16[1,1280,1024]{1,2,0:T(8,128)(2,1)S(1)} fusion(f32[1,1280,1024]{1,2,0:T(8,128)} %copy.71, f32[1,1280,1024]{1,2,0:T(8,128)} %get-tuple-element.124, f32[1,1280,1024]{1,2,0:T(8,128)} %copy.65, f32[1024]{0:T(1024)S(1)} %broadcast_multiply_fusion.6, f32[1024]{0:T(1024)S(1)} %broadcast_multiply_fusion.7, f32[1280]{0:T(1024)S(1)} %mul.438, ...), kind=kLoop, calls=%fused_computation.40 | loop fusion | flops 11796480 | bytes 18371584 | tf_op jit(solution)/shard_map/convert_element_type | solution.py:309
  401.7 2.6 copy.72
  404.4 17.2 %all-to-all-done.1 = bf16[4,320,1024]{2,1,0:T(8,128)(2,1)} async-done(((bf16[4,320,1024]{2,1,0:T(8,128)(2,1)}), bf16[4,320,1024]{2,1,0:T(8,128)(2,1)}, u32[]{:S(2)}, u32[]{:S(2)}) %all-to-all-start.1) | async-done | bytes 2621472 | tf_op jit(solution)/shard_map/all_to_all | solution.py:185
  421.6 3.7 all-to-all-start.3
  425.3 2.6 dynamic-slice_reduce_fusion
  428.2 55.0 %shard_map.255 = (f32[3,200,128]{2,1,0:T(8,128)}, f32[80,5,3,160]{3,2,1,0:T(4,128)}, f32[3,240,128]{2,1,0:T(8,128)}) custom-call(f32[4,200,128]{2,1,0:T(8,128)} %reduce-scatter.9.cloned.1.call-done.refs_0_, f32[80,5,4,160]{3,2,1,0:T(4,128)} %reshape.1448.refs_1_, f32[4,240,128]{2,1,0:T(8,128)} %reduce-scatter.17.cloned.1.call-done.refs_2_), custom_call_target="tpu_custom_call" | custom-call | bytes 3850240 | tf_op jit(solution)/shard_map/pallas_call | solution.py:87
  483.2 2.4 reduce_sum.245
  487.7 23.1 %all_gather.42 = f32[4,500,128]{2,1,0:T(8,128)} all-gather(f32[1,500,128]{2,1,0:T(8,128)S(1)} %add.226), channel_id=1, replica_groups=mesh['batch'=4,'seq'=2,'ch'=4] {'batch'}, dimensions={0}, use_global_device_ids=true | all-gather | bytes 1280000 | tf_op jit(solution)/shard_map/all_gather | solution.py:341
  511.9 15.7 %all_gather.40 = f32[4,240,128]{2,1,0:T(8,128)S(1)} all-gather(f32[1,240,128]{2,1,0:T(8,128)S(1)} %bitcast_add_fusion.3), channel_id=1, replica_groups=mesh['batch'=4,'seq'=2,'ch'=4] {'batch'}, dimensions={0}, use_global_device_ids=true | all-gather | bytes 614400 | tf_op jit(solution)/shard_map/all_gather | solution.py:341
  527.6 2.8 all_gather.41
  535.7 15.4 %all_gather.44 = f32[4,200,128]{2,1,0:T(8,128)S(1)} all-gather(f32[1,200,128]{2,1,0:T(8,128)S(1)} %bitcast_add_fusion.4), channel_id=1, replica_groups=mesh['batch'=4,'seq'=2,'ch'=4] {'batch'}, dimensions={0}, use_global_device_ids=true | all-gather | bytes 512000 | tf_op jit(solution)/shard_map/all_gather | solution.py:341
  555.8 4.8 reshape_reshape.7
  560.6 5.1 copy.77
  565.7 3.6 copy.99
  (169 shorter events, 61.7 us)
Async XLA Ops:
  7.2 38.5 %copy-start = (bf16[5,160,640]{2,1,0:T(8,128)(2,1)S(1)}, bf16[5,160,640]{2,1,0:T(8,128)(2,1)}, u32[]{:S(2)}) copy-start(bf16[5,160,640]{2,1,0:T(8,128)(2,1)} %param.23) | copy-start | bytes 3072004
  7.2 85.2 %all-gather.7.cloned.1.call-start = ((), (), s32[]{:S(2)}) async-start(), calls=%async_computation.10 | async-start | bytes 2457600 | tf_op jit(solution)/shard_map/all_gather | solution.py:243
  37.0 9.6 %copy-start.17 = (f32[1920]{0:T(1024)S(1)}, f32[1920]{0:T(1024)}, u32[]{:S(2)}) copy-start(f32[1920]{0:T(1024)} %concatenate.43.refs_0_) | copy-start | bytes 23044
  37.0 9.6 %copy-start.18 = (f32[4,1920]{1,0:T(4,128)S(1)}, f32[4,1920]{1,0:T(4,128)}, u32[]{:S(2)}) copy-start(f32[4,1920]{1,0:T(4,128)} %get-tuple-element.23) | copy-start | bytes 92164
  37.0 41.1 %all-to-all-start = ((bf16[4,320,1024]{2,1,0:T(8,128)(2,1)}), bf16[4,320,1024]{2,1,0:T(8,128)(2,1)}, u32[]{:S(2)}, u32[]{:S(2)}) async-start(bf16[4,320,1024]{2,1,0:T(8,128)(2,1)} %param.15), calls=%async_computation | async-start | bytes 5242880 | tf_op jit(solution)/shard_map/all_to_all | solution.py:172
  41.7 80.3 %all-gather.15.cloned.1.call-start = ((), (), s32[]{:S(2)}) async-start(), calls=%async_computation.20 | async-start | bytes 2560000 | tf_op jit(solution)/shard_map/all_gather | solution.py:235
  42.6 88.8 %collective-permute-start = (s32[1,64]{1,0:T(1,128)S(1)}, s32[1,64]{1,0:T(1,128)S(1)}, u32[]{:S(2)}, u32[]{:S(2)}) collective-permute-start(s32[1,64]{1,0:T(1,128)S(1)} %get-tuple-element.116), channel_id=1, source_target_pairs={{0,4},{1,5},{2,6},{3,7},{8,12},{9,13},{10,14},{11,15},{16,20},{17,... | collective-permute-start | bytes 776 | tf_op jit(solution)/shard_map/ppermute | solution.py:151
  44.4 86.9 %collective-permute-start.2 = (s32[1,64]{1,0:T(1,128)S(1)}, s32[1,64]{1,0:T(1,128)S(1)}, u32[]{:S(2)}, u32[]{:S(2)}) collective-permute-start(s32[1,64]{1,0:T(1,128)S(1)} %get-tuple-element.117), channel_id=1, source_target_pairs={{4,0},{5,1},{6,2},{7,3},{12,8},{13,9},{14,10},{15,11},{20,16},{21,... | collective-permute-start | bytes 776 | tf_op jit(solution)/shard_map/ppermute | solution.py:152
  48.0 30.2 %copy-start.20 = (f32[4,320]{1,0:T(4,128)}, f32[4,320]{1,0:T(4,128)S(1)}, u32[]{:S(2)}) copy-start(f32[4,320]{1,0:T(4,128)S(1)} %get-tuple-element.104) | copy-start | bytes 15364
  48.0 30.2 %copy-start.22 = (f32[4,320]{1,0:T(4,128)}, f32[4,320]{1,0:T(4,128)S(1)}, u32[]{:S(2)}) copy-start(f32[4,320]{1,0:T(4,128)S(1)} %get-tuple-element.106) | copy-start | bytes 15364
  78.1 81.4 %all-to-all-start.2 = ((bf16[4,320,1024]{2,1,0:T(8,128)(2,1)}), bf16[4,320,1024]{2,1,0:T(8,128)(2,1)}, u32[]{:S(2)}, u32[]{:S(2)}) async-start(bf16[4,320,1024]{2,1,0:T(8,128)(2,1)} %param.29), calls=%async_computation.2 | async-start | bytes 5242880 | tf_op jit(solution)/shard_map/all_to_all | solution.py:172
  82.7 63.9 %all-gather.9.cloned.1.call-start = ((), (), s32[]{:S(2)}) async-start(), calls=%async_computation.11 | async-start | bytes 6144000 | tf_op jit(solution)/shard_map/all_gather | solution.py:244
  109.2 26.5 %copy-start.2 = (f32[1024,640]{1,0:T(8,128)}, f32[1024,640]{1,0:T(8,128)S(1)}, u32[]{:S(2)}) copy-start(f32[1024,640]{1,0:T(8,128)S(1)} %get-tuple-element.119) | copy-start | bytes 7864324
  122.0 65.1 %reduce-scatter.7.cloned.1.call-start = ((), (), s32[]{:S(2)}) async-start(), calls=%async_computation.13 | async-start | bytes 4915200 | tf_op jit(solution)/shard_map/reduce_scatter | solution.py:278
  129.3 3.4 collective-permute-start.1
  131.5 12.3 %collective-permute-start.3 = (bf16[1,640,64]{1,2,0:T(8,128)(2,1)S(1)}, bf16[1,640,64]{1,2,0:T(8,128)(2,1)S(1)}, u32[]{:S(2)}, u32[]{:S(2)}) collective-permute-start(bf16[1,640,64]{1,2,0:T(8,128)(2,1)S(1)} %get-tuple-element.96), channel_id=1, source_target_pairs={{4,0},{5,1},{6,2},{7,3},{12,8},{13,9},{14,10},{15,11},{20,16},{21,... | collective-permute-start | bytes 245768 | tf_op jit(solution)/shard_map/ppermute | solution.py:152
  149.3 9.6 %copy-start.5 = (bf16[5,4,160,640]{3,2,1,0:T(8,128)(2,1)}, bf16[5,4,160,640]{3,2,1,0:T(8,128)(2,1)S(1)}, u32[]{:S(2)}) copy-start(bf16[5,4,160,640]{3,2,1,0:T(8,128)(2,1)S(1)} %copy.64) | copy-start | bytes 12288004
  158.9 40.8 %copy-start.6 = (f32[1024,640]{1,0:T(8,128)}, f32[1024,640]{1,0:T(8,128)S(1)}, u32[]{:S(2)}) copy-start(f32[1024,640]{1,0:T(8,128)S(1)} %get-tuple-element.121) | copy-start | bytes 7864324
  175.8 1.0 copy-start.14
  175.8 23.9 %all-gather.11.cloned.1.call-start = ((), (), s32[]{:S(2)}) async-start(), calls=%async_computation.12 | async-start | bytes 2457600 | tf_op jit(solution)/shard_map/all_gather | solution.py:245
  177.5 62.0 %reduce-scatter.9.cloned.1.call-start = ((), (), s32[]{:S(2)}) async-start(), calls=%async_computation.14 | async-start | bytes 2048000 | tf_op jit(solution)/shard_map/reduce_scatter | solution.py:279
  187.1 91.1 %reduce-scatter.11.cloned.1.call-start = ((), (), s32[]{:S(2)}) async-start(), calls=%async_computation.15 | async-start | bytes 12288000 | tf_op jit(solution)/shard_map/reduce_scatter | solution.py:278
  211.4 3.6 copy-start.10
  239.5 113.4 %reduce-scatter.13.cloned.1.call-start = ((), (), s32[]{:S(2)}) async-start(), calls=%async_computation.16 | async-start | bytes 5120000 | tf_op jit(solution)/shard_map/reduce_scatter | solution.py:279
  239.5 21.1 %collective-permute-start.4 = (bf16[1,640,64]{1,2,0:T(8,128)(2,1)S(1)}, bf16[1,640,64]{1,2,0:T(8,128)(2,1)S(1)}, u32[]{:S(2)}, u32[]{:S(2)}) collective-permute-start(bf16[1,640,64]{1,2,0:T(8,128)(2,1)S(1)} %get-tuple-element.95), channel_id=1, source_target_pairs={{4,0},{5,1},{6,2},{7,3},{12,8},{13,9},{14,10},{15,11},{20,16},{21,... | collective-permute-start | bytes 245768 | tf_op jit(solution)/shard_map/ppermute | solution.py:152
  257.9 3.8 collective-permute-start.5
  261.4 2.2 copy-start.13
  261.7 2.8 copy-start.3
  278.1 1.7 copy-start.4
  278.3 91.1 %reduce-scatter.15.cloned.1.call-start = ((), (), s32[]{:S(2)}) async-start(), calls=%async_computation.17 | async-start | bytes 5898240 | tf_op jit(solution)/shard_map/reduce_scatter | solution.py:278
  282.2 1.1 copy-start.11
  283.6 20.0 %copy-start.12 = (bf16[1,640,1024]{1,2,0:T(8,128)(2,1)S(1)}, bf16[1,640,1024]{1,2,0:T(8,128)(2,1)}, u32[]{:S(2)}) copy-start(bf16[1,640,1024]{1,2,0:T(8,128)(2,1)} %copy-done.11) | copy-start | bytes 3932164
  283.6 20.0 %copy-start.21 = (f32[4,320]{1,0:T(4,128)S(1)}, f32[4,320]{1,0:T(4,128)}, u32[]{:S(2)}) copy-start(f32[4,320]{1,0:T(4,128)} %copy-done.20) | copy-start | bytes 15364
  283.6 20.0 %copy-start.23 = (f32[4,320]{1,0:T(4,128)S(1)}, f32[4,320]{1,0:T(4,128)}, u32[]{:S(2)}) copy-start(f32[4,320]{1,0:T(4,128)} %copy-done.22) | copy-start | bytes 15364
  356.8 0.7 copy-start.19
  356.8 12.6 %copy-start.7 = (f32[1024,640]{1,0:T(8,128)S(1)}, f32[1024,640]{1,0:T(8,128)}, u32[]{:S(2)}) copy-start(f32[1024,640]{1,0:T(8,128)} %copy-done.6) | copy-start | bytes 7864324
  356.8 71.4 %reduce-scatter.17.cloned.1.call-start = ((), (), s32[]{:S(2)}) async-start(), calls=%async_computation.18 | async-start | bytes 2457600 | tf_op jit(solution)/shard_map/reduce_scatter | solution.py:279
  385.7 35.9 %all-to-all-start.1 = ((bf16[4,320,1024]{2,1,0:T(8,128)(2,1)}), bf16[4,320,1024]{2,1,0:T(8,128)(2,1)}, u32[]{:S(2)}, u32[]{:S(2)}) async-start(bf16[4,320,1024]{2,1,0:T(8,128)(2,1)} %bitcast.18), calls=%async_computation.1 | async-start | bytes 5242880 | tf_op jit(solution)/shard_map/all_to_all | solution.py:185
  421.6 89.2 %all-to-all-start.3 = ((bf16[4,320,1024]{2,1,0:T(8,128)(2,1)}), bf16[4,320,1024]{2,1,0:T(8,128)(2,1)S(1)}, u32[]{:S(2)}, u32[]{:S(2)}) async-start(bf16[4,320,1024]{2,1,0:T(8,128)(2,1)} %bitcast.260), calls=%async_computation.5 | async-start | bytes 5242880 | tf_op jit(solution)/shard_map/all_to_all | solution.py:185
  425.3 130.6 %all-gather.13.cloned.1.call-start = ((), (), s32[]{:S(2)}) async-start(), calls=%async_computation.19 | async-start | bytes 3096576 | tf_op jit(solution)/shard_map/all_gather | solution.py:343
  486.6 24.1 %copy-start.15 = (f32[3,240,128]{2,1,0:T(8,128)S(1)}, f32[3,240,128]{2,1,0:T(8,128)}, u32[]{:S(2)}) copy-start(f32[3,240,128]{2,1,0:T(8,128)} %get-tuple-element.29) | copy-start | bytes 1105924
  510.8 24.0 %copy-start.8 = (bf16[4,320,1024]{2,1,0:T(8,128)(2,1)}, bf16[4,320,1024]{2,1,0:T(8,128)(2,1)S(1)}, u32[]{:S(2)}) copy-start(bf16[4,320,1024]{2,1,0:T(8,128)(2,1)S(1)} %all-to-all-done.3) | copy-start | bytes 7864324
  527.6 7.2 %copy-start.16 = (f32[3,200,128]{2,1,0:T(8,128)S(1)}, f32[3,200,128]{2,1,0:T(8,128)}, u32[]{:S(2)}) copy-start(f32[3,200,128]{2,1,0:T(8,128)} %get-tuple-element.31) | copy-start | bytes 921604
  532.7 21.8 %slice-start = ((f32[384,640]{1,0:T(8,128)}), f32[3,640]{1,0:T(4,128)S(1)}, s32[]{:S(2)}) async-start(f32[384,640]{1,0:T(8,128)} %reshape.1449), calls=%async_computation.21 | async-start | bytes 20480 | tf_op jit(solution)/shard_map/slice | solution.py:350
  565.7 3.6 copy-start.9
  565.7 5.1 copy-start.1
Sparse Core Ops, SparseCore 0:
  37.1 11.0 all-gather.6
  50.6 71.3 all-gather.14
  123.5 12.9 all-gather.8
  175.9 11.1 reduce-scatter.6
  188.6 11.0 all-gather.10
  201.9 37.4 reduce-scatter.8
  241.8 15.6 reduce-scatter.10
  278.4 74.4 reduce-scatter.12
  356.9 12.3 reduce-scatter.14
  371.6 42.5 reduce-scatter.16
  510.9 8.2 all-gather.12

commit v8 on v7

--- a/solution.py
+++ b/solution.py
@@ -52,7 +52,7 @@
         peer = lax.rem(me + j, count)
         for i in range(count_arrays):
             lead = (slice(None),) * axes[i]
-            if gather:
+            if gather[i]:
                 src, dst = x_refs[i], o_refs[i].at[me]
             else:
                 slot = (j - 1) if reduce else me
@@ -76,14 +76,17 @@
     sizes = {a: lax.axis_size(a) for a in MESH_AXES}
     count = math.prod(sizes[a] for a in group)
     axes = tuple(axes or (0,) * len(xs))
+    if isinstance(gather, bool):
+        gather = (gather,) * len(xs)
+    gather = tuple(gather)
     if count == 1:
-        return [x[None] if gather else x for x in xs]
-    shapes = [jax.ShapeDtypeStruct((count,) + x.shape if gather else x.shape, x.dtype) for x in xs]
+        return [x[None] if g else x for x, g in zip(xs, gather)]
+    shapes = [jax.ShapeDtypeStruct((count,) + x.shape if g else x.shape, x.dtype) for x, g in zip(xs, gather)]
     if reduce:
         shapes = [
             jax.ShapeDtypeStruct(x.shape[:a] + (count - 1,) + x.shape[a + 1 :], x.dtype) for x, a in zip(xs, axes)
         ]
-    moved = sum(x.size * x.dtype.itemsize * (count if gather else 1) for x in xs)
+    moved = sum(x.size * x.dtype.itemsize * (count if g else 1) for x, g in zip(xs, gather))
     outs = pl.pallas_call(
         functools.partial(_exchange_kernel, sizes, group, gather, reduce, axes),
         out_shape=shapes,
@@ -103,8 +106,8 @@
             own = lax.dynamic_index_in_dim(x, me, axis, keepdims=False)
             placed.append(own + jnp.sum(out, axis=axis))
         return placed
-    for x, out, axis in zip(xs, outs, axes):
-        own = x if gather else lax.dynamic_index_in_dim(x, me, axis, keepdims=False)
+    for x, out, axis, g in zip(xs, outs, axes, gather):
+        own = x if g else lax.dynamic_index_in_dim(x, me, axis, keepdims=False)
         placed.append(lax.dynamic_update_index_in_dim(out, own, me, axis))
     return placed
 
@@ -231,7 +234,14 @@
         lax.dynamic_slice_in_dim(w_conv, sidx * (hloc // seqs), hloc // seqs, 1),
         lax.dynamic_slice_in_dim(w_outer, sidx * (hloc // seqs), hloc // seqs, 0),
     ]
-    small_all, w_in, w_out = exchange([jnp.concatenate(smalls), halves[0], halves[2]], ("ch",), 0, gather=True)
+    if q_count == 1:
+        small_all, w_in, w_out, x = exchange(
+            [jnp.concatenate(smalls), halves[0], halves[2], inputs], ("ch",), 0, gather=(True, True, True, False)
+        )
+        x = _join(x, nch)
+    else:
+        small_all, w_in, w_out = exchange([jnp.concatenate(smalls), halves[0], halves[2]], ("ch",), 0, gather=True)
+        x = to_positions(inputs, nch, q_count)
     w_cv = lax.all_gather(halves[1], "ch", axis=0)
     cut = 0
     full = []
@@ -244,7 +254,6 @@
     w_cv = lax.all_gather(w_cv, "seq", axis=2, tiled=True).transpose(1, 0, 2, 3).reshape(KERNEL_TAPS, hid, hid)
     w_out = lax.all_gather(w_out, "seq", axis=1, tiled=True).reshape(hid, dim)
 
-    x = to_positions(inputs, nch, q_count)
     cot = to_positions(cotangent, nch, q_count)
     prow = x.shape[0]
     if q_count == 1:

time: 590 us -> 592 us (level)
  Pallas kernels: 78.2 us -> 106 us
  waiting for transfers between devices: 128 us -> 109 us
    all_to_all x2 -> x1, waiting for transfers between devices: 30 us -> 0.01 us  [to_positions(): x = lax.all_to_all(x, 'ch', 0, 0, tiled=True)]
    pallas_call x2, Pallas kernels: 78.2 us -> 106 us  [exchange(): pl.pallas_call(functools.partial(_exchange_kernel, sizes, group, gather,...]
    all_gather x1, waiting for transfers between devices: 12.2 us -> 23.2 us  [local(): w_cv = lax.all_gather(halves[1], 'ch', axis=0)]
    unnamed x53 -> x57, local copies, waits for them, and re-layouts: 17.7 us -> 17.9 us
  transfers between devices with their start and end apart: 21 -> 20, of which waited for: 8 -> 7; matrix products, arithmetic and copies ran while one was open for 38% -> 38% of each run, Pallas kernels for 10% -> 9%
where the time goes in v8:
time: 592 us; the launch traced here: 580 us
  matrix products  118 us (20%)
  waiting for transfers between devices  109 us (18%)
  Pallas kernels  106 us (18%)
  local copies, waits for them, and re-layouts  96.4 us (16%)
  blocking collectives  59.2 us (10%)
  other arithmetic  52.2 us (9%)
  starting transfers between devices  24.1 us (4%)
  between operations  14.7 us (2%)
    pallas_call x2, Pallas kernels, exchange(): pl.pallas_call(functools.partial(_exchange_kernel, sizes, group, gather,...  106 us
    all_gather x3, blocking collectives, local(): parts = [lax.all_gather(p, 'batch', axis=0) for p in parts]  54.1 us
    reduce_scatter x3, waiting for transfers between devices, reduce_seq_batch(): return lax.psum_scatter(g, 'batch', scatter_dimension=split_dim, tiled=True)  43.8 us
    all_gather x1, waiting for transfers between devices, local(): w_cv = lax.all_gather(halves[1], 'ch', axis=0)  23.2 us
    dot_general x1, matrix products, local(): jnp.einsum('dh,rhl->rdl', w_in, grad_inner, preferred_element_type=jnp.fl...  20 us
    unnamed x57, local copies, waits for them, and re-layouts  17.9 us
    all_to_all x2, waiting for transfers between devices, to_channels(): x = lax.all_to_all(x, 'ch', 0, 0, tiled=True)  17.2 us
    dot_general x1, matrix products, local(): jnp.einsum('dh,rdl->rhl', w_in, hidden0, preferred_element_type=jnp.float32)  17.1 us
  transfers between devices with their start and end apart: 20, of which 7 were waited for; matrix products, arithmetic and copies ran while one was open for 38% of the time, Pallas kernels for 9%

profile of v8, /device:TPU:0, one launch (start us, length us, event | category | flops | bytes accessed | tf_op | source)
XLA Modules:
  0.0 580.5 jit_solution(8512219140838165241)
XLA Ops:
  12.1 51.4 %shard_map.254 = (f32[4,1920]{1,0:T(4,128)}, bf16[4,160,640]{2,1,0:T(8,128)(2,1)}, bf16[4,80,1280]{2,1,0:T(8,128)(2,1)}, bf16[4,320,1024]{2,1,0:T(8,128)(2,1)}) custom-call(f32[1920]{0:T(1024)} %concatenate.42.refs_0_, bf16[160,640]{1,0:T(8,128)(2,1)} %constant_dynamic-slice_fusion.2.refs_1_, bf16[80,1280]{1,0:T(8,128)(2,1)} %constant_dynamic-slice_fusion.1.refs_2_, ...), custom_call_target="tpu_custom_call" | custom-call | bytes 8581120 | tf_op jit(solution)/shard_map/pallas_call | solution.py:90
  64.3 4.7 all-to-all-start.1
  79.3 2.9 convert_element_type.149
  83.7 17.1 %fusion.83 = (f32[1024]{0:T(1024)S(1)}, f32[1024,640]{1,0:T(8,128)S(1)}) fusion(f32[640]{0:T(1024)S(1)} %add.206, bf16[1280,640]{1,0:T(8,128)(2,1)} %bitcast.267, f32[1280]{0:T(1024)S(1)} %add.203, f32[1280]{0:T(1024)S(1)} %mul.438, f32[1024]{0:T(1024)S(1)} %add_rsqrt_fusion.2, f32[1,1280,1,1,1,1,1024]{6,1,5,4,3,2,0:T(8,128)} %bitcast.256, ...), kind=kOutput, calls=%fused_computation.159 | convolution fusion | flops 1769470976 | bytes 9527808 | tf_op jit(solution)/shard_map/dh,rdl->rhl/dot_general | solution.py:270
  101.3 23.2 %all-gather.15.cloned.1.call-done = bf16[20,80,640]{2,1,0:T(8,128)(2,1)} async-done(((bf16[5,80,640]{2,1,0:T(8,128)(2,1)}), bf16[20,80,640]{2,1,0:T(8,128)(2,1)}) %all-gather.15.cloned.1.call-update) | async-done | bytes 2048016 | tf_op jit(solution)/shard_map/all_gather | solution.py:245
  124.6 7.3 %multiply_convert_fusion.1 = bf16[1,640,1024]{1,2,0:T(8,128)(2,1)S(1)} fusion(f32[640]{0:T(1024)S(1)} %add.210, f32[640]{0:T(1024)S(1)} %mul.448, f32[1024]{0:T(1024)S(1)} %add_rsqrt_fusion.1, f32[1024]{0:T(1024)S(1)} %broadcast_multiply_fusion.5, f32[640]{0:T(1024)S(1)} %add.206, f32[1024,640]{1,0:T(8,128)S(1)} %get-tuple-element.121), kind=kLoop, calls=%fused_computation.141 | loop fusion | flops 45875200 | bytes 3948032 | tf_op jit(solution)/shard_map/convert_element_type | solution.py:272
  138.1 8.0 %constant_dynamic-update-slice_fusion = bf16[1,3200,1024]{1,2,0:T(8,128)(2,1)} fusion(bf16[1,3200,1024]{1,2,0:T(8,128)(2,1)} %fusion.110, f32[640]{0:T(1024)S(1)} %add.210, f32[640]{0:T(1024)S(1)} %mul.448, f32[1024]{0:T(1024)S(1)} %add_rsqrt_fusion.1, f32[1024]{0:T(1024)S(1)} %broadcast_multiply_fusion.5, f32[640]{0:T(1024)S(1)} %add.206, ...), kind=kLoop, calls=%fused_computation.211 | loop fusion | flops 45875200 | bytes 3948032
  149.0 2.6 copy.65
  151.6 9.6 %fusion.85 = (f32[1024]{0:T(1024)S(1)}, f32[1024,640]{1,0:T(8,128)S(1)}) fusion(f32[640]{0:T(1024)S(1)} %add.213, bf16[3200,640]{1,0:T(8,128)(2,1)S(1)} %bitcast.258, bf16[1,3200,1024]{1,2,0:T(8,128)(2,1)} %fusion.108), kind=kOutput, calls=%fused_computation.161 | convolution fusion | flops 4195613696 | bytes 13277696 | tf_op jit(solution)/shard_map/co,rcl->rol/dot_general | solution.py:276
  161.8 11.8 %fusion.177 = f32[640,1280]{1,0:T(8,128)} fusion(bf16[1280,1024]{1,0:T(8,128)(2,1)} %bitcast.20, f32[640]{0:T(1024)S(1)} %add.217, f32[640]{0:T(1024)S(1)} %mul.458, f32[1024]{0:T(1024)S(1)} %add_rsqrt_fusion, f32[1024]{0:T(1024)S(1)} %broadcast_multiply_fusion.4, f32[640]{0:T(1024)S(1)} %add.213, f32[1024,640]{1,0:T(8,128)S(1)} %get-tuple-element.123), kind=kOutput, calls=%fused_computation.301 | convolution fusion | flops 1723596800 | bytes 8535552 | tf_op jit(solution)/shard_map/rhl,rdl->hd/dot_general | solution.py:283
  173.6 4.5 reshape.1435
  179.9 9.4 %copy.75 = bf16[1,3200,1024]{2,1,0:T(8,128)(2,1)} copy(bf16[1,3200,1024]{1,2,0:T(8,128)(2,1)} %fusion.108) | data formatting | bytes 13107200 | tf_op jit(solution)/shard_map/concatenate | solution.py:167
  190.2 12.5 %all-gather.11.cloned.1.call-done = bf16[4,160,1280]{2,1,0:T(8,128)(2,1)} async-done(((bf16[4,80,1280]{2,1,0:T(8,128)(2,1)}), bf16[4,160,1280]{2,1,0:T(8,128)(2,1)}) %all-gather.11.cloned.1.call-update) | async-done | bytes 1638416 | tf_op jit(solution)/shard_map/all_gather | solution.py:255
  202.7 11.7 %fusion.60 = (f32[640]{0:T(1024)S(1)}, f32[1024]{0:T(1024)S(1)}, f32[1024]{0:T(1024)S(1)}, f32[640]{0:T(1024)S(1)}, f32[1,640,1024]{1,2,0:T(8,128)S(1)}) fusion(f32[1024]{0:T(1024)S(1)} %add_rsqrt_fusion, f32[1024]{0:T(1024)S(1)} %broadcast_multiply_fusion.4, f32[640]{0:T(1024)S(1)} %add.213, f32[1024,640]{1,0:T(8,128)S(1)} %get-tuple-element.123, ...), kind=kOutput, calls=%fused_computation.110 | convolution fusion | flops 1732113152 | bytes 9531904 | tf_op jit(solution)/shard_map/hd,rdl->rhl/dot_general | solution.py:291
  214.4 2.6 convert_reduce_fusion.1
  218.0 7.1 %fusion.111 = f32[640,25,128]{2,0,1:T(8,128)} fusion(bf16[25,128,1024]{2,1,0:T(8,128)(2,1)S(1)} %bitcast.261, bf16[1,640,1024]{1,2,0:T(8,128)(2,1)S(1)} %get-tuple-element.95), kind=kOutput, calls=%fused_computation.199 | convolution fusion | flops 4194304000 | bytes 16056320 | tf_op jit(solution)/shard_map/rol,rkcil->okci/dot_general | solution.py:297
  225.1 17.3 %reduce-scatter.9.cloned.1.call-done.refs_0_ = f32[4,200,128]{2,1,0:T(8,128)} async-done(((f32[4,800,128]{2,1,0:T(8,128)}), f32[4,200,128]{2,1,0:T(8,128)}) %reduce-scatter.9.cloned.1.call-update) | async-done | bytes 409616 | tf_op jit(solution)/shard_map/reduce_scatter | solution.py:288
  242.5 5.9 %copy.66 = f32[1,1280,1024]{1,2,0:T(8,128)} copy(f32[1,1280,1024]{2,1,0:T(8,128)} %bitcast.257) | data formatting | bytes 10485760 | tf_op jit(solution)/shard_map/convert_element_type | solution.py:267
  252.0 8.4 %copy.71 = bf16[5,640,640]{2,1,0:T(8,128)(2,1)} copy(bf16[5,640,640]{1,2,0:T(8,128)(2,1)} %bitcast.259) | data formatting | bytes 8192000 | tf_op jit(solution)/shard_map/transpose | solution.py:305
  260.6 3.0 collective-permute-start.5
  267.5 13.6 %fusion.66 = (f32[640]{0:T(1024)S(1)}, f32[1024]{0:T(1024)S(1)}, f32[1024]{0:T(1024)S(1)}, f32[640]{0:T(1024)S(1)}, f32[1,640,1024]{1,2,0:T(8,128)}) fusion(f32[1024]{0:T(1024)S(1)} %add_rsqrt_fusion.1, f32[1024]{0:T(1024)S(1)} %broadcast_multiply_fusion.5, f32[640]{0:T(1024)S(1)} %add.206, f32[1024,640]{1,0:T(8,128)S(1)} %copy-done.3, f32[640]{0:T(1024)S(1)} %mul.448, ...), kind=kOutput, calls=%fused_computation.121 | convolution fusion | flops 4248695808 | bytes 15921664 | tf_op jit(solution)/shard_map/oc,rol->rcl/dot_general | solution.py:306
  282.8 2.4 fusion.65
  286.6 20.0 %multiply_reduce_fusion = (f32[1280]{0:T(1024)S(1)}, f32[1024]{0:T(1024)S(1)}, f32[1024]{0:T(1024)S(1)}, f32[1280]{0:T(1024)S(1)}, f32[1,1280,1024]{1,2,0:T(8,128)}) fusion(f32[1,1280,1024]{1,2,0:T(8,128)} %copy.66, f32[1024]{0:T(1024)S(1)} %broadcast_multiply_fusion.8, f32[1024]{0:T(1024)S(1)} %add_rsqrt_fusion.2, f32[1280]{0:T(1024)S(1)} %mul.438, ...), kind=kOutput, calls=%fused_computation.25 | convolution fusion | flops 1785196032 | bytes 13471744 | tf_op jit(solution)/shard_map/dh,rhl->rdl/dot_general | solution.py:314
  307.0 15.5 %fusion.79 = f32[4,320,640]{2,1,0:T(8,128)S(1)} fusion(bf16[4,320,1024]{2,1,0:T(8,128)(2,1)S(1)} %copy-done.6, f32[4,320]{1,0:T(4,128)S(1)} %copy-done.25, f32[4,320]{1,0:T(4,128)S(1)} %copy-done.23, f32[1024]{0:T(1024)S(1)} %add_rsqrt_fusion.2, f32[1024]{0:T(1024)S(1)} %broadcast_multiply_fusion.8, bf16[1,640,1024]{1,2,0:T(8,128)(2,1)} %copy-done.13), kind=kOutput, calls=%fused_computation.155 | convolution fusion | flops 1769472000 | bytes 7227392 | tf_op jit(solution)/shard_map/rdl,rhl->dh/dot_general | solution.py:313
  324.8 4.7 reshape.1446
  329.5 26.5 %reduce-scatter.13.cloned.1.call-done = f32[80,25,128]{2,0,1:T(8,128)} async-done(((f32[320,25,128]{2,0,1:T(8,128)}), f32[80,25,128]{2,0,1:T(8,128)}) %reduce-scatter.13.cloned.1.call-update) | async-done | bytes 1024016 | tf_op jit(solution)/shard_map/reduce_scatter | solution.py:288
  357.5 2.4 reshape.1448.refs_1_
  360.7 11.7 %reduce-scatter.15.cloned.1.call-done = f32[4,960,128]{2,1,0:T(8,128)} async-done(((f32[4,1920,128]{2,1,0:T(8,128)}), f32[4,960,128]{2,1,0:T(8,128)}) %reduce-scatter.15.cloned.1.call-update) | async-done | bytes 1966096 | tf_op jit(solution)/shard_map/reduce_scatter | solution.py:287
  372.5 11.7 %fusion.15 = bf16[1,1280,1024]{1,2,0:T(8,128)(2,1)} fusion(f32[1,1280,1024]{1,2,0:T(8,128)} %copy.66, bf16[640,1280]{1,0:T(8,128)(2,1)} %bitcast.270, f32[1280]{0:T(1024)S(1)} %add.221, f32[640]{0:T(1024)S(1)} %add.217, f32[640]{0:T(1024)S(1)} %mul.458, f32[1024]{0:T(1024)S(1)} %add_rsqrt_fusion, f32[1024]{0:T(1024)S(1)} %broadcast_multiply_fusion.4, ...), kind=kOutput, calls=%fused_computation.19 | convolution fusion | flops 1727528960 | bytes 12145152 | tf_op jit(solution)/shard_map/hd,rhl->rdl/dot_general | solution.py:279
  384.2 4.4 copy.67
  388.6 4.6 all-to-all-start
  393.1 4.9 copy.72
  398.1 6.5 %add_convert_fusion = bf16[1,1280,1024]{1,2,0:T(8,128)(2,1)S(1)} fusion(f32[1,1280,1024]{1,2,0:T(8,128)} %copy.72, f32[1,1280,1024]{1,2,0:T(8,128)} %get-tuple-element.126, f32[1,1280,1024]{1,2,0:T(8,128)} %copy.66, f32[1024]{0:T(1024)S(1)} %broadcast_multiply_fusion.6, f32[1024]{0:T(1024)S(1)} %broadcast_multiply_fusion.7, f32[1280]{0:T(1024)S(1)} %mul.438, ...), kind=kLoop, calls=%fused_computation.40 | loop fusion | flops 11796480 | bytes 18371584 | tf_op jit(solution)/shard_map/convert_element_type | solution.py:318
  404.6 2.6 copy.73
  407.2 17.2 %all-to-all-done = bf16[4,320,1024]{2,1,0:T(8,128)(2,1)} async-done(((bf16[4,320,1024]{2,1,0:T(8,128)(2,1)}), bf16[4,320,1024]{2,1,0:T(8,128)(2,1)}, u32[]{:S(2)}, u32[]{:S(2)}) %all-to-all-start) | async-done | bytes 2621472 | tf_op jit(solution)/shard_map/all_to_all | solution.py:188
  424.4 3.7 all-to-all-start.2
  428.4 2.6 dynamic-slice_reduce_fusion
  431.3 54.8 %shard_map.255 = (f32[3,200,128]{2,1,0:T(8,128)}, f32[80,5,3,160]{3,2,1,0:T(4,128)}, f32[3,240,128]{2,1,0:T(8,128)}) custom-call(f32[4,200,128]{2,1,0:T(8,128)} %reduce-scatter.9.cloned.1.call-done.refs_0_, f32[80,5,4,160]{3,2,1,0:T(4,128)} %reshape.1448.refs_1_, f32[4,240,128]{2,1,0:T(8,128)} %reduce-scatter.17.cloned.1.call-done.refs_2_), custom_call_target="tpu_custom_call" | custom-call | bytes 3850240 | tf_op jit(solution)/shard_map/pallas_call | solution.py:90
  486.1 2.4 reduce_sum.245
  490.5 23.0 %all_gather.42 = f32[4,500,128]{2,1,0:T(8,128)} all-gather(f32[1,500,128]{2,1,0:T(8,128)S(1)} %add.230), channel_id=1, replica_groups=mesh['batch'=4,'seq'=2,'ch'=4] {'batch'}, dimensions={0}, use_global_device_ids=true | all-gather | bytes 1280000 | tf_op jit(solution)/shard_map/all_gather | solution.py:350
  514.7 15.7 %all_gather.40 = f32[4,240,128]{2,1,0:T(8,128)S(1)} all-gather(f32[1,240,128]{2,1,0:T(8,128)S(1)} %bitcast_add_fusion.3), channel_id=1, replica_groups=mesh['batch'=4,'seq'=2,'ch'=4] {'batch'}, dimensions={0}, use_global_device_ids=true | all-gather | bytes 614400 | tf_op jit(solution)/shard_map/all_gather | solution.py:350
  530.4 2.8 all_gather.41
  533.2 2.3 reshape.1449
  538.6 15.4 %all_gather.44 = f32[4,200,128]{2,1,0:T(8,128)S(1)} all-gather(f32[1,200,128]{2,1,0:T(8,128)S(1)} %bitcast_add_fusion.4), channel_id=1, replica_groups=mesh['batch'=4,'seq'=2,'ch'=4] {'batch'}, dimensions={0}, use_global_device_ids=true | all-gather | bytes 512000 | tf_op jit(solution)/shard_map/all_gather | solution.py:350
  553.9 2.4 all_gather.45
  558.7 4.8 reshape_reshape.7
  563.4 5.1 copy.78
  568.6 3.6 copy.101
  (172 shorter events, 57.3 us)
Async XLA Ops:
  7.2 65.8 %copy-start = (bf16[5,160,640]{2,1,0:T(8,128)(2,1)S(1)}, bf16[5,160,640]{2,1,0:T(8,128)(2,1)}, u32[]{:S(2)}) copy-start(bf16[5,160,640]{2,1,0:T(8,128)(2,1)} %param.23) | copy-start | bytes 3072004
  7.2 56.3 %copy-start.15 = (bf16[320,640]{1,0:T(8,128)(2,1)S(1)}, bf16[320,640]{1,0:T(8,128)(2,1)}, u32[]{:S(2)}) copy-start(bf16[320,640]{1,0:T(8,128)(2,1)} %param.19) | copy-start | bytes 1228804
  7.2 76.5 %all-gather.7.cloned.1.call-start = ((), (), s32[]{:S(2)}) async-start(), calls=%async_computation.9 | async-start | bytes 2457600 | tf_op jit(solution)/shard_map/all_gather | solution.py:253
  64.3 9.7 %copy-start.19 = (f32[1920]{0:T(1024)S(1)}, f32[1920]{0:T(1024)}, u32[]{:S(2)}) copy-start(f32[1920]{0:T(1024)} %concatenate.42.refs_0_) | copy-start | bytes 23044
  64.3 9.7 %copy-start.20 = (f32[4,1920]{1,0:T(4,128)S(1)}, f32[4,1920]{1,0:T(4,128)}, u32[]{:S(2)}) copy-start(f32[4,1920]{1,0:T(4,128)} %get-tuple-element.25) | copy-start | bytes 92164
  64.3 97.5 %all-to-all-start.1 = ((bf16[4,320,1024]{2,1,0:T(8,128)(2,1)}), bf16[4,320,1024]{2,1,0:T(8,128)(2,1)}, u32[]{:S(2)}, u32[]{:S(2)}) async-start(bf16[4,320,1024]{2,1,0:T(8,128)(2,1)} %param.29), calls=%async_computation.1 | async-start | bytes 5242880 | tf_op jit(solution)/shard_map/all_to_all | solution.py:175
  69.0 55.5 %all-gather.15.cloned.1.call-start = ((), (), s32[]{:S(2)}) async-start(), calls=%async_computation.19 | async-start | bytes 2560000 | tf_op jit(solution)/shard_map/all_gather | solution.py:245
  69.9 63.8 %collective-permute-start = (s32[1,64]{1,0:T(1,128)S(1)}, s32[1,64]{1,0:T(1,128)S(1)}, u32[]{:S(2)}, u32[]{:S(2)}) collective-permute-start(s32[1,64]{1,0:T(1,128)S(1)} %get-tuple-element.118), channel_id=1, source_target_pairs={{0,4},{1,5},{2,6},{3,7},{8,12},{9,13},{10,14},{11,15},{16,20},{17,... | collective-permute-start | bytes 776 | tf_op jit(solution)/shard_map/ppermute | solution.py:154
  71.7 61.9 %collective-permute-start.2 = (s32[1,64]{1,0:T(1,128)S(1)}, s32[1,64]{1,0:T(1,128)S(1)}, u32[]{:S(2)}, u32[]{:S(2)}) collective-permute-start(s32[1,64]{1,0:T(1,128)S(1)} %get-tuple-element.119), channel_id=1, source_target_pairs={{4,0},{5,1},{6,2},{7,3},{12,8},{13,9},{14,10},{15,11},{20,16},{21,... | collective-permute-start | bytes 776 | tf_op jit(solution)/shard_map/ppermute | solution.py:155
  73.9 75.1 %all-gather.9.cloned.1.call-start = ((), (), s32[]{:S(2)}) async-start(), calls=%async_computation.10 | async-start | bytes 6144000 | tf_op jit(solution)/shard_map/all_gather | solution.py:254
  74.8 8.7 %copy-start.22 = (f32[4,320]{1,0:T(4,128)}, f32[4,320]{1,0:T(4,128)S(1)}, u32[]{:S(2)}) copy-start(f32[4,320]{1,0:T(4,128)S(1)} %get-tuple-element.106) | copy-start | bytes 15364
  74.8 8.8 %copy-start.24 = (f32[4,320]{1,0:T(4,128)}, f32[4,320]{1,0:T(4,128)S(1)}, u32[]{:S(2)}) copy-start(f32[4,320]{1,0:T(4,128)S(1)} %get-tuple-element.108) | copy-start | bytes 15364
  76.8 2.5 copy-start.5
  100.7 37.3 %copy-start.2 = (f32[1024,640]{1,0:T(8,128)}, f32[1024,640]{1,0:T(8,128)S(1)}, u32[]{:S(2)}) copy-start(f32[1024,640]{1,0:T(8,128)S(1)} %get-tuple-element.121) | copy-start | bytes 7864324
  124.5 65.5 %reduce-scatter.7.cloned.1.call-start = ((), (), s32[]{:S(2)}) async-start(), calls=%async_computation.12 | async-start | bytes 4915200 | tf_op jit(solution)/shard_map/reduce_scatter | solution.py:287
  131.9 3.2 collective-permute-start.1
  133.8 12.3 %collective-permute-start.3 = (bf16[1,640,64]{1,2,0:T(8,128)(2,1)S(1)}, bf16[1,640,64]{1,2,0:T(8,128)(2,1)S(1)}, u32[]{:S(2)}, u32[]{:S(2)}) collective-permute-start(bf16[1,640,64]{1,2,0:T(8,128)(2,1)S(1)} %get-tuple-element.98), channel_id=1, source_target_pairs={{4,0},{5,1},{6,2},{7,3},{12,8},{13,9},{14,10},{15,11},{20,16},{21,... | collective-permute-start | bytes 245768 | tf_op jit(solution)/shard_map/ppermute | solution.py:155
  151.6 9.6 %copy-start.7 = (bf16[5,4,160,640]{3,2,1,0:T(8,128)(2,1)}, bf16[5,4,160,640]{3,2,1,0:T(8,128)(2,1)S(1)}, u32[]{:S(2)}) copy-start(bf16[5,4,160,640]{3,2,1,0:T(8,128)(2,1)S(1)} %copy.65) | copy-start | bytes 12288004
  161.2 41.4 %copy-start.8 = (f32[1024,640]{1,0:T(8,128)}, f32[1024,640]{1,0:T(8,128)S(1)}, u32[]{:S(2)}) copy-start(f32[1024,640]{1,0:T(8,128)S(1)} %get-tuple-element.123) | copy-start | bytes 7864324
  178.1 1.0 copy-start.16
  178.1 24.5 %all-gather.11.cloned.1.call-start = ((), (), s32[]{:S(2)}) async-start(), calls=%async_computation.11 | async-start | bytes 2457600 | tf_op jit(solution)/shard_map/all_gather | solution.py:255
  179.8 62.6 %reduce-scatter.9.cloned.1.call-start = ((), (), s32[]{:S(2)}) async-start(), calls=%async_computation.13 | async-start | bytes 2048000 | tf_op jit(solution)/shard_map/reduce_scatter | solution.py:288
  190.1 91.1 %reduce-scatter.11.cloned.1.call-start = ((), (), s32[]{:S(2)}) async-start(), calls=%async_computation.14 | async-start | bytes 12288000 | tf_op jit(solution)/shard_map/reduce_scatter | solution.py:287
  214.4 3.6 copy-start.12
  242.4 113.5 %reduce-scatter.13.cloned.1.call-start = ((), (), s32[]{:S(2)}) async-start(), calls=%async_computation.15 | async-start | bytes 5120000 | tf_op jit(solution)/shard_map/reduce_scatter | solution.py:288
  248.4 15.2 %collective-permute-start.4 = (bf16[1,640,64]{1,2,0:T(8,128)(2,1)S(1)}, bf16[1,640,64]{1,2,0:T(8,128)(2,1)S(1)}, u32[]{:S(2)}, u32[]{:S(2)}) collective-permute-start(bf16[1,640,64]{1,2,0:T(8,128)(2,1)S(1)} %get-tuple-element.97), channel_id=1, source_target_pairs={{4,0},{5,1},{6,2},{7,3},{12,8},{13,9},{14,10},{15,11},{20,16},{21,... | collective-permute-start | bytes 245768 | tf_op jit(solution)/shard_map/ppermute | solution.py:155
  260.6 4.0 collective-permute-start.5
  264.4 2.2 copy-start.14
  264.7 2.8 copy-start.3
  281.0 1.7 copy-start.4
  281.3 91.1 %reduce-scatter.15.cloned.1.call-start = ((), (), s32[]{:S(2)}) async-start(), calls=%async_computation.16 | async-start | bytes 5898240 | tf_op jit(solution)/shard_map/reduce_scatter | solution.py:287
  285.2 1.1 copy-start.13
  286.6 20.4 %copy-start.6 = (bf16[4,320,1024]{2,1,0:T(8,128)(2,1)S(1)}, bf16[4,320,1024]{2,1,0:T(8,128)(2,1)}, u32[]{:S(2)}) copy-start(bf16[4,320,1024]{2,1,0:T(8,128)(2,1)} %dynamic-slice_dynamic-update-slice_fusion) | copy-start | bytes 7864324
  286.6 20.4 %copy-start.23 = (f32[4,320]{1,0:T(4,128)S(1)}, f32[4,320]{1,0:T(4,128)}, u32[]{:S(2)}) copy-start(f32[4,320]{1,0:T(4,128)} %copy-done.22) | copy-start | bytes 15364
  286.6 20.4 %copy-start.25 = (f32[4,320]{1,0:T(4,128)S(1)}, f32[4,320]{1,0:T(4,128)}, u32[]{:S(2)}) copy-start(f32[4,320]{1,0:T(4,128)} %copy-done.24) | copy-start | bytes 15364
  359.9 0.7 copy-start.21
  359.9 12.5 %copy-start.9 = (f32[1024,640]{1,0:T(8,128)S(1)}, f32[1024,640]{1,0:T(8,128)}, u32[]{:S(2)}) copy-start(f32[1024,640]{1,0:T(8,128)} %copy-done.8) | copy-start | bytes 7864324
  359.9 71.3 %reduce-scatter.17.cloned.1.call-start = ((), (), s32[]{:S(2)}) async-start(), calls=%async_computation.17 | async-start | bytes 2457600 | tf_op jit(solution)/shard_map/reduce_scatter | solution.py:288
  388.6 35.9 %all-to-all-start = ((bf16[4,320,1024]{2,1,0:T(8,128)(2,1)}), bf16[4,320,1024]{2,1,0:T(8,128)(2,1)}, u32[]{:S(2)}, u32[]{:S(2)}) async-start(bf16[4,320,1024]{2,1,0:T(8,128)(2,1)} %bitcast.18), calls=%async_computation | async-start | bytes 5242880 | tf_op jit(solution)/shard_map/all_to_all | solution.py:188
  424.4 89.2 %all-to-all-start.2 = ((bf16[4,320,1024]{2,1,0:T(8,128)(2,1)}), bf16[4,320,1024]{2,1,0:T(8,128)(2,1)S(1)}, u32[]{:S(2)}, u32[]{:S(2)}) async-start(bf16[4,320,1024]{2,1,0:T(8,128)(2,1)} %bitcast.260), calls=%async_computation.4 | async-start | bytes 5242880 | tf_op jit(solution)/shard_map/all_to_all | solution.py:188
  428.1 130.6 %all-gather.13.cloned.1.call-start = ((), (), s32[]{:S(2)}) async-start(), calls=%async_computation.18 | async-start | bytes 3096576 | tf_op jit(solution)/shard_map/all_gather | solution.py:352
  489.5 24.1 %copy-start.17 = (f32[3,240,128]{2,1,0:T(8,128)S(1)}, f32[3,240,128]{2,1,0:T(8,128)}, u32[]{:S(2)}) copy-start(f32[3,240,128]{2,1,0:T(8,128)} %get-tuple-element.31) | copy-start | bytes 1105924
  513.6 24.0 %copy-start.10 = (bf16[4,320,1024]{2,1,0:T(8,128)(2,1)}, bf16[4,320,1024]{2,1,0:T(8,128)(2,1)S(1)}, u32[]{:S(2)}) copy-start(bf16[4,320,1024]{2,1,0:T(8,128)(2,1)S(1)} %all-to-all-done.2) | copy-start | bytes 7864324
  530.4 7.2 %copy-start.18 = (f32[3,200,128]{2,1,0:T(8,128)S(1)}, f32[3,200,128]{2,1,0:T(8,128)}, u32[]{:S(2)}) copy-start(f32[3,200,128]{2,1,0:T(8,128)} %get-tuple-element.33) | copy-start | bytes 921604
  535.5 21.8 %slice-start = ((f32[384,640]{1,0:T(8,128)}), f32[3,640]{1,0:T(4,128)S(1)}, s32[]{:S(2)}) async-start(f32[384,640]{1,0:T(8,128)} %reshape.1449), calls=%async_computation.20 | async-start | bytes 20480 | tf_op jit(solution)/shard_map/slice | solution.py:359
  568.6 3.6 copy-start.11
  568.6 5.1 copy-start.1
Sparse Core Ops, SparseCore 0:
  64.4 11.0 all-gather.6
  77.9 46.5 all-gather.14
  126.1 13.5 all-gather.8
  178.2 11.8 reduce-scatter.6
  191.5 11.0 all-gather.10
  204.9 37.4 reduce-scatter.8
  244.7 15.6 reduce-scatter.10
  281.4 74.5 reduce-scatter.12
  360.1 12.3 reduce-scatter.14
  374.7 42.5 reduce-scatter.16
  513.7 8.2 all-gather.12

commit v9 on v8

--- a/solution.py
+++ b/solution.py
@@ -235,14 +235,13 @@
         lax.dynamic_slice_in_dim(w_outer, sidx * (hloc // seqs), hloc // seqs, 0),
     ]
     if q_count == 1:
-        small_all, w_in, w_out, x = exchange(
-            [jnp.concatenate(smalls), halves[0], halves[2], inputs], ("ch",), 0, gather=(True, True, True, False)
+        small_all, w_in, w_cv, w_out, x = exchange(
+            [jnp.concatenate(smalls)] + halves + [inputs], ("ch",), 0, gather=(True, True, True, True, False)
         )
         x = _join(x, nch)
     else:
-        small_all, w_in, w_out = exchange([jnp.concatenate(smalls), halves[0], halves[2]], ("ch",), 0, gather=True)
+        small_all, w_in, w_cv, w_out = exchange([jnp.concatenate(smalls)] + halves, ("ch",), 0, gather=True)
         x = to_positions(inputs, nch, q_count)
-    w_cv = lax.all_gather(halves[1], "ch", axis=0)
     cut = 0
     full = []
     for v in smalls:

time: 592 us -> 598 us (1.010)
  Pallas kernels: 106 us -> 128 us
  waiting for transfers between devices: 109 us -> 89.6 us
    all_gather x1 -> x0, waiting for transfers between devices: 23.2 us -> none  [local(): w_cv = lax.all_gather(halves[1], 'ch', axis=0)]
    pallas_call x2, Pallas kernels: 106 us -> 128 us  [exchange(): pl.pallas_call(functools.partial(_exchange_kernel, sizes, group, gather,...]
    unnamed x57 -> x55, local copies, waits for them, and re-layouts: 17.9 us -> 19.3 us
  transfers between devices with their start and end apart: 20 -> 19, of which waited for: 7 -> 6; matrix products, arithmetic and copies ran while one was open for 38% -> 37% of each run, Pallas kernels for 9% -> 9%
where the time goes in v9:
time: 598 us; the launch traced here: 587 us
  Pallas kernels  128 us (21%)
  matrix products  120 us (20%)
  local copies, waits for them, and re-layouts  99.3 us (17%)
  waiting for transfers between devices  89.6 us (15%)
  blocking collectives  59.4 us (10%)
  other arithmetic  50.7 us (8%)
  starting transfers between devices  24.8 us (4%)
  between operations  15 us (3%)
    pallas_call x2, Pallas kernels, exchange(): pl.pallas_call(functools.partial(_exchange_kernel, sizes, group, gather,...  128 us
    all_gather x3, blocking collectives, local(): parts = [lax.all_gather(p, 'batch', axis=0) for p in parts]  54.2 us
    reduce_scatter x3, waiting for transfers between devices, reduce_seq_batch(): return lax.psum_scatter(g, 'batch', scatter_dimension=split_dim, tiled=True)  44.5 us
    dot_general x1, matrix products, local(): jnp.einsum('dh,rhl->rdl', w_in, grad_inner, preferred_element_type=jnp.fl...  20 us
    unnamed x55, local copies, waits for them, and re-layouts  19.3 us
    all_to_all x2, waiting for transfers between devices, to_channels(): x = lax.all_to_all(x, 'ch', 0, 0, tiled=True)  18.8 us
    dot_general x1, matrix products, local(): jnp.einsum('dh,rdl->rhl', w_in, hidden0, preferred_element_type=jnp.float32)  17.8 us
    dot_general x1, matrix products, local(): jnp.einsum('rdl,rhl->dh', hidden0, grad_inner, preferred_element_type=jnp...  15.5 us
  transfers between devices with their start and end apart: 19, of which 6 were waited for; matrix products, arithmetic and copies ran while one was open for 37% of the time, Pallas kernels for 9%

profile of v9, /device:TPU:0, one launch (start us, length us, event | category | flops | bytes accessed | tf_op | source)
XLA Modules:
  0.0 586.5 jit_solution(18113708036678904732)
XLA Ops:
  13.9 73.4 %shard_map.254 = (f32[4,1920]{1,0:T(4,128)}, bf16[4,160,640]{2,1,0:T(8,128)(2,1)}, bf16[4,5,80,640]{3,2,1,0:T(8,128)(2,1)}, bf16[4,80,1280]{2,1,0:T(8,128)(2,1)}, bf16[4,320,1024]{2,1,0:T(8,128)(2,1)}) custom-call(f32[1920]{0:T(1024)} %concatenate.42.refs_0_, bf16[160,640]{1,0:T(8,128)(2,1)} %constant_dynamic-slice_fusion.2.refs_1_, ...), custom_call_target="tpu_custom_call" | custom-call | bytes 12677120 | tf_op jit(solution)/shard_map/pallas_call | solution.py:90
  88.1 3.7 all-to-all-start.1
  100.6 2.3 convert_reduce_fusion
  103.2 2.9 convert_element_type.149
  107.5 17.8 %fusion.83 = (f32[1024]{0:T(1024)S(1)}, f32[1024,640]{1,0:T(8,128)S(1)}) fusion(f32[640]{0:T(1024)S(1)} %add.208, bf16[1280,640]{1,0:T(8,128)(2,1)} %bitcast.271, f32[1280]{0:T(1024)S(1)} %add.205, f32[1280]{0:T(1024)S(1)} %mul.438, f32[1024]{0:T(1024)S(1)} %add_rsqrt_fusion.2, f32[1,1280,1,1,1,1,1024]{6,1,5,4,3,2,0:T(8,128)} %bitcast.260, ...), kind=kOutput, calls=%fused_computation.159 | convolution fusion | flops 1769470976 | bytes 9527808 | tf_op jit(solution)/shard_map/dh,rdl->rhl/dot_general | solution.py:269
  125.9 7.3 %multiply_convert_fusion.1 = bf16[1,640,1024]{1,2,0:T(8,128)(2,1)S(1)} fusion(f32[640]{0:T(1024)S(1)} %add.212, f32[640]{0:T(1024)S(1)} %mul.448, f32[1024]{0:T(1024)S(1)} %add_rsqrt_fusion.1, f32[1024]{0:T(1024)S(1)} %broadcast_multiply_fusion.5, f32[640]{0:T(1024)S(1)} %add.208, f32[1024,640]{1,0:T(8,128)S(1)} %get-tuple-element.109), kind=kLoop, calls=%fused_computation.141 | loop fusion | flops 45875200 | bytes 3948032 | tf_op jit(solution)/shard_map/convert_element_type | solution.py:271
  133.2 3.0 collective-permute-start.1
  140.7 8.0 %constant_dynamic-update-slice_fusion = bf16[1,3200,1024]{1,2,0:T(8,128)(2,1)} fusion(bf16[1,3200,1024]{1,2,0:T(8,128)(2,1)} %fusion.110, f32[640]{0:T(1024)S(1)} %add.212, f32[640]{0:T(1024)S(1)} %mul.448, f32[1024]{0:T(1024)S(1)} %add_rsqrt_fusion.1, f32[1024]{0:T(1024)S(1)} %broadcast_multiply_fusion.5, f32[640]{0:T(1024)S(1)} %add.208, ...), kind=kLoop, calls=%fused_computation.212 | loop fusion | flops 45875200 | bytes 3948032
  151.6 2.6 copy.53
  154.2 9.6 %fusion.85 = (f32[1024]{0:T(1024)S(1)}, f32[1024,640]{1,0:T(8,128)S(1)}) fusion(f32[640]{0:T(1024)S(1)} %add.215, bf16[3200,640]{1,0:T(8,128)(2,1)S(1)} %bitcast.262, bf16[1,3200,1024]{1,2,0:T(8,128)(2,1)} %fusion.108), kind=kOutput, calls=%fused_computation.161 | convolution fusion | flops 4195613696 | bytes 13277696 | tf_op jit(solution)/shard_map/co,rcl->rol/dot_general | solution.py:275
  165.4 12.4 %fusion.177 = f32[640,1280]{1,0:T(8,128)} fusion(bf16[1280,1024]{1,0:T(8,128)(2,1)S(1)} %bitcast.256, f32[640]{0:T(1024)S(1)} %add.219, f32[640]{0:T(1024)S(1)} %mul.458, f32[1024]{0:T(1024)S(1)} %add_rsqrt_fusion, f32[1024]{0:T(1024)S(1)} %broadcast_multiply_fusion.4, f32[640]{0:T(1024)S(1)} %add.215, f32[1024,640]{1,0:T(8,128)} %copy-done.8), kind=kOutput, calls=%fused_computation.302 | convolution fusion | flops 1723596800 | bytes 8535552 | tf_op jit(solution)/shard_map/rhl,rdl->hd/dot_general | solution.py:282
  177.8 4.5 reshape.1435
  184.0 9.7 %copy.63 = bf16[1,3200,1024]{2,1,0:T(8,128)(2,1)} copy(bf16[1,3200,1024]{1,2,0:T(8,128)(2,1)} %fusion.108) | data formatting | bytes 13107200 | tf_op jit(solution)/shard_map/concatenate | solution.py:167
  195.7 12.5 %all-gather.9.cloned.1.call-done = bf16[4,160,1280]{2,1,0:T(8,128)(2,1)} async-done(((bf16[4,80,1280]{2,1,0:T(8,128)(2,1)}), bf16[4,160,1280]{2,1,0:T(8,128)(2,1)}) %all-gather.9.cloned.1.call-update) | async-done | bytes 1638416 | tf_op jit(solution)/shard_map/all_gather | solution.py:254
  208.3 11.8 %fusion.60 = (f32[640]{0:T(1024)S(1)}, f32[1024]{0:T(1024)S(1)}, f32[1024]{0:T(1024)S(1)}, f32[640]{0:T(1024)S(1)}, f32[1,640,1024]{1,2,0:T(8,128)S(1)}) fusion(f32[1024]{0:T(1024)S(1)} %add_rsqrt_fusion, f32[1024]{0:T(1024)S(1)} %broadcast_multiply_fusion.4, f32[640]{0:T(1024)S(1)} %add.215, f32[1024,640]{1,0:T(8,128)} %copy-done.8, f32[640]{0:T(1024)S(1)} %mul.458, ...), kind=kOutput, calls=%fused_computation.110 | convolution fusion | flops 1732113152 | bytes 9531904 | tf_op jit(solution)/shard_map/hd,rdl->rhl/dot_general | solution.py:290
  222.9 7.1 %fusion.111 = f32[640,25,128]{2,0,1:T(8,128)} fusion(bf16[25,128,1024]{2,1,0:T(8,128)(2,1)S(1)} %bitcast.266, bf16[1,640,1024]{1,2,0:T(8,128)(2,1)S(1)} %get-tuple-element.83), kind=kOutput, calls=%fused_computation.199 | convolution fusion | flops 4194304000 | bytes 16056320 | tf_op jit(solution)/shard_map/rol,rkcil->okci/dot_general | solution.py:296
  230.1 18.0 %reduce-scatter.9.cloned.1.call-done.refs_0_ = f32[4,200,128]{2,1,0:T(8,128)} async-done(((f32[4,800,128]{2,1,0:T(8,128)}), f32[4,200,128]{2,1,0:T(8,128)}) %reduce-scatter.9.cloned.1.call-update) | async-done | bytes 409616 | tf_op jit(solution)/shard_map/reduce_scatter | solution.py:287
  248.1 5.9 %copy.54 = f32[1,1280,1024]{1,2,0:T(8,128)} copy(f32[1,1280,1024]{2,1,0:T(8,128)} %bitcast.261) | data formatting | bytes 10485760 | tf_op jit(solution)/shard_map/convert_element_type | solution.py:266
  257.5 8.3 %copy.59 = bf16[5,640,640]{2,1,0:T(8,128)(2,1)} copy(bf16[5,640,640]{1,2,0:T(8,128)(2,1)} %bitcast.263) | data formatting | bytes 8192000 | tf_op jit(solution)/shard_map/transpose | solution.py:304
  266.1 3.3 collective-permute-start.5
  273.2 13.6 %fusion.66 = (f32[640]{0:T(1024)S(1)}, f32[1024]{0:T(1024)S(1)}, f32[1024]{0:T(1024)S(1)}, f32[640]{0:T(1024)S(1)}, f32[1,640,1024]{1,2,0:T(8,128)}) fusion(f32[1024]{0:T(1024)S(1)} %add_rsqrt_fusion.1, f32[1024]{0:T(1024)S(1)} %broadcast_multiply_fusion.5, f32[640]{0:T(1024)S(1)} %add.208, f32[1024,640]{1,0:T(8,128)S(1)} %copy-done.1, f32[640]{0:T(1024)S(1)} %mul.448, ...), kind=kOutput, calls=%fused_computation.121 | convolution fusion | flops 4248695808 | bytes 15921664 | tf_op jit(solution)/shard_map/oc,rol->rcl/dot_general | solution.py:305
  288.5 2.4 fusion.65
  292.3 20.0 %multiply_reduce_fusion = (f32[1280]{0:T(1024)S(1)}, f32[1024]{0:T(1024)S(1)}, f32[1024]{0:T(1024)S(1)}, f32[1280]{0:T(1024)S(1)}, f32[1,1280,1024]{1,2,0:T(8,128)}) fusion(f32[1,1280,1024]{1,2,0:T(8,128)} %copy.54, f32[1024]{0:T(1024)S(1)} %broadcast_multiply_fusion.8, f32[1024]{0:T(1024)S(1)} %add_rsqrt_fusion.2, f32[1280]{0:T(1024)S(1)} %mul.438, ...), kind=kOutput, calls=%fused_computation.25 | convolution fusion | flops 1785196032 | bytes 13471744 | tf_op jit(solution)/shard_map/dh,rhl->rdl/dot_general | solution.py:313
  312.7 15.5 %fusion.79 = f32[4,320,640]{2,1,0:T(8,128)S(1)} fusion(bf16[4,320,1024]{2,1,0:T(8,128)(2,1)S(1)} %copy-done.6, f32[4,320]{1,0:T(4,128)S(1)} %copy-done.24, f32[4,320]{1,0:T(4,128)S(1)} %copy-done.22, f32[1024]{0:T(1024)S(1)} %add_rsqrt_fusion.2, f32[1024]{0:T(1024)S(1)} %broadcast_multiply_fusion.8, bf16[1,640,1024]{1,2,0:T(8,128)(2,1)} %copy-done.12), kind=kOutput, calls=%fused_computation.155 | convolution fusion | flops 1769472000 | bytes 7227392 | tf_op jit(solution)/shard_map/rdl,rhl->dh/dot_general | solution.py:312
  330.5 4.7 reshape.1446
  335.2 26.5 %reduce-scatter.13.cloned.1.call-done = f32[80,25,128]{2,0,1:T(8,128)} async-done(((f32[320,25,128]{2,0,1:T(8,128)}), f32[80,25,128]{2,0,1:T(8,128)}) %reduce-scatter.13.cloned.1.call-update) | async-done | bytes 1024016 | tf_op jit(solution)/shard_map/reduce_scatter | solution.py:287
  363.2 2.4 reshape.1448.refs_1_
  366.3 11.7 %reduce-scatter.15.cloned.1.call-done = f32[4,960,128]{2,1,0:T(8,128)} async-done(((f32[4,1920,128]{2,1,0:T(8,128)}), f32[4,960,128]{2,1,0:T(8,128)}) %reduce-scatter.15.cloned.1.call-update) | async-done | bytes 1966096 | tf_op jit(solution)/shard_map/reduce_scatter | solution.py:286
  378.1 11.7 %fusion.15 = bf16[1,1280,1024]{1,2,0:T(8,128)(2,1)} fusion(f32[1,1280,1024]{1,2,0:T(8,128)} %copy.54, bf16[640,1280]{1,0:T(8,128)(2,1)} %bitcast.274, f32[1280]{0:T(1024)S(1)} %add.223, f32[640]{0:T(1024)S(1)} %add.219, f32[640]{0:T(1024)S(1)} %mul.458, f32[1024]{0:T(1024)S(1)} %add_rsqrt_fusion, f32[1024]{0:T(1024)S(1)} %broadcast_multiply_fusion.4, ...), kind=kOutput, calls=%fused_computation.19 | convolution fusion | flops 1727528960 | bytes 12145152 | tf_op jit(solution)/shard_map/hd,rhl->rdl/dot_general | solution.py:278
  389.9 4.4 copy.55
  394.2 4.8 all-to-all-start
  399.1 3.4 copy.60
  402.5 6.5 %add_convert_fusion = bf16[1,1280,1024]{1,2,0:T(8,128)(2,1)S(1)} fusion(f32[1,1280,1024]{1,2,0:T(8,128)} %copy.60, f32[1,1280,1024]{1,2,0:T(8,128)} %get-tuple-element.114, f32[1,1280,1024]{1,2,0:T(8,128)} %copy.54, f32[1024]{0:T(1024)S(1)} %broadcast_multiply_fusion.6, f32[1024]{0:T(1024)S(1)} %broadcast_multiply_fusion.7, f32[1280]{0:T(1024)S(1)} %mul.438, ...), kind=kLoop, calls=%fused_computation.40 | loop fusion | flops 11796480 | bytes 18371584 | tf_op jit(solution)/shard_map/convert_element_type | solution.py:317
  409.0 2.6 copy.61
  411.6 18.8 %all-to-all-done = bf16[4,320,1024]{2,1,0:T(8,128)(2,1)} async-done(((bf16[4,320,1024]{2,1,0:T(8,128)(2,1)}), bf16[4,320,1024]{2,1,0:T(8,128)(2,1)}, u32[]{:S(2)}, u32[]{:S(2)}) %all-to-all-start) | async-done | bytes 2621472 | tf_op jit(solution)/shard_map/all_to_all | solution.py:188
  430.4 3.7 all-to-all-start.2
  434.3 2.6 dynamic-slice_reduce_fusion
  437.2 54.8 %shard_map.255 = (f32[3,200,128]{2,1,0:T(8,128)}, f32[80,5,3,160]{3,2,1,0:T(4,128)}, f32[3,240,128]{2,1,0:T(8,128)}) custom-call(f32[4,200,128]{2,1,0:T(8,128)} %reduce-scatter.9.cloned.1.call-done.refs_0_, f32[80,5,4,160]{3,2,1,0:T(4,128)} %reshape.1448.refs_1_, f32[4,240,128]{2,1,0:T(8,128)} %reduce-scatter.17.cloned.1.call-done.refs_2_), custom_call_target="tpu_custom_call" | custom-call | bytes 3850240 | tf_op jit(solution)/shard_map/pallas_call | solution.py:90
  492.0 2.4 reduce_sum.245
  496.5 23.1 %all_gather.34 = f32[4,500,128]{2,1,0:T(8,128)} all-gather(f32[1,500,128]{2,1,0:T(8,128)S(1)} %add.232), channel_id=1, replica_groups=mesh['batch'=4,'seq'=2,'ch'=4] {'batch'}, dimensions={0}, use_global_device_ids=true | all-gather | bytes 1280000 | tf_op jit(solution)/shard_map/all_gather | solution.py:349
  520.5 15.7 %all_gather.32 = f32[4,240,128]{2,1,0:T(8,128)S(1)} all-gather(f32[1,240,128]{2,1,0:T(8,128)S(1)} %bitcast_add_fusion.3), channel_id=1, replica_groups=mesh['batch'=4,'seq'=2,'ch'=4] {'batch'}, dimensions={0}, use_global_device_ids=true | all-gather | bytes 614400 | tf_op jit(solution)/shard_map/all_gather | solution.py:349
  536.3 2.8 all_gather.33
  539.0 2.3 reshape.1449
  544.4 15.5 %all_gather.36 = f32[4,200,128]{2,1,0:T(8,128)S(1)} all-gather(f32[1,200,128]{2,1,0:T(8,128)S(1)} %bitcast_add_fusion.4), channel_id=1, replica_groups=mesh['batch'=4,'seq'=2,'ch'=4] {'batch'}, dimensions={0}, use_global_device_ids=true | all-gather | bytes 512000 | tf_op jit(solution)/shard_map/all_gather | solution.py:349
  559.9 2.4 all_gather.37
  564.6 4.8 reshape_reshape.7
  569.4 5.1 copy.66
  574.5 3.5 copy.90
  (168 shorter events, 59.7 us)
Async XLA Ops:
  7.2 100.3 %all-gather.5.cloned.1.call-start = ((), (), s32[]{:S(2)}) async-start(), calls=%async_computation.9 | async-start | bytes 2457600 | tf_op jit(solution)/shard_map/all_gather | solution.py:252
  7.2 80.1 %copy-start.14 = (bf16[320,640]{1,0:T(8,128)(2,1)S(1)}, bf16[320,640]{1,0:T(8,128)(2,1)}, u32[]{:S(2)}) copy-start(bf16[320,640]{1,0:T(8,128)(2,1)} %param.19) | copy-start | bytes 1228804
  88.1 77.3 %all-to-all-start.1 = ((bf16[4,320,1024]{2,1,0:T(8,128)(2,1)}), bf16[4,320,1024]{2,1,0:T(8,128)(2,1)S(1)}, u32[]{:S(2)}, u32[]{:S(2)}) async-start(bf16[4,320,1024]{2,1,0:T(8,128)(2,1)} %param.29), calls=%async_computation.1 | async-start | bytes 5242880 | tf_op jit(solution)/shard_map/all_to_all | solution.py:175
  91.7 6.0 %copy-start.18 = (f32[1920]{0:T(1024)S(1)}, f32[1920]{0:T(1024)}, u32[]{:S(2)}) copy-start(f32[1920]{0:T(1024)} %concatenate.42.refs_0_) | copy-start | bytes 23044
  91.7 6.1 %copy-start.19 = (f32[4,1920]{1,0:T(4,128)S(1)}, f32[4,1920]{1,0:T(4,128)}, u32[]{:S(2)}) copy-start(f32[4,1920]{1,0:T(4,128)} %get-tuple-element.26) | copy-start | bytes 92164
  91.8 59.8 %all-gather.7.cloned.1.call-start = ((), (), s32[]{:S(2)}) async-start(), calls=%async_computation.10 | async-start | bytes 6144000 | tf_op jit(solution)/shard_map/all_gather | solution.py:253
  92.6 43.6 %collective-permute-start = (s32[1,64]{1,0:T(1,128)S(1)}, s32[1,64]{1,0:T(1,128)S(1)}, u32[]{:S(2)}, u32[]{:S(2)}) collective-permute-start(s32[1,64]{1,0:T(1,128)S(1)} %get-tuple-element.106), channel_id=1, source_target_pairs={{0,4},{1,5},{2,6},{3,7},{8,12},{9,13},{10,14},{11,15},{16,20},{17,... | collective-permute-start | bytes 776 | tf_op jit(solution)/shard_map/ppermute | solution.py:154
  94.5 41.8 %collective-permute-start.2 = (s32[1,64]{1,0:T(1,128)S(1)}, s32[1,64]{1,0:T(1,128)S(1)}, u32[]{:S(2)}, u32[]{:S(2)}) collective-permute-start(s32[1,64]{1,0:T(1,128)S(1)} %get-tuple-element.107), channel_id=1, source_target_pairs={{4,0},{5,1},{6,2},{7,3},{12,8},{13,9},{14,10},{15,11},{20,16},{21,... | collective-permute-start | bytes 776 | tf_op jit(solution)/shard_map/ppermute | solution.py:155
  97.7 97.9 %reduce-scatter.7.cloned.1.call-start = ((), (), s32[]{:S(2)}) async-start(), calls=%async_computation.12 | async-start | bytes 4915200 | tf_op jit(solution)/shard_map/reduce_scatter | solution.py:286
  98.6 8.7 %copy-start.21 = (f32[4,320]{1,0:T(4,128)}, f32[4,320]{1,0:T(4,128)S(1)}, u32[]{:S(2)}) copy-start(f32[4,320]{1,0:T(4,128)S(1)} %get-tuple-element.94) | copy-start | bytes 15364
  98.6 8.8 %copy-start.23 = (f32[4,320]{1,0:T(4,128)}, f32[4,320]{1,0:T(4,128)S(1)}, u32[]{:S(2)}) copy-start(f32[4,320]{1,0:T(4,128)S(1)} %get-tuple-element.96) | copy-start | bytes 15364
  100.6 2.5 copy-start.5
  125.3 15.4 %copy-start = (f32[1024,640]{1,0:T(8,128)}, f32[1024,640]{1,0:T(8,128)S(1)}, u32[]{:S(2)}) copy-start(f32[1024,640]{1,0:T(8,128)S(1)} %get-tuple-element.109) | copy-start | bytes 7864324
  133.2 4.5 collective-permute-start.1
  136.4 12.3 %collective-permute-start.3 = (bf16[1,640,64]{1,2,0:T(8,128)(2,1)S(1)}, bf16[1,640,64]{1,2,0:T(8,128)(2,1)S(1)}, u32[]{:S(2)}, u32[]{:S(2)}) collective-permute-start(bf16[1,640,64]{1,2,0:T(8,128)(2,1)S(1)} %get-tuple-element.86), channel_id=1, source_target_pairs={{4,0},{5,1},{6,2},{7,3},{12,8},{13,9},{14,10},{15,11},{20,16},{21,... | collective-permute-start | bytes 245768 | tf_op jit(solution)/shard_map/ppermute | solution.py:155
  154.2 9.6 %copy-start.7 = (bf16[5,4,160,640]{3,2,1,0:T(8,128)(2,1)}, bf16[5,4,160,640]{3,2,1,0:T(8,128)(2,1)S(1)}, u32[]{:S(2)}) copy-start(bf16[5,4,160,640]{3,2,1,0:T(8,128)(2,1)S(1)} %copy.53) | copy-start | bytes 12288004
  163.9 1.5 copy-start.8
  165.4 42.9 %copy-start.3 = (bf16[4,320,1024]{2,1,0:T(8,128)(2,1)}, bf16[4,320,1024]{2,1,0:T(8,128)(2,1)S(1)}, u32[]{:S(2)}) copy-start(bf16[4,320,1024]{2,1,0:T(8,128)(2,1)S(1)} %all-to-all-done.1) | copy-start | bytes 7864324
  182.3 1.0 copy-start.15
  182.3 26.0 %all-gather.9.cloned.1.call-start = ((), (), s32[]{:S(2)}) async-start(), calls=%async_computation.11 | async-start | bytes 2457600 | tf_op jit(solution)/shard_map/all_gather | solution.py:254
  184.0 64.0 %reduce-scatter.9.cloned.1.call-start = ((), (), s32[]{:S(2)}) async-start(), calls=%async_computation.13 | async-start | bytes 2048000 | tf_op jit(solution)/shard_map/reduce_scatter | solution.py:287
  195.7 91.3 %reduce-scatter.11.cloned.1.call-start = ((), (), s32[]{:S(2)}) async-start(), calls=%async_computation.14 | async-start | bytes 12288000 | tf_op jit(solution)/shard_map/reduce_scatter | solution.py:286
  208.3 11.8 %copy-start.9 = (f32[1024,640]{1,0:T(8,128)S(1)}, f32[1024,640]{1,0:T(8,128)}, u32[]{:S(2)}) copy-start(f32[1024,640]{1,0:T(8,128)} %copy-done.8) | copy-start | bytes 7864324
  220.1 2.9 copy-start.11
  248.0 113.6 %reduce-scatter.13.cloned.1.call-start = ((), (), s32[]{:S(2)}) async-start(), calls=%async_computation.15 | async-start | bytes 5120000 | tf_op jit(solution)/shard_map/reduce_scatter | solution.py:287
  254.0 15.4 %collective-permute-start.4 = (bf16[1,640,64]{1,2,0:T(8,128)(2,1)S(1)}, bf16[1,640,64]{1,2,0:T(8,128)(2,1)S(1)}, u32[]{:S(2)}, u32[]{:S(2)}) collective-permute-start(bf16[1,640,64]{1,2,0:T(8,128)(2,1)S(1)} %get-tuple-element.85), channel_id=1, source_target_pairs={{4,0},{5,1},{6,2},{7,3},{12,8},{13,9},{14,10},{15,11},{20,16},{21,... | collective-permute-start | bytes 245768 | tf_op jit(solution)/shard_map/ppermute | solution.py:155
  266.1 4.3 collective-permute-start.5
  270.1 2.2 copy-start.13
  270.4 2.8 copy-start.1
  286.8 1.7 copy-start.2
  287.0 91.1 %reduce-scatter.15.cloned.1.call-start = ((), (), s32[]{:S(2)}) async-start(), calls=%async_computation.16 | async-start | bytes 5898240 | tf_op jit(solution)/shard_map/reduce_scatter | solution.py:286
  290.9 1.1 copy-start.12
  292.3 20.4 %copy-start.6 = (bf16[4,320,1024]{2,1,0:T(8,128)(2,1)S(1)}, bf16[4,320,1024]{2,1,0:T(8,128)(2,1)}, u32[]{:S(2)}) copy-start(bf16[4,320,1024]{2,1,0:T(8,128)(2,1)} %dynamic-slice_dynamic-update-slice_fusion) | copy-start | bytes 7864324
  292.3 20.4 %copy-start.22 = (f32[4,320]{1,0:T(4,128)S(1)}, f32[4,320]{1,0:T(4,128)}, u32[]{:S(2)}) copy-start(f32[4,320]{1,0:T(4,128)} %copy-done.21) | copy-start | bytes 15364
  292.3 20.4 %copy-start.24 = (f32[4,320]{1,0:T(4,128)S(1)}, f32[4,320]{1,0:T(4,128)}, u32[]{:S(2)}) copy-start(f32[4,320]{1,0:T(4,128)} %copy-done.23) | copy-start | bytes 15364
  365.6 0.7 copy-start.20
  365.6 12.5 %copy-start.10 = (f32[1024,640]{1,0:T(8,128)S(1)}, f32[1024,640]{1,0:T(8,128)}, u32[]{:S(2)}) copy-start(f32[1024,640]{1,0:T(8,128)} %copy-done.8) | copy-start | bytes 7864324
  365.6 71.6 %reduce-scatter.17.cloned.1.call-start = ((), (), s32[]{:S(2)}) async-start(), calls=%async_computation.17 | async-start | bytes 2457600 | tf_op jit(solution)/shard_map/reduce_scatter | solution.py:287
  394.2 4.8 copy-start.4
  394.2 36.2 %all-to-all-start = ((bf16[4,320,1024]{2,1,0:T(8,128)(2,1)}), bf16[4,320,1024]{2,1,0:T(8,128)(2,1)}, u32[]{:S(2)}, u32[]{:S(2)}) async-start(bf16[4,320,1024]{2,1,0:T(8,128)(2,1)} %bitcast.265), calls=%async_computation | async-start | bytes 5242880 | tf_op jit(solution)/shard_map/all_to_all | solution.py:188
  430.4 89.2 %all-to-all-start.2 = ((bf16[4,320,1024]{2,1,0:T(8,128)(2,1)}), bf16[4,320,1024]{2,1,0:T(8,128)(2,1)S(1)}, u32[]{:S(2)}, u32[]{:S(2)}) async-start(bf16[4,320,1024]{2,1,0:T(8,128)(2,1)} %bitcast.264), calls=%async_computation.4 | async-start | bytes 5242880 | tf_op jit(solution)/shard_map/all_to_all | solution.py:188
  434.1 130.6 %all-gather.11.cloned.1.call-start = ((), (), s32[]{:S(2)}) async-start(), calls=%async_computation.18 | async-start | bytes 3096576 | tf_op jit(solution)/shard_map/all_gather | solution.py:351
  495.5 24.1 %copy-start.16 = (f32[3,240,128]{2,1,0:T(8,128)S(1)}, f32[3,240,128]{2,1,0:T(8,128)}, u32[]{:S(2)}) copy-start(f32[3,240,128]{2,1,0:T(8,128)} %get-tuple-element.33) | copy-start | bytes 1105924
  536.3 7.2 %copy-start.17 = (f32[3,200,128]{2,1,0:T(8,128)S(1)}, f32[3,200,128]{2,1,0:T(8,128)}, u32[]{:S(2)}) copy-start(f32[3,200,128]{2,1,0:T(8,128)} %get-tuple-element.35) | copy-start | bytes 921604
  541.4 21.9 %slice-start = ((f32[384,640]{1,0:T(8,128)}), f32[3,640]{1,0:T(4,128)S(1)}, s32[]{:S(2)}) async-start(f32[384,640]{1,0:T(8,128)} %reshape.1449), calls=%async_computation.19 | async-start | bytes 20480 | tf_op jit(solution)/shard_map/slice | solution.py:358
Sparse Core Ops, SparseCore 0:
  88.2 11.0 all-gather.4
  100.8 14.6 all-gather.6
  182.4 13.2 reduce-scatter.6
  197.1 11.0 all-gather.8
  210.5 37.4 reduce-scatter.8
  250.2 15.6 reduce-scatter.10
  287.1 74.4 reduce-scatter.12
  365.7 12.3 reduce-scatter.14
  380.5 42.7 reduce-scatter.16
  519.7 8.2 all-gather.10

commit v10 on v7

--- a/solution.py
+++ b/solution.py
@@ -337,12 +337,18 @@
     parts = [part_outer, part_conv, part_inner]
     parts = exchange(parts, ("ch",), 1, axes=(0, 2, 0), reduce=True)
     piece_shapes = [p.shape for p in parts]
-    parts = [p.reshape(p.size // 128, 128) if p.size % 128 == 0 else p for p in parts]
-    parts = [lax.all_gather(p, "batch", axis=0) for p in parts]
-    parts = [
-        lax.all_gather(p, "seq", axis=0, tiled=True).reshape((seqs * batches,) + shape)
-        for p, shape in zip(parts, piece_shapes)
-    ]
+    piece_sizes = [p.size for p in parts]
+    joined = jnp.concatenate([p.reshape(-1) for p in parts])
+    joined_len = joined.shape[0]
+    joined_pad = -(-joined_len // 1024) * 1024
+    joined = jnp.pad(joined, (0, joined_pad - joined_len)).reshape(joined_pad // 128, 128)
+    joined = lax.all_gather(joined, "batch", axis=0)
+    joined = lax.all_gather(joined, "seq", axis=0, tiled=True).reshape(seqs * batches, joined_pad)
+    parts = []
+    cut = 0
+    for size, shape in zip(piece_sizes, piece_shapes):
+        parts.append(joined[:, cut : cut + size].reshape((seqs * batches,) + shape))
+        cut += size
     red_w_outer = parts[0].reshape(hloc, dim)
     red_w_conv = parts[1].reshape(hid, KERNEL_TAPS, hloc).transpose(1, 2, 0)
     red_inner = parts[2].reshape(dloc + vec_rows, hid)

time: 590 us -> 595 us (level)
  waiting for transfers between devices: 128 us -> 176 us
  Pallas kernels: 78.2 us -> 54.2 us
  blocking collectives: 59.2 us -> 35.9 us
  other arithmetic: 55.8 us -> 61.8 us
    all_gather x5 -> x0, blocking collectives: 59.2 us -> none  [the longest x3 54.1 us: local(): parts = [lax.all_gather(p, 'batch', axis=0) for p in parts]]
    reduce_scatter x3, waiting for transfers between devices: 44.3 us -> 86.7 us  [reduce_seq_batch(): return lax.psum_scatter(g, 'batch', scatter_dimension=split_dim, tiled=True)]
    all_to_all x0 -> x1, blocking collectives: none -> 35.9 us  [to_channels(): x = lax.all_to_all(x, 'ch', 0, 0, tiled=True)]
    pallas_call x2, Pallas kernels: 78.2 us -> 54.2 us  [exchange(): pl.pallas_call(functools.partial(_exchange_kernel, sizes, group, gather,...]
    all_gather x1 -> x2, waiting for transfers between devices: 0.01 us -> 21.8 us  [the longest x1 21.8 us: local(): joined = lax.all_gather(joined, 'batch', axis=0)]
    all_to_all x2 -> x1, waiting for transfers between devices: 17.2 us -> 0.01 us  [to_channels(): x = lax.all_to_all(x, 'ch', 0, 0, tiled=True)]
    unnamed x53 -> x66, local copies, waits for them, and re-layouts: 17.7 us -> 20.4 us
  transfers between devices with their start and end apart: 21 -> 21, of which waited for: 8 -> 9; matrix products, arithmetic and copies ran while one was open for 38% -> 36% of each run, Pallas kernels for 10% -> 0%
where the time goes in v10:
time: 595 us; the launch traced here: 583 us
  waiting for transfers between devices  176 us (30%)
  matrix products  118 us (20%)
  local copies, waits for them, and re-layouts  97.3 us (16%)
  other arithmetic  61.8 us (10%)
  Pallas kernels  54.2 us (9%)
  blocking collectives  35.9 us (6%)
  starting transfers between devices  24.9 us (4%)
  between operations  15.3 us (3%)
    reduce_scatter x3, waiting for transfers between devices, reduce_seq_batch(): return lax.psum_scatter(g, 'batch', scatter_dimension=split_dim, tiled=True)  86.7 us
    pallas_call x2, Pallas kernels, exchange(): pl.pallas_call(functools.partial(_exchange_kernel, sizes, group, gather,...  54.2 us
    all_to_all x1, blocking collectives, to_channels(): x = lax.all_to_all(x, 'ch', 0, 0, tiled=True)  35.9 us
    all_to_all x2, waiting for transfers between devices, to_positions(): x = lax.all_to_all(x, 'ch', 0, 0, tiled=True)  30 us
    all_gather x1, waiting for transfers between devices, local(): joined = lax.all_gather(joined, 'batch', axis=0)  21.8 us
    unnamed x66, local copies, waits for them, and re-layouts  20.4 us
    dot_general x1, matrix products, local(): jnp.einsum('dh,rhl->rdl', w_in, grad_inner, preferred_element_type=jnp.fl...  20.2 us
    dot_general x1, matrix products, local(): jnp.einsum('dh,rdl->rhl', w_in, hidden0, preferred_element_type=jnp.float32)  16.8 us
  transfers between devices with their start and end apart: 21, of which 9 were waited for; matrix products, arithmetic and copies ran while one was open for 36% of the time, Pallas kernels for 0%

profile of v10, /device:TPU:0, one launch (start us, length us, event | category | flops | bytes accessed | tf_op | source)
XLA Modules:
  0.0 583.1 jit_solution(11793439510524187596)
XLA Ops:
  12.1 23.3 %shard_map.254 = (f32[4,1920]{1,0:T(4,128)}, bf16[4,160,640]{2,1,0:T(8,128)(2,1)}, bf16[4,80,1280]{2,1,0:T(8,128)(2,1)}) custom-call(f32[1920]{0:T(1024)} %concatenate.46.refs_0_, bf16[160,640]{1,0:T(8,128)(2,1)} %constant_dynamic-slice_fusion.2.refs_1_, bf16[80,1280]{1,0:T(8,128)(2,1)} %constant_dynamic-slice_fusion.1.refs_2_), custom_call_target="tpu_custom_call" | custom-call | bytes 3338240 | tf_op jit(solution)/shard_map/pallas_call | solution.py:87
  37.0 4.7 all-to-all-start
  48.2 30.0 %all-to-all-done = bf16[4,320,1024]{2,1,0:T(8,128)(2,1)} async-done(((bf16[4,320,1024]{2,1,0:T(8,128)(2,1)}), bf16[4,320,1024]{2,1,0:T(8,128)(2,1)}, u32[]{:S(2)}, u32[]{:S(2)}) %all-to-all-start) | async-done | bytes 2621472 | tf_op jit(solution)/shard_map/all_to_all | solution.py:172
  78.2 4.6 all-to-all-start.2
  82.8 2.5 convert_reduce_fusion
  85.3 2.5 multiply_reduce_fusion.2
  87.8 4.7 convert_element_type.151
  92.5 16.8 %fusion.83 = (f32[1024]{0:T(1024)S(1)}, f32[1024,640]{1,0:T(8,128)S(1)}) fusion(f32[640]{0:T(1024)S(1)} %add.198, bf16[1280,640]{1,0:T(8,128)(2,1)} %bitcast.281, f32[1280]{0:T(1024)S(1)} %add.195, f32[1280]{0:T(1024)S(1)} %mul.438, f32[1024]{0:T(1024)S(1)} %add_rsqrt_fusion.2, f32[1,1280,1,1,1,1,1024]{6,1,5,4,3,2,0:T(8,128)} %bitcast.266, ...), kind=kOutput, calls=%fused_computation.160 | convolution fusion | flops 1769470976 | bytes 9527808 | tf_op jit(solution)/shard_map/dh,rdl->rhl/dot_general | solution.py:261
  109.8 12.2 %all-gather.18.cloned.1.call-done = bf16[20,80,640]{2,1,0:T(8,128)(2,1)} async-done(((bf16[5,80,640]{2,1,0:T(8,128)(2,1)}), bf16[20,80,640]{2,1,0:T(8,128)(2,1)}) %all-gather.18.cloned.1.call-update) | async-done | bytes 2048016 | tf_op jit(solution)/shard_map/all_gather | solution.py:235
  122.1 7.3 %multiply_convert_fusion.1 = bf16[1,640,1024]{1,2,0:T(8,128)(2,1)S(1)} fusion(f32[640]{0:T(1024)S(1)} %add.202, f32[640]{0:T(1024)S(1)} %mul.448, f32[1024]{0:T(1024)S(1)} %add_rsqrt_fusion.1, f32[1024]{0:T(1024)S(1)} %broadcast_multiply_fusion.5, f32[640]{0:T(1024)S(1)} %add.198, f32[1024,640]{1,0:T(8,128)S(1)} %get-tuple-element.119), kind=kLoop, calls=%fused_computation.142 | loop fusion | flops 45875200 | bytes 3948032 | tf_op jit(solution)/shard_map/convert_element_type | solution.py:263
  135.8 8.0 %constant_dynamic-update-slice_fusion = bf16[1,3200,1024]{1,2,0:T(8,128)(2,1)} fusion(bf16[1,3200,1024]{1,2,0:T(8,128)(2,1)} %fusion.110, f32[640]{0:T(1024)S(1)} %add.202, f32[640]{0:T(1024)S(1)} %mul.448, f32[1024]{0:T(1024)S(1)} %add_rsqrt_fusion.1, f32[1024]{0:T(1024)S(1)} %broadcast_multiply_fusion.5, f32[640]{0:T(1024)S(1)} %add.198, ...), kind=kLoop, calls=%fused_computation.215 | loop fusion | flops 45875200 | bytes 3948032
  146.7 2.6 copy.64
  149.3 9.4 %fusion.85 = (f32[1024]{0:T(1024)S(1)}, f32[1024,640]{1,0:T(8,128)S(1)}) fusion(f32[640]{0:T(1024)S(1)} %add.205, bf16[3200,640]{1,0:T(8,128)(2,1)S(1)} %bitcast.268, bf16[1,3200,1024]{1,2,0:T(8,128)(2,1)} %fusion.108), kind=kOutput, calls=%fused_computation.162 | convolution fusion | flops 4195613696 | bytes 13277696 | tf_op jit(solution)/shard_map/co,rcl->rol/dot_general | solution.py:267
  159.3 11.8 %fusion.178 = f32[640,1280]{1,0:T(8,128)} fusion(bf16[1280,1024]{1,0:T(8,128)(2,1)} %bitcast.20, f32[640]{0:T(1024)S(1)} %add.209, f32[640]{0:T(1024)S(1)} %mul.458, f32[1024]{0:T(1024)S(1)} %add_rsqrt_fusion, f32[1024]{0:T(1024)S(1)} %broadcast_multiply_fusion.4, f32[640]{0:T(1024)S(1)} %add.205, f32[1024,640]{1,0:T(8,128)S(1)} %get-tuple-element.121), kind=kOutput, calls=%fused_computation.305 | convolution fusion | flops 1723596800 | bytes 8535552 | tf_op jit(solution)/shard_map/rhl,rdl->hd/dot_general | solution.py:274
  171.1 4.5 reshape.1422
  177.4 9.5 %copy.73 = bf16[1,3200,1024]{2,1,0:T(8,128)(2,1)} copy(bf16[1,3200,1024]{1,2,0:T(8,128)(2,1)} %fusion.108) | data formatting | bytes 13107200 | tf_op jit(solution)/shard_map/concatenate | solution.py:164
  187.1 12.5 %all-gather.12.cloned.1.call-done = bf16[4,160,1280]{2,1,0:T(8,128)(2,1)} async-done(((bf16[4,80,1280]{2,1,0:T(8,128)(2,1)}), bf16[4,160,1280]{2,1,0:T(8,128)(2,1)}) %all-gather.12.cloned.1.call-update) | async-done | bytes 1638416 | tf_op jit(solution)/shard_map/all_gather | solution.py:245
  199.6 12.0 %fusion.60 = (f32[640]{0:T(1024)S(1)}, f32[1024]{0:T(1024)S(1)}, f32[1024]{0:T(1024)S(1)}, f32[640]{0:T(1024)S(1)}, f32[1,640,1024]{1,2,0:T(8,128)S(1)}) fusion(f32[1024]{0:T(1024)S(1)} %add_rsqrt_fusion, f32[1024]{0:T(1024)S(1)} %broadcast_multiply_fusion.4, f32[640]{0:T(1024)S(1)} %add.205, f32[1024,640]{1,0:T(8,128)S(1)} %get-tuple-element.121, ...), kind=kOutput, calls=%fused_computation.111 | convolution fusion | flops 1732113152 | bytes 9531904 | tf_op jit(solution)/shard_map/hd,rdl->rhl/dot_general | solution.py:282
  211.6 2.6 convert_reduce_fusion.1
  215.2 7.1 %fusion.112 = f32[640,25,128]{2,0,1:T(8,128)} fusion(bf16[25,128,1024]{2,1,0:T(8,128)(2,1)S(1)} %bitcast.274, bf16[1,640,1024]{1,2,0:T(8,128)(2,1)S(1)} %get-tuple-element.93), kind=kOutput, calls=%fused_computation.201 | convolution fusion | flops 4194304000 | bytes 16056320 | tf_op jit(solution)/shard_map/rol,rkcil->okci/dot_general | solution.py:288
  222.3 17.0 %reduce-scatter.9.cloned.1.call-done.refs_0_ = f32[4,200,128]{2,1,0:T(8,128)} async-done(((f32[4,800,128]{2,1,0:T(8,128)}), f32[4,200,128]{2,1,0:T(8,128)}) %reduce-scatter.9.cloned.1.call-update) | async-done | bytes 409616 | tf_op jit(solution)/shard_map/reduce_scatter | solution.py:279
  240.7 2.2 convert_reduce_fusion.3
  242.9 6.4 %copy.65 = f32[1,1280,1024]{1,2,0:T(8,128)} copy(f32[1,1280,1024]{2,1,0:T(8,128)} %bitcast.267) | data formatting | bytes 10485760 | tf_op jit(solution)/shard_map/convert_element_type | solution.py:258
  249.3 8.3 %copy.70 = bf16[5,640,640]{2,1,0:T(8,128)(2,1)} copy(bf16[5,640,640]{1,2,0:T(8,128)(2,1)} %bitcast.269) | data formatting | bytes 8192000 | tf_op jit(solution)/shard_map/transpose | solution.py:296
  257.9 2.7 collective-permute-start.5
  264.4 13.5 %fusion.66 = (f32[640]{0:T(1024)S(1)}, f32[1024]{0:T(1024)S(1)}, f32[1024]{0:T(1024)S(1)}, f32[640]{0:T(1024)S(1)}, f32[1,640,1024]{1,2,0:T(8,128)}) fusion(f32[1024]{0:T(1024)S(1)} %add_rsqrt_fusion.1, f32[1024]{0:T(1024)S(1)} %broadcast_multiply_fusion.5, f32[640]{0:T(1024)S(1)} %add.198, f32[1024,640]{1,0:T(8,128)S(1)} %copy-done.3, f32[640]{0:T(1024)S(1)} %mul.448, ...), kind=kOutput, calls=%fused_computation.122 | convolution fusion | flops 4248695808 | bytes 15921664 | tf_op jit(solution)/shard_map/oc,rol->rcl/dot_general | solution.py:297
  279.6 2.4 fusion.65
  283.4 20.2 %multiply_reduce_fusion = (f32[1280]{0:T(1024)S(1)}, f32[1024]{0:T(1024)}, f32[1024]{0:T(1024)}, f32[1280]{0:T(1024)S(1)}, f32[1,1280,1024]{1,2,0:T(8,128)}) fusion(f32[1,1280,1024]{1,2,0:T(8,128)} %copy.65, f32[1024]{0:T(1024)S(1)} %broadcast_multiply_fusion.8, f32[1024]{0:T(1024)S(1)} %add_rsqrt_fusion.2, f32[1280]{0:T(1024)S(1)} %mul.438, ...), kind=kOutput, calls=%fused_computation.25 | convolution fusion | flops 1785196032 | bytes 13471744 | tf_op jit(solution)/shard_map/dh,rhl->rdl/dot_general | solution.py:305
  304.0 15.3 %fusion.79 = f32[4,320,640]{2,1,0:T(8,128)S(1)} fusion(bf16[4,320,1024]{2,1,0:T(8,128)(2,1)} %all-to-all-done, f32[4,320]{1,0:T(4,128)S(1)} %copy-done.23, f32[4,320]{1,0:T(4,128)S(1)} %copy-done.21, f32[1024]{0:T(1024)S(1)} %add_rsqrt_fusion.2, f32[1024]{0:T(1024)S(1)} %broadcast_multiply_fusion.8, bf16[1,640,1024]{1,2,0:T(8,128)(2,1)S(1)} %copy-done.12), kind=kOutput, calls=%fused_computation.156 | convolution fusion | flops 1769472000 | bytes 7227392 | tf_op jit(solution)/shard_map/rdl,rhl->dh/dot_general | solution.py:304
  321.5 4.7 reshape.1435
  326.1 26.6 %reduce-scatter.13.cloned.1.call-done = f32[80,25,128]{2,0,1:T(8,128)} async-done(((f32[320,25,128]{2,0,1:T(8,128)}), f32[80,25,128]{2,0,1:T(8,128)}) %reduce-scatter.13.cloned.1.call-update) | async-done | bytes 1024016 | tf_op jit(solution)/shard_map/reduce_scatter | solution.py:279
  355.6 12.4 %reduce-scatter.15.cloned.1.call-done = f32[4,960,128]{2,1,0:T(8,128)} async-done(((f32[4,1920,128]{2,1,0:T(8,128)}), f32[4,960,128]{2,1,0:T(8,128)}) %reduce-scatter.15.cloned.1.call-update) | async-done | bytes 1966096 | tf_op jit(solution)/shard_map/reduce_scatter | solution.py:278
  369.8 43.1 %reduce-scatter.17.cloned.1.call-done.refs_2_ = f32[4,240,128]{2,1,0:T(8,128)} async-done(((f32[4,960,128]{2,1,0:T(8,128)}), f32[4,240,128]{2,1,0:T(8,128)}) %reduce-scatter.17.cloned.1.call-update) | async-done | bytes 491536 | tf_op jit(solution)/shard_map/reduce_scatter | solution.py:279
  412.9 30.9 %shard_map.255 = (f32[3,200,128]{2,1,0:T(8,128)}, f32[80,5,3,160]{3,2,1,0:T(4,128)}, f32[3,240,128]{2,1,0:T(8,128)}) custom-call(f32[4,200,128]{2,1,0:T(8,128)} %reduce-scatter.9.cloned.1.call-done.refs_0_, f32[80,5,4,160]{3,2,1,0:T(4,128)} %copy-done.9, f32[4,240,128]{2,1,0:T(8,128)} %reduce-scatter.17.cloned.1.call-done.refs_2_), custom_call_target="tpu_custom_call" | custom-call | bytes 3850240 | tf_op jit(solution)/shard_map/pallas_call | solution.py:87
  447.1 2.6 reduce_sum.245
  454.6 11.7 %fusion.15 = bf16[1,1280,1024]{1,2,0:T(8,128)(2,1)} fusion(f32[1,1280,1024]{1,2,0:T(8,128)} %copy.65, bf16[640,1280]{1,0:T(8,128)(2,1)} %bitcast.284, f32[1280]{0:T(1024)S(1)} %add.213, f32[640]{0:T(1024)S(1)} %copy-done.27, f32[640]{0:T(1024)S(1)} %copy-done.25, f32[1024]{0:T(1024)S(1)} %add_rsqrt_fusion, f32[1024]{0:T(1024)S(1)} %broadcast_multiply_fusion.4, ...), kind=kOutput, calls=%fused_computation.19 | convolution fusion | flops 1727528960 | bytes 12145152 | tf_op jit(solution)/shard_map/hd,rhl->rdl/dot_general | solution.py:270
  466.3 4.4 copy.66
  470.6 4.6 all-to-all-start.1
  475.3 21.8 %all-gather.14.cloned.1.call-done = f32[4,944,128]{2,1,0:T(8,128)} async-done(((f32[1,944,128]{2,1,0:T(8,128)}), f32[4,944,128]{2,1,0:T(8,128)}) %all-gather.14.cloned.1.call-update) | async-done | bytes 1933328 | tf_op jit(solution)/shard_map/all_gather | solution.py:345
  497.1 4.9 copy.71
  502.0 8.4 %add_convert_fusion = bf16[1,1280,1024]{1,2,0:T(8,128)(2,1)S(1)} fusion(f32[1,1280,1024]{1,2,0:T(8,128)} %copy.71, f32[1,1280,1024]{1,2,0:T(8,128)} %get-tuple-element.124, f32[1,1280,1024]{1,2,0:T(8,128)} %copy.65, f32[1024]{0:T(1024)S(1)} %broadcast_multiply_fusion.6, f32[1024]{0:T(1024)S(1)} %broadcast_multiply_fusion.7, f32[1280]{0:T(1024)S(1)} %copy-done.18, ...), kind=kLoop, calls=%fused_computation.40 | loop fusion | flops 11796480 | bytes 18371584 | tf_op jit(solution)/shard_map/convert_element_type | solution.py:309
  510.4 2.6 copy.72
  513.0 35.9 %all_to_all.20 = bf16[4,320,1024]{2,1,0:T(8,128)(2,1)} all-to-all(bf16[4,320,1024]{2,1,0:T(8,128)(2,1)} %bitcast.273), channel_id=1, replica_groups=mesh['batch'=4,'seq'=2,'ch'=4] {'ch'}, dimensions={0} | all-to-all | bytes 5242880 | tf_op jit(solution)/shard_map/all_to_all | solution.py:185
  549.0 3.3 copy.87
  558.7 2.3 reshape_reshape.15
  561.0 4.6 reshape_reshape.14
  565.6 5.1 copy.77
  570.7 3.6 copy.102
  (182 shorter events, 57.9 us)
Async XLA Ops:
  7.2 38.6 %copy-start = (bf16[5,160,640]{2,1,0:T(8,128)(2,1)S(1)}, bf16[5,160,640]{2,1,0:T(8,128)(2,1)}, u32[]{:S(2)}) copy-start(bf16[5,160,640]{2,1,0:T(8,128)(2,1)} %param.23) | copy-start | bytes 3072004
  7.2 85.3 %all-gather.8.cloned.1.call-start = ((), (), s32[]{:S(2)}) async-start(), calls=%async_computation.10 | async-start | bytes 2457600 | tf_op jit(solution)/shard_map/all_gather | solution.py:243
  37.0 9.6 %copy-start.15 = (f32[1920]{0:T(1024)S(1)}, f32[1920]{0:T(1024)}, u32[]{:S(2)}) copy-start(f32[1920]{0:T(1024)} %concatenate.46.refs_0_) | copy-start | bytes 23044
  37.0 9.6 %copy-start.16 = (f32[4,1920]{1,0:T(4,128)S(1)}, f32[4,1920]{1,0:T(4,128)}, u32[]{:S(2)}) copy-start(f32[4,1920]{1,0:T(4,128)} %get-tuple-element.23) | copy-start | bytes 92164
  37.0 41.2 %all-to-all-start = ((bf16[4,320,1024]{2,1,0:T(8,128)(2,1)}), bf16[4,320,1024]{2,1,0:T(8,128)(2,1)}, u32[]{:S(2)}, u32[]{:S(2)}) async-start(bf16[4,320,1024]{2,1,0:T(8,128)(2,1)} %param.15), calls=%async_computation | async-start | bytes 5242880 | tf_op jit(solution)/shard_map/all_to_all | solution.py:172
  41.7 80.3 %all-gather.18.cloned.1.call-start = ((), (), s32[]{:S(2)}) async-start(), calls=%async_computation.21 | async-start | bytes 2560000 | tf_op jit(solution)/shard_map/all_gather | solution.py:235
  42.6 88.8 %collective-permute-start = (s32[1,64]{1,0:T(1,128)S(1)}, s32[1,64]{1,0:T(1,128)S(1)}, u32[]{:S(2)}, u32[]{:S(2)}) collective-permute-start(s32[1,64]{1,0:T(1,128)S(1)} %get-tuple-element.116), channel_id=1, source_target_pairs={{0,4},{1,5},{2,6},{3,7},{8,12},{9,13},{10,14},{11,15},{16,20},{17,... | collective-permute-start | bytes 776 | tf_op jit(solution)/shard_map/ppermute | solution.py:151
  44.4 86.9 %collective-permute-start.2 = (s32[1,64]{1,0:T(1,128)S(1)}, s32[1,64]{1,0:T(1,128)S(1)}, u32[]{:S(2)}, u32[]{:S(2)}) collective-permute-start(s32[1,64]{1,0:T(1,128)S(1)} %get-tuple-element.117), channel_id=1, source_target_pairs={{4,0},{5,1},{6,2},{7,3},{12,8},{13,9},{14,10},{15,11},{20,16},{21,... | collective-permute-start | bytes 776 | tf_op jit(solution)/shard_map/ppermute | solution.py:152
  47.1 164.5 %copy-start.24 = (f32[640]{0:T(1024)}, f32[640]{0:T(1024)S(1)}, u32[]{:S(2)}) copy-start(f32[640]{0:T(1024)S(1)} %mul.458) | copy-start | bytes 7684
  47.3 152.3 %copy-start.26 = (f32[640]{0:T(1024)}, f32[640]{0:T(1024)S(1)}, u32[]{:S(2)}) copy-start(f32[640]{0:T(1024)S(1)} %add.209) | copy-start | bytes 7684
  48.0 30.2 %copy-start.20 = (f32[4,320]{1,0:T(4,128)}, f32[4,320]{1,0:T(4,128)S(1)}, u32[]{:S(2)}) copy-start(f32[4,320]{1,0:T(4,128)S(1)} %get-tuple-element.104) | copy-start | bytes 15364
  48.0 30.2 %copy-start.22 = (f32[4,320]{1,0:T(4,128)}, f32[4,320]{1,0:T(4,128)S(1)}, u32[]{:S(2)}) copy-start(f32[4,320]{1,0:T(4,128)S(1)} %get-tuple-element.106) | copy-start | bytes 15364
  48.1 235.3 %copy-start.17 = (f32[1280]{0:T(1024)}, f32[1280]{0:T(1024)S(1)}, u32[]{:S(2)}) copy-start(f32[1280]{0:T(1024)S(1)} %mul.438) | copy-start | bytes 15364
  78.2 81.2 %all-to-all-start.2 = ((bf16[4,320,1024]{2,1,0:T(8,128)(2,1)}), bf16[4,320,1024]{2,1,0:T(8,128)(2,1)}, u32[]{:S(2)}, u32[]{:S(2)}) async-start(bf16[4,320,1024]{2,1,0:T(8,128)(2,1)} %param.29), calls=%async_computation.2 | async-start | bytes 5242880 | tf_op jit(solution)/shard_map/all_to_all | solution.py:172
  82.7 63.9 %all-gather.10.cloned.1.call-start = ((), (), s32[]{:S(2)}) async-start(), calls=%async_computation.11 | async-start | bytes 6144000 | tf_op jit(solution)/shard_map/all_gather | solution.py:244
  109.3 26.5 %copy-start.2 = (f32[1024,640]{1,0:T(8,128)}, f32[1024,640]{1,0:T(8,128)S(1)}, u32[]{:S(2)}) copy-start(f32[1024,640]{1,0:T(8,128)S(1)} %get-tuple-element.119) | copy-start | bytes 7864324
  122.0 65.0 %reduce-scatter.7.cloned.1.call-start = ((), (), s32[]{:S(2)}) async-start(), calls=%async_computation.13 | async-start | bytes 4915200 | tf_op jit(solution)/shard_map/reduce_scatter | solution.py:278
  129.4 3.4 collective-permute-start.1
  131.5 12.3 %collective-permute-start.3 = (bf16[1,640,64]{1,2,0:T(8,128)(2,1)S(1)}, bf16[1,640,64]{1,2,0:T(8,128)(2,1)S(1)}, u32[]{:S(2)}, u32[]{:S(2)}) collective-permute-start(bf16[1,640,64]{1,2,0:T(8,128)(2,1)S(1)} %get-tuple-element.96), channel_id=1, source_target_pairs={{4,0},{5,1},{6,2},{7,3},{12,8},{13,9},{14,10},{15,11},{20,16},{21,... | collective-permute-start | bytes 245768 | tf_op jit(solution)/shard_map/ppermute | solution.py:152
  149.3 9.4 %copy-start.5 = (bf16[5,4,160,640]{3,2,1,0:T(8,128)(2,1)}, bf16[5,4,160,640]{3,2,1,0:T(8,128)(2,1)S(1)}, u32[]{:S(2)}) copy-start(bf16[5,4,160,640]{3,2,1,0:T(8,128)(2,1)S(1)} %copy.64) | copy-start | bytes 12288004
  158.8 40.8 %copy-start.6 = (f32[1024,640]{1,0:T(8,128)}, f32[1024,640]{1,0:T(8,128)S(1)}, u32[]{:S(2)}) copy-start(f32[1024,640]{1,0:T(8,128)S(1)} %get-tuple-element.121) | copy-start | bytes 7864324
  175.7 23.9 %all-gather.12.cloned.1.call-start = ((), (), s32[]{:S(2)}) async-start(), calls=%async_computation.12 | async-start | bytes 2457600 | tf_op jit(solution)/shard_map/all_gather | solution.py:245
  177.4 62.0 %reduce-scatter.9.cloned.1.call-start = ((), (), s32[]{:S(2)}) async-start(), calls=%async_computation.14 | async-start | bytes 2048000 | tf_op jit(solution)/shard_map/reduce_scatter | solution.py:279
  187.0 91.0 %reduce-scatter.11.cloned.1.call-start = ((), (), s32[]{:S(2)}) async-start(), calls=%async_computation.15 | async-start | bytes 12288000 | tf_op jit(solution)/shard_map/reduce_scatter | solution.py:278
  211.6 3.6 copy-start.10
  239.4 113.3 %reduce-scatter.13.cloned.1.call-start = ((), (), s32[]{:S(2)}) async-start(), calls=%async_computation.16 | async-start | bytes 5120000 | tf_op jit(solution)/shard_map/reduce_scatter | solution.py:279
  239.4 21.1 %collective-permute-start.4 = (bf16[1,640,64]{1,2,0:T(8,128)(2,1)S(1)}, bf16[1,640,64]{1,2,0:T(8,128)(2,1)S(1)}, u32[]{:S(2)}, u32[]{:S(2)}) collective-permute-start(bf16[1,640,64]{1,2,0:T(8,128)(2,1)S(1)} %get-tuple-element.95), channel_id=1, source_target_pairs={{4,0},{5,1},{6,2},{7,3},{12,8},{13,9},{14,10},{15,11},{20,16},{21,... | collective-permute-start | bytes 245768 | tf_op jit(solution)/shard_map/ppermute | solution.py:152
  257.9 3.7 collective-permute-start.5
  261.3 2.2 copy-start.13
  261.5 2.8 copy-start.3
  278.1 89.9 %reduce-scatter.15.cloned.1.call-start = ((), (), s32[]{:S(2)}) async-start(), calls=%async_computation.17 | async-start | bytes 5898240 | tf_op jit(solution)/shard_map/reduce_scatter | solution.py:278
  283.4 20.6 %copy-start.12 = (bf16[1,640,1024]{1,2,0:T(8,128)(2,1)S(1)}, bf16[1,640,1024]{1,2,0:T(8,128)(2,1)}, u32[]{:S(2)}) copy-start(bf16[1,640,1024]{1,2,0:T(8,128)(2,1)} %copy-done.11) | copy-start | bytes 3932164
  283.4 20.6 %copy-start.21 = (f32[4,320]{1,0:T(4,128)S(1)}, f32[4,320]{1,0:T(4,128)}, u32[]{:S(2)}) copy-start(f32[4,320]{1,0:T(4,128)} %copy-done.20) | copy-start | bytes 15364
  283.4 20.6 %copy-start.23 = (f32[4,320]{1,0:T(4,128)S(1)}, f32[4,320]{1,0:T(4,128)}, u32[]{:S(2)}) copy-start(f32[4,320]{1,0:T(4,128)} %copy-done.22) | copy-start | bytes 15364
  355.5 12.8 %copy-start.9 = (f32[80,5,4,160]{3,2,1,0:T(4,128)}, f32[80,5,4,160]{3,2,1,0:T(4,128)S(1)}, u32[]{:S(2)}) copy-start(f32[80,5,4,160]{3,2,1,0:T(4,128)S(1)} %reshape.1425.refs_1_) | copy-start | bytes 3072004
  355.5 57.4 %reduce-scatter.17.cloned.1.call-start = ((), (), s32[]{:S(2)}) async-start(), calls=%async_computation.18 | async-start | bytes 2457600 | tf_op jit(solution)/shard_map/reduce_scatter | solution.py:279
  368.0 129.0 %all-gather.14.cloned.1.call-start = ((), (), s32[]{:S(2)}) async-start(), calls=%async_computation.19 | async-start | bytes 2416640 | tf_op jit(solution)/shard_map/all_gather | solution.py:345
  447.1 7.4 %copy-start.7 = (f32[1024,640]{1,0:T(8,128)S(1)}, f32[1024,640]{1,0:T(8,128)}, u32[]{:S(2)}) copy-start(f32[1024,640]{1,0:T(8,128)} %copy-done.6) | copy-start | bytes 7864324
  450.7 3.8 copy-start.19
  450.7 3.9 copy-start.25
  450.7 3.9 copy-start.27
  470.6 42.4 %all-to-all-start.1 = ((bf16[4,320,1024]{2,1,0:T(8,128)(2,1)}), bf16[4,320,1024]{2,1,0:T(8,128)(2,1)}, u32[]{:S(2)}, u32[]{:S(2)}) async-start(bf16[4,320,1024]{2,1,0:T(8,128)(2,1)} %bitcast.18), calls=%async_computation.1 | async-start | bytes 5242880 | tf_op jit(solution)/shard_map/all_to_all | solution.py:185
  475.2 73.8 %all-gather.16.cloned.1.call-start = ((), (), s32[]{:S(2)}) async-start(), calls=%async_computation.20 | async-start | bytes 5799936 | tf_op jit(solution)/shard_map/all_gather | solution.py:346
  497.1 4.9 copy-start.29
  497.1 4.9 copy-start.28
  497.1 4.9 copy-start.18
  570.7 3.6 copy-start.8
  570.7 5.1 copy-start.1
  (3 other events, 3.8 us)
Sparse Core Ops, SparseCore 0:
  37.1 11.0 all-gather.7
  50.6 71.3 all-gather.17
  123.5 12.9 all-gather.9
  175.8 11.1 reduce-scatter.6
  188.5 11.0 all-gather.11
  201.8 37.4 reduce-scatter.8
  241.7 15.6 reduce-scatter.10
  278.2 74.4 reduce-scatter.12
  355.7 12.2 reduce-scatter.14
  370.3 42.5 reduce-scatter.16
  454.6 42.4 all-gather.13
  498.5 12.0 all-gather.15

commit v11 on v10

--- a/solution.py
+++ b/solution.py
@@ -269,6 +269,7 @@
     hidden2 = gelu_exact(normed2).astype(jnp.bfloat16)
     branch = jnp.einsum("hd,rhl->rdl", w_out, hidden2, preferred_element_type=jnp.float32)
     output = (residual + branch + b_out[:, None]).astype(jnp.bfloat16)
+    output = to_channels(output, nch, q_count, rows)
 
     grad_b_outer = jnp.sum(cot.astype(jnp.float32), axis=(0, 2))
     grad_w_outer = jnp.einsum("rhl,rdl->hd", hidden2, cot, preferred_element_type=jnp.float32)
@@ -299,7 +300,7 @@
     grad_norm1_gain = jnp.sum(grad_normed1 * unit1, axis=(0, 2))
     grad_norm1_shift = jnp.sum(grad_normed1, axis=(0, 2))
     grad_inner = normalize_back(grad_normed1, unit1, scale1, g1).astype(jnp.bfloat16)
-    grad_inner, _ = lax.optimization_barrier((grad_inner, part_outer))
+    grad_inner, _, output = lax.optimization_barrier((grad_inner, part_outer, output))
     grad_b_inner = jnp.sum(grad_inner.astype(jnp.float32), axis=(0, 2))
     grad_w_inner = jnp.einsum("rdl,rhl->dh", hidden0, grad_inner, preferred_element_type=jnp.float32)
     grad_hidden0 = jnp.einsum("dh,rhl->rdl", w_in, grad_inner, preferred_element_type=jnp.float32)
@@ -308,7 +309,6 @@
     grad_norm0_shift = jnp.sum(grad_normed0, axis=(0, 2))
     input_grad = (cot.astype(jnp.float32) + normalize_back(grad_normed0, unit0, scale0, g0)).astype(jnp.bfloat16)
 
-    output = to_channels(output, nch, q_count, rows)
     input_grad = to_channels(input_grad, nch, q_count, rows)
 
     vectors = [

time: 595 us -> 612 us (1.029)
  waiting for transfers between devices: 176 us -> 227 us
  blocking collectives: 35.9 us -> 0 us
    all_to_all x1 -> x0, blocking collectives: 35.9 us -> none  [to_channels(): x = lax.all_to_all(x, 'ch', 0, 0, tiled=True)]
    all_to_all x1 -> x2, waiting for transfers between devices: 0.01 us -> 30.6 us  [to_channels(): x = lax.all_to_all(x, 'ch', 0, 0, tiled=True)]
    all_gather x1, waiting for transfers between devices: 21.8 us -> 42.5 us  [local(): joined = lax.all_gather(joined, 'batch', axis=0)]
    unnamed x66 -> x68, local copies, waits for them, and re-layouts: 20.4 us -> 22 us
  transfers between devices with their start and end apart: 21 -> 22, of which waited for: 9 -> 10; matrix products, arithmetic and copies ran while one was open for 36% -> 35% of each run, Pallas kernels for 0% -> 0%
where the time goes in v11:
time: 612 us; the launch traced here: 600 us
  waiting for transfers between devices  227 us (37%)
  matrix products  117 us (19%)
  local copies, waits for them, and re-layouts  96.1 us (16%)
  other arithmetic  60.1 us (10%)
  Pallas kernels  54.2 us (9%)
  starting transfers between devices  30.2 us (5%)
  between operations  15.1 us (2%)
    reduce_scatter x3, waiting for transfers between devices, reduce_seq_batch(): return lax.psum_scatter(g, 'batch', scatter_dimension=split_dim, tiled=True)  87.1 us
    pallas_call x2, Pallas kernels, exchange(): pl.pallas_call(functools.partial(_exchange_kernel, sizes, group, gather,...  54.2 us
    all_gather x1, waiting for transfers between devices, local(): joined = lax.all_gather(joined, 'batch', axis=0)  42.5 us
    all_to_all x2, waiting for transfers between devices, to_channels(): x = lax.all_to_all(x, 'ch', 0, 0, tiled=True)  30.6 us
    all_to_all x2, waiting for transfers between devices, to_positions(): x = lax.all_to_all(x, 'ch', 0, 0, tiled=True)  29.4 us
    unnamed x68, local copies, waits for them, and re-layouts  22 us
    dot_general x1, matrix products, local(): jnp.einsum('dh,rhl->rdl', w_in, grad_inner, preferred_element_type=jnp.fl...  19.5 us
    dot_general x1, matrix products, local(): jnp.einsum('dh,rdl->rhl', w_in, hidden0, preferred_element_type=jnp.float32)  16.8 us
  transfers between devices with their start and end apart: 22, of which 10 were waited for; matrix products, arithmetic and copies ran while one was open for 35% of the time, Pallas kernels for 0%

profile of v11, /device:TPU:0, one launch (start us, length us, event | category | flops | bytes accessed | tf_op | source)
XLA Modules:
  0.0 600.1 jit_solution(10862074600678423843)
XLA Ops:
  12.1 23.3 %shard_map.254 = (f32[4,1920]{1,0:T(4,128)}, bf16[4,160,640]{2,1,0:T(8,128)(2,1)}, bf16[4,80,1280]{2,1,0:T(8,128)(2,1)}) custom-call(f32[1920]{0:T(1024)} %concatenate.45.refs_0_, bf16[160,640]{1,0:T(8,128)(2,1)} %constant_dynamic-slice_fusion.2.refs_1_, bf16[80,1280]{1,0:T(8,128)(2,1)} %constant_dynamic-slice_fusion.1.refs_2_), custom_call_target="tpu_custom_call" | custom-call | bytes 3338240 | tf_op jit(solution)/shard_map/pallas_call | solution.py:87
  37.0 4.7 all-to-all-start
  43.9 3.0 collective-permute-start.1
  48.8 29.4 %all-to-all-done = bf16[4,320,1024]{2,1,0:T(8,128)(2,1)} async-done(((bf16[4,320,1024]{2,1,0:T(8,128)(2,1)}), bf16[4,320,1024]{2,1,0:T(8,128)(2,1)}, u32[]{:S(2)}, u32[]{:S(2)}) %all-to-all-start) | async-done | bytes 2621472 | tf_op jit(solution)/shard_map/all_to_all | solution.py:172
  78.2 4.6 all-to-all-start.1
  82.8 2.5 convert_reduce_fusion
  85.4 2.5 multiply_reduce_fusion.2
  87.9 4.7 convert_element_type.151
  92.6 16.8 %fusion.83 = (f32[1024]{0:T(1024)S(1)}, f32[1024,640]{1,0:T(8,128)S(1)}) fusion(f32[640]{0:T(1024)S(1)} %add.196, bf16[1280,640]{1,0:T(8,128)(2,1)} %bitcast.282, f32[1280]{0:T(1024)S(1)} %add.193, f32[1280]{0:T(1024)S(1)} %mul.438, f32[1024]{0:T(1024)S(1)} %add_rsqrt_fusion.2, f32[1,1280,1,1,1,1,1024]{6,1,5,4,3,2,0:T(8,128)} %bitcast.266, ...), kind=kOutput, calls=%fused_computation.160 | convolution fusion | flops 1769470976 | bytes 9527808 | tf_op jit(solution)/shard_map/dh,rdl->rhl/dot_general | solution.py:261
  109.9 12.1 %all-gather.18.cloned.1.call-done = bf16[20,80,640]{2,1,0:T(8,128)(2,1)} async-done(((bf16[5,80,640]{2,1,0:T(8,128)(2,1)}), bf16[20,80,640]{2,1,0:T(8,128)(2,1)}) %all-gather.18.cloned.1.call-update) | async-done | bytes 2048016 | tf_op jit(solution)/shard_map/all_gather | solution.py:235
  122.1 7.3 %multiply_convert_fusion.1 = bf16[1,640,1024]{1,2,0:T(8,128)(2,1)S(1)} fusion(f32[640]{0:T(1024)S(1)} %add.200, f32[640]{0:T(1024)S(1)} %mul.449, f32[1024]{0:T(1024)S(1)} %add_rsqrt_fusion.1, f32[1024]{0:T(1024)S(1)} %broadcast_multiply_fusion.5, f32[640]{0:T(1024)S(1)} %add.196, f32[1024,640]{1,0:T(8,128)S(1)} %get-tuple-element.121), kind=kLoop, calls=%fused_computation.142 | loop fusion | flops 45875200 | bytes 3948032 | tf_op jit(solution)/shard_map/convert_element_type | solution.py:263
  135.8 8.0 %constant_dynamic-update-slice_fusion = bf16[1,3200,1024]{1,2,0:T(8,128)(2,1)} fusion(bf16[1,3200,1024]{1,2,0:T(8,128)(2,1)} %fusion.110, f32[640]{0:T(1024)S(1)} %add.200, f32[640]{0:T(1024)S(1)} %mul.449, f32[1024]{0:T(1024)S(1)} %add_rsqrt_fusion.1, f32[1024]{0:T(1024)S(1)} %broadcast_multiply_fusion.5, f32[640]{0:T(1024)S(1)} %add.196, ...), kind=kLoop, calls=%fused_computation.215 | loop fusion | flops 45875200 | bytes 3948032
  146.7 2.6 copy.64
  149.3 9.6 %fusion.85 = (f32[1024]{0:T(1024)S(1)}, f32[1024,640]{1,0:T(8,128)S(1)}) fusion(f32[640]{0:T(1024)S(1)} %add.205, bf16[3200,640]{1,0:T(8,128)(2,1)S(1)} %bitcast.268, bf16[1,3200,1024]{1,2,0:T(8,128)(2,1)} %fusion.108), kind=kOutput, calls=%fused_computation.162 | convolution fusion | flops 4195613696 | bytes 13277696 | tf_op jit(solution)/shard_map/co,rcl->rol/dot_general | solution.py:267
  159.6 11.8 %fusion.179 = f32[640,1280]{1,0:T(8,128)} fusion(bf16[1280,1024]{1,0:T(8,128)(2,1)} %bitcast.14, f32[640]{0:T(1024)S(1)} %add.209, f32[640]{0:T(1024)S(1)} %mul.460, f32[1024]{0:T(1024)S(1)} %add_rsqrt_fusion, f32[1024]{0:T(1024)S(1)} %broadcast_multiply_fusion.4, f32[640]{0:T(1024)S(1)} %add.205, f32[1024,640]{1,0:T(8,128)S(1)} %get-tuple-element.123), kind=kOutput, calls=%fused_computation.305 | convolution fusion | flops 1723596800 | bytes 8535552 | tf_op jit(solution)/shard_map/rhl,rdl->hd/dot_general | solution.py:275
  171.3 4.5 reshape.1422
  177.6 9.5 %copy.73 = bf16[1,3200,1024]{2,1,0:T(8,128)(2,1)} copy(bf16[1,3200,1024]{1,2,0:T(8,128)(2,1)} %fusion.108) | data formatting | bytes 13107200 | tf_op jit(solution)/shard_map/concatenate | solution.py:164
  187.2 12.5 %all-gather.12.cloned.1.call-done = bf16[4,160,1280]{2,1,0:T(8,128)(2,1)} async-done(((bf16[4,80,1280]{2,1,0:T(8,128)(2,1)}), bf16[4,160,1280]{2,1,0:T(8,128)(2,1)}) %all-gather.12.cloned.1.call-update) | async-done | bytes 1638416 | tf_op jit(solution)/shard_map/all_gather | solution.py:245
  199.7 11.7 %fusion.60 = (f32[640]{0:T(1024)S(1)}, f32[1024]{0:T(1024)S(1)}, f32[1024]{0:T(1024)S(1)}, f32[640]{0:T(1024)S(1)}, f32[1,640,1024]{1,2,0:T(8,128)S(1)}) fusion(f32[1024]{0:T(1024)S(1)} %add_rsqrt_fusion, f32[1024]{0:T(1024)S(1)} %broadcast_multiply_fusion.4, f32[640]{0:T(1024)S(1)} %add.205, f32[1024,640]{1,0:T(8,128)S(1)} %get-tuple-element.123, ...), kind=kOutput, calls=%fused_computation.111 | convolution fusion | flops 1732113152 | bytes 9531904 | tf_op jit(solution)/shard_map/hd,rdl->rhl/dot_general | solution.py:283
  211.5 2.6 convert_reduce_fusion.1
  215.1 7.1 %fusion.112 = f32[640,25,128]{2,0,1:T(8,128)} fusion(bf16[25,128,1024]{2,1,0:T(8,128)(2,1)S(1)} %bitcast.275, bf16[1,640,1024]{1,2,0:T(8,128)(2,1)S(1)} %get-tuple-element.95), kind=kOutput, calls=%fused_computation.201 | convolution fusion | flops 4194304000 | bytes 16056320 | tf_op jit(solution)/shard_map/rol,rkcil->okci/dot_general | solution.py:289
  222.2 17.3 %reduce-scatter.9.cloned.1.call-done.refs_0_ = f32[4,200,128]{2,1,0:T(8,128)} async-done(((f32[4,800,128]{2,1,0:T(8,128)}), f32[4,200,128]{2,1,0:T(8,128)}) %reduce-scatter.9.cloned.1.call-update) | async-done | bytes 409616 | tf_op jit(solution)/shard_map/reduce_scatter | solution.py:280
  239.6 6.0 copy.68
  245.6 3.0 convert_reduce_fusion.3
  249.9 12.3 %fusion.15 = bf16[1,1280,1024]{1,2,0:T(8,128)(2,1)} fusion(f32[1,1280,1024]{1,2,0:T(8,128)} %copy.68, bf16[640,1280]{1,0:T(8,128)(2,1)} %bitcast.285, f32[1280]{0:T(1024)S(1)} %add.213, f32[640]{0:T(1024)S(1)} %add.209, f32[640]{0:T(1024)S(1)} %mul.460, f32[1024]{0:T(1024)S(1)} %add_rsqrt_fusion, f32[1024]{0:T(1024)S(1)} %broadcast_multiply_fusion.4, ...), kind=kOutput, calls=%fused_computation.19 | convolution fusion | flops 1727528960 | bytes 12145152 | tf_op jit(solution)/shard_map/hd,rhl->rdl/dot_general | solution.py:270
  262.2 4.4 copy.69
  266.6 4.6 all-to-all-start.2
  271.2 3.2 collective-permute-start.5
  274.4 8.3 %copy.67 = bf16[5,640,640]{2,1,0:T(8,128)(2,1)} copy(bf16[5,640,640]{1,2,0:T(8,128)(2,1)} %bitcast.269) | data formatting | bytes 8192000 | tf_op jit(solution)/shard_map/transpose | solution.py:297
  286.7 13.3 %fusion.66 = (f32[640]{0:T(1024)S(1)}, f32[1024]{0:T(1024)S(1)}, f32[1024]{0:T(1024)S(1)}, f32[640]{0:T(1024)S(1)}, f32[1,640,1024]{1,2,0:T(8,128)}) fusion(f32[1024]{0:T(1024)S(1)} %add_rsqrt_fusion.1, f32[1024]{0:T(1024)S(1)} %broadcast_multiply_fusion.5, f32[640]{0:T(1024)S(1)} %add.196, f32[1024,640]{1,0:T(8,128)S(1)} %copy-done.3, f32[640]{0:T(1024)S(1)} %mul.449, ...), kind=kOutput, calls=%fused_computation.122 | convolution fusion | flops 4248695808 | bytes 15921664 | tf_op jit(solution)/shard_map/oc,rol->rcl/dot_general | solution.py:298
  301.7 3.2 fusion.65
  305.0 19.5 %multiply_reduce_fusion = (f32[1280]{0:T(1024)S(1)}, f32[1024]{0:T(1024)S(1)}, f32[1024]{0:T(1024)S(1)}, f32[1280]{0:T(1024)S(1)}, f32[1,1280,1024]{1,2,0:T(8,128)}) fusion(f32[1,1280,1024]{1,2,0:T(8,128)} %copy.68, f32[1024]{0:T(1024)S(1)} %copy-done.20, f32[1024]{0:T(1024)S(1)} %copy-done.28, f32[1280]{0:T(1024)S(1)} %copy-done.22, ...), kind=kOutput, calls=%fused_computation.25 | convolution fusion | flops 1785196032 | bytes 13471744 | tf_op jit(solution)/shard_map/dh,rhl->rdl/dot_general | solution.py:306
  325.2 15.3 %fusion.79 = f32[4,320,640]{2,1,0:T(8,128)S(1)} fusion(bf16[4,320,1024]{2,1,0:T(8,128)(2,1)} %all-to-all-done, f32[4,320]{1,0:T(4,128)S(1)} %copy-done.24, f32[4,320]{1,0:T(4,128)S(1)} %copy-done.26, f32[1024]{0:T(1024)S(1)} %copy-done.28, f32[1024]{0:T(1024)S(1)} %copy-done.20, bf16[1,640,1024]{1,2,0:T(8,128)(2,1)S(1)} %copy-done.13), kind=kOutput, calls=%fused_computation.156 | convolution fusion | flops 1769472000 | bytes 7227392 | tf_op jit(solution)/shard_map/rdl,rhl->dh/dot_general | solution.py:305
  342.7 4.7 reshape.1435
  347.4 26.7 %reduce-scatter.13.cloned.1.call-done = f32[80,25,128]{2,0,1:T(8,128)} async-done(((f32[320,25,128]{2,0,1:T(8,128)}), f32[80,25,128]{2,0,1:T(8,128)}) %reduce-scatter.13.cloned.1.call-update) | async-done | bytes 1024016 | tf_op jit(solution)/shard_map/reduce_scatter | solution.py:280
  377.0 12.4 %reduce-scatter.15.cloned.1.call-done = f32[4,960,128]{2,1,0:T(8,128)} async-done(((f32[4,1920,128]{2,1,0:T(8,128)}), f32[4,960,128]{2,1,0:T(8,128)}) %reduce-scatter.15.cloned.1.call-update) | async-done | bytes 1966096 | tf_op jit(solution)/shard_map/reduce_scatter | solution.py:279
  391.1 43.2 %reduce-scatter.17.cloned.1.call-done.refs_2_ = f32[4,240,128]{2,1,0:T(8,128)} async-done(((f32[4,960,128]{2,1,0:T(8,128)}), f32[4,240,128]{2,1,0:T(8,128)}) %reduce-scatter.17.cloned.1.call-update) | async-done | bytes 491536 | tf_op jit(solution)/shard_map/reduce_scatter | solution.py:280
  434.3 30.9 %shard_map.255 = (f32[3,200,128]{2,1,0:T(8,128)}, f32[80,5,3,160]{3,2,1,0:T(4,128)}, f32[3,240,128]{2,1,0:T(8,128)}) custom-call(f32[4,200,128]{2,1,0:T(8,128)} %reduce-scatter.9.cloned.1.call-done.refs_0_, f32[80,5,4,160]{3,2,1,0:T(4,128)} %copy-done.11, f32[4,240,128]{2,1,0:T(8,128)} %reduce-scatter.17.cloned.1.call-done.refs_2_), custom_call_target="tpu_custom_call" | custom-call | bytes 3850240 | tf_op jit(solution)/shard_map/pallas_call | solution.py:87
  471.8 42.5 %all-gather.14.cloned.1.call-done = f32[4,944,128]{2,1,0:T(8,128)} async-done(((f32[1,944,128]{2,1,0:T(8,128)}), f32[4,944,128]{2,1,0:T(8,128)}) %all-gather.14.cloned.1.call-update) | async-done | bytes 1933328 | tf_op jit(solution)/shard_map/all_gather | solution.py:345
  514.3 4.9 copy.71
  519.2 8.4 %add_convert_fusion = bf16[1,1280,1024]{1,2,0:T(8,128)(2,1)S(1)} fusion(f32[1,1280,1024]{1,2,0:T(8,128)} %copy.71, f32[1,1280,1024]{1,2,0:T(8,128)} %get-tuple-element.126, f32[1,1280,1024]{1,2,0:T(8,128)} %copy.68, f32[1024]{0:T(1024)S(1)} %broadcast_multiply_fusion.6, f32[1024]{0:T(1024)S(1)} %broadcast_multiply_fusion.7, f32[1280]{0:T(1024)S(1)} %copy-done.22, ...), kind=kLoop, calls=%fused_computation.40 | loop fusion | flops 11796480 | bytes 18371584 | tf_op jit(solution)/shard_map/convert_element_type | solution.py:310
  527.6 2.6 copy.72
  530.2 3.7 all-to-all-start.3
  533.9 30.6 %all-to-all-done.3 = bf16[4,320,1024]{2,1,0:T(8,128)(2,1)S(1)} async-done(((bf16[4,320,1024]{2,1,0:T(8,128)(2,1)}), bf16[4,320,1024]{2,1,0:T(8,128)(2,1)S(1)}, u32[]{:S(2)}, u32[]{:S(2)}) %all-to-all-start.3) | async-done | bytes 2621472 | tf_op jit(solution)/shard_map/all_to_all | solution.py:185
  564.5 4.3 copy.87
  577.1 4.6 reshape_reshape.14
  581.7 5.1 copy.77
  588.0 3.6 copy.102
  (185 shorter events, 55.9 us)
Async XLA Ops:
  7.2 39.8 %copy-start = (bf16[5,160,640]{2,1,0:T(8,128)(2,1)S(1)}, bf16[5,160,640]{2,1,0:T(8,128)(2,1)}, u32[]{:S(2)}) copy-start(bf16[5,160,640]{2,1,0:T(8,128)(2,1)} %param.23) | copy-start | bytes 3072004
  7.2 85.3 %all-gather.8.cloned.1.call-start = ((), (), s32[]{:S(2)}) async-start(), calls=%async_computation.10 | async-start | bytes 2457600 | tf_op jit(solution)/shard_map/all_gather | solution.py:243
  37.0 10.8 %copy-start.17 = (f32[1920]{0:T(1024)S(1)}, f32[1920]{0:T(1024)}, u32[]{:S(2)}) copy-start(f32[1920]{0:T(1024)} %concatenate.45.refs_0_) | copy-start | bytes 23044
  37.0 10.8 %copy-start.18 = (f32[4,1920]{1,0:T(4,128)S(1)}, f32[4,1920]{1,0:T(4,128)}, u32[]{:S(2)}) copy-start(f32[4,1920]{1,0:T(4,128)} %get-tuple-element.24) | copy-start | bytes 92164
  37.0 41.2 %all-to-all-start = ((bf16[4,320,1024]{2,1,0:T(8,128)(2,1)}), bf16[4,320,1024]{2,1,0:T(8,128)(2,1)}, u32[]{:S(2)}, u32[]{:S(2)}) async-start(bf16[4,320,1024]{2,1,0:T(8,128)(2,1)} %param.15), calls=%async_computation | async-start | bytes 5242880 | tf_op jit(solution)/shard_map/all_to_all | solution.py:172
  41.8 80.3 %all-gather.18.cloned.1.call-start = ((), (), s32[]{:S(2)}) async-start(), calls=%async_computation.21 | async-start | bytes 2560000 | tf_op jit(solution)/shard_map/all_gather | solution.py:235
  42.6 88.8 %collective-permute-start = (s32[1,64]{1,0:T(1,128)S(1)}, s32[1,64]{1,0:T(1,128)S(1)}, u32[]{:S(2)}, u32[]{:S(2)}) collective-permute-start(s32[1,64]{1,0:T(1,128)S(1)} %get-tuple-element.119), channel_id=1, source_target_pairs={{4,0},{5,1},{6,2},{7,3},{12,8},{13,9},{14,10},{15,11},{20,16},{21,... | collective-permute-start | bytes 776 | tf_op jit(solution)/shard_map/ppermute | solution.py:152
  43.9 87.5 %collective-permute-start.1 = (s32[1,64]{1,0:T(1,128)S(1)}, s32[1,64]{1,0:T(1,128)S(1)}, u32[]{:S(2)}, u32[]{:S(2)}) collective-permute-start(s32[1,64]{1,0:T(1,128)S(1)} %get-tuple-element.118), channel_id=1, source_target_pairs={{0,4},{1,5},{2,6},{3,7},{8,12},{9,13},{10,14},{11,15},{16,20},{17,... | collective-permute-start | bytes 776 | tf_op jit(solution)/shard_map/ppermute | solution.py:151
  48.2 30.0 %copy-start.23 = (f32[4,320]{1,0:T(4,128)}, f32[4,320]{1,0:T(4,128)S(1)}, u32[]{:S(2)}) copy-start(f32[4,320]{1,0:T(4,128)S(1)} %get-tuple-element.101) | copy-start | bytes 15364
  48.2 30.0 %copy-start.25 = (f32[4,320]{1,0:T(4,128)}, f32[4,320]{1,0:T(4,128)S(1)}, u32[]{:S(2)}) copy-start(f32[4,320]{1,0:T(4,128)S(1)} %get-tuple-element.102) | copy-start | bytes 15364
  48.3 44.3 %copy-start.21 = (f32[1280]{0:T(1024)}, f32[1280]{0:T(1024)S(1)}, u32[]{:S(2)}) copy-start(f32[1280]{0:T(1024)S(1)} %mul.438) | copy-start | bytes 15364
  48.4 44.2 %copy-start.29 = (f32[1280]{0:T(1024)}, f32[1280]{0:T(1024)S(1)}, u32[]{:S(2)}) copy-start(f32[1280]{0:T(1024)S(1)} %add.193) | copy-start | bytes 15364
  78.2 81.4 %all-to-all-start.1 = ((bf16[4,320,1024]{2,1,0:T(8,128)(2,1)}), bf16[4,320,1024]{2,1,0:T(8,128)(2,1)}, u32[]{:S(2)}, u32[]{:S(2)}) async-start(bf16[4,320,1024]{2,1,0:T(8,128)(2,1)} %param.29), calls=%async_computation.1 | async-start | bytes 5242880 | tf_op jit(solution)/shard_map/all_to_all | solution.py:172
  82.8 63.9 %all-gather.10.cloned.1.call-start = ((), (), s32[]{:S(2)}) async-start(), calls=%async_computation.11 | async-start | bytes 6144000 | tf_op jit(solution)/shard_map/all_gather | solution.py:244
  85.3 7.2 %copy-start.19 = (f32[1024]{0:T(1024)}, f32[1024]{0:T(1024)S(1)}, u32[]{:S(2)}) copy-start(f32[1024]{0:T(1024)S(1)} %broadcast_multiply_fusion.8) | copy-start | bytes 12292
  87.8 4.7 copy-start.27
  109.4 26.4 %copy-start.2 = (f32[1024,640]{1,0:T(8,128)}, f32[1024,640]{1,0:T(8,128)S(1)}, u32[]{:S(2)}) copy-start(f32[1024,640]{1,0:T(8,128)S(1)} %get-tuple-element.121) | copy-start | bytes 7864324
  122.0 65.1 %reduce-scatter.7.cloned.1.call-start = ((), (), s32[]{:S(2)}) async-start(), calls=%async_computation.13 | async-start | bytes 4915200 | tf_op jit(solution)/shard_map/reduce_scatter | solution.py:279
  129.4 3.4 collective-permute-start.2
  131.5 12.3 %collective-permute-start.3 = (bf16[1,640,64]{1,2,0:T(8,128)(2,1)S(1)}, bf16[1,640,64]{1,2,0:T(8,128)(2,1)S(1)}, u32[]{:S(2)}, u32[]{:S(2)}) collective-permute-start(bf16[1,640,64]{1,2,0:T(8,128)(2,1)S(1)} %get-tuple-element.98), channel_id=1, source_target_pairs={{4,0},{5,1},{6,2},{7,3},{12,8},{13,9},{14,10},{15,11},{20,16},{21,... | collective-permute-start | bytes 245768 | tf_op jit(solution)/shard_map/ppermute | solution.py:152
  149.3 9.6 %copy-start.5 = (bf16[5,4,160,640]{3,2,1,0:T(8,128)(2,1)}, bf16[5,4,160,640]{3,2,1,0:T(8,128)(2,1)S(1)}, u32[]{:S(2)}) copy-start(bf16[5,4,160,640]{3,2,1,0:T(8,128)(2,1)S(1)} %copy.64) | copy-start | bytes 12288004
  159.0 40.8 %copy-start.7 = (f32[1024,640]{1,0:T(8,128)}, f32[1024,640]{1,0:T(8,128)S(1)}, u32[]{:S(2)}) copy-start(f32[1024,640]{1,0:T(8,128)S(1)} %get-tuple-element.123) | copy-start | bytes 7864324
  175.8 23.9 %all-gather.12.cloned.1.call-start = ((), (), s32[]{:S(2)}) async-start(), calls=%async_computation.12 | async-start | bytes 2457600 | tf_op jit(solution)/shard_map/all_gather | solution.py:245
  177.5 62.0 %reduce-scatter.9.cloned.1.call-start = ((), (), s32[]{:S(2)}) async-start(), calls=%async_computation.14 | async-start | bytes 2048000 | tf_op jit(solution)/shard_map/reduce_scatter | solution.py:280
  187.2 113.0 %reduce-scatter.11.cloned.1.call-start = ((), (), s32[]{:S(2)}) async-start(), calls=%async_computation.15 | async-start | bytes 12288000 | tf_op jit(solution)/shard_map/reduce_scatter | solution.py:279
  211.5 3.6 copy-start.12
  245.6 4.3 copy-start.8
  248.6 34.3 %collective-permute-start.4 = (bf16[1,640,64]{1,2,0:T(8,128)(2,1)S(1)}, bf16[1,640,64]{1,2,0:T(8,128)(2,1)S(1)}, u32[]{:S(2)}, u32[]{:S(2)}) collective-permute-start(bf16[1,640,64]{1,2,0:T(8,128)(2,1)S(1)} %get-tuple-element.97), channel_id=1, source_target_pairs={{4,0},{5,1},{6,2},{7,3},{12,8},{13,9},{14,10},{15,11},{20,16},{21,... | collective-permute-start | bytes 245768 | tf_op jit(solution)/shard_map/ppermute | solution.py:152
  266.6 38.3 %all-to-all-start.2 = ((bf16[4,320,1024]{2,1,0:T(8,128)(2,1)}), bf16[4,320,1024]{2,1,0:T(8,128)(2,1)}, u32[]{:S(2)}, u32[]{:S(2)}) async-start(bf16[4,320,1024]{2,1,0:T(8,128)(2,1)} %bitcast.273), calls=%async_computation.4 | async-start | bytes 5242880 | tf_op jit(solution)/shard_map/all_to_all | solution.py:185
  271.2 102.9 %reduce-scatter.13.cloned.1.call-start = ((), (), s32[]{:S(2)}) async-start(), calls=%async_computation.16 | async-start | bytes 5120000 | tf_op jit(solution)/shard_map/reduce_scatter | solution.py:280
  271.2 12.6 %collective-permute-start.5 = (bf16[1,640,64]{1,2,0:T(8,128)(2,1)S(1)}, bf16[1,640,64]{1,2,0:T(8,128)(2,1)S(1)}, u32[]{:S(2)}, u32[]{:S(2)}) collective-permute-start(bf16[1,640,64]{1,2,0:T(8,128)(2,1)S(1)} %get-tuple-element.96), channel_id=1, source_target_pairs={{0,4},{1,5},{2,6},{3,7},{8,12},{9,13},{10,14},{11,15},{16,20},{17,... | collective-permute-start | bytes 245768 | tf_op jit(solution)/shard_map/ppermute | solution.py:151
  283.6 2.2 copy-start.14
  283.9 2.8 copy-start.3
  300.2 89.2 %reduce-scatter.15.cloned.1.call-start = ((), (), s32[]{:S(2)}) async-start(), calls=%async_computation.17 | async-start | bytes 5898240 | tf_op jit(solution)/shard_map/reduce_scatter | solution.py:279
  301.7 3.2 copy-start.20
  301.7 3.2 copy-start.22
  301.7 3.3 copy-start.28
  301.7 3.3 copy-start.30
  304.9 19.7 %copy-start.13 = (bf16[1,640,1024]{1,2,0:T(8,128)(2,1)S(1)}, bf16[1,640,1024]{1,2,0:T(8,128)(2,1)}, u32[]{:S(2)}) copy-start(bf16[1,640,1024]{1,2,0:T(8,128)(2,1)} %fusion.65) | copy-start | bytes 3932164
  376.9 12.7 %copy-start.11 = (f32[80,5,4,160]{3,2,1,0:T(4,128)}, f32[80,5,4,160]{3,2,1,0:T(4,128)S(1)}, u32[]{:S(2)}) copy-start(f32[80,5,4,160]{3,2,1,0:T(4,128)S(1)} %reshape.1425.refs_1_) | copy-start | bytes 3072004
  376.9 57.4 %reduce-scatter.17.cloned.1.call-start = ((), (), s32[]{:S(2)}) async-start(), calls=%async_computation.18 | async-start | bytes 2457600 | tf_op jit(solution)/shard_map/reduce_scatter | solution.py:280
  389.4 124.9 %all-gather.14.cloned.1.call-start = ((), (), s32[]{:S(2)}) async-start(), calls=%async_computation.19 | async-start | bytes 2416640 | tf_op jit(solution)/shard_map/all_gather | solution.py:345
  465.2 3.8 copy-start.16
  471.8 92.7 %all-gather.16.cloned.1.call-start = ((), (), s32[]{:S(2)}) async-start(), calls=%async_computation.20 | async-start | bytes 5799936 | tf_op jit(solution)/shard_map/all_gather | solution.py:346
  530.2 34.2 %all-to-all-start.3 = ((bf16[4,320,1024]{2,1,0:T(8,128)(2,1)}), bf16[4,320,1024]{2,1,0:T(8,128)(2,1)S(1)}, u32[]{:S(2)}, u32[]{:S(2)}) async-start(bf16[4,320,1024]{2,1,0:T(8,128)(2,1)} %bitcast.274), calls=%async_computation.5 | async-start | bytes 5242880 | tf_op jit(solution)/shard_map/all_to_all | solution.py:185
  564.5 4.3 copy-start.9
  588.0 3.6 copy-start.10
  588.0 5.1 copy-start.1
  (5 other events, 6.1 us)
Sparse Core Ops, SparseCore 0:
  37.1 11.0 all-gather.7
  50.6 71.3 all-gather.17
  123.6 12.9 all-gather.9
  175.9 11.1 reduce-scatter.6
  188.6 11.0 all-gather.11
  202.0 37.4 reduce-scatter.8
  241.8 15.6 reduce-scatter.10
  300.3 73.7 reduce-scatter.12
  377.0 12.2 reduce-scatter.14
  391.6 42.5 reduce-scatter.16
  471.9 42.3 all-gather.13
  515.8 12.0 all-gather.15
